TPU v7x, 32 devices: a whole 2x2x4 slice. The times are simulated.
32 devices in a mesh: fsdp: 16 (over z, y, x), dp: 2 (over core).
Axes of the slice: x: 2, y: 2, z: 4, core: 2. Of those that a mesh axis runs over, the one named last changes fastest.
Arguments:
- byte_ids: int32 [64, 1024], P(('fsdp', 'dp')), may hold values from 0 to 255
- lengths: int32 [64], P(('fsdp', 'dp')), may hold values from 256 to 1024, as said below
- cotangent: bfloat16 [64, 512, 768], P(('fsdp', 'dp')), may hold values from -6 to 6
- table: float32 [256, 768], P('fsdp'), may hold values from -6 to 6
- kernel: float32 [3072, 768], P('fsdp'), may hold values from -0.109375 to 0.109375
- project: float32 [768, 2304], P('fsdp'), may hold values from -0.21875 to 0.21875
- combine: float32 [768, 768], P('fsdp'), may hold values from -2.5 to 2.5
- expand: float32 [768, 4096], P('fsdp'), may hold values from -0.21875 to 0.21875
- contract: float32 [2048, 768], P('fsdp'), may hold values from -0.125 to 0.125
- vectors: float32 [4, 768], P(None, 'fsdp'), as said below
- table_first: float32 [256, 768], P('fsdp')
- table_rows: float32 [256], P('fsdp'), as said below
- table_columns: float32 [768], replicated, as said below
- kernel_first: float32 [3072, 768], P('fsdp')
- kernel_rows: float32 [3072], P('fsdp'), as said below
- kernel_columns: float32 [768], replicated, as said below
- project_first: float32 [768, 2304], P('fsdp')
- project_rows: float32 [768], P('fsdp'), as said below
- project_columns: float32 [2304], replicated, as said below
- combine_first: float32 [768, 768], P('fsdp')
- combine_rows: float32 [768], P('fsdp'), as said below
- combine_columns: float32 [768], replicated, as said below
- expand_first: float32 [768, 4096], P('fsdp')
- expand_rows: float32 [768], P('fsdp'), as said below
- expand_columns: float32 [4096], replicated, as said below
- contract_first: float32 [2048, 768], P('fsdp')
- contract_rows: float32 [2048], P('fsdp'), as said below
- contract_columns: float32 [768], replicated, as said below
- vectors_first: float32 [4, 768], P(None, 'fsdp')
- vectors_second: float32 [4, 768], P(None, 'fsdp'), as said below
Outputs:
- encoded: float32 [64, 512, 768], P(('fsdp', 'dp'))
- global_norm: float32 [], replicated
- table_next: float32 [256, 768], P('fsdp')
- table_momentum: float32 [256, 768], P('fsdp')
- table_rowstat: float32 [256], P('fsdp')
- table_colstat: float32 [768], replicated
- table_copy: bfloat16 [256, 768], P('fsdp')
- kernel_next: float32 [3072, 768], P('fsdp')
- kernel_momentum: float32 [3072, 768], P('fsdp')
- kernel_rowstat: float32 [3072], P('fsdp')
- kernel_colstat: float32 [768], replicated
- kernel_copy: bfloat16 [3072, 768], P('fsdp')
- project_next: float32 [768, 2304], P('fsdp')
- project_momentum: float32 [768, 2304], P('fsdp')
- project_rowstat: float32 [768], P('fsdp')
- project_colstat: float32 [2304], replicated
- project_copy: bfloat16 [768, 2304], P('fsdp')
- combine_next: float32 [768, 768], P('fsdp')
- combine_momentum: float32 [768, 768], P('fsdp')
- combine_rowstat: float32 [768], P('fsdp')
- combine_colstat: float32 [768], replicated
- combine_copy: bfloat16 [768, 768], P('fsdp')
- expand_next: float32 [768, 4096], P('fsdp')
- expand_momentum: float32 [768, 4096], P('fsdp')
- expand_rowstat: float32 [768], P('fsdp')
- expand_colstat: float32 [4096], replicated
- expand_copy: bfloat16 [768, 4096], P('fsdp')
- contract_next: float32 [2048, 768], P('fsdp')
- contract_momentum: float32 [2048, 768], P('fsdp')
- contract_rowstat: float32 [2048], P('fsdp')
- contract_colstat: float32 [768], replicated
- contract_copy: bfloat16 [2048, 768], P('fsdp')
- vectors_next: float32 [4, 768], P(None, 'fsdp')
- vectors_momentum: float32 [4, 768], P(None, 'fsdp')
- vectors_variance: float32 [4, 768], P(None, 'fsdp')
- vectors_copy: bfloat16 [4, 768], P(None, 'fsdp')
Inputs may be any that keep to these rules, and one draw needn't show every extreme that they name: lengths reach 1024 and 256 in every draw. `vectors`: gains are positive. `table_rows`: every entry is positive. `table_columns`: every entry is positive. `kernel_rows`: every entry is positive. `kernel_columns`: every entry is positive. `project_rows`: every entry is positive. `project_columns`: every entry is positive. `combine_rows`: every entry is positive. `combine_columns`: every entry is positive. `expand_rows`: every entry is positive. `expand_columns`: every entry is positive. `contract_rows`: every entry is positive. `contract_columns`: every entry is positive. `vectors_second`: every entry is positive.
All inputs are finite; a program needn't handle non-finite values.
Results may differ from a plain program's by a relative error of at most 0.018.
Values may be sent and summed in bfloat16 or wider, within the bound.
A program may use at most 320 MiB of HBM per device.

v0:
```python
import jax
import jax.numpy as jnp
from jax import lax
from jax.sharding import PartitionSpec as P

D = 768
H = 12
V = 256
KS = 4


eps_norm = 1e-06
beta_one = 0.9
beta_two = 0.999
eps_square = 1e-30
eps_divide = 1e-08
learn_rate = 1.0
weight_decay = 0.01
clip_limit = 1.0
first_fix = 1.0 - 0.9**10
second_fix = 1.0 - 0.999**10
masked_score = -1000000000.0


def pool_mean(hidden, block_size):
    count_rows = hidden.shape[0]
    count_blocks = -(-count_rows // block_size)
    padded = jnp.pad(hidden, ((0, count_blocks * block_size - count_rows), (0, 0)))
    totals = padded.reshape(count_blocks, block_size, hidden.shape[1]).sum(axis=1)
    offsets = jnp.arange(count_blocks, dtype=jnp.int32) * block_size
    counts = jnp.minimum(block_size, count_rows - offsets).astype(hidden.dtype)
    return jnp.repeat(totals / counts[:, None], block_size, axis=0)[:count_rows]


def gbst_mix(hidden, scorer):
    pooled = jnp.stack([pool_mean(hidden, block_size) for block_size in (1, 2, 3, 4)])
    scores = jnp.sum(pooled * scorer, axis=-1)
    mixing = jax.nn.softmax(scores, axis=0)
    blended = jnp.sum(mixing[:, :, None] * pooled, axis=0)
    return blended.reshape(blended.shape[0] // 2, 2, blended.shape[1]).mean(axis=1)


def mix_items(hidden_all, scorer):
    return jax.vmap(gbst_mix, in_axes=(0, None))(hidden_all, scorer)


def rms_norm(values, gain):
    return values * lax.rsqrt(jnp.mean(values * values, axis=-1, keepdims=True) + eps_norm) * gain


def gated(joined):
    half_size = joined.shape[-1] // 2
    return jax.nn.gelu(joined[..., :half_size], approximate=True) * joined[..., half_size:]


def masked_scores(queries, keys_all, key_valid):
    raw_scores = jnp.einsum("qhe,khe->hqk", queries, keys_all, preferred_element_type=jnp.float32)
    return jnp.where(key_valid[None, None, :], raw_scores * (D // H) ** (-0.5), masked_score)


def attend_forward(packed):
    queries, keys_all, values_all, key_valid = packed
    scores = masked_scores(queries, keys_all, key_valid)
    row_max = jnp.max(scores, axis=-1, keepdims=True)
    expd = jnp.exp(scores - row_max)
    row_total = jnp.sum(expd, axis=-1, keepdims=True)
    weights_att = (expd / row_total).astype(jnp.bfloat16)
    attended = jnp.einsum(
        "hqk,khe->qhe", weights_att, values_all, preferred_element_type=jnp.float32
    )
    return (attended.astype(jnp.bfloat16), row_max + jnp.log(row_total))


def attend_backward(packed):
    queries, keys_all, values_all, key_valid, upstream, log_total = packed
    count_tok = queries.shape[0]
    scores = masked_scores(queries, keys_all, key_valid)
    weights_att = jnp.exp(scores - log_total)
    grad_weights = jnp.einsum(
        "qhe,khe->hqk", upstream, values_all, preferred_element_type=jnp.float32
    )
    row_dot = jnp.sum(grad_weights * weights_att, axis=-1, keepdims=True)
    grad_scores = (weights_att * (grad_weights - row_dot) * (D // H) ** (-0.5)).astype(jnp.bfloat16)
    grad_query = jnp.einsum(
        "hqk,khe->qhe", grad_scores, keys_all, preferred_element_type=jnp.float32
    )
    grad_key = jnp.einsum("hqk,qhe->khe", grad_scores, queries, preferred_element_type=jnp.float32)
    grad_value = jnp.einsum(
        "hqk,qhe->khe",
        weights_att.astype(jnp.bfloat16),
        upstream,
        preferred_element_type=jnp.float32,
    )
    return jnp.concatenate(
        [
            grad_query.reshape(count_tok, D),
            grad_key.reshape(count_tok, D),
            grad_value.reshape(count_tok, D),
        ],
        axis=-1,
    ).astype(jnp.bfloat16)


def body(
    byte_ids,
    lengths,
    cotangent,
    table,
    kernel,
    project,
    combine,
    expand,
    contract,
    vectors,
    table_first,
    table_rows,
    table_columns,
    kernel_first,
    kernel_rows,
    kernel_columns,
    project_first,
    project_rows,
    project_columns,
    combine_first,
    combine_rows,
    combine_columns,
    expand_first,
    expand_rows,
    expand_columns,
    contract_first,
    contract_rows,
    contract_columns,
    vectors_first,
    vectors_second,
):
    masters = (table, kernel, project, combine, expand, contract, vectors)
    lowered = [master.astype(jnp.bfloat16) for master in masters]
    gathered = (
        lax.all_gather(lowered[0], "fsdp", axis=0, tiled=True),
        lax.all_gather(lowered[1], "fsdp", axis=0, tiled=True),
        lax.all_gather(lowered[2], "fsdp", axis=0, tiled=True),
        lax.all_gather(lowered[3], "fsdp", axis=0, tiled=True),
        lax.all_gather(lowered[4], "fsdp", axis=0, tiled=True),
        lax.all_gather(lowered[5], "fsdp", axis=0, tiled=True),
        lax.all_gather(lowered[6], "fsdp", axis=1, tiled=True),
    )
    (
        complete_table,
        complete_kernel,
        full_project,
        full_combine,
        full_expand,
        full_contract,
        full_vectors,
    ) = gathered
    vector_vals = full_vectors.astype(jnp.float32)
    count_items, count_bytes = byte_ids.shape
    count_tok = count_bytes // 2
    head_size = D // H
    positions = lax.broadcasted_iota(jnp.int32, (count_items, count_bytes), 1)
    byte_mask = (positions < lengths[:, None]).astype(jnp.bfloat16)
    one_hot_bytes = (byte_ids[:, :, None] == lax.broadcasted_iota(jnp.int32, (1, 1, V), 2)).astype(
        jnp.bfloat16
    )
    embedded_bytes = jnp.einsum(
        "rpq,qc->rpc", one_hot_bytes, complete_table, preferred_element_type=jnp.float32
    )
    embedded_bytes = embedded_bytes.astype(jnp.bfloat16) * byte_mask[:, :, None]
    padded = jnp.concatenate(
        [jnp.zeros((count_items, KS - 1, D), jnp.bfloat16), embedded_bytes], axis=1
    )
    byte_windows = jnp.concatenate(
        [padded[:, shift_at : shift_at + count_bytes] for shift_at in range(KS)], axis=2
    )
    hidden = (
        jnp.einsum("hby,yj->hbj", byte_windows, complete_kernel, preferred_element_type=jnp.float32)
        + vector_vals[2]
    )
    tokens, gbst_pull = jax.vjp(mix_items, hidden, vector_vals[3])
    normed_full, norm_one_pull = jax.vjp(rms_norm, tokens, vector_vals[0])
    normed_one = normed_full.astype(jnp.bfloat16)
    joined_qkv = jnp.einsum(
        "std,de->ste", normed_one, full_project, preferred_element_type=jnp.float32
    )
    joined_qkv = joined_qkv.astype(jnp.bfloat16)
    queries = joined_qkv[..., :D].reshape(count_items, count_tok, H, head_size)
    keys_all = joined_qkv[..., D : 2 * D].reshape(count_items, count_tok, H, head_size)
    values_all = joined_qkv[..., 2 * D :].reshape(count_items, count_tok, H, head_size)
    key_valid = 2 * lax.broadcasted_iota(jnp.int32, (count_items, count_tok), 1) < lengths[:, None]
    attended, log_total = lax.map(attend_forward, (queries, keys_all, values_all, key_valid))
    attended_flat = attended.reshape(count_items, count_tok, D)
    branch = jnp.einsum(
        "std,de->ste", attended_flat, full_combine, preferred_element_type=jnp.float32
    )
    middle = tokens + branch
    normed_two_full, norm_two_pull = jax.vjp(rms_norm, middle, vector_vals[1])
    normed_two = normed_two_full.astype(jnp.bfloat16)
    joined = jnp.einsum("std,de->ste", normed_two, full_expand, preferred_element_type=jnp.float32)
    activated_full, gated_pull = jax.vjp(gated, joined)
    activated = activated_full.astype(jnp.bfloat16)
    encoded = middle + jnp.einsum(
        "stf,fd->std", activated, full_contract, preferred_element_type=jnp.float32
    )
    regathered = (
        lax.all_gather(lowered[0], "fsdp", axis=0, tiled=True),
        lax.all_gather(lowered[1], "fsdp", axis=0, tiled=True),
        lax.all_gather(lowered[2], "fsdp", axis=0, tiled=True),
        lax.all_gather(lowered[3], "fsdp", axis=0, tiled=True),
        lax.all_gather(lowered[4], "fsdp", axis=0, tiled=True),
        lax.all_gather(lowered[5], "fsdp", axis=0, tiled=True),
        lax.all_gather(lowered[6], "fsdp", axis=1, tiled=True),
    )
    (
        back_table,
        backward_kernel_matrix,
        back_project,
        back_combine,
        back_expand,
        back_contract,
        back_vectors,
    ) = regathered
    grad_out = cotangent.astype(jnp.float32)
    grad_contract = jnp.einsum(
        "stf,std->fd", activated, cotangent, preferred_element_type=jnp.float32
    )
    grad_activated = jnp.einsum(
        "std,fd->stf", cotangent, back_contract, preferred_element_type=jnp.float32
    )
    (grad_joined,) = gated_pull(grad_activated)
    grad_joined_low = grad_joined.astype(jnp.bfloat16)
    grad_expand = jnp.einsum(
        "std,ste->de", normed_two, grad_joined_low, preferred_element_type=jnp.float32
    )
    grad_normed_two = jnp.einsum(
        "ste,de->std", grad_joined_low, back_expand, preferred_element_type=jnp.float32
    )
    grad_middle_norm, grad_gain_two = norm_two_pull(grad_normed_two)
    grad_middle = grad_out + grad_middle_norm
    grad_branch_low = grad_middle.astype(jnp.bfloat16)
    grad_combine = jnp.einsum(
        "std,ste->de", attended_flat, grad_branch_low, preferred_element_type=jnp.float32
    )
    grad_attended = jnp.einsum(
        "ste,de->std", grad_branch_low, back_combine, preferred_element_type=jnp.float32
    )
    grad_attended = grad_attended.astype(jnp.bfloat16).reshape(count_items, count_tok, H, head_size)
    grad_qkv = lax.map(
        attend_backward, (queries, keys_all, values_all, key_valid, grad_attended, log_total)
    )
    grad_project = jnp.einsum(
        "std,ste->de", normed_one, grad_qkv, preferred_element_type=jnp.float32
    )
    grad_normed_one = jnp.einsum(
        "ste,de->std", grad_qkv, back_project, preferred_element_type=jnp.float32
    )
    grad_tokens_norm, grad_gain_one = norm_one_pull(grad_normed_one)
    grad_tokens = grad_middle + grad_tokens_norm
    grad_hidden, grad_scorer = gbst_pull(grad_tokens)
    gradient_hidden_reduced = grad_hidden.astype(jnp.bfloat16)
    grad_bias = jnp.sum(gradient_hidden_reduced.astype(jnp.float32), axis=(0, 1))
    grad_kernel = jnp.einsum(
        "xwu,xwo->uo", byte_windows, gradient_hidden_reduced, preferred_element_type=jnp.float32
    )
    grad_windows = jnp.einsum(
        "njc,ic->nji",
        gradient_hidden_reduced,
        backward_kernel_matrix,
        preferred_element_type=jnp.float32,
    )
    grad_padded = jnp.zeros((count_items, count_bytes + KS - 1, D), jnp.float32)
    for shift_at in range(KS):
        piece_grad = grad_windows[:, :, shift_at * D : (shift_at + 1) * D]
        grad_padded = grad_padded + jnp.pad(
            piece_grad, ((0, 0), (shift_at, KS - 1 - shift_at), (0, 0))
        )
    gradient_embedded_bytes = grad_padded[:, KS - 1 :].astype(jnp.bfloat16) * byte_mask[:, :, None]
    grad_table = jnp.einsum(
        "xpg,xpz->gz", one_hot_bytes, gradient_embedded_bytes, preferred_element_type=jnp.float32
    )
    grad_vectors = jnp.stack([grad_gain_one, grad_gain_two, grad_bias, grad_scorer])
    shards = (
        lax.psum_scatter(grad_table, "fsdp", scatter_dimension=0, tiled=True),
        lax.psum_scatter(grad_kernel, "fsdp", scatter_dimension=0, tiled=True),
        lax.psum_scatter(grad_project, "fsdp", scatter_dimension=0, tiled=True),
        lax.psum_scatter(grad_combine, "fsdp", scatter_dimension=0, tiled=True),
        lax.psum_scatter(grad_expand, "fsdp", scatter_dimension=0, tiled=True),
        lax.psum_scatter(grad_contract, "fsdp", scatter_dimension=0, tiled=True),
        lax.psum_scatter(grad_vectors, "fsdp", scatter_dimension=1, tiled=True),
    )
    shards = (
        lax.psum(shards[0].astype(jnp.bfloat16), "dp").astype(jnp.float32),
        lax.psum(shards[1].astype(jnp.bfloat16), "dp").astype(jnp.float32),
        lax.psum(shards[2].astype(jnp.bfloat16), "dp").astype(jnp.float32),
        lax.psum(shards[3].astype(jnp.bfloat16), "dp").astype(jnp.float32),
        lax.psum(shards[4].astype(jnp.bfloat16), "dp").astype(jnp.float32),
        lax.psum(shards[5].astype(jnp.bfloat16), "dp").astype(jnp.float32),
        lax.psum(shards[6].astype(jnp.bfloat16), "dp").astype(jnp.float32),
    )
    count_fsdp = lax.axis_size("fsdp")
    firsts = (table_first, kernel_first, project_first, combine_first, expand_first, contract_first)
    rows_old = (table_rows, kernel_rows, project_rows, combine_rows, expand_rows, contract_rows)
    cols_old = (
        table_columns,
        kernel_columns,
        project_columns,
        combine_columns,
        expand_columns,
        contract_columns,
    )
    col_widths = [shards[index_param].shape[1] for index_param in range(6)]
    rows_full = [shards[index_param].shape[0] * count_fsdp for index_param in range(6)]
    col_starts = [sum(col_widths[:index_param]) for index_param in range(6)]
    squares = [shard * shard for shard in shards]
    local_totals = jnp.stack([jnp.sum(square) for square in squares])
    weight_sq = jnp.stack(
        [jnp.sum(masters[index_param] * masters[index_param]) for index_param in range(6)]
    )
    vector_sq = jnp.sum(vectors * vectors, axis=1)
    rowstats = []
    mean_rows = []
    sum_all = lax.psum(jnp.sum(local_totals), "fsdp")
    global_norm = jnp.sqrt(sum_all)
    factor = jnp.minimum(1.0, clip_limit / global_norm)
    clipped_sq = [
        shards[index_param] * factor * (shards[index_param] * factor) for index_param in range(6)
    ]
    for index_param in range(6):
        row_part = jnp.mean(clipped_sq[index_param], axis=1)
        rowstats.append(
            beta_two * rows_old[index_param] + (1.0 - beta_two) * (row_part + eps_square)
        )
    new_rows = jnp.stack([jnp.sum(entry) for entry in rowstats])
    column_all = jnp.concatenate(
        [jnp.sum(clipped_sq[index_param], axis=0) for index_param in range(6)]
    )
    sum_rows, sum_weights, sum_vectors, column_scaled = lax.psum(
        (new_rows, weight_sq, vector_sq, column_all), "fsdp"
    )
    for index_param in range(6):
        mean_rows.append(sum_rows[index_param] / rows_full[index_param])
    results = [encoded, global_norm]
    for index_param in range(6):
        master = masters[index_param]
        clipped = shards[index_param] * factor
        momentum = beta_one * firsts[index_param] + (1.0 - beta_one) * clipped
        column_piece = lax.slice_in_dim(
            column_scaled,
            col_starts[index_param],
            col_starts[index_param] + col_widths[index_param],
        )
        colstat = beta_two * cols_old[index_param] + (1.0 - beta_two) * (
            column_piece / rows_full[index_param] + eps_square
        )
        rowstat = rowstats[index_param]
        second = rowstat[:, None] * colstat[None, :] / mean_rows[index_param] / second_fix
        update = momentum / first_fix / (jnp.sqrt(second) + eps_divide)
        spread = jnp.maximum(
            jnp.sqrt(sum_weights[index_param] / (rows_full[index_param] * col_widths[index_param])),
            0.001,
        )
        nextval = master * (1.0 - learn_rate * weight_decay) - learn_rate * spread * update
        results += [nextval, momentum, rowstat, colstat, nextval.astype(jnp.bfloat16)]
    clipped = shards[6] * factor
    momentum = beta_one * vectors_first + (1.0 - beta_one) * clipped
    variance = beta_two * vectors_second + (1.0 - beta_two) * (clipped * clipped + eps_square)
    update = momentum / first_fix / (jnp.sqrt(variance / second_fix) + eps_divide)
    spread = jnp.maximum(jnp.sqrt(sum_vectors / D), 0.001)[:, None]
    nextval = vectors * (1.0 - learn_rate * weight_decay) - learn_rate * spread * update
    results += [nextval, momentum, variance, nextval.astype(jnp.bfloat16)]
    return tuple(results)


def solution(mesh):
    in_specs = (
        P(("fsdp", "dp"), None),
        P(("fsdp", "dp")),
        P(("fsdp", "dp"), None, None),
        P("fsdp", None),
        P("fsdp", None),
        P("fsdp", None),
        P("fsdp", None),
        P("fsdp", None),
        P("fsdp", None),
        P(None, "fsdp"),
        P("fsdp", None),
        P("fsdp"),
        P(),
        P("fsdp", None),
        P("fsdp"),
        P(),
        P("fsdp", None),
        P("fsdp"),
        P(),
        P("fsdp", None),
        P("fsdp"),
        P(),
        P("fsdp", None),
        P("fsdp"),
        P(),
        P("fsdp", None),
        P("fsdp"),
        P(),
        P(None, "fsdp"),
        P(None, "fsdp"),
    )
    out_specs = (
        P(("fsdp", "dp"), None, None),
        P(),
        P("fsdp", None),
        P("fsdp", None),
        P("fsdp"),
        P(),
        P("fsdp", None),
        P("fsdp", None),
        P("fsdp", None),
        P("fsdp"),
        P(),
        P("fsdp", None),
        P("fsdp", None),
        P("fsdp", None),
        P("fsdp"),
        P(),
        P("fsdp", None),
        P("fsdp", None),
        P("fsdp", None),
        P("fsdp"),
        P(),
        P("fsdp", None),
        P("fsdp", None),
        P("fsdp", None),
        P("fsdp"),
        P(),
        P("fsdp", None),
        P("fsdp", None),
        P("fsdp", None),
        P("fsdp"),
        P(),
        P("fsdp", None),
        P(None, "fsdp"),
        P(None, "fsdp"),
        P(None, "fsdp"),
        P(None, "fsdp"),
    )
    return jax.shard_map(body, mesh=mesh, in_specs=in_specs, out_specs=out_specs, check_vma=False)
```

profile of v0, /device:TPU:0, one launch (start us, length us, event | category | flops | bytes accessed | tf_op | source)
XLA Modules:
  0.0 1729.2 jit_solution(7530002485717873711)
XLA Ops:
  21.9 45.6 %all_gather.26 = bf16[256,768]{1,0:T(8,128)(2,1)S(1)} all-gather(bf16[16,768]{1,0:T(8,128)(2,1)S(1)} %get-tuple-element.260), channel_id=1, replica_groups=mesh['fsdp'=16,'dp'=2] {'fsdp'}, dimensions={0}, use_global_device_ids=true | all-gather | bytes 417792 | tf_op jit(solution)/shard_map/all_gather | solution.py:139
  76.2 36.2 %all-gather = bf16[16,48,4]{1,2,0:T(4,128)(2,1)S(1)} all-gather(bf16[1,48,4]{1,2,0:T(4,128)(2,1)S(1)} %get-tuple-element.268), channel_id=1, replica_groups=mesh['fsdp'=16,'dp'=2] {'fsdp'}, dimensions={0}, use_global_device_ids=true | all-gather | bytes 6528 | tf_op jit(solution)/shard_map/all_gather | solution.py:145
  113.2 13.9 broadcast_add_fusion
  244.2 15.2 multiply_reduce_fusion.3
  259.4 10.9 bitcast_reduce_fusion
  286.2 20.4 %while.22 = (s32[]{:T(128)}, bf16[2,512,12,64]{1,3,2,0:T(8,128)(2,1)}, f32[2,12,512,1]{2,1,3,0:T(8,128)S(1)}, bf16[2,512,12,64]{1,3,2,0:T(8,128)(2,1)}, pred[2,5...) while((s32[]{:T(128)}, ...), condition=%wide.region_12.13_spmd, body=%wide.region_9.0_spmd.sunk | while | flops 843442176 | bytes 47428216 | solution.py:190
  312.6 13.5 all-gather.13.cloned.1.call-done
  326.2 13.2 fusion.102
  339.3 56.5 %all-gather.15.cloned.1.call-done = bf16[2048,768]{1,0:T(8,128)(2,1)} async-done(((bf16[128,768]{1,0:T(8,128)(2,1)}), bf16[2048,768]{1,0:T(8,128)(2,1)}) %all-gather.15.cloned.1.call-update) | async-done | bytes 3145744 | tf_op jit(solution)/shard_map/all_gather | solution.py:144
  395.8 18.5 %fusion.121 = (f32[2,512,2048]{2,1,0:T(8,128)}, f32[2,512,2048]{2,1,0:T(8,128)}, bf16[2,512,2048]{2,1,0:T(8,128)(2,1)}) fusion(f32[2,512,4096]{2,1,0:T(8,128)} %fusion.102, bf16[2,512,768]{2,1,0:T(8,128)(2,1)} %param.36, bf16[2048,768]{1,0:T(8,128)(2,1)} %all-gather.15.cloned.1.call-done), kind=kOutput, calls=%fused_computation.145 | convolution fusion | flops 3271557120 | bytes 42467328 | tf_op jit(solution)/shard_map/std,fd->stf/dot_general | solution.py:226
  414.3 14.7 multiply_reduce_fusion.5
  454.2 133.0 %while.23 = (s32[]{:T(128)}, bf16[2,512,2304]{1,2,0:T(8,128)(2,1)}, bf16[2,512,12,64]{1,3,2,0:T(8,128)(2,1)S(1)}, pred[2,512]{1,0:T(4,128)(4,1)S(1)}, bf16[2,512...) while((s32[]{:T(128)}, bf16[2,512,2304]{1,2,0:T(8,128)(2,1)}, ...), condition=%wide.region_17.18_spmd, body=%wide.region_15.17_spmd.sunk | while | flops 2103325696 | bytes 170082000 | solution.py:247
  467.4 23.8 %fusion.280 = bf16[12,64,512]{2,1,0:T(8,128)(2,1)} fusion(f32[12,512,512]{1,2,0:T(8,128)} %fusion.279, f32[12,512,512]{1,2,0:T(8,128)} %fusion.277, f32[12,512]{1,0:T(8,128)S(1)} %dynamic-slice_bitcast_fusion.2, pred[512]{0:T(512)(128)(4,1)S(1)} %dynamic-slice_reduce_fusion.5, bf16[2,512,12,64]{1,3,2,0:T(8,128)(2,1)S(1)} %get-tuple-element.429, ...), kind=kOutput, calls=%fused_computation.43.clone.1 | convolution fusion | flops 437656064 | bytes 51971584 | tf_op jit(solution)/shard_map/while/body/eval_jaxpr/hqk,qhe->khe/dot_general | solution.py:87
  491.2 20.1 %fusion.281 = bf16[12,64,512]{2,1,0:T(8,128)(2,1)} fusion(f32[12,512,512]{1,2,0:T(8,128)} %fusion.279, f32[12,512,512]{1,2,0:T(8,128)} %fusion.277, f32[12,512]{1,0:T(8,128)S(1)} %dynamic-slice_bitcast_fusion.2, pred[512]{0:T(512)(128)(4,1)S(1)} %dynamic-slice_reduce_fusion.5, bf16[2,512,12,64]{1,3,2,0:T(8,128)(2,1)S(1)} %get-tuple-element.427, ...), kind=kOutput, calls=%fused_computation.42.clone.1 | convolution fusion | flops 437656064 | bytes 51971584 | tf_op jit(solution)/shard_map/while/body/eval_jaxpr/hqk,khe->qhe/dot_general | solution.py:84
  533.6 23.8 %fusion.280 = bf16[12,64,512]{2,1,0:T(8,128)(2,1)} fusion(f32[12,512,512]{1,2,0:T(8,128)} %fusion.279, f32[12,512,512]{1,2,0:T(8,128)} %fusion.277, f32[12,512]{1,0:T(8,128)S(1)} %dynamic-slice_bitcast_fusion.2, pred[512]{0:T(512)(128)(4,1)S(1)} %dynamic-slice_reduce_fusion.5, bf16[2,512,12,64]{1,3,2,0:T(8,128)(2,1)S(1)} %get-tuple-element.429, ...), kind=kOutput, calls=%fused_computation.43.clone.1 | convolution fusion | flops 437656064 | bytes 51971584 | tf_op jit(solution)/shard_map/while/body/eval_jaxpr/hqk,qhe->khe/dot_general | solution.py:87
  557.4 20.1 %fusion.281 = bf16[12,64,512]{2,1,0:T(8,128)(2,1)} fusion(f32[12,512,512]{1,2,0:T(8,128)} %fusion.279, f32[12,512,512]{1,2,0:T(8,128)} %fusion.277, f32[12,512]{1,0:T(8,128)S(1)} %dynamic-slice_bitcast_fusion.2, pred[512]{0:T(512)(128)(4,1)S(1)} %dynamic-slice_reduce_fusion.5, bf16[2,512,12,64]{1,3,2,0:T(8,128)(2,1)S(1)} %get-tuple-element.427, ...), kind=kOutput, calls=%fused_computation.42.clone.1 | convolution fusion | flops 437656064 | bytes 51971584 | tf_op jit(solution)/shard_map/while/body/eval_jaxpr/hqk,khe->qhe/dot_general | solution.py:84
  621.3 13.3 multiply_reduce_fusion.2
  643.9 12.9 slice_bitcast_fusion.1
  747.8 11.9 convert_reduce_fusion
  759.6 19.4 %convolution_bitcast_fusion.1 = f32[3072,768]{1,0:T(8,128)} fusion(bf16[2,1024,768]{2,1,0:T(8,128)(2,1)} %get-tuple-element.230, bf16[2,1024,768]{2,1,0:T(8,128)(2,1)S(1)} %copy-done.16, bf16[2,1024,768]{2,1,0:T(8,128)(2,1)} %get-tuple-element.248, bf16[2,1024,768]{2,1,0:T(8,128)(2,1)} %get-tuple-element.247, bf16[2,1024,768]{2,1,0:T(8,128)(2,1)} %get-tuple-element.246), kind=kOutput, calls=%fused_computation.113 | convolution fusion | flops 9714008064 | bytes 25165824 | tf_op jit(solution)/shard_map/xwu,xwo->uo/dot_general | solution.py:261
  781.0 17.3 convolution_bitcast_fusion
  808.9 18.1 %fusion.104 = f32[2,1024,3072]{2,1,0:T(8,128)} fusion(bf16[2,1024,768]{2,1,0:T(8,128)(2,1)} %get-tuple-element.230, bf16[3072,768]{1,0:T(8,128)(2,1)} %all-gather.7.cloned.1.call-done), kind=kOutput, calls=%fused_computation.118 | convolution fusion | flops 9663676416 | bytes 33030144 | tf_op jit(solution)/shard_map/njc,ic->nji/dot_general | solution.py:264
  826.9 17.5 %fusion.229 = (f32[2,1024,768]{2,1,0:T(8,128)}, f32[2,1024,768]{2,1,0:T(8,128)}, f32[2,1024,768]{2,1,0:T(8,128)}, f32[2,1024,768]{2,1,0:T(8,128)}) fusion(f32[2,1024,3072]{2,1,0:T(8,128)} %fusion.104), kind=kLoop, calls=%fused_computation.323 | loop fusion | bytes 50331648 | tf_op jit(solution)/shard_map/slice | solution.py:272
  844.8 10.8 fusion.128
  858.9 13.7 reduce-scatter.14.cloned.1.call-done
  874.4 174.7 %reduce-scatter.12.cloned.1.call-done = f32[192,768]{1,0:T(8,128)} async-done(((f32[3072,768]{1,0:T(8,128)}), f32[192,768]{1,0:T(8,128)}) %reduce-scatter.12.cloned.1.call-update) | async-done | bytes 589840 | tf_op jit(solution)/shard_map/reduce_scatter | solution.py:283
  1050.9 206.7 %reduce-scatter.18.cloned.1.call-done = f32[48,4096]{1,0:T(8,128)} async-done(((f32[768,4096]{1,0:T(8,128)}), f32[48,4096]{1,0:T(8,128)}) %reduce-scatter.18.cloned.1.call-update) | async-done | bytes 786448 | tf_op jit(solution)/shard_map/reduce_scatter | solution.py:286
  1264.0 120.5 %reduce-scatter.22.cloned.1.call-done = f32[48,4]{1,0:T(8,128)} async-done(((f32[768,4]{1,0:T(8,128)}), f32[48,4]{1,0:T(8,128)}) %reduce-scatter.22.cloned.1.call-update) | async-done | bytes 784
  1385.3 125.7 %reduce-scatter.10.cloned.1.call-done = f32[16,768]{1,0:T(8,128)} async-done(((f32[256,768]{1,0:T(8,128)}), f32[16,768]{1,0:T(8,128)}) %reduce-scatter.10.cloned.1.call-update) | async-done | bytes 49168 | tf_op jit(solution)/shard_map/reduce_scatter | solution.py:282
  1516.4 18.1 %all-reduce.14.cloned.1.call-done = (bf16[192,768]{1,0:T(8,128)(2,1)}, bf16[48,2304]{1,0:T(8,128)(2,1)}, bf16[48,768]{1,0:T(8,128)(2,1)}, bf16[48,4096]{1,0:T(8,128)(2,1)}, bf16[128,768]{1,0:T(8,128)(2,1)}) async-done(((bf16[192,768]{1,0:T(8,128)(2,1)}, bf16[48,2304]{1,0:T(8,128)(2,1)}, bf16[48,768]{1,0:T(8,128)(2,1)}, bf16[48,4096]{1,0:T(8,128)(2,1)}, bf16[128,768]{1,0:T(8,128)(2,1)}), ...) | async-done | bytes 1179664 | tf_op jit(solution)/shard_map/psum | solution.py:292
  1555.8 42.8 %psum.91 = f32[]{:T(128)} all-reduce(f32[]{:T(128)S(6)} %reduce_sum.583), channel_id=1, replica_groups=mesh['fsdp'=16,'dp'=2] {'fsdp'}, use_global_device_ids=true, to_apply=%region_49.50 | all-reduce | flops 1 | bytes 8 | tf_op jit(solution)/shard_map/psum | solution.py:321
  1625.7 72.3 %all-reduce.9 = (f32[6]{0:T(128)S(1)}, f32[9472]{0:T(1024)S(1)}, f32[6]{0:T(128)S(1)}, f32[4]{0:T(128)S(1)}) all-reduce(f32[6]{0:T(128)S(1)} %stack.91, f32[9472]{0:T(1024)} %constant_dynamic-update-slice_fusion, f32[6]{0:T(128)} %stack.84, f32[4]{0:T(128)} %get-tuple-element.267), channel_id=1, replica_groups=mesh['fsdp'=16,'dp'=2] {'fsdp'}, use_global_device_ids=true, to_apply=%region_76.77 | all-reduce | flops 9488 | bytes 75904 | tf_op jit(solution)/shard_map/psum | solution.py:336
  (366 shorter events, 476.8 us)
Async XLA Ops:
  7.2 106.0 %all-gather.7.cloned.1.call-start = ((), (), s32[]{:S(2)}) async-start(), calls=%async_computation.7 | async-start | bytes 5013504 | tf_op jit(solution)/shard_map/all_gather | solution.py:140
  9.9 261.7 %all-gather.9.cloned.1.call-start = ((), (), s32[]{:S(2)}) async-start(), calls=%async_computation.8 | async-start | bytes 3760128 | tf_op jit(solution)/shard_map/all_gather | solution.py:141
  12.5 294.0 %all-gather.11.cloned.1.call-start = ((), (), s32[]{:S(2)}) async-start(), calls=%async_computation.9 | async-start | bytes 1253376 | tf_op jit(solution)/shard_map/all_gather | solution.py:142
  14.9 311.3 %all-gather.13.cloned.1.call-start = ((), (), s32[]{:S(2)}) async-start(), calls=%async_computation.10 | async-start | bytes 6684672 | tf_op jit(solution)/shard_map/all_gather | solution.py:143
  17.8 378.0 %all-gather.15.cloned.1.call-start = ((), (), s32[]{:S(2)}) async-start(), calls=%async_computation.11 | async-start | bytes 3342336 | tf_op jit(solution)/shard_map/all_gather | solution.py:144
  20.3 835.4 %reduce-scatter.16.cloned.1.call-start = ((), (), s32[]{:S(2)}) async-start(), calls=%async_computation.15 | async-start | bytes 2506752 | tf_op jit(solution)/shard_map/reduce_scatter | solution.py:285
  20.3 147.7 %copy-start.53 = (f32[342]{0:T(512)}, f32[342]{0:T(512)S(1)}, u32[]{:S(2)}) copy-start(f32[342]{0:T(512)S(1)} %minimum_convert_fusion.1) | copy-start | bytes 4108
  20.3 174.7 %copy-start.51 = (f32[512]{0:T(512)}, f32[512]{0:T(512)S(1)}, u32[]{:S(2)}) copy-start(f32[512]{0:T(512)S(1)} %minimum_convert_fusion.2) | copy-start | bytes 6148
  20.4 194.7 %copy-start.64 = (f32[256]{0:T(256)}, f32[256]{0:T(256)S(1)}, u32[]{:S(2)}) copy-start(f32[256]{0:T(256)S(1)} %minimum_convert_fusion.3) | copy-start | bytes 3076
  20.4 206.5 %copy-start.44 = (f32[1024]{0:T(1024)}, f32[1024]{0:T(1024)S(1)}, u32[]{:S(2)}) copy-start(f32[1024]{0:T(1024)S(1)} %minimum_convert_fusion) | copy-start | bytes 12292
  113.1 117.3 %copy-start.48 = (f32[768]{0:T(1024)}, f32[768]{0:T(1024)S(1)}, u32[]{:S(2)}) copy-start(f32[768]{0:T(1024)S(1)} %get-tuple-element.152) | copy-start | bytes 9220
  113.1 158.5 %copy-start.55 = (f32[768]{0:T(1024)}, f32[768]{0:T(1024)S(1)}, u32[]{:S(2)}) copy-start(f32[768]{0:T(1024)S(1)} %get-tuple-element.151) | copy-start | bytes 9220
  437.9 419.4 %reduce-scatter.20.cloned.1.call-start = ((), (), s32[]{:S(2)}) async-start(), calls=%async_computation.17 | async-start | bytes 6684672 | tf_op jit(solution)/shard_map/reduce_scatter | solution.py:287
  446.8 425.9 %reduce-scatter.14.cloned.1.call-start = ((), (), s32[]{:S(2)}) async-start(), calls=%async_computation.14 | async-start | bytes 7520256 | tf_op jit(solution)/shard_map/reduce_scatter | solution.py:284
  454.2 133.0 %copy-start.56 = (f32[768]{0:T(1024)S(1)}, f32[768]{0:T(1024)}, u32[]{:S(2)}) copy-start(f32[768]{0:T(1024)} %copy-done.55) | copy-start | bytes 9220
  454.2 133.0 %copy-start.68 = (f32[2,512]{1,0:T(2,128)S(1)}, f32[2,512]{1,0:T(2,128)}, u32[]{:S(2)}) copy-start(f32[2,512]{1,0:T(2,128)} %copy-done.67) | copy-start | bytes 12292
  597.6 451.5 %reduce-scatter.12.cloned.1.call-start = ((), (), s32[]{:S(2)}) async-start(), calls=%async_computation.13 | async-start | bytes 10027008 | tf_op jit(solution)/shard_map/reduce_scatter | solution.py:283
  779.1 478.5 %reduce-scatter.18.cloned.1.call-start = ((), (), s32[]{:S(2)}) async-start(), calls=%async_computation.16 | async-start | bytes 13369344 | tf_op jit(solution)/shard_map/reduce_scatter | solution.py:286
  798.3 586.2 %reduce-scatter.22.cloned.1.call-start = ((), (), s32[]{:S(2)}) async-start(), calls=%async_computation.18 | async-start | bytes 417792
  844.5 666.5 %reduce-scatter.10.cloned.1.call-start = ((), (), s32[]{:S(2)}) async-start(), calls=%async_computation.12 | async-start | bytes 835584 | tf_op jit(solution)/shard_map/reduce_scatter | solution.py:282
  855.6 679.0 %all-reduce.14.cloned.1.call-start = ((), (), s32[]{:S(2)}) async-start(), calls=%async_computation.19 | async-start | bytes 2359296 | tf_op jit(solution)/shard_map/psum | solution.py:292
  1547.5 155.2 %copy-start.62 = (f32[4096]{0:T(1024)S(1)}, f32[4096]{0:T(1024)}, u32[]{:S(2)}) copy-start(f32[4096]{0:T(1024)} %param.58) | copy-start | bytes 49156
  1555.8 160.2 %copy-start.23 = (bf16[48,768]{1,0:T(8,128)(2,1)S(1)}, bf16[48,768]{1,0:T(8,128)(2,1)}, u32[]{:S(2)}) copy-start(bf16[48,768]{1,0:T(8,128)(2,1)} %get-tuple-element.192) | copy-start | bytes 221188
  1555.8 160.2 %copy-start.24 = (f32[48,768]{1,0:T(8,128)S(1)}, f32[48,768]{1,0:T(8,128)}, u32[]{:S(2)}) copy-start(f32[48,768]{1,0:T(8,128)} %param.40) | copy-start | bytes 442372
  1555.8 160.2 %copy-start.34 = (f32[48,768]{1,0:T(8,128)S(1)}, f32[48,768]{1,0:T(8,128)}, u32[]{:S(2)}) copy-start(f32[48,768]{1,0:T(8,128)} %param.53) | copy-start | bytes 442372
  1555.8 161.8 %copy-start.19 = (bf16[48,2304]{1,0:T(8,128)(2,1)S(1)}, bf16[48,2304]{1,0:T(8,128)(2,1)}, u32[]{:S(2)}) copy-start(bf16[48,2304]{1,0:T(8,128)(2,1)} %get-tuple-element.191) | copy-start | bytes 663556
  1555.8 161.8 %copy-start.20 = (f32[48,2304]{1,0:T(8,128)S(1)}, f32[48,2304]{1,0:T(8,128)}, u32[]{:S(2)}) copy-start(f32[48,2304]{1,0:T(8,128)} %param.39) | copy-start | bytes 1327108
  1555.8 161.8 %copy-start.26 = (f32[48,2304]{1,0:T(8,128)S(1)}, f32[48,2304]{1,0:T(8,128)}, u32[]{:S(2)}) copy-start(f32[48,2304]{1,0:T(8,128)} %param.50) | copy-start | bytes 1327108
  1555.8 163.1 %copy-start.17 = (bf16[192,768]{1,0:T(8,128)(2,1)S(1)}, bf16[192,768]{1,0:T(8,128)(2,1)}, u32[]{:S(2)}) copy-start(bf16[192,768]{1,0:T(8,128)(2,1)} %get-tuple-element.190) | copy-start | bytes 884740
  1555.8 163.1 %copy-start.18 = (f32[192,768]{1,0:T(8,128)S(1)}, f32[192,768]{1,0:T(8,128)}, u32[]{:S(2)}) copy-start(f32[192,768]{1,0:T(8,128)} %param.38) | copy-start | bytes 1769476
  1555.8 163.1 %copy-start.25 = (f32[192,768]{1,0:T(8,128)S(1)}, f32[192,768]{1,0:T(8,128)}, u32[]{:S(2)}) copy-start(f32[192,768]{1,0:T(8,128)} %param.47) | copy-start | bytes 1769476
  1603.8 116.8 %copy-start.30 = (bf16[16,768]{1,0:T(8,128)(2,1)S(1)}, bf16[16,768]{1,0:T(8,128)(2,1)}, u32[]{:S(2)}) copy-start(bf16[16,768]{1,0:T(8,128)(2,1)} %copy-done.29) | copy-start | bytes 73732
  (63 other events, 961.8 us)
Sparse Core Ops, SparseCore 0:
  11.4 86.9 all-gather.6
  101.7 69.8 all-gather.8
  175.0 54.6 all-gather.10
  232.9 93.1 all-gather.12
  329.3 66.4 all-gather.14
  438.0 126.9 reduce-scatter.15
  571.1 144.7 reduce-scatter.19
  722.1 150.5 reduce-scatter.13
  879.3 169.7 reduce-scatter.11
  1054.6 202.9 reduce-scatter.17
  1263.5 120.9 reduce-scatter.21
  1389.6 121.3 reduce-scatter.9
  1515.4 19.1 all-reduce.13
where the time goes:
time: 1740 us; the launch traced here: 1730 us
  waiting for transfers between devices  730 us (42%)
  matrix products  327 us (19%)
  local copies, waits for them, and re-layouts  228 us (13%)
  other arithmetic  213 us (12%)
  blocking collectives  200 us (11%)
  between operations  29.7 us (2%)
    reduce_scatter x1, waiting for transfers between devices, body(): lax.psum_scatter(grad_expand, 'fsdp', scatter_dimension=0, tiled=True)  207 us
    reduce_scatter x1, waiting for transfers between devices, body(): lax.psum_scatter(grad_kernel, 'fsdp', scatter_dimension=0, tiled=True)  175 us
    reduce_scatter x1, waiting for transfers between devices, body(): lax.psum_scatter(grad_table, 'fsdp', scatter_dimension=0, tiled=True)  126 us
    unnamed x14, waiting for transfers between devices  121 us
    psum x1, blocking collectives, body(): lax.psum((new_rows, weight_sq, vector_sq, column_all), 'fsdp')  72.3 us
    all_gather x1, waiting for transfers between devices, body(): lax.all_gather(lowered[5], 'fsdp', axis=0, tiled=True)  56.5 us
    dot_general x2, matrix products, attend_backward(): jnp.einsum('hqk,qhe->khe', grad_scores, queries, preferred_element_type=j...  47.6 us
    all_gather x1, blocking collectives, body(): lax.all_gather(lowered[0], 'fsdp', axis=0, tiled=True)  45.6 us
  transfers between devices with their start and end apart: 13, of which 8 were waited for; matrix products, arithmetic and copies ran while one was open for 38% of the time, Pallas kernels for 0%

commit v1 on v0

--- a/solution.py
+++ b/solution.py
@@ -134,25 +134,37 @@
     vectors_second,
 ):
     masters = (table, kernel, project, combine, expand, contract, vectors)
-    lowered = [master.astype(jnp.bfloat16) for master in masters]
-    gathered = (
-        lax.all_gather(lowered[0], "fsdp", axis=0, tiled=True),
-        lax.all_gather(lowered[1], "fsdp", axis=0, tiled=True),
-        lax.all_gather(lowered[2], "fsdp", axis=0, tiled=True),
-        lax.all_gather(lowered[3], "fsdp", axis=0, tiled=True),
-        lax.all_gather(lowered[4], "fsdp", axis=0, tiled=True),
-        lax.all_gather(lowered[5], "fsdp", axis=0, tiled=True),
-        lax.all_gather(lowered[6], "fsdp", axis=1, tiled=True),
-    )
-    (
-        complete_table,
-        complete_kernel,
-        full_project,
-        full_combine,
-        full_expand,
-        full_contract,
-        full_vectors,
-    ) = gathered
+    groups = ("fsdp", "dp")
+    count_all = lax.axis_size("fsdp") * lax.axis_size("dp")
+    core = lax.axis_index("dp")
+
+    def own_half(value, axis=0):
+        size = value.shape[axis] // 2
+        return lax.dynamic_slice_in_dim(value, core * size, size, axis=axis)
+
+    rows_table, rows_kernel, rows_contract = (
+        table.shape[0] // 2, kernel.shape[0] // 2, contract.shape[0] // 2)
+    vec_width = vectors.shape[1] // 2
+    vec_piece = own_half(vectors, axis=1).astype(jnp.bfloat16)
+    vec_block = jnp.pad(vec_piece, ((0, 8 - 4), (0, D - vec_width)))
+    first_group = jnp.concatenate(
+        [own_half(table).astype(jnp.bfloat16), own_half(kernel).astype(jnp.bfloat16),
+         own_half(contract).astype(jnp.bfloat16), vec_block], axis=0)
+    second_group = jnp.concatenate(
+        [own_half(project), own_half(combine), own_half(expand)], axis=1).astype(jnp.bfloat16)
+    first_all = lax.all_gather(first_group, groups, axis=0, tiled=True)
+    first_all = first_all.reshape(count_all, first_group.shape[0], D)
+    second_all = lax.all_gather(second_group, groups, axis=0, tiled=True)
+    at_kernel = rows_table
+    at_contract = at_kernel + rows_kernel
+    at_vec = at_contract + rows_contract
+    complete_table = first_all[:, :at_kernel].reshape(V, D)
+    complete_kernel = first_all[:, at_kernel:at_contract].reshape(KS * D, D)
+    full_contract = first_all[:, at_contract:at_vec].reshape(-1, D)
+    full_vectors = first_all[:, at_vec:at_vec + 4, :vec_width].transpose(1, 0, 2).reshape(4, D)
+    full_project = second_all[:, : 3 * D]
+    full_combine = second_all[:, 3 * D : 4 * D]
+    full_expand = second_all[:, 4 * D :]
     vector_vals = full_vectors.astype(jnp.float32)
     count_items, count_bytes = byte_ids.shape
     count_tok = count_bytes // 2
@@ -201,24 +213,9 @@
     encoded = middle + jnp.einsum(
         "stf,fd->std", activated, full_contract, preferred_element_type=jnp.float32
     )
-    regathered = (
-        lax.all_gather(lowered[0], "fsdp", axis=0, tiled=True),
-        lax.all_gather(lowered[1], "fsdp", axis=0, tiled=True),
-        lax.all_gather(lowered[2], "fsdp", axis=0, tiled=True),
-        lax.all_gather(lowered[3], "fsdp", axis=0, tiled=True),
-        lax.all_gather(lowered[4], "fsdp", axis=0, tiled=True),
-        lax.all_gather(lowered[5], "fsdp", axis=0, tiled=True),
-        lax.all_gather(lowered[6], "fsdp", axis=1, tiled=True),
-    )
-    (
-        back_table,
-        backward_kernel_matrix,
-        back_project,
-        back_combine,
-        back_expand,
-        back_contract,
-        back_vectors,
-    ) = regathered
+    back_contract, back_expand, back_combine, back_project = (
+        full_contract, full_expand, full_combine, full_project)
+    backward_kernel_matrix = complete_kernel
     grad_out = cotangent.astype(jnp.float32)
     grad_contract = jnp.einsum(
         "stf,std->fd", activated, cotangent, preferred_element_type=jnp.float32
@@ -278,25 +275,36 @@
         "xpg,xpz->gz", one_hot_bytes, gradient_embedded_bytes, preferred_element_type=jnp.float32
     )
     grad_vectors = jnp.stack([grad_gain_one, grad_gain_two, grad_bias, grad_scorer])
-    shards = (
-        lax.psum_scatter(grad_table, "fsdp", scatter_dimension=0, tiled=True),
-        lax.psum_scatter(grad_kernel, "fsdp", scatter_dimension=0, tiled=True),
-        lax.psum_scatter(grad_project, "fsdp", scatter_dimension=0, tiled=True),
-        lax.psum_scatter(grad_combine, "fsdp", scatter_dimension=0, tiled=True),
-        lax.psum_scatter(grad_expand, "fsdp", scatter_dimension=0, tiled=True),
-        lax.psum_scatter(grad_contract, "fsdp", scatter_dimension=0, tiled=True),
-        lax.psum_scatter(grad_vectors, "fsdp", scatter_dimension=1, tiled=True),
-    )
-    shards = (
-        lax.psum(shards[0].astype(jnp.bfloat16), "dp").astype(jnp.float32),
-        lax.psum(shards[1].astype(jnp.bfloat16), "dp").astype(jnp.float32),
-        lax.psum(shards[2].astype(jnp.bfloat16), "dp").astype(jnp.float32),
-        lax.psum(shards[3].astype(jnp.bfloat16), "dp").astype(jnp.float32),
-        lax.psum(shards[4].astype(jnp.bfloat16), "dp").astype(jnp.float32),
-        lax.psum(shards[5].astype(jnp.bfloat16), "dp").astype(jnp.float32),
-        lax.psum(shards[6].astype(jnp.bfloat16), "dp").astype(jnp.float32),
-    )
-    count_fsdp = lax.axis_size("fsdp")
+    width_project, width_expand = grad_project.shape[1], grad_expand.shape[1]
+    late_width = grad_contract.size // grad_project.shape[0]
+    early = jnp.concatenate(
+        [grad_project, grad_combine, grad_expand, grad_contract.reshape(-1, late_width)], axis=1
+    ).astype(jnp.bfloat16)
+    early_part = lax.psum_scatter(early, groups, scatter_dimension=0, tiled=True)
+    piece_vec = grad_vectors.reshape(4, count_all, vec_width).transpose(1, 0, 2)
+    piece_vec = jnp.pad(piece_vec.reshape(count_all, 1, 4 * vec_width),
+                        ((0, 0), (0, 7), (0, D - 4 * vec_width)))
+    late = jnp.concatenate(
+        [grad_kernel.reshape(count_all, -1, D), grad_table.reshape(count_all, -1, D), piece_vec],
+        axis=1).astype(jnp.bfloat16)
+    late_rows = late.shape[1]
+    late_part = lax.psum_scatter(late.reshape(-1, D), groups, scatter_dimension=0, tiled=True)
+    early_f = early_part.astype(jnp.float32)
+    late_f = late_part.astype(jnp.float32)
+    cut_a = width_project
+    cut_b = cut_a + D
+    cut_c = cut_b + width_expand
+    k_rows = grad_kernel.shape[0] // count_all
+    t_rows = grad_table.shape[0] // count_all
+    pieces = (
+        late_f[k_rows : k_rows + t_rows],
+        late_f[:k_rows],
+        early_f[:, :cut_a],
+        early_f[:, cut_a:cut_b],
+        early_f[:, cut_b:cut_c],
+        early_f[:, cut_c:].reshape(-1, D),
+    )
+    vec_part = late_f[k_rows + t_rows, : 4 * vec_width].reshape(4, vec_width)
     firsts = (table_first, kernel_first, project_first, combine_first, expand_first, contract_first)
     rows_old = (table_rows, kernel_rows, project_rows, combine_rows, expand_rows, contract_rows)
     cols_old = (
@@ -307,37 +315,52 @@
         expand_columns,
         contract_columns,
     )
+    grad_sq = [jnp.sum(piece * piece) for piece in pieces] + [jnp.sum(vec_part * vec_part)]
+    row_old_sums = [jnp.sum(own_half(entry)) for entry in rows_old]
+    weight_sq = [jnp.sum(jnp.square(own_half(masters[index_param]))) for index_param in range(6)]
+    vector_sq = jnp.sum(jnp.square(own_half(vectors, axis=1)), axis=1)
+    column_all = jnp.concatenate([jnp.sum(piece * piece, axis=0) for piece in pieces])
+    stats = jnp.concatenate(
+        [jnp.stack(grad_sq), jnp.stack(row_old_sums), jnp.stack(weight_sq), vector_sq, column_all])
+    stats = lax.psum(stats, groups)
+    sum_sq, sum_rows_old, sum_weights = stats[:7], stats[7:13], stats[13:19]
+    sum_vectors, column_scaled_raw = stats[19:23], stats[23:]
+    early_own = lax.all_gather(early_part, "dp", axis=0, tiled=True).astype(jnp.float32)
+    late_own = lax.all_gather(late_part.reshape(1, late_rows, D), "dp", axis=0, tiled=True)
+    late_own = late_own.astype(jnp.float32)
+    shards = (
+        late_own[:, k_rows : k_rows + t_rows].reshape(-1, D),
+        late_own[:, :k_rows].reshape(-1, D),
+        early_own[:, :cut_a],
+        early_own[:, cut_a:cut_b],
+        early_own[:, cut_b:cut_c],
+        early_own[:, cut_c:].reshape(-1, D),
+        late_own[:, k_rows + t_rows, : 4 * vec_width]
+        .reshape(2, 4, vec_width)
+        .transpose(1, 0, 2)
+        .reshape(4, 2 * vec_width),
+    )
+    count_fsdp = lax.axis_size("fsdp")
     col_widths = [shards[index_param].shape[1] for index_param in range(6)]
     rows_full = [shards[index_param].shape[0] * count_fsdp for index_param in range(6)]
     col_starts = [sum(col_widths[:index_param]) for index_param in range(6)]
-    squares = [shard * shard for shard in shards]
-    local_totals = jnp.stack([jnp.sum(square) for square in squares])
-    weight_sq = jnp.stack(
-        [jnp.sum(masters[index_param] * masters[index_param]) for index_param in range(6)]
-    )
-    vector_sq = jnp.sum(vectors * vectors, axis=1)
+    global_norm = jnp.sqrt(jnp.sum(sum_sq))
+    factor = jnp.minimum(1.0, clip_limit / global_norm)
+    factor_sq = factor * factor
+    column_scaled = column_scaled_raw * factor_sq
     rowstats = []
     mean_rows = []
-    sum_all = lax.psum(jnp.sum(local_totals), "fsdp")
-    global_norm = jnp.sqrt(sum_all)
-    factor = jnp.minimum(1.0, clip_limit / global_norm)
-    clipped_sq = [
-        shards[index_param] * factor * (shards[index_param] * factor) for index_param in range(6)
-    ]
     for index_param in range(6):
-        row_part = jnp.mean(clipped_sq[index_param], axis=1)
+        clipped_sq = shards[index_param] * factor * (shards[index_param] * factor)
+        row_part = jnp.mean(clipped_sq, axis=1)
         rowstats.append(
             beta_two * rows_old[index_param] + (1.0 - beta_two) * (row_part + eps_square)
         )
-    new_rows = jnp.stack([jnp.sum(entry) for entry in rowstats])
-    column_all = jnp.concatenate(
-        [jnp.sum(clipped_sq[index_param], axis=0) for index_param in range(6)]
-    )
-    sum_rows, sum_weights, sum_vectors, column_scaled = lax.psum(
-        (new_rows, weight_sq, vector_sq, column_all), "fsdp"
-    )
-    for index_param in range(6):
-        mean_rows.append(sum_rows[index_param] / rows_full[index_param])
+        total_new = beta_two * sum_rows_old[index_param] + (1.0 - beta_two) * (
+            factor_sq * sum_sq[index_param] / col_widths[index_param]
+            + rows_full[index_param] * eps_square
+        )
+        mean_rows.append(total_new / rows_full[index_param])
     results = [encoded, global_norm]
     for index_param in range(6):
         master = masters[index_param]

time: 1740 us -> 1120 us (0.64)
  waiting for transfers between devices: 730 us -> 271 us
  blocking collectives: 200 us -> 44.8 us
  matrix products: 327 us -> 303 us
    reduce_scatter x6 -> x2, waiting for transfers between devices: 521 us -> 195 us  [the longest x1 164 us: body(): lax.psum_scatter(early, groups, scatter_dimension=0, tiled=True)]
    unnamed x14 -> x4, waiting for transfers between devices: 121 us -> 0.07 us
    psum x3 -> x1, blocking collectives: 119 us -> 39.9 us  [body(): stats = lax.psum(stats, groups)]
    all_gather x2, blocking collectives: 81.8 us -> 4.9 us  [the longest x1 2.65 us: body(): lax.all_gather(early_part, 'dp', axis=0, tiled=True).astype(jnp.float32)]
    unnamed x159 -> x171, local copies, waits for them, and re-layouts: 43.4 us -> 20.7 us
    psum x1 -> x0, waiting for transfers between devices: 18.1 us -> none  [body(): lax.psum(shards[1].astype(jnp.bfloat16), 'dp').astype(jnp.float32)]
    reduce_sum x25, other arithmetic: 38.8 us -> 21.3 us  [the longest x6 8.45 us: body(): jnp.sum(jnp.square(own_half(masters[index_param])))]
    all_gather x5 -> x2, waiting for transfers between devices: 70 us -> 76 us  [the longest x1 76 us: body(): first_all = lax.all_gather(first_group, groups, axis=0, tiled=True)]
  transfers between devices with their start and end apart: 13 -> 4, of which waited for: 8 -> 3; matrix products, arithmetic and copies ran while one was open for 38% -> 24% of each run, Pallas kernels for 0% -> 0%
where the time goes in v1:
time: 1120 us; the launch traced here: 1110 us
  matrix products  303 us (27%)
  waiting for transfers between devices  271 us (24%)
  local copies, waits for them, and re-layouts  239 us (21%)
  other arithmetic  226 us (20%)
  blocking collectives  44.8 us (4%)
  between operations  29.2 us (3%)
    reduce_scatter x1, waiting for transfers between devices, body(): lax.psum_scatter(early, groups, scatter_dimension=0, tiled=True)  164 us
    all_gather x1, waiting for transfers between devices, body(): first_all = lax.all_gather(first_group, groups, axis=0, tiled=True)  76 us
    dot_general x2, matrix products, attend_backward(): jnp.einsum('hqk,qhe->khe', grad_scores, queries, preferred_element_type=j...  47.6 us
    dot_general x2, matrix products, attend_backward(): jnp.einsum('hqk,khe->qhe', grad_scores, keys_all, preferred_element_type=...  39.9 us
    psum x1, blocking collectives, body(): stats = lax.psum(stats, groups)  39.9 us
    reshape x4, local copies, waits for them, and re-layouts, pool_mean(): padded.reshape(count_blocks, block_size, hidden.shape[1]).sum(axis=1)  32.9 us
    reduce_scatter x1, waiting for transfers between devices, body(): lax.psum_scatter(late.reshape(-1, D), groups, scatter_dimension=0, tiled=...  31.8 us
    reduce_sum x2, other arithmetic, gbst_mix(): blended = jnp.sum(mixing[:, :, None] * pooled, axis=0)  26.5 us
  transfers between devices with their start and end apart: 4, of which 3 were waited for; matrix products, arithmetic and copies ran while one was open for 24% of the time, Pallas kernels for 0%

profile of v1, /device:TPU:0, one launch (start us, length us, event | category | flops | bytes accessed | tf_op | source)
XLA Modules:
  0.0 1113.9 jit_solution(17692676537140586452)
XLA Ops:
  16.8 76.0 %all-gather.4.cloned.1.call-done = bf16[5632,768]{1,0:T(8,128)(2,1)} async-done(((bf16[176,768]{1,0:T(8,128)(2,1)}), bf16[5632,768]{1,0:T(8,128)(2,1)}) %all-gather.4.cloned.1.call-update) | async-done | bytes 8650768 | tf_op jit(solution)/shard_map/all_gather | solution.py:155
  109.8 14.6 %broadcast_add_fusion = f32[2,1024,768]{2,1,0:T(8,128)} fusion(f32[768]{0:T(1024)S(1)} %add.337, bf16[3072,768,1]{1,0,2:T(8,128)(2,1)S(1)} %bitcast.276, bf16[2,1024,768]{2,1,0:T(8,128)(2,1)} %copy-done.17, bf16[2,1024,768]{2,1,0:T(8,128)(2,1)} %get-tuple-element.221, bf16[2,1024,768]{2,1,0:T(8,128)(2,1)} %get-tuple-element.220, ...), kind=kOutput, calls=%fused_computation.136 | convolution fusion | flops 9715580928 | bytes 23596032 | tf_op jit(solution)/shard_map/hby,yj->hbj/dot_general | solution.py:188
  132.0 10.3 copy.256
  195.6 10.3 reduce_sum.537
  219.7 10.3 copy_bitcast_fusion
  230.0 11.8 %multiply_reduce_fusion.4 = f32[2,4,1024]{2,0,1:T(2,128)S(1)} fusion(f32[768]{0:T(1024)S(1)} %mul.942, f32[1,2,1024,768]{3,2,1,0:T(8,128)} %reshape.495, f32[1,2,1024,768]{3,2,1,0:T(8,128)} %get-tuple-element.262, f32[1,2,1024,768]{3,2,1,0:T(8,128)} %reshape.491, f32[1,2,1024,768]{3,2,1,0:T(8,128)} %get-tuple-element.263), kind=kLoop, calls=%fused_computation.80 | loop fusion | flops 31449088 | bytes 25201664 | tf_op jit(solution)/shard_map/jvp(vmap())/reduce_sum | solution.py:37
  242.0 15.0 %multiply_reduce_fusion.3 = f32[2,1024,768]{2,1,0:T(8,128)} fusion(f32[2,4,1024]{2,0,1:T(2,128)S(1)} %bitcast.286, f32[1,2,1024,768]{3,2,1,0:T(8,128)} %reshape.495, f32[1,2,1024,768]{3,2,1,0:T(8,128)} %get-tuple-element.262, f32[1,2,1024,768]{3,2,1,0:T(8,128)} %reshape.491, f32[1,2,1024,768]{3,2,1,0:T(8,128)} %get-tuple-element.263), kind=kLoop, calls=%fused_computation.79 | loop fusion | flops 29884416 | bytes 31490048 | tf_op jit(solution)/shard_map/jvp(vmap())/reduce_sum | solution.py:39
  257.0 10.9 bitcast_reduce_fusion
  285.5 20.1 %while.22 = (s32[]{:T(128)}, bf16[2,512,12,64]{1,3,2,0:T(8,128)(2,1)}, f32[2,12,512,1]{2,1,3,0:T(8,128)S(1)}, bf16[2,512,12,64]{1,3,2,0:T(8,128)(2,1)}, pred[2,5...) while((s32[]{:T(128)}, ...), condition=%wide.region_12.13_spmd, body=%wide.region_9.12_spmd.sunk | while | flops 843442176 | bytes 47428224 | solution.py:202
  310.1 14.4 %fusion.103 = f32[2,512,4096]{2,1,0:T(8,128)} fusion(bf16[768,7168]{1,0:T(8,128)(2,1)} %all-gather.6.cloned.1.call-done, f32[2,512,768]{2,1,0:T(8,128)S(1)} %get-tuple-element.257, f32[768]{0:T(1024)S(1)} %copy-done.59, f32[2,512]{1,0:T(2,128)S(1)} %fusion.159), kind=kOutput, calls=%fused_computation.120 | convolution fusion | flops 6444810240 | bytes 26221568 | tf_op jit(solution)/shard_map/std,de->ste/dot_general | solution.py:210
  324.5 17.2 %bitcast_multiply_fusion.1 = (f32[2,512,2048]{2,1,0:T(8,128)}, f32[2,512,2048]{2,1,0:T(8,128)}, bf16[2,512,2048]{2,1,0:T(8,128)(2,1)}) fusion(f32[2,512,4096]{2,1,0:T(8,128)} %fusion.103, bf16[2048,768,1]{1,0,2:T(8,128)(2,1)S(1)} %bitcast.278, bf16[2,512,768]{2,1,0:T(8,128)(2,1)S(1)} %copy-done.26), kind=kOutput, calls=%fused_computation.97 | convolution fusion | flops 3271557120 | bytes 42467328 | tf_op jit(solution)/shard_map/std,fd->stf/dot_general | solution.py:223
  341.7 14.7 %multiply_reduce_fusion.5 = (bf16[768]{0:T(1024)(128)(2,1)}, f32[2,512]{1,0:T(2,128)S(1)}, f32[2,512,768]{2,1,0:T(8,128)}) fusion(f32[2,512,768]{2,1,0:T(8,128)} %copy-done.19, f32[2,512]{1,0:T(2,128)S(1)} %fusion.159, f32[768]{0:T(1024)S(1)} %copy-done.59, bf16[768,7168]{1,0:T(8,128)(2,1)} %all-gather.6.cloned.1.call-done, ...), kind=kOutput, calls=%fused_computation.128 | convolution fusion | flops 6455556096 | bytes 29372928 | tf_op jit(solution)/shard_map/ste,de->std/dot_general | solution.py:231
  368.6 121.0 %while.23 = (s32[]{:T(128)}, bf16[2,512,2304]{1,2,0:T(8,128)(2,1)}, bf16[2,512,12,64]{1,3,2,0:T(8,128)(2,1)S(1)}, pred[2,512]{1,0:T(4,128)(4,1)S(1)}, bf16[2,512...) while((s32[]{:T(128)}, bf16[2,512,2304]{1,2,0:T(8,128)(2,1)}, ...), condition=%wide.region_17.18_spmd, body=%wide.region_15.17_spmd.sunk | while | flops 2103325696 | bytes 214128336 | solution.py:244
  382.3 20.0 %fusion.237 = bf16[12,64,512]{2,1,0:T(8,128)(2,1)} fusion(f32[12,512,512]{1,2,0:T(8,128)} %fusion.235, f32[12,512,512]{1,2,0:T(8,128)} %copy-done, f32[12,512]{1,0:T(8,128)S(1)} %dynamic-slice_bitcast_fusion.2, pred[512]{0:T(512)(128)(4,1)S(1)} %dynamic-slice_reduce_fusion.11, bf16[2,512,12,64]{1,3,2,0:T(8,128)(2,1)S(1)} %get-tuple-element.404, ...), kind=kOutput, calls=%fused_computation.42.clone.1 | convolution fusion | flops 437656064 | bytes 51971076 | tf_op jit(solution)/shard_map/while/body/eval_jaxpr/hqk,khe->qhe/dot_general | solution.py:84
  402.3 23.8 %fusion.236 = bf16[12,64,512]{2,1,0:T(8,128)(2,1)} fusion(f32[12,512,512]{1,2,0:T(8,128)} %fusion.235, f32[12,512,512]{1,2,0:T(8,128)} %copy-done, f32[12,512]{1,0:T(8,128)S(1)} %dynamic-slice_bitcast_fusion.2, pred[512]{0:T(512)(128)(4,1)S(1)} %dynamic-slice_reduce_fusion.11, bf16[2,512,12,64]{1,3,2,0:T(8,128)(2,1)S(1)} %get-tuple-element.406, ...), kind=kOutput, calls=%fused_computation.43.clone.1 | convolution fusion | flops 437656064 | bytes 51971076 | tf_op jit(solution)/shard_map/while/body/eval_jaxpr/hqk,qhe->khe/dot_general | solution.py:87
  442.5 20.0 %fusion.237 = bf16[12,64,512]{2,1,0:T(8,128)(2,1)} fusion(f32[12,512,512]{1,2,0:T(8,128)} %fusion.235, f32[12,512,512]{1,2,0:T(8,128)} %copy-done, f32[12,512]{1,0:T(8,128)S(1)} %dynamic-slice_bitcast_fusion.2, pred[512]{0:T(512)(128)(4,1)S(1)} %dynamic-slice_reduce_fusion.11, bf16[2,512,12,64]{1,3,2,0:T(8,128)(2,1)S(1)} %get-tuple-element.404, ...), kind=kOutput, calls=%fused_computation.42.clone.1 | convolution fusion | flops 437656064 | bytes 51971076 | tf_op jit(solution)/shard_map/while/body/eval_jaxpr/hqk,khe->qhe/dot_general | solution.py:84
  462.5 23.8 %fusion.236 = bf16[12,64,512]{2,1,0:T(8,128)(2,1)} fusion(f32[12,512,512]{1,2,0:T(8,128)} %fusion.235, f32[12,512,512]{1,2,0:T(8,128)} %copy-done, f32[12,512]{1,0:T(8,128)S(1)} %dynamic-slice_bitcast_fusion.2, pred[512]{0:T(512)(128)(4,1)S(1)} %dynamic-slice_reduce_fusion.11, bf16[2,512,12,64]{1,3,2,0:T(8,128)(2,1)S(1)} %get-tuple-element.406, ...), kind=kOutput, calls=%fused_computation.43.clone.1 | convolution fusion | flops 437656064 | bytes 51971076 | tf_op jit(solution)/shard_map/while/body/eval_jaxpr/hqk,qhe->khe/dot_general | solution.py:87
  489.7 9.0 multiply_reduce_fusion.6
  513.0 11.5 %multiply_reduce_fusion.2 = f32[2,4,1024]{2,0,1:T(2,128)S(1)} fusion(f32[2,1024,768]{2,1,0:T(8,128)} %reshape.503, f32[1,2,1024,768]{3,2,1,0:T(8,128)} %reshape.495, f32[1,2,1024,768]{3,2,1,0:T(8,128)} %get-tuple-element.262, f32[1,2,1024,768]{3,2,1,0:T(8,128)} %reshape.491, f32[1,2,1024,768]{3,2,1,0:T(8,128)} %get-tuple-element.263), kind=kLoop, calls=%fused_computation.78 | loop fusion | flops 31449088 | bytes 31490048 | tf_op jit(solution)/shard_map/transpose(jvp(vmap()))/reduce_sum | solution.py:39
  533.7 9.2 multiply_add_fusion
  542.9 12.4 %slice_bitcast_fusion.1 = (f32[2,1024,768]{2,1,0:T(8,128)S(1)}, f32[1,2,1024,768]{3,2,1,0:T(8,128)}, f32[1,2,1024,768]{3,2,1,0:T(8,128)}) fusion(f32[4,2,1024,768]{3,2,1,0:T(8,128)} %multiply_add_fusion), kind=kLoop, calls=%fused_computation.109 | loop fusion | bytes 37748736 | tf_op jit(solution)/shard_map/transpose(jvp(vmap()))/unstack | solution.py:36
  596.2 10.3 reduce_sum.552
  645.8 11.5 %fusion.178 = (bf16[768]{0:T(1024)(128)(2,1)S(1)}, bf16[2,1024,768]{2,1,0:T(8,128)(2,1)}) fusion(f32[1024]{0:T(1024)S(1)} %copy-done.47, f32[4,2,1024,768]{3,2,1,0:T(8,128)} %multiply_add_fusion, f32[2,1024,768]{2,1,0:T(8,128)} %reshape.507, f32[2,1024,768]{2,1,0:T(8,128)} %reshape.504, f32[2,1024,768]{2,0,1:T(2,128)} %pad.85), kind=kLoop, calls=%fused_computation.312 | loop fusion | flops 9436416 | bytes 28317184 | tf_op jit(solution)/shard_map/reduce_sum | solution.py:257
  657.3 19.1 %bitcast_convert_fusion.1 = bf16[3072,768]{1,0:T(8,128)(2,1)} fusion(bf16[2,1024,768]{2,1,0:T(8,128)(2,1)} %get-tuple-element.203, bf16[2,1024,768]{2,1,0:T(8,128)(2,1)S(1)} %copy-done.18, bf16[2,1024,768]{2,1,0:T(8,128)(2,1)} %get-tuple-element.221, bf16[2,1024,768]{2,1,0:T(8,128)(2,1)} %get-tuple-element.220, bf16[2,1024,768]{2,1,0:T(8,128)(2,1)} %get-tuple-element.219), kind=kOutput, calls=%fused_computation.89 | convolution fusion | flops 9716367360 | bytes 20447232 | tf_op jit(solution)/shard_map/xwu,xwo->uo/dot_general | solution.py:258
  676.4 17.5 %fusion.184 = f32[2,1024,3072]{2,1,0:T(8,128)} fusion(bf16[2,1024,768]{2,1,0:T(8,128)(2,1)} %get-tuple-element.203, bf16[3072,768,1]{1,0,2:T(8,128)(2,1)} %bitcast.273), kind=kOutput, calls=%fused_computation.317 | convolution fusion | flops 9663676416 | bytes 33030144 | tf_op jit(solution)/shard_map/njc,ic->nji/dot_general | solution.py:261
  694.5 15.5 %fusion.180 = (f32[2,1024,768]{2,1,0:T(8,128)S(1)}, f32[2,1024,768]{2,1,0:T(8,128)}, f32[2,1024,768]{2,1,0:T(8,128)}, f32[2,1024,768]{2,1,0:T(8,128)}) fusion(f32[2,1024,3072]{2,1,0:T(8,128)} %fusion.184), kind=kLoop, calls=%fused_computation.313 | loop fusion | bytes 50331648 | tf_op jit(solution)/shard_map/slice | solution.py:269
  742.6 17.0 %bitcast_convert_fusion = bf16[768,4096]{1,0:T(8,128)(2,1)} fusion(f32[2,512,2048]{2,1,0:T(8,128)} %get-tuple-element.214, f32[2,512,2048]{2,1,0:T(8,128)} %get-tuple-element.213, f32[2,512,768]{2,1,0:T(8,128)} %copy-done.19, f32[768]{0:T(1024)S(1)} %copy-done.60, f32[2,512]{1,0:T(2,128)S(1)} %copy-done.66), kind=kOutput, calls=%fused_computation.84 | convolution fusion | flops 6456344576 | bytes 26221568 | tf_op jit(solution)/shard_map/std,ste->de/dot_general | solution.py:228
  766.8 9.5 pad_maximum_fusion
  799.3 31.8 %reduce-scatter.3.cloned.1.call-done = bf16[112,768]{1,0:T(8,128)(2,1)} async-done(((bf16[3584,768]{1,0:T(8,128)(2,1)}), bf16[112,768]{1,0:T(8,128)(2,1)}) %reduce-scatter.3.cloned.1.call-update) | async-done | bytes 172048 | tf_op jit(solution)/shard_map/reduce_scatter | solution.py:291
  836.3 163.7 %reduce-scatter.5.cloned.1.call-done = bf16[24,9216]{1,0:T(8,128)(2,1)} async-done(((bf16[768,9216]{1,0:T(8,128)(2,1)}), bf16[24,9216]{1,0:T(8,128)(2,1)}) %reduce-scatter.5.cloned.1.call-update) | async-done | bytes 442384 | tf_op jit(solution)/shard_map/reduce_scatter | solution.py:283
  1006.6 13.1 %concatenate.49 = f32[9495]{0:T(1024)S(1)} concatenate(f32[1]{0:T(128)} %bitcast.54, f32[1]{0:T(128)} %bitcast.55, f32[1]{0:T(128)} %bitcast.60, f32[1]{0:T(128)} %bitcast.61, f32[1]{0:T(128)} %bitcast.62, f32[1]{0:T(128)} %bitcast.63, f32[1]{0:T(128)} %bitcast.64, f32[1]{0:T(128)} %bitcast.65, f32[1]{0:T(128)} %bitcast.66, f32[1]{0:T(128)} %bitcast.67, f32[1]{0:T(128)} %bitcast.68, ...), dimensions={0} | concatenate | bytes 75960 | tf_op jit(solution)/shard_map/concatenate | solution.py:323
  1019.7 39.9 %psum.7 = f32[9495]{0:T(1024)S(1)} all-reduce(f32[9495]{0:T(1024)S(1)} %concatenate.49), channel_id=1, replica_groups=mesh['fsdp'=16,'dp'=2] {'fsdp','dp'}, use_global_device_ids=true, to_apply=%region_56.57 | all-reduce | flops 9495 | bytes 75960 | tf_op jit(solution)/shard_map/psum | solution.py:325
  (385 shorter events, 399.8 us)
Async XLA Ops:
  7.2 85.6 %all-gather.4.cloned.1.call-start = ((), (), s32[]{:S(2)}) async-start(), calls=%async_computation.2 | async-start | bytes 8921088 | tf_op jit(solution)/shard_map/all_gather | solution.py:155
  11.5 259.6 %all-gather.6.cloned.1.call-start = ((), (), s32[]{:S(2)}) async-start(), calls=%async_computation.3 | async-start | bytes 11354112 | tf_op jit(solution)/shard_map/all_gather | solution.py:157
  15.2 816.0 %reduce-scatter.3.cloned.1.call-start = ((), (), s32[]{:S(2)}) async-start(), calls=%async_computation.4 | async-start | bytes 5677056 | tf_op jit(solution)/shard_map/reduce_scatter | solution.py:291
  15.2 143.5 %copy-start.69 = (f32[256]{0:T(256)}, f32[256]{0:T(256)S(1)}, u32[]{:S(2)}) copy-start(f32[256]{0:T(256)S(1)} %minimum_convert_fusion.3) | copy-start | bytes 3076
  15.3 190.6 %copy-start.51 = (f32[512]{0:T(512)}, f32[512]{0:T(512)S(1)}, u32[]{:S(2)}) copy-start(f32[512]{0:T(512)S(1)} %minimum_convert_fusion.2) | copy-start | bytes 6148
  15.3 169.9 %copy-start.53 = (f32[342]{0:T(512)}, f32[342]{0:T(512)S(1)}, u32[]{:S(2)}) copy-start(f32[342]{0:T(512)S(1)} %minimum_convert_fusion.1) | copy-start | bytes 4108
  15.3 204.4 %copy-start.46 = (f32[1024]{0:T(1024)}, f32[1024]{0:T(1024)S(1)}, u32[]{:S(2)}) copy-start(f32[1024]{0:T(1024)S(1)} %minimum_convert_fusion) | copy-start | bytes 12292
  16.1 86.5 %copy-start.40 = (bf16[2,1024]{1,0:T(2,128)(2,1)}, bf16[2,1024]{1,0:T(2,128)(2,1)S(1)}, u32[]{:S(2)}) copy-start(bf16[2,1024]{1,0:T(2,128)(2,1)S(1)} %compare_convert_fusion) | copy-start | bytes 12292
  152.1 119.0 %copy-start.55 = (f32[768]{0:T(1024)}, f32[768]{0:T(1024)S(1)}, u32[]{:S(2)}) copy-start(f32[768]{0:T(1024)S(1)} %mul.952) | copy-start | bytes 9220
  152.2 77.8 %copy-start.44 = (f32[768]{0:T(1024)}, f32[768]{0:T(1024)S(1)}, u32[]{:S(2)}) copy-start(f32[768]{0:T(1024)S(1)} %mul.942) | copy-start | bytes 9220
  241.8 28.6 %copy-start.23 = (f32[2,4,1024]{2,0,1:T(2,128)}, f32[2,4,1024]{2,0,1:T(2,128)S(1)}, u32[]{:S(2)}) copy-start(f32[2,4,1024]{2,0,1:T(2,128)S(1)} %multiply_reduce_fusion.4) | copy-start | bytes 98308
  241.9 28.5 %copy-start.32 = (f32[2,1024]{1,0:T(2,128)}, f32[2,1024]{1,0:T(2,128)S(1)}, u32[]{:S(2)}) copy-start(f32[2,1024]{1,0:T(2,128)S(1)} %reduce_max.18) | copy-start | bytes 24580
  241.9 28.5 %copy-start.34 = (f32[2,1024]{1,0:T(2,128)}, f32[2,1024]{1,0:T(2,128)S(1)}, u32[]{:S(2)}) copy-start(f32[2,1024]{1,0:T(2,128)S(1)} %fusion.170) | copy-start | bytes 24580
  310.0 46.4 %copy-start.65 = (f32[2,512]{1,0:T(2,128)}, f32[2,512]{1,0:T(2,128)S(1)}, u32[]{:S(2)}) copy-start(f32[2,512]{1,0:T(2,128)S(1)} %fusion.159) | copy-start | bytes 12292
  368.6 121.0 %copy-start.56 = (f32[768]{0:T(1024)S(1)}, f32[768]{0:T(1024)}, u32[]{:S(2)}) copy-start(f32[768]{0:T(1024)} %copy-done.55) | copy-start | bytes 9220
  368.6 121.0 %copy-start.75 = (f32[2,512]{1,0:T(2,128)S(1)}, f32[2,512]{1,0:T(2,128)}, u32[]{:S(2)}) copy-start(f32[2,512]{1,0:T(2,128)} %copy-done.74) | copy-start | bytes 12292
  504.3 20.4 %slice-start = ((s8[6291456]{0:T(1024)(128)(4,1)}), s8[2097152]{0:T(1024)(128)(4,1)S(1)}, s32[]{:S(2)}) async-start(s8[6291456]{0:T(1024)(128)(4,1)} %bitcast.255), calls=%async_computation.6 | async-start | bytes 4194304
  676.4 17.6 %copy-start.77 = (bf16[768]{0:T(1024)(128)(2,1)S(1)}, bf16[768]{0:T(1024)(128)(2,1)}, u32[]{:S(2)}) copy-start(bf16[768]{0:T(1024)(128)(2,1)} %get-tuple-element.136) | copy-start | bytes 4612
  694.5 15.5 %copy-start.41 = (bf16[2,1024]{1,0:T(2,128)(2,1)S(1)}, bf16[2,1024]{1,0:T(2,128)(2,1)}, u32[]{:S(2)}) copy-start(bf16[2,1024]{1,0:T(2,128)(2,1)} %copy-done.40) | copy-start | bytes 12292
  721.5 278.4 %reduce-scatter.5.cloned.1.call-start = ((), (), s32[]{:S(2)}) async-start(), calls=%async_computation.5 | async-start | bytes 14598144 | tf_op jit(solution)/shard_map/reduce_scatter | solution.py:283
  742.6 17.0 %copy-start.4 = (f32[2,512,768]{2,0,1:T(2,128)S(1)}, f32[2,512,768]{2,0,1:T(2,128)}, u32[]{:S(2)}) copy-start(f32[2,512,768]{2,0,1:T(2,128)} %copy-done.2) | copy-start | bytes 9437188
  742.6 17.0 %copy-start.57 = (f32[768]{0:T(1024)S(1)}, f32[768]{0:T(1024)}, u32[]{:S(2)}) copy-start(f32[768]{0:T(1024)} %copy-done.55) | copy-start | bytes 9220
  742.6 17.0 %copy-start.76 = (f32[2,512]{1,0:T(2,128)S(1)}, f32[2,512]{1,0:T(2,128)}, u32[]{:S(2)}) copy-start(f32[2,512]{1,0:T(2,128)} %copy-done.74) | copy-start | bytes 12292
  833.4 248.5 %copy-start.67 = (f32[4096]{0:T(1024)S(1)}, f32[4096]{0:T(1024)}, u32[]{:S(2)}) copy-start(f32[4096]{0:T(1024)} %param.58) | copy-start | bytes 49156
  1001.0 90.9 %copy-start.72 = (f32[768]{0:T(1024)S(1)}, f32[768]{0:T(1024)}, u32[]{:S(2)}) copy-start(f32[768]{0:T(1024)} %param.61) | copy-start | bytes 9220
  1001.0 90.9 %copy-start.73 = (f32[768]{0:T(1024)S(1)}, f32[768]{0:T(1024)}, u32[]{:S(2)}) copy-start(f32[768]{0:T(1024)} %param.55) | copy-start | bytes 9220
  1001.1 93.2 %copy-start.36 = (f32[16,768]{1,0:T(8,128)S(1)}, f32[16,768]{1,0:T(8,128)}, u32[]{:S(2)}) copy-start(f32[16,768]{1,0:T(8,128)} %param.37) | copy-start | bytes 147460
  1001.1 94.8 %copy-start.30 = (f32[48,768]{1,0:T(8,128)S(1)}, f32[48,768]{1,0:T(8,128)}, u32[]{:S(2)}) copy-start(f32[48,768]{1,0:T(8,128)} %param.40) | copy-start | bytes 442372
  1006.4 93.7 %copy-start.20 = (f32[48,4096]{1,0:T(8,128)S(1)}, f32[48,4096]{1,0:T(8,128)}, u32[]{:S(2)}) copy-start(f32[48,4096]{1,0:T(8,128)} %param.41) | copy-start | bytes 2359300
  1082.0 23.9 %copy-start.39 = (f32[2304]{0:T(1024)}, f32[2304]{0:T(1024)S(1)}, u32[]{:S(2)}) copy-start(f32[2304]{0:T(1024)S(1)} %fusion.145) | copy-start | bytes 27652
  1082.0 23.9 %copy-start.38 = (f32[4096]{0:T(1024)}, f32[4096]{0:T(1024)S(1)}, u32[]{:S(2)}) copy-start(f32[4096]{0:T(1024)S(1)} %fusion.142) | copy-start | bytes 49156
  1086.4 19.5 %copy-start.71 = (f32[192]{0:T(256)}, f32[192]{0:T(256)S(1)}, u32[]{:S(2)}) copy-start(f32[192]{0:T(256)S(1)} %multiply_add_fusion.10) | copy-start | bytes 2308
  (62 other events, 534.2 us)
Sparse Core Ops, SparseCore 0:
  11.6 81.1 all-gather.3
  96.2 87.5 all-gather.5
  721.6 109.4 reduce-scatter.2
  838.0 161.8 reduce-scatter.4

commit v2 on v1

--- a/solution.py
+++ b/solution.py
@@ -38,6 +38,98 @@
     mixing = jax.nn.softmax(scores, axis=0)
     blended = jnp.sum(mixing[:, :, None] * pooled, axis=0)
     return blended.reshape(blended.shape[0] // 2, 2, blended.shape[1]).mean(axis=1)
+
+
+HIGHEST = lax.Precision.HIGHEST
+HIGH_3 = lax.Precision.HIGH
+
+def pool_vec(values, block_size):
+
+    count = values.shape[-1]
+    blocks = -(-count // block_size)
+    padded = jnp.pad(values, [(0, 0)] * (values.ndim - 1) + [(0, blocks * block_size - count)])
+    totals = padded.reshape(values.shape[:-1] + (blocks, block_size)).sum(axis=-1)
+    offsets = jnp.arange(blocks, dtype=jnp.int32) * block_size
+    counts = jnp.minimum(block_size, count - offsets).astype(values.dtype)
+    return jnp.repeat(totals / counts, block_size, axis=-1)[..., :count]
+
+OFFSETS = (-2, -1, 0, 1, 2, 3)
+
+def block_len(position, block_size, count):
+    return jnp.minimum(block_size, count - block_size * (position // block_size)).astype(jnp.float32)
+
+def gbst_weights(hidden, scorer):
+    count = hidden.shape[1]
+    first = jnp.einsum("nld,d->nl", hidden, scorer, precision=HIGHEST)
+    scores = jnp.stack([pool_vec(first, b) for b in (1, 2, 3, 4)], axis=1)
+    return jax.nn.softmax(scores, axis=1)
+
+def diagonals(mixing, count):
+
+    tok = lax.broadcasted_iota(jnp.int32, (1, count // 2), 1)
+    rows = []
+    for o in OFFSETS:
+        col = 2 * tok + o
+        total = jnp.zeros((mixing.shape[0], count // 2), jnp.float32)
+        for p in (0, 1):
+            pos = 2 * tok + p
+            for index_b, b in enumerate((1, 2, 3, 4)):
+                same = (jnp.floor_divide(col, b) == pos // b) & (col >= 0) & (col < count)
+                weight = mixing[:, index_b, p::2] / block_len(pos, b, count)
+                total = total + jnp.where(same, weight, 0.0)
+        rows.append(0.5 * total)
+    return jnp.stack(rows, axis=1)
+
+def band_matrix(coef, count):
+    tok = lax.broadcasted_iota(jnp.int32, (1, count // 2, count), 1)
+    col = lax.broadcasted_iota(jnp.int32, (1, count // 2, count), 2)
+    gap = col - 2 * tok
+    band = jnp.zeros((coef.shape[0], count // 2, count), jnp.float32)
+    for index_o, o in enumerate(OFFSETS):
+        band = jnp.where(gap == o, coef[:, index_o, :, None], band)
+    return band
+
+@jax.custom_vjp
+def gbst_tokens(hidden, scorer):
+    return gbst_fwd(hidden, scorer)[0]
+
+def gbst_fwd(hidden, scorer):
+    count = hidden.shape[1]
+    mixing = gbst_weights(hidden, scorer)
+    band = band_matrix(diagonals(mixing, count), count)
+    tokens = jnp.einsum("ntj,njd->ntd", band, hidden, precision=HIGH_3)
+    return tokens, (hidden, scorer, mixing, band)
+
+def gbst_bwd(saved, grad_tokens):
+    hidden, scorer, mixing, band = saved
+    count = hidden.shape[1]
+    cross = jnp.einsum("ntd,njd->ntj", grad_tokens, hidden, precision=HIGH_3)
+    tok = lax.broadcasted_iota(jnp.int32, (1, count // 2, count), 1)
+    col = lax.broadcasted_iota(jnp.int32, (1, count // 2, count), 2)
+    gap = col - 2 * tok
+    diag = jnp.stack([jnp.sum(jnp.where(gap == o, cross, 0.0), axis=2) for o in OFFSETS], axis=1)
+    tok1 = lax.broadcasted_iota(jnp.int32, (1, count // 2), 1)
+    grad_mix = []
+    for index_b, b in enumerate((1, 2, 3, 4)):
+        per_parity = []
+        for p in (0, 1):
+            pos = 2 * tok1 + p
+            total = jnp.zeros((hidden.shape[0], count // 2), jnp.float32)
+            for index_o, o in enumerate(OFFSETS):
+                col1 = 2 * tok1 + o
+                same = (jnp.floor_divide(col1, b) == pos // b) & (col1 >= 0) & (col1 < count)
+                total = total + jnp.where(same, diag[:, index_o], 0.0)
+            per_parity.append(0.5 * total / block_len(pos, b, count))
+        grad_mix.append(jnp.stack(per_parity, axis=-1).reshape(hidden.shape[0], count))
+    grad_mix = jnp.stack(grad_mix, axis=1)
+    grad_scores = mixing * (grad_mix - jnp.sum(mixing * grad_mix, axis=1, keepdims=True))
+    spread = sum(pool_vec(grad_scores[:, index_b], b) for index_b, b in enumerate((1, 2, 3, 4)))
+    grad_hidden = jnp.einsum("ntj,ntd->njd", band, grad_tokens, precision=HIGH_3)
+    grad_hidden = grad_hidden + spread[:, :, None] * scorer
+    grad_scorer = jnp.einsum("nj,njd->d", spread, hidden, precision=HIGHEST)
+    return grad_hidden, grad_scorer
+
+gbst_tokens.defvjp(gbst_fwd, gbst_bwd)
 
 
 def mix_items(hidden_all, scorer):
@@ -188,7 +280,7 @@
         jnp.einsum("hby,yj->hbj", byte_windows, complete_kernel, preferred_element_type=jnp.float32)
         + vector_vals[2]
     )
-    tokens, gbst_pull = jax.vjp(mix_items, hidden, vector_vals[3])
+    tokens, gbst_pull = jax.vjp(gbst_tokens, hidden, vector_vals[3])
     normed_full, norm_one_pull = jax.vjp(rms_norm, tokens, vector_vals[0])
     normed_one = normed_full.astype(jnp.bfloat16)
     joined_qkv = jnp.einsum(
@@ -258,19 +350,18 @@
     grad_kernel = jnp.einsum(
         "xwu,xwo->uo", byte_windows, gradient_hidden_reduced, preferred_element_type=jnp.float32
     )
-    grad_windows = jnp.einsum(
-        "njc,ic->nji",
-        gradient_hidden_reduced,
-        backward_kernel_matrix,
+    grad_padded = jnp.pad(gradient_hidden_reduced, ((0, 0), (0, KS - 1), (0, 0)))
+    grad_shifted = jnp.concatenate(
+        [grad_padded[:, KS - 1 - shift_at : KS - 1 - shift_at + count_bytes] for shift_at in range(KS)],
+        axis=2,
+    ).reshape(count_items, count_bytes, KS, D)
+    grad_embedded = jnp.einsum(
+        "njko,kco->njc",
+        grad_shifted,
+        backward_kernel_matrix.reshape(KS, D, D),
         preferred_element_type=jnp.float32,
     )
-    grad_padded = jnp.zeros((count_items, count_bytes + KS - 1, D), jnp.float32)
-    for shift_at in range(KS):
-        piece_grad = grad_windows[:, :, shift_at * D : (shift_at + 1) * D]
-        grad_padded = grad_padded + jnp.pad(
-            piece_grad, ((0, 0), (shift_at, KS - 1 - shift_at), (0, 0))
-        )
-    gradient_embedded_bytes = grad_padded[:, KS - 1 :].astype(jnp.bfloat16) * byte_mask[:, :, None]
+    gradient_embedded_bytes = grad_embedded.astype(jnp.bfloat16) * byte_mask[:, :, None]
     grad_table = jnp.einsum(
         "xpg,xpz->gz", one_hot_bytes, gradient_embedded_bytes, preferred_element_type=jnp.float32
     )

time: 1120 us -> 900 us (0.80)
  local copies, waits for them, and re-layouts: 239 us -> 80.8 us
  other arithmetic: 226 us -> 115 us
  matrix products: 303 us -> 331 us
  waiting for transfers between devices: 271 us -> 289 us
    reduce_sum x15 -> x8, other arithmetic: 118 us -> 1.15 us  [the longest x4 0.57 us: body(): tokens, gbst_pull = jax.vjp(gbst_tokens, hidden, vector_vals[3])]
    reshape x7 -> x18, local copies, waits for them, and re-layouts: 57.9 us -> 5.17 us  [the longest x10 2.98 us: body(): tokens, gbst_pull = jax.vjp(gbst_tokens, hidden, vector_vals[3])]
    all_gather x1, waiting for transfers between devices: 0.01 us -> 31.4 us  [body(): second_all = lax.all_gather(second_group, groups, axis=0, tiled=True)]
    another operation x7 -> x9, local copies, waits for them, and re-layouts: 33.7 us -> 6.29 us  [the longest x2 16 us: pool_mean(): return jnp.repeat(totals / counts[:, None], block_size, axis=0)[:count_rows]]
    broadcast_in_dim x7 -> x6, local copies, waits for them, and re-layouts: 27.6 us -> 0.91 us  [the longest x3 0.46 us: pool_vec(): return jnp.repeat(totals / counts, block_size, axis=-1)[..., :count]]
    dot_general x1 -> x5, matrix products: 17.5 us -> 40.2 us  [the longest x3 25.2 us: body(): tokens, gbst_pull = jax.vjp(gbst_tokens, hidden, vector_vals[3])]
    pad x3 -> x2, local copies, waits for them, and re-layouts: 20.2 us -> 0.01 us  [the longest x1 0.01 us: pool_vec(): jnp.pad(values, [(0, 0)] * (values.ndim - 1) + [(0, blocks * block_size -...]
    slice x3 -> x11, local copies, waits for them, and re-layouts: 20.3 us -> 1.85 us  [the longest x8 1.83 us: diagonals(): weight = mixing[:, index_b, p::2] / block_len(pos, b, count)]
  transfers between devices with their start and end apart: 4 -> 4, of which waited for: 3 -> 4; matrix products, arithmetic and copies ran while one was open for 24% -> 17% of each run, Pallas kernels for 0% -> 0%
where the time goes in v2:
time: 900 us; the launch traced here: 892 us
  matrix products  331 us (37%)
  waiting for transfers between devices  289 us (32%)
  other arithmetic  115 us (13%)
  local copies, waits for them, and re-layouts  80.8 us (9%)
  blocking collectives  44.8 us (5%)
  between operations  30.4 us (3%)
    reduce_scatter x1, waiting for transfers between devices, body(): lax.psum_scatter(early, groups, scatter_dimension=0, tiled=True)  164 us
    all_gather x1, waiting for transfers between devices, body(): first_all = lax.all_gather(first_group, groups, axis=0, tiled=True)  63.7 us
    dot_general x2, matrix products, attend_backward(): jnp.einsum('hqk,qhe->khe', grad_scores, queries, preferred_element_type=j...  47.6 us
    dot_general x2, matrix products, attend_backward(): jnp.einsum('hqk,khe->qhe', grad_scores, keys_all, preferred_element_type=...  40 us
    psum x1, blocking collectives, body(): stats = lax.psum(stats, groups)  39.9 us
    all_gather x1, waiting for transfers between devices, body(): second_all = lax.all_gather(second_group, groups, axis=0, tiled=True)  31.4 us
    reduce_scatter x1, waiting for transfers between devices, body(): lax.psum_scatter(late.reshape(-1, D), groups, scatter_dimension=0, tiled=...  30.4 us
    dot_general x3, matrix products, body(): tokens, gbst_pull = jax.vjp(gbst_tokens, hidden, vector_vals[3])  25.2 us
  transfers between devices with their start and end apart: 4, of which 4 were waited for; matrix products, arithmetic and copies ran while one was open for 17% of the time, Pallas kernels for 0%

profile of v2, /device:TPU:0, one launch (start us, length us, event | category | flops | bytes accessed | tf_op | source)
XLA Modules:
  0.0 892.4 jit_solution(8703267487620833877)
XLA Ops:
  29.1 63.7 %all-gather.4.cloned.1.call-done = bf16[5632,768]{1,0:T(8,128)(2,1)} async-done(((bf16[176,768]{1,0:T(8,128)(2,1)}), bf16[5632,768]{1,0:T(8,128)(2,1)}) %all-gather.4.cloned.1.call-update) | async-done | bytes 8650768 | tf_op jit(solution)/shard_map/all_gather | solution.py:247
  109.7 14.0 %fusion.121 = f32[2,1024,768]{2,1,0:T(8,128)S(1)} fusion(bf16[3072,768,1]{1,0,2:T(8,128)(2,1)} %bitcast.639, bf16[2,1024,768]{2,1,0:T(8,128)(2,1)} %copy-done.15, bf16[2,1024,768]{2,1,0:T(8,128)(2,1)} %get-tuple-element.224, bf16[2,1024,768]{2,1,0:T(8,128)(2,1)} %get-tuple-element.223, bf16[2,1024,768]{2,1,0:T(8,128)(2,1)} %get-tuple-element.222), kind=kOutput, calls=%fused_computation.151 | convolution fusion | flops 9714008064 | bytes 23592960 | tf_op jit(solution)/shard_map/hby,yj->hbj/dot_general | solution.py:280
  140.4 11.9 %multiply_reduce_fusion.6 = (f32[2,512]{1,0:T(2,128)S(1)}, f32[2,512,768]{2,1,0:T(8,128)S(1)}) fusion(f32[2,1024,768]{2,1,0:T(8,128)} %copy-done.1, f32[768]{0:T(1024)S(1)} %add.1794, f32[2,512]{1,0:T(2,128)S(1)} %add_multiply_fusion, f32[2,512]{1,0:T(2,128)S(1)} %add_multiply_fusion.1, f32[2,512]{1,0:T(2,128)S(1)} %add_multiply_fusion.2, ...), kind=kOutput, calls=%fused_computation.137 | convolution fusion | flops 4841274368 | bytes 12614656 | tf_op jit(solution)/shard_map/jvp(ntj,njd->ntd)/dot_general | solution.py:100
  152.4 31.4 %all-gather.6.cloned.1.call-done = bf16[768,7168]{1,0:T(8,128)(2,1)} async-done(((bf16[24,7168]{1,0:T(8,128)(2,1)}), bf16[768,7168]{1,0:T(8,128)(2,1)}) %all-gather.6.cloned.1.call-update) | async-done | bytes 11010064 | tf_op jit(solution)/shard_map/all_gather | solution.py:249
  183.8 6.1 convolution_convert_fusion
  198.4 19.9 %while.22 = (s32[]{:T(128)}, bf16[2,512,12,64]{1,3,2,0:T(8,128)(2,1)}, f32[2,12,512,1]{2,1,3,0:T(8,128)S(1)}, bf16[2,512,12,64]{1,3,2,0:T(8,128)(2,1)}, pred[2,5...) while((s32[]{:T(128)}, ...), condition=%wide.region_8.9_spmd, body=%wide.region_5.8_spmd.sunk | while | flops 843442176 | bytes 47428224 | solution.py:294
  222.7 14.4 %fusion.109 = f32[2,512,4096]{2,1,0:T(8,128)} fusion(bf16[768,7168]{1,0:T(8,128)(2,1)} %all-gather.6.cloned.1.call-done, f32[2,512,768]{2,1,0:T(8,128)S(1)} %get-tuple-element.282, f32[768]{0:T(1024)S(1)} %mul.1595, f32[2,512]{1,0:T(2,128)S(1)} %fusion.275), kind=kOutput, calls=%fused_computation.114 | convolution fusion | flops 6444810240 | bytes 26221568 | tf_op jit(solution)/shard_map/std,de->ste/dot_general | solution.py:302
  237.1 17.1 %bitcast_multiply_fusion.1 = (f32[2,512,2048]{2,1,0:T(8,128)}, f32[2,512,2048]{2,1,0:T(8,128)}, bf16[2,512,2048]{2,1,0:T(8,128)(2,1)}) fusion(f32[2,512,4096]{2,1,0:T(8,128)} %fusion.109, bf16[2048,768,1]{1,0,2:T(8,128)(2,1)S(1)} %bitcast.643, bf16[2,512,768]{2,1,0:T(8,128)(2,1)S(1)} %copy-done.21), kind=kOutput, calls=%fused_computation.95 | convolution fusion | flops 3271557120 | bytes 42467328 | tf_op jit(solution)/shard_map/std,fd->stf/dot_general | solution.py:315
  254.2 14.7 %multiply_reduce_fusion.1 = (bf16[768]{0:T(1024)(128)(2,1)}, f32[2,512]{1,0:T(2,128)S(1)}, f32[2,512,768]{2,1,0:T(8,128)}) fusion(f32[2,512,768]{2,1,0:T(8,128)} %copy-done.8, f32[2,512]{1,0:T(2,128)S(1)} %fusion.275, f32[768]{0:T(1024)S(1)} %mul.1595, bf16[768,7168]{1,0:T(8,128)(2,1)} %all-gather.6.cloned.1.call-done, ...), kind=kOutput, calls=%fused_computation.130 | convolution fusion | flops 6455556096 | bytes 29372928 | tf_op jit(solution)/shard_map/ste,de->std/dot_general | solution.py:323
  281.3 121.0 %while.23 = (s32[]{:T(128)}, bf16[2,512,2304]{1,2,0:T(8,128)(2,1)}, bf16[2,512,12,64]{1,3,2,0:T(8,128)(2,1)S(1)}, pred[2,512]{1,0:T(4,128)(4,1)S(1)}, bf16[2,512...) while((s32[]{:T(128)}, bf16[2,512,2304]{1,2,0:T(8,128)(2,1)}, ...), condition=%wide.region_13.14_spmd, body=%wide.region_11.13_spmd.sunk | while | flops 2103325696 | bytes 214128336 | solution.py:336
  288.4 6.3 fusion.439
  294.8 20.0 %fusion.441 = bf16[12,64,512]{2,1,0:T(8,128)(2,1)} fusion(f32[12,512,512]{1,2,0:T(8,128)} %fusion.439, f32[12,512,512]{1,2,0:T(8,128)} %copy-done, f32[12,512]{1,0:T(8,128)S(1)} %dynamic-slice_bitcast_fusion.2, pred[512]{0:T(512)(128)(4,1)S(1)} %dynamic-slice_reduce_fusion.11, bf16[2,512,12,64]{1,3,2,0:T(8,128)(2,1)S(1)} %get-tuple-element.477, ...), kind=kOutput, calls=%fused_computation.42.clone.1 | convolution fusion | flops 437656064 | bytes 51971076 | tf_op jit(solution)/shard_map/while/body/eval_jaxpr/hqk,khe->qhe/dot_general | solution.py:176
  314.8 23.8 %fusion.440 = bf16[12,64,512]{2,1,0:T(8,128)(2,1)} fusion(f32[12,512,512]{1,2,0:T(8,128)} %fusion.439, f32[12,512,512]{1,2,0:T(8,128)} %copy-done, f32[12,512]{1,0:T(8,128)S(1)} %dynamic-slice_bitcast_fusion.2, pred[512]{0:T(512)(128)(4,1)S(1)} %dynamic-slice_reduce_fusion.11, bf16[2,512,12,64]{1,3,2,0:T(8,128)(2,1)S(1)} %get-tuple-element.479, ...), kind=kOutput, calls=%fused_computation.43.clone.1 | convolution fusion | flops 437656064 | bytes 51971076 | tf_op jit(solution)/shard_map/while/body/eval_jaxpr/hqk,qhe->khe/dot_general | solution.py:179
  348.6 6.3 fusion.439
  355.0 20.0 %fusion.441 = bf16[12,64,512]{2,1,0:T(8,128)(2,1)} fusion(f32[12,512,512]{1,2,0:T(8,128)} %fusion.439, f32[12,512,512]{1,2,0:T(8,128)} %copy-done, f32[12,512]{1,0:T(8,128)S(1)} %dynamic-slice_bitcast_fusion.2, pred[512]{0:T(512)(128)(4,1)S(1)} %dynamic-slice_reduce_fusion.11, bf16[2,512,12,64]{1,3,2,0:T(8,128)(2,1)S(1)} %get-tuple-element.477, ...), kind=kOutput, calls=%fused_computation.42.clone.1 | convolution fusion | flops 437656064 | bytes 51971076 | tf_op jit(solution)/shard_map/while/body/eval_jaxpr/hqk,khe->qhe/dot_general | solution.py:176
  375.0 23.8 %fusion.440 = bf16[12,64,512]{2,1,0:T(8,128)(2,1)} fusion(f32[12,512,512]{1,2,0:T(8,128)} %fusion.439, f32[12,512,512]{1,2,0:T(8,128)} %copy-done, f32[12,512]{1,0:T(8,128)S(1)} %dynamic-slice_bitcast_fusion.2, pred[512]{0:T(512)(128)(4,1)S(1)} %dynamic-slice_reduce_fusion.11, bf16[2,512,12,64]{1,3,2,0:T(8,128)(2,1)S(1)} %get-tuple-element.479, ...), kind=kOutput, calls=%fused_computation.43.clone.1 | convolution fusion | flops 437656064 | bytes 51971076 | tf_op jit(solution)/shard_map/while/body/eval_jaxpr/hqk,qhe->khe/dot_general | solution.py:179
  402.4 9.0 %multiply_reduce_fusion.2 = (bf16[768]{0:T(1024)(128)(2,1)S(1)}, f32[2,512]{1,0:T(2,128)S(1)}, f32[2,512,768]{2,1,0:T(8,128)S(1)}) fusion(f32[2,512,768]{2,1,0:T(8,128)} %copy-done.6, f32[2,512]{1,0:T(2,128)S(1)} %copy-done.68, f32[768]{0:T(1024)S(1)} %copy-done.66, bf16[2,512,2304]{1,2,0:T(8,128)(2,1)} %get-tuple-element.118, ...), kind=kOutput, calls=%fused_computation.131 | convolution fusion | flops 3628595456 | bytes 14561792 | tf_op jit(solution)/shard_map/ste,de->std/dot_general | solution.py:342
  415.4 8.6 select_reduce_fusion.2
  432.2 11.3 %add_convert_fusion.1 = bf16[2,1024,768]{2,1,0:T(8,128)(2,1)S(1)} fusion(f32[768]{0:T(1024)S(1)} %copy-done.95, f32[2,1024]{1,0:T(2,128)S(1)} %fusion.205, f32[2,512,768]{2,1,0:T(8,128)} %copy-done.16, f32[2,512]{1,0:T(2,128)S(1)} %copy-done.92, f32[2,512]{1,0:T(2,128)S(1)} %copy-done.90, f32[2,512]{1,0:T(2,128)S(1)} %copy-done.99, ...), kind=kOutput, calls=%fused_computation.102 | convolution fusion | flops 4842848256 | bytes 9473024 | tf_op jit(solution)/shard_map/transpose(jvp(ntj,ntd->njd))/dot_general | solution.py:283
  443.5 17.7 %bitcast_convert_fusion.1 = bf16[3072,768]{1,0:T(8,128)(2,1)} fusion(bf16[2,1024,768]{2,1,0:T(8,128)(2,1)S(1)} %add_convert_fusion.1, bf16[2,1024,768]{2,1,0:T(8,128)(2,1)} %copy-done.15, bf16[2,1024,768]{2,1,0:T(8,128)(2,1)} %get-tuple-element.224, bf16[2,1024,768]{2,1,0:T(8,128)(2,1)} %get-tuple-element.223, bf16[2,1024,768]{2,1,0:T(8,128)(2,1)} %get-tuple-element.222), kind=kOutput, calls=%fused_computation.87 | convolution fusion | flops 9716367360 | bytes 20447232 | tf_op jit(solution)/shard_map/xwu,xwo->uo/dot_general | solution.py:350
  471.5 9.5 %pad_maximum_fusion.2 = bf16[2,1024,3072]{2,1,0:T(8,128)(2,1)} fusion(bf16[2,1024,768]{2,1,0:T(8,128)(2,1)S(1)} %add_convert_fusion.1, bf16[2,1024,768]{2,1,0:T(8,128)(2,1)} %get-tuple-element.220, bf16[2,1024,768]{2,1,0:T(8,128)(2,1)} %get-tuple-element.219, bf16[2,1024,768]{2,1,0:T(8,128)(2,1)} %get-tuple-element.218), kind=kLoop, calls=%fused_computation.81 | loop fusion | flops 50331648 | bytes 25165824 | tf_op jit(solution)/shard_map/concatenate | solution.py:354
  481.0 15.9 %fusion.169 = bf16[32,8,768]{2,1,0:T(8,128)(2,1)S(1)} fusion(bf16[4,768,768,1]{2,1,0,3:T(8,128)(2,1)} %bitcast.640, bf16[2,128,4,8,768]{4,3,2,1,0:T(8,128)(2,1)} %bitcast.634, bf16[2,1024]{1,0:T(2,128)(2,1)S(1)} %copy-done.103, s32[2,1024]{1,0:T(2,128)S(1)} %copy-done.148), kind=kOutput, calls=%fused_computation.192 | convolution fusion | flops 10472849408 | bytes 17707008 | tf_op jit(solution)/shard_map/xpg,xpz->gz/dot_general | solution.py:365
  497.0 5.8 fusion.99
  504.2 7.4 bitcast_convert_fusion.3
  524.7 16.8 %bitcast_convert_fusion = bf16[768,4096]{1,0:T(8,128)(2,1)} fusion(f32[2,512,2048]{2,1,0:T(8,128)} %get-tuple-element.213, f32[2,512,2048]{2,1,0:T(8,128)} %get-tuple-element.212, f32[2,512,768]{2,1,0:T(8,128)} %copy-done.8, f32[768]{0:T(1024)S(1)} %copy-done.70, f32[2,512]{1,0:T(2,128)S(1)} %copy-done.76), kind=kOutput, calls=%fused_computation.82 | convolution fusion | flops 6456344576 | bytes 26221568 | tf_op jit(solution)/shard_map/std,ste->de/dot_general | solution.py:320
  541.6 7.6 bitcast_convert_fusion.2
  549.2 9.5 %pad_maximum_fusion = bf16[768,9216]{1,0:T(8,128)(2,1)} fusion(bf16[768,2048]{1,0:T(8,128)(2,1)S(1)} %reshape.4477, bf16[768,4096]{1,0:T(8,128)(2,1)S(1)} %copy-done.12, bf16[768,768]{1,0:T(8,128)(2,1)S(1)} %copy-done.13, bf16[768,2304]{1,0:T(8,128)(2,1)S(1)} %bitcast_convert_fusion.2), kind=kLoop, calls=%fused_computation.76 | loop fusion | flops 56623104 | bytes 28311552 | tf_op jit(solution)/shard_map/concatenate | solution.py:371
  573.4 8.3 convolution_add_fusion.1
  581.7 30.4 %reduce-scatter.3.cloned.1.call-done = bf16[112,768]{1,0:T(8,128)(2,1)} async-done(((bf16[3584,768]{1,0:T(8,128)(2,1)}), bf16[112,768]{1,0:T(8,128)(2,1)}) %reduce-scatter.3.cloned.1.call-update) | async-done | bytes 172048 | tf_op jit(solution)/shard_map/reduce_scatter | solution.py:382
  617.3 163.8 %reduce-scatter.5.cloned.1.call-done = bf16[24,9216]{1,0:T(8,128)(2,1)} async-done(((bf16[768,9216]{1,0:T(8,128)(2,1)}), bf16[24,9216]{1,0:T(8,128)(2,1)}) %reduce-scatter.5.cloned.1.call-update) | async-done | bytes 442384 | tf_op jit(solution)/shard_map/reduce_scatter | solution.py:374
  787.7 12.4 %concatenate.53 = f32[9495]{0:T(1024)S(1)} concatenate(f32[1]{0:T(128)} %bitcast.65, f32[1]{0:T(128)} %bitcast.66, f32[1]{0:T(128)} %bitcast.71, f32[1]{0:T(128)} %bitcast.72, f32[1]{0:T(128)} %bitcast.73, f32[1]{0:T(128)} %bitcast.74, f32[1]{0:T(128)} %bitcast.75, f32[1]{0:T(128)} %bitcast.76, f32[1]{0:T(128)} %bitcast.77, f32[1]{0:T(128)} %bitcast.78, f32[1]{0:T(128)} %bitcast.79, ...), dimensions={0} | concatenate | bytes 75960 | tf_op jit(solution)/shard_map/concatenate | solution.py:414
  800.1 39.9 %psum.7 = f32[9495]{0:T(1024)S(1)} all-reduce(f32[9495]{0:T(1024)S(1)} %concatenate.53), channel_id=1, replica_groups=mesh['fsdp'=16,'dp'=2] {'fsdp','dp'}, use_global_device_ids=true, to_apply=%region_56.57 | all-reduce | flops 9495 | bytes 75960 | tf_op jit(solution)/shard_map/psum | solution.py:416
  (566 shorter events, 213.5 us)
Async XLA Ops:
  7.2 85.5 %all-gather.4.cloned.1.call-start = ((), (), s32[]{:S(2)}) async-start(), calls=%async_computation.2 | async-start | bytes 8921088 | tf_op jit(solution)/shard_map/all_gather | solution.py:247
  11.5 172.4 %all-gather.6.cloned.1.call-start = ((), (), s32[]{:S(2)}) async-start(), calls=%async_computation.3 | async-start | bytes 11354112 | tf_op jit(solution)/shard_map/all_gather | solution.py:249
  15.2 597.0 %reduce-scatter.3.cloned.1.call-start = ((), (), s32[]{:S(2)}) async-start(), calls=%async_computation.4 | async-start | bytes 5677056 | tf_op jit(solution)/shard_map/reduce_scatter | solution.py:382
  15.3 121.0 %copy-start.84 = (pred[512]{0:T(512)(128)(4,1)}, pred[512]{0:T(512)(128)(4,1)S(1)}, u32[]{:S(2)}) copy-start(pred[512]{0:T(512)(128)(4,1)S(1)} %get-tuple-element.331) | copy-start | bytes 1540
  15.3 121.1 %copy-start.82 = (pred[512]{0:T(512)(128)(4,1)}, pred[512]{0:T(512)(128)(4,1)S(1)}, u32[]{:S(2)}) copy-start(pred[512]{0:T(512)(128)(4,1)S(1)} %get-tuple-element.332) | copy-start | bytes 1540
  15.3 124.2 %copy-start.104 = (pred[512]{0:T(512)(128)(4,1)}, pred[512]{0:T(512)(128)(4,1)S(1)}, u32[]{:S(2)}) copy-start(pred[512]{0:T(512)(128)(4,1)S(1)} %get-tuple-element.330) | copy-start | bytes 1540
  15.3 124.2 %copy-start.114 = (pred[512]{0:T(512)(128)(4,1)}, pred[512]{0:T(512)(128)(4,1)S(1)}, u32[]{:S(2)}) copy-start(pred[512]{0:T(512)(128)(4,1)S(1)} %get-tuple-element.329) | copy-start | bytes 1540
  15.9 123.6 %copy-start.106 = (pred[512]{0:T(512)(128)(4,1)}, pred[512]{0:T(512)(128)(4,1)S(1)}, u32[]{:S(2)}) copy-start(pred[512]{0:T(512)(128)(4,1)S(1)} %get-tuple-element.328) | copy-start | bytes 1540
  16.6 120.5 %copy-start.108 = (pred[512]{0:T(512)(128)(4,1)}, pred[512]{0:T(512)(128)(4,1)S(1)}, u32[]{:S(2)}) copy-start(pred[512]{0:T(512)(128)(4,1)S(1)} %get-tuple-element.324) | copy-start | bytes 1540
  16.6 120.5 %copy-start.120 = (pred[512]{0:T(512)(128)(4,1)}, pred[512]{0:T(512)(128)(4,1)S(1)}, u32[]{:S(2)}) copy-start(pred[512]{0:T(512)(128)(4,1)S(1)} %get-tuple-element.323) | copy-start | bytes 1540
  17.1 120.0 %copy-start.110 = (pred[512]{0:T(512)(128)(4,1)}, pred[512]{0:T(512)(128)(4,1)S(1)}, u32[]{:S(2)}) copy-start(pred[512]{0:T(512)(128)(4,1)S(1)} %get-tuple-element.322) | copy-start | bytes 1540
  17.7 119.4 %copy-start.132 = (pred[512]{0:T(512)(128)(4,1)}, pred[512]{0:T(512)(128)(4,1)S(1)}, u32[]{:S(2)}) copy-start(pred[512]{0:T(512)(128)(4,1)S(1)} %get-tuple-element.319) | copy-start | bytes 1540
  17.7 118.5 %copy-start.112 = (pred[512]{0:T(512)(128)(4,1)}, pred[512]{0:T(512)(128)(4,1)S(1)}, u32[]{:S(2)}) copy-start(pred[512]{0:T(512)(128)(4,1)S(1)} %get-tuple-element.318) | copy-start | bytes 1540
  17.7 118.5 %copy-start.128 = (pred[512]{0:T(512)(128)(4,1)}, pred[512]{0:T(512)(128)(4,1)S(1)}, u32[]{:S(2)}) copy-start(pred[512]{0:T(512)(128)(4,1)S(1)} %get-tuple-element.317) | copy-start | bytes 1540
  18.3 118.0 %copy-start.116 = (pred[512]{0:T(512)(128)(4,1)}, pred[512]{0:T(512)(128)(4,1)S(1)}, u32[]{:S(2)}) copy-start(pred[512]{0:T(512)(128)(4,1)S(1)} %get-tuple-element.316) | copy-start | bytes 1540
  18.9 117.5 %copy-start.134 = (pred[512]{0:T(512)(128)(4,1)}, pred[512]{0:T(512)(128)(4,1)S(1)}, u32[]{:S(2)}) copy-start(pred[512]{0:T(512)(128)(4,1)S(1)} %get-tuple-element.313) | copy-start | bytes 1540
  18.9 119.0 %copy-start.118 = (pred[512]{0:T(512)(128)(4,1)}, pred[512]{0:T(512)(128)(4,1)S(1)}, u32[]{:S(2)}) copy-start(pred[512]{0:T(512)(128)(4,1)S(1)} %get-tuple-element.312) | copy-start | bytes 1540
  18.9 119.0 %copy-start.130 = (pred[512]{0:T(512)(128)(4,1)}, pred[512]{0:T(512)(128)(4,1)S(1)}, u32[]{:S(2)}) copy-start(pred[512]{0:T(512)(128)(4,1)S(1)} %get-tuple-element.311) | copy-start | bytes 1540
  19.5 118.4 %copy-start.122 = (pred[512]{0:T(512)(128)(4,1)}, pred[512]{0:T(512)(128)(4,1)S(1)}, u32[]{:S(2)}) copy-start(pred[512]{0:T(512)(128)(4,1)S(1)} %get-tuple-element.310) | copy-start | bytes 1540
  20.6 118.1 %copy-start.124 = (pred[512]{0:T(512)(128)(4,1)}, pred[512]{0:T(512)(128)(4,1)S(1)}, u32[]{:S(2)}) copy-start(pred[512]{0:T(512)(128)(4,1)S(1)} %get-tuple-element.306) | copy-start | bytes 1540
  21.1 117.5 %copy-start.126 = (pred[512]{0:T(512)(128)(4,1)}, pred[512]{0:T(512)(128)(4,1)S(1)}, u32[]{:S(2)}) copy-start(pred[512]{0:T(512)(128)(4,1)S(1)} %get-tuple-element.304) | copy-start | bytes 1540
  24.5 115.0 %copy-start.37 = (f32[512]{0:T(512)}, f32[512]{0:T(512)S(1)}, u32[]{:S(2)}) copy-start(f32[512]{0:T(512)S(1)} %get-tuple-element.290) | copy-start | bytes 6148
  24.5 115.0 %copy-start.41 = (f32[512]{0:T(512)}, f32[512]{0:T(512)S(1)}, u32[]{:S(2)}) copy-start(f32[512]{0:T(512)S(1)} %get-tuple-element.289) | copy-start | bytes 6148
  24.5 115.0 %copy-start.43 = (f32[512]{0:T(512)}, f32[512]{0:T(512)S(1)}, u32[]{:S(2)}) copy-start(f32[512]{0:T(512)S(1)} %get-tuple-element.336) | copy-start | bytes 6148
  24.6 115.0 %copy-start.45 = (f32[512]{0:T(512)}, f32[512]{0:T(512)S(1)}, u32[]{:S(2)}) copy-start(f32[512]{0:T(512)S(1)} %get-tuple-element.335) | copy-start | bytes 6148
  24.6 115.0 %copy-start.39 = (f32[512]{0:T(512)}, f32[512]{0:T(512)S(1)}, u32[]{:S(2)}) copy-start(f32[512]{0:T(512)S(1)} %get-tuple-element.288) | copy-start | bytes 6148
  24.6 115.0 %copy-start.49 = (f32[512]{0:T(512)}, f32[512]{0:T(512)S(1)}, u32[]{:S(2)}) copy-start(f32[512]{0:T(512)S(1)} %get-tuple-element.287) | copy-start | bytes 6148
  136.1 132.8 %copy-start.69 = (f32[768]{0:T(1024)}, f32[768]{0:T(1024)S(1)}, u32[]{:S(2)}) copy-start(f32[768]{0:T(1024)S(1)} %mul.1595) | copy-start | bytes 9220
  281.3 121.1 %copy-start.66 = (f32[768]{0:T(1024)S(1)}, f32[768]{0:T(1024)}, u32[]{:S(2)}) copy-start(f32[768]{0:T(1024)} %copy-done.65) | copy-start | bytes 9220
  281.3 121.1 %copy-start.68 = (f32[2,512]{1,0:T(2,128)S(1)}, f32[2,512]{1,0:T(2,128)}, u32[]{:S(2)}) copy-start(f32[2,512]{1,0:T(2,128)} %copy-done.67) | copy-start | bytes 12292
  502.8 278.2 %reduce-scatter.5.cloned.1.call-start = ((), (), s32[]{:S(2)}) async-start(), calls=%async_computation.5 | async-start | bytes 14598144 | tf_op jit(solution)/shard_map/reduce_scatter | solution.py:374
  614.4 173.3 %copy-start.137 = (f32[4]{0:T(128)S(1)}, f32[4]{0:T(128)}, u32[]{:S(2)}) copy-start(f32[4]{0:T(128)} %multiply_reduce_fusion.19) | copy-start | bytes 52
  (126 other events, 2547.7 us)
Sparse Core Ops, SparseCore 0:
  11.6 81.1 all-gather.3
  96.2 87.5 all-gather.5
  503.0 109.1 reduce-scatter.2
  619.0 162.0 reduce-scatter.4

commit v3 on v2

--- a/solution.py
+++ b/solution.py
@@ -1,6 +1,8 @@
 import jax
 import jax.numpy as jnp
 from jax import lax
+from jax.experimental import pallas as pl
+from jax.experimental.pallas import tpu as pltpu
 from jax.sharding import PartitionSpec as P
 
 D = 768
@@ -191,6 +193,101 @@
         ],
         axis=-1,
     ).astype(jnp.bfloat16)
+
+
+def head_scores(q_part, k_block, valid):
+    raw = lax.dot_general(q_part, k_block, (((1,), (1,)), ((), ())), preferred_element_type=jnp.float32)
+    return jnp.where(valid, raw * (D // H) ** (-0.5), masked_score)
+
+
+def head_softmax(scores):
+    row_max = jnp.max(scores, axis=1, keepdims=True)
+    expd = jnp.exp(scores - row_max)
+    return expd / jnp.sum(expd, axis=1, keepdims=True)
+
+
+def attn_fwd_kernel(len_ref, q_ref, k_ref, v_ref, o_ref):
+    length = len_ref[pl.program_id(0)]
+    q, k, v = q_ref[0], k_ref[0], v_ref[0]
+    count_tok, width = q.shape
+    lane = lax.broadcasted_iota(jnp.int32, (1, width), 1)
+    valid = 2 * lax.broadcasted_iota(jnp.int32, (1, count_tok), 1) < length
+    total = jnp.zeros((count_tok, width), jnp.float32)
+    for head in range(width // (D // H)):
+        mine = lane // (D // H) == head
+        weights = head_softmax(head_scores(jnp.where(mine, q, 0), k, valid)).astype(jnp.bfloat16)
+        total = total + jnp.dot(weights, jnp.where(mine, v, 0), preferred_element_type=jnp.float32)
+    o_ref[0] = total.astype(o_ref.dtype)
+
+
+def attn_bwd_kernel(len_ref, q_ref, k_ref, v_ref, do_ref, dq_ref, dk_ref, dv_ref):
+    length = len_ref[pl.program_id(0)]
+    q, k, v, upstream = q_ref[0], k_ref[0], v_ref[0], do_ref[0]
+    count_tok, width = q.shape
+    lane = lax.broadcasted_iota(jnp.int32, (1, width), 1)
+    valid = 2 * lax.broadcasted_iota(jnp.int32, (1, count_tok), 1) < length
+    grad_q = jnp.zeros((count_tok, width), jnp.float32)
+    grad_k = jnp.zeros((count_tok, width), jnp.float32)
+    grad_v = jnp.zeros((count_tok, width), jnp.float32)
+    back = (((0,), (0,)), ((), ()))
+    for head in range(width // (D // H)):
+        mine = lane // (D // H) == head
+        q_part = jnp.where(mine, q, 0)
+        weights = head_softmax(head_scores(q_part, k, valid))
+        up_part = jnp.where(mine, upstream, 0)
+        grad_weights = lax.dot_general(up_part, v, (((1,), (1,)), ((), ())), preferred_element_type=jnp.float32)
+        row_dot = jnp.sum(grad_weights * weights, axis=1, keepdims=True)
+        grad_scores = (weights * (grad_weights - row_dot) * (D // H) ** (-0.5)).astype(jnp.bfloat16)
+        grad_q = grad_q + jnp.dot(grad_scores, jnp.where(mine, k, 0), preferred_element_type=jnp.float32)
+        grad_k = grad_k + lax.dot_general(grad_scores, q_part, back, preferred_element_type=jnp.float32)
+        grad_v = grad_v + lax.dot_general(weights.astype(jnp.bfloat16), up_part, back, preferred_element_type=jnp.float32)
+    dq_ref[0] = grad_q.astype(dq_ref.dtype)
+    dk_ref[0] = grad_k.astype(dk_ref.dtype)
+    dv_ref[0] = grad_v.astype(dv_ref.dtype)
+
+
+def attention_forward(joined_qkv, lengths):
+    count_items, count_tok, _ = joined_qkv.shape
+    blocks = D // 128
+    spec = lambda shift: pl.BlockSpec((1, count_tok, 128), lambda i, h, lens: (i, 0, h + shift))
+    return pl.pallas_call(
+        attn_fwd_kernel,
+        out_shape=jax.ShapeDtypeStruct((count_items, count_tok, D), jnp.bfloat16),
+        grid_spec=pltpu.PrefetchScalarGridSpec(
+            num_scalar_prefetch=1,
+            grid=(count_items, blocks),
+            in_specs=[spec(0), spec(blocks), spec(2 * blocks)],
+            out_specs=spec(0),
+        ),
+        cost_estimate=pl.CostEstimate(
+            flops=count_items * H * count_tok * count_tok * 128 * 4,
+            transcendentals=count_items * H * count_tok * count_tok,
+            bytes_accessed=count_items * count_tok * D * 2 * 4,
+        ),
+    )(lengths, joined_qkv, joined_qkv, joined_qkv)
+
+
+def attention_backward(joined_qkv, upstream, lengths):
+    count_items, count_tok, _ = joined_qkv.shape
+    blocks = D // 128
+    spec = lambda shift: pl.BlockSpec((1, count_tok, 128), lambda i, h, lens: (i, 0, h + shift))
+    part = jax.ShapeDtypeStruct((count_items, count_tok, D), jnp.bfloat16)
+    grads = pl.pallas_call(
+        attn_bwd_kernel,
+        out_shape=(part, part, part),
+        grid_spec=pltpu.PrefetchScalarGridSpec(
+            num_scalar_prefetch=1,
+            grid=(count_items, blocks),
+            in_specs=[spec(0), spec(blocks), spec(2 * blocks), spec(0)],
+            out_specs=(spec(0), spec(0), spec(0)),
+        ),
+        cost_estimate=pl.CostEstimate(
+            flops=count_items * H * count_tok * count_tok * 128 * 10,
+            transcendentals=count_items * H * count_tok * count_tok,
+            bytes_accessed=count_items * count_tok * D * 2 * 7,
+        ),
+    )(lengths, joined_qkv, joined_qkv, joined_qkv, upstream)
+    return jnp.concatenate(grads, axis=-1)
 
 
 def body(
@@ -287,12 +384,7 @@
         "std,de->ste", normed_one, full_project, preferred_element_type=jnp.float32
     )
     joined_qkv = joined_qkv.astype(jnp.bfloat16)
-    queries = joined_qkv[..., :D].reshape(count_items, count_tok, H, head_size)
-    keys_all = joined_qkv[..., D : 2 * D].reshape(count_items, count_tok, H, head_size)
-    values_all = joined_qkv[..., 2 * D :].reshape(count_items, count_tok, H, head_size)
-    key_valid = 2 * lax.broadcasted_iota(jnp.int32, (count_items, count_tok), 1) < lengths[:, None]
-    attended, log_total = lax.map(attend_forward, (queries, keys_all, values_all, key_valid))
-    attended_flat = attended.reshape(count_items, count_tok, D)
+    attended_flat = attention_forward(joined_qkv, lengths)
     branch = jnp.einsum(
         "std,de->ste", attended_flat, full_combine, preferred_element_type=jnp.float32
     )
@@ -332,10 +424,7 @@
     grad_attended = jnp.einsum(
         "ste,de->std", grad_branch_low, back_combine, preferred_element_type=jnp.float32
     )
-    grad_attended = grad_attended.astype(jnp.bfloat16).reshape(count_items, count_tok, H, head_size)
-    grad_qkv = lax.map(
-        attend_backward, (queries, keys_all, values_all, key_valid, grad_attended, log_total)
-    )
+    grad_qkv = attention_backward(joined_qkv, grad_attended.astype(jnp.bfloat16), lengths)
     grad_project = jnp.einsum(
         "std,ste->de", normed_one, grad_qkv, preferred_element_type=jnp.float32
     )

time: 900 us -> 824 us (0.916)
  matrix products: 331 us -> 208 us
  Pallas kernels: 0 us -> 55.9 us
  other arithmetic: 115 us -> 95.1 us
  waiting for transfers between devices: 289 us -> 305 us
    dot_general x14 -> x0, matrix products: 126 us -> none  [the longest x2 47.6 us: attend_backward(): jnp.einsum('hqk,qhe->khe', grad_scores, queries, preferred_element_type=j...]
    pallas_call x0 -> x2, Pallas kernels: none -> 55.9 us  [the longest x1 34.3 us: attention_backward(): pl.pallas_call(attn_bwd_kernel, out_shape=(part, part, part), grid_spec=p...]
    all_gather x1, waiting for transfers between devices: 63.7 us -> 73.2 us  [body(): first_all = lax.all_gather(first_group, groups, axis=0, tiled=True)]
where the time goes in v3:
time: 824 us; the launch traced here: 817 us
  waiting for transfers between devices  305 us (37%)
  matrix products  208 us (25%)
  other arithmetic  95.1 us (12%)
  local copies, waits for them, and re-layouts  78.3 us (10%)
  Pallas kernels  55.9 us (7%)
  blocking collectives  44.7 us (5%)
  between operations  29.6 us (4%)
    reduce_scatter x1, waiting for transfers between devices, body(): lax.psum_scatter(early, groups, scatter_dimension=0, tiled=True)  164 us
    all_gather x1, waiting for transfers between devices, body(): first_all = lax.all_gather(first_group, groups, axis=0, tiled=True)  73.2 us
    psum x1, blocking collectives, body(): stats = lax.psum(stats, groups)  39.8 us
    all_gather x1, waiting for transfers between devices, body(): second_all = lax.all_gather(second_group, groups, axis=0, tiled=True)  36.1 us
    pallas_call x1, Pallas kernels, attention_backward(): pl.pallas_call(attn_bwd_kernel, out_shape=(part, part, part), grid_spec=p...  34.3 us
    reduce_scatter x1, waiting for transfers between devices, body(): lax.psum_scatter(late.reshape(-1, D), groups, scatter_dimension=0, tiled=...  32.3 us
    dot_general x3, matrix products, body(): tokens, gbst_pull = jax.vjp(gbst_tokens, hidden, vector_vals[3])  27.2 us
    pallas_call x1, Pallas kernels, attention_forward(): pl.pallas_call(attn_fwd_kernel, out_shape=jax.ShapeDtypeStruct((count_ite...  21.5 us
  transfers between devices with their start and end apart: 4, of which 4 were waited for; matrix products, arithmetic and copies ran while one was open for 17% of the time, Pallas kernels for 0%

profile of v3, /device:TPU:0, one launch (start us, length us, event | category | flops | bytes accessed | tf_op | source)
XLA Modules:
  0.0 816.9 jit_solution(3858643631368260749)
XLA Ops:
  19.5 73.2 %all-gather.4.cloned.1.call-done = bf16[5632,768]{1,0:T(8,128)(2,1)} async-done(((bf16[176,768]{1,0:T(8,128)(2,1)}), bf16[5632,768]{1,0:T(8,128)(2,1)}) %all-gather.4.cloned.1.call-update) | async-done | bytes 8650768 | tf_op jit(solution)/shard_map/all_gather | solution.py:344
  92.8 4.9 slice.366
  101.2 4.6 pad_slice_fusion.5
  105.8 14.0 %fusion.32 = f32[2,1024,768]{2,1,0:T(8,128)S(1)} fusion(bf16[3072,768,1]{1,0,2:T(8,128)(2,1)} %bitcast.547, bf16[2,1024,768]{2,1,0:T(8,128)(2,1)} %copy-done.10, bf16[2,1024,768]{2,1,0:T(8,128)(2,1)} %get-tuple-element.97, bf16[2,1024,768]{2,1,0:T(8,128)(2,1)} %get-tuple-element.96, bf16[2,1024,768]{2,1,0:T(8,128)(2,1)} %get-tuple-element.95), kind=kOutput, calls=%fused_computation.76 | convolution fusion | flops 9714008064 | bytes 23592960 | tf_op jit(solution)/shard_map/hby,yj->hbj/dot_general | solution.py:377
  135.9 11.7 %multiply_reduce_fusion.5 = (f32[2,512]{1,0:T(2,128)S(1)}, f32[2,512,768]{2,1,0:T(8,128)S(1)}) fusion(f32[2,1024,768]{2,1,0:T(8,128)} %copy-done, f32[768]{0:T(1024)S(1)} %add.1773, f32[2,512]{1,0:T(2,128)S(1)} %add_multiply_fusion, f32[2,512]{1,0:T(2,128)S(1)} %add_multiply_fusion.1, f32[2,512]{1,0:T(2,128)S(1)} %add_multiply_fusion.2, ...), kind=kOutput, calls=%fused_computation.62 | convolution fusion | flops 4841274368 | bytes 12614656 | tf_op jit(solution)/shard_map/jvp(ntj,njd->ntd)/dot_general | solution.py:102
  147.7 36.1 %all-gather.6.cloned.1.call-done = bf16[768,7168]{1,0:T(8,128)(2,1)} async-done(((bf16[24,7168]{1,0:T(8,128)(2,1)}), bf16[768,7168]{1,0:T(8,128)(2,1)}) %all-gather.6.cloned.1.call-update) | async-done | bytes 11010064 | tf_op jit(solution)/shard_map/all_gather | solution.py:346
  183.8 7.5 convolution_convert_fusion.q_ref.k_ref.v_ref
  191.3 21.5 %shard_map.565 = bf16[2,512,768]{2,1,0:T(8,128)(2,1)} custom-call(s32[2]{0:T(128)} %len_ref.3, bf16[2,512,2304]{2,1,0:T(8,128)(2,1)} %convolution_convert_fusion.q_ref.k_ref.v_ref, bf16[2,512,2304]{2,1,0:T(8,128)(2,1)} %convolution_convert_fusion.q_ref.k_ref.v_ref, bf16[2,512,2304]{2,1,0:T(8,128)(2,1)} %convolution_convert_fusion.q_ref.k_ref.v_ref), custom_call_target="tpu_custom_call" | custom-call | flops 3221225472 | bytes 6291456 | tf_op jit(solution)/shard_map/pallas_call | solution.py:253
  212.9 4.2 multiply_reduce_fusion.4
  217.2 14.1 %fusion.20 = f32[2,512,4096]{2,1,0:T(8,128)} fusion(bf16[768,7168]{1,0:T(8,128)(2,1)} %all-gather.6.cloned.1.call-done, f32[2,512,768]{2,1,0:T(8,128)S(1)} %get-tuple-element.155, f32[768]{0:T(1024)S(1)} %mul.1575, f32[2,512]{1,0:T(2,128)S(1)} %fusion.186), kind=kOutput, calls=%fused_computation.39 | convolution fusion | flops 6444810240 | bytes 26221568 | tf_op jit(solution)/shard_map/std,de->ste/dot_general | solution.py:394
  231.3 17.5 %bitcast_multiply_fusion.1 = (f32[2,512,2048]{2,1,0:T(8,128)}, f32[2,512,2048]{2,1,0:T(8,128)}, bf16[2,512,2048]{2,1,0:T(8,128)(2,1)}) fusion(f32[2,512,4096]{2,1,0:T(8,128)} %fusion.20, bf16[2048,768,1]{1,0,2:T(8,128)(2,1)S(1)} %bitcast.551, bf16[2,512,768]{2,1,0:T(8,128)(2,1)S(1)} %copy-done.18), kind=kOutput, calls=%fused_computation.20 | convolution fusion | flops 3271557120 | bytes 42467328 | tf_op jit(solution)/shard_map/std,fd->stf/dot_general | solution.py:407
  248.8 14.3 %multiply_reduce_fusion = (bf16[768]{0:T(1024)(128)(2,1)}, f32[2,512]{1,0:T(2,128)S(1)}, f32[2,512,768]{2,1,0:T(8,128)}) fusion(f32[2,512,768]{2,1,0:T(8,128)S(1)} %get-tuple-element.155, f32[2,512]{1,0:T(2,128)S(1)} %fusion.186, f32[768]{0:T(1024)S(1)} %mul.1575, bf16[768,7168]{1,0:T(8,128)(2,1)} %all-gather.6.cloned.1.call-done, ...), kind=kOutput, calls=%fused_computation.55 | convolution fusion | flops 6455556096 | bytes 29372928 | tf_op jit(solution)/shard_map/ste,de->std/dot_general | solution.py:415
  271.8 34.3 %shard_map.566 = (bf16[2,512,768]{2,1,0:T(8,128)(2,1)}, bf16[2,512,768]{2,1,0:T(8,128)(2,1)}, bf16[2,512,768]{2,1,0:T(8,128)(2,1)}) custom-call(s32[2]{0:T(128)} %len_ref.3, bf16[2,512,2304]{2,1,0:T(8,128)(2,1)} %convolution_convert_fusion.q_ref.k_ref.v_ref, bf16[2,512,2304]{2,1,0:T(8,128)(2,1)} %convolution_convert_fusion.q_ref.k_ref.v_ref, ...), custom_call_target="tpu_custom_call" | custom-call | flops 8053063680 | bytes 11010048 | tf_op jit(solution)/shard_map/pallas_call | solution.py:275
  309.5 8.8 %multiply_reduce_fusion.1 = (bf16[768]{0:T(1024)(128)(2,1)}, f32[2,512]{1,0:T(2,128)S(1)}, f32[2,512,768]{2,1,0:T(8,128)S(1)}) fusion(f32[2,512,768]{2,1,0:T(8,128)S(1)} %copy-done.4, f32[2,512]{1,0:T(2,128)S(1)} %fusion.185, f32[768]{0:T(1024)S(1)} %mul.1569, bf16[2,512,2304]{2,1,0:T(8,128)(2,1)S(1)} %constant_dynamic-update-slice_fusion, ...), kind=kOutput, calls=%fused_computation.56 | convolution fusion | flops 3628595456 | bytes 14561792 | tf_op jit(solution)/shard_map/ste,de->std/dot_general | solution.py:431
  320.2 8.6 %select_reduce_fusion.2 = (f32[2,512]{1,0:T(2,128)S(1)}, f32[2,512]{1,0:T(2,128)S(1)}, f32[2,512]{1,0:T(2,128)S(1)}, f32[2,512]{1,0:T(2,128)S(1)}, f32[2,512]{1,0:T(2,128)S(1)}, /*index=5*/f32[2,512]{1,0:T(2,128)S(1)}) fusion(pred[512,1024]{1,0:T(8,128)(4,1)S(1)} %copy-done.25, pred[512,1024]{1,0:T(8,128)(4,1)S(1)} %copy-done.24, ...), kind=kOutput, calls=%fused_computation.44 | convolution fusion | flops 4845987840 | bytes 12610560 | tf_op jit(solution)/shard_map/transpose(jvp(ntd,njd->ntj))/dot_general | solution.py:380
  348.6 13.2 %add_convert_fusion.1 = bf16[2,1024,768]{2,1,0:T(8,128)(2,1)} fusion(f32[768]{0:T(1024)} %mul.1619, f32[2,1024]{1,0:T(2,128)S(1)} %fusion.116, f32[2,512,768]{2,1,0:T(8,128)} %copy-done.11, f32[2,512]{1,0:T(2,128)} %copy-done.57, f32[2,512]{1,0:T(2,128)} %copy-done.56, f32[2,512]{1,0:T(2,128)} %copy-done.59, f32[2,512]{1,0:T(2,128)} %copy-done.58, ...), kind=kOutput, calls=%fused_computation.27 | convolution fusion | flops 4842848256 | bytes 9473024 | tf_op jit(solution)/shard_map/transpose(jvp(ntj,ntd->njd))/dot_general | solution.py:380
  361.8 18.6 %bitcast_convert_fusion.1 = bf16[3072,768]{1,0:T(8,128)(2,1)} fusion(bf16[2,1024,768]{2,1,0:T(8,128)(2,1)} %add_convert_fusion.1, bf16[2,1024,768]{2,1,0:T(8,128)(2,1)} %copy-done.10, bf16[2,1024,768]{2,1,0:T(8,128)(2,1)} %get-tuple-element.97, bf16[2,1024,768]{2,1,0:T(8,128)(2,1)} %get-tuple-element.96, bf16[2,1024,768]{2,1,0:T(8,128)(2,1)} %get-tuple-element.95), kind=kOutput, calls=%fused_computation.12 | convolution fusion | flops 9716367360 | bytes 20447232 | tf_op jit(solution)/shard_map/xwu,xwo->uo/dot_general | solution.py:439
  380.4 8.4 %pad_slice_fusion.2 = (bf16[2,1024,768]{2,1,0:T(8,128)(2,1)}, bf16[2,1024,768]{2,1,0:T(8,128)(2,1)}, bf16[2,1024,768]{2,1,0:T(8,128)(2,1)}, bf16[768]{0:T(1024)(128)(2,1)S(1)}) fusion(bf16[2,1024,768]{2,1,0:T(8,128)(2,1)} %add_convert_fusion.1), kind=kLoop, calls=%fused_computation.71 | loop fusion | flops 1572096 | bytes 12584448 | tf_op jit(solution)/shard_map/slice | solution.py:444
  388.9 5.3 fusion.85
  394.7 10.6 %pad_maximum_fusion.2 = bf16[2,1024,3072]{2,1,0:T(8,128)(2,1)} fusion(bf16[2,1024,768]{2,1,0:T(8,128)(2,1)} %add_convert_fusion.1, bf16[2,1024,768]{2,1,0:T(8,128)(2,1)} %get-tuple-element.93, bf16[2,1024,768]{2,1,0:T(8,128)(2,1)} %get-tuple-element.92, bf16[2,1024,768]{2,1,0:T(8,128)(2,1)} %get-tuple-element.91), kind=kLoop, calls=%fused_computation.6 | loop fusion | flops 50331648 | bytes 25165824 | tf_op jit(solution)/shard_map/concatenate | solution.py:443
  405.2 15.8 %fusion.80 = bf16[32,8,768]{2,1,0:T(8,128)(2,1)S(1)} fusion(bf16[4,768,768,1]{2,1,0,3:T(8,128)(2,1)} %bitcast.548, bf16[2,128,4,8,768]{4,3,2,1,0:T(8,128)(2,1)} %bitcast.542, bf16[2,1024]{1,0:T(2,128)(2,1)} %copy-done.61, s32[2,1024]{1,0:T(2,128)} %param.30), kind=kOutput, calls=%fused_computation.117 | convolution fusion | flops 10472849408 | bytes 17707008 | tf_op jit(solution)/shard_map/xpg,xpz->gz/dot_general | solution.py:454
  421.0 5.8 fusion.10
  433.1 8.0 bitcast_convert_fusion.3
  441.2 5.8 reshape.4378
  447.0 16.9 %bitcast_convert_fusion = bf16[768,4096]{1,0:T(8,128)(2,1)} fusion(f32[2,512,2048]{2,1,0:T(8,128)} %get-tuple-element.89, f32[2,512,2048]{2,1,0:T(8,128)} %get-tuple-element.88, f32[2,512,768]{2,1,0:T(8,128)} %copy-done.1, f32[768]{0:T(1024)S(1)} %copy-done.43, f32[2,512]{1,0:T(2,128)S(1)} %copy-done.49), kind=kOutput, calls=%fused_computation.7 | convolution fusion | flops 6456344576 | bytes 26221568 | tf_op jit(solution)/shard_map/std,ste->de/dot_general | solution.py:412
  463.9 7.5 bitcast_convert_fusion.2
  471.5 9.6 %pad_maximum_fusion = bf16[768,9216]{1,0:T(8,128)(2,1)} fusion(bf16[768,2048]{1,0:T(8,128)(2,1)S(1)} %reshape.4378, bf16[768,4096]{1,0:T(8,128)(2,1)S(1)} %copy-done.7, bf16[768,768]{1,0:T(8,128)(2,1)S(1)} %copy-done.8, bf16[768,2304]{1,0:T(8,128)(2,1)S(1)} %bitcast_convert_fusion.2), kind=kLoop, calls=%fused_computation.1 | loop fusion | flops 56623104 | bytes 28311552 | tf_op jit(solution)/shard_map/concatenate | solution.py:460
  495.3 8.3 %convolution_add_fusion.1 = f32[2,512,768]{2,1,0:T(8,128)} fusion(f32[2,512,768]{2,1,0:T(8,128)S(1)} %copy-done.2, bf16[2,512,2048]{2,1,0:T(8,128)(2,1)} %get-tuple-element.90, bf16[2048,768,1]{1,0,2:T(8,128)(2,1)} %bitcast.550), kind=kOutput, calls=%fused_computation.112 | convolution fusion | flops 3222011904 | bytes 13631488 | tf_op jit(solution)/shard_map/stf,fd->std/dot_general | solution.py:397
  503.6 32.3 %reduce-scatter.3.cloned.1.call-done = bf16[112,768]{1,0:T(8,128)(2,1)} async-done(((bf16[3584,768]{1,0:T(8,128)(2,1)}), bf16[112,768]{1,0:T(8,128)(2,1)}) %reduce-scatter.3.cloned.1.call-update) | async-done | bytes 172048 | tf_op jit(solution)/shard_map/reduce_scatter | solution.py:471
  541.0 163.8 %reduce-scatter.5.cloned.1.call-done = bf16[24,9216]{1,0:T(8,128)(2,1)} async-done(((bf16[768,9216]{1,0:T(8,128)(2,1)}), bf16[24,9216]{1,0:T(8,128)(2,1)}) %reduce-scatter.5.cloned.1.call-update) | async-done | bytes 442384 | tf_op jit(solution)/shard_map/reduce_scatter | solution.py:463
  708.6 12.4 %concatenate.40 = f32[9495]{0:T(1024)S(1)} concatenate(f32[1]{0:T(128)} %bitcast.43, f32[1]{0:T(128)} %bitcast.44, f32[1]{0:T(128)} %bitcast.49, f32[1]{0:T(128)} %bitcast.50, f32[1]{0:T(128)} %bitcast.51, f32[1]{0:T(128)} %bitcast.52, f32[1]{0:T(128)} %bitcast.53, f32[1]{0:T(128)} %bitcast.54, f32[1]{0:T(128)} %bitcast.55, f32[1]{0:T(128)} %bitcast.56, f32[1]{0:T(128)} %bitcast.57, ...), dimensions={0} | concatenate | bytes 75960 | tf_op jit(solution)/shard_map/concatenate | solution.py:503
  721.0 39.8 %psum.7 = f32[9495]{0:T(1024)S(1)} all-reduce(f32[9495]{0:T(1024)S(1)} %concatenate.40), channel_id=1, replica_groups=mesh['fsdp'=16,'dp'=2] {'fsdp','dp'}, use_global_device_ids=true, to_apply=%region_49.50 | all-reduce | flops 9495 | bytes 75960 | tf_op jit(solution)/shard_map/psum | solution.py:505
  (375 shorter events, 129.8 us)
Async XLA Ops:
  7.2 85.6 %all-gather.4.cloned.1.call-start = ((), (), s32[]{:S(2)}) async-start(), calls=%async_computation.2 | async-start | bytes 8921088 | tf_op jit(solution)/shard_map/all_gather | solution.py:344
  11.5 172.3 %all-gather.6.cloned.1.call-start = ((), (), s32[]{:S(2)}) async-start(), calls=%async_computation.3 | async-start | bytes 11354112 | tf_op jit(solution)/shard_map/all_gather | solution.py:346
  15.2 520.7 %reduce-scatter.3.cloned.1.call-start = ((), (), s32[]{:S(2)}) async-start(), calls=%async_computation.4 | async-start | bytes 5677056 | tf_op jit(solution)/shard_map/reduce_scatter | solution.py:471
  15.2 112.3 %copy-start.60 = (f32[256]{0:T(256)}, f32[256]{0:T(256)S(1)}, u32[]{:S(2)}) copy-start(f32[256]{0:T(256)S(1)} %minimum_convert_fusion.11) | copy-start | bytes 3076
  16.6 82.2 %copy-start.61 = (bf16[2,1024]{1,0:T(2,128)(2,1)}, bf16[2,1024]{1,0:T(2,128)(2,1)S(1)}, u32[]{:S(2)}) copy-start(bf16[2,1024]{1,0:T(2,128)(2,1)S(1)} %compare_convert_fusion) | copy-start | bytes 12292
  134.8 183.6 %copy-start.38 = (f32[768]{0:T(1024)}, f32[768]{0:T(1024)S(1)}, u32[]{:S(2)}) copy-start(f32[768]{0:T(1024)S(1)} %mul.1569) | copy-start | bytes 9220
  134.9 128.2 %copy-start.42 = (f32[768]{0:T(1024)}, f32[768]{0:T(1024)S(1)}, u32[]{:S(2)}) copy-start(f32[768]{0:T(1024)S(1)} %mul.1575) | copy-start | bytes 9220
  135.6 12.0 %copy-start.58 = (f32[2,512]{1,0:T(2,128)}, f32[2,512]{1,0:T(2,128)S(1)}, u32[]{:S(2)}) copy-start(f32[2,512]{1,0:T(2,128)S(1)} %add_multiply_fusion.3) | copy-start | bytes 12292
  135.6 12.0 %copy-start.59 = (f32[2,512]{1,0:T(2,128)}, f32[2,512]{1,0:T(2,128)S(1)}, u32[]{:S(2)}) copy-start(f32[2,512]{1,0:T(2,128)S(1)} %add_multiply_fusion.2) | copy-start | bytes 12292
  135.7 11.9 %copy-start.54 = (f32[2,512]{1,0:T(2,128)}, f32[2,512]{1,0:T(2,128)S(1)}, u32[]{:S(2)}) copy-start(f32[2,512]{1,0:T(2,128)S(1)} %add_multiply_fusion.5) | copy-start | bytes 12292
  147.7 43.7 %copy-start.3 = (f32[2,512,768]{2,1,0:T(8,128)}, f32[2,512,768]{2,1,0:T(8,128)S(1)}, u32[]{:S(2)}) copy-start(f32[2,512,768]{2,1,0:T(8,128)S(1)} %get-tuple-element.153) | copy-start | bytes 9437188
  147.7 170.7 %copy-start.40 = (f32[2,512]{1,0:T(2,128)}, f32[2,512]{1,0:T(2,128)S(1)}, u32[]{:S(2)}) copy-start(f32[2,512]{1,0:T(2,128)S(1)} %fusion.185) | copy-start | bytes 12292
  217.1 46.0 %copy-start.1 = (f32[2,512,768]{2,1,0:T(8,128)}, f32[2,512,768]{2,1,0:T(8,128)S(1)}, u32[]{:S(2)}) copy-start(f32[2,512,768]{2,1,0:T(8,128)S(1)} %get-tuple-element.155) | copy-start | bytes 9437188
  217.1 46.0 %copy-start.48 = (f32[2,512]{1,0:T(2,128)}, f32[2,512]{1,0:T(2,128)S(1)}, u32[]{:S(2)}) copy-start(f32[2,512]{1,0:T(2,128)S(1)} %fusion.186) | copy-start | bytes 12292
  217.1 14.2 %copy-start.9 = (bf16[32,64,768]{2,1,0:T(8,128)(2,1)S(1)}, bf16[32,64,768]{2,1,0:T(8,128)(2,1)}, u32[]{:S(2)}) copy-start(bf16[32,64,768]{2,1,0:T(8,128)(2,1)} %slice.378) | copy-start | bytes 9437188
  217.1 14.2 %copy-start.18 = (bf16[2,512,768]{2,1,0:T(8,128)(2,1)S(1)}, bf16[2,512,768]{2,1,0:T(8,128)(2,1)}, u32[]{:S(2)}) copy-start(bf16[2,512,768]{2,1,0:T(8,128)(2,1)} %param.32) | copy-start | bytes 4718596
  426.9 278.0 %reduce-scatter.5.cloned.1.call-start = ((), (), s32[]{:S(2)}) async-start(), calls=%async_computation.5 | async-start | bytes 14598144 | tf_op jit(solution)/shard_map/reduce_scatter | solution.py:463
  447.0 16.9 %copy-start.39 = (f32[768]{0:T(1024)S(1)}, f32[768]{0:T(1024)}, u32[]{:S(2)}) copy-start(f32[768]{0:T(1024)} %copy-done.38) | copy-start | bytes 9220
  447.0 16.9 %copy-start.41 = (f32[2,512]{1,0:T(2,128)S(1)}, f32[2,512]{1,0:T(2,128)}, u32[]{:S(2)}) copy-start(f32[2,512]{1,0:T(2,128)} %copy-done.40) | copy-start | bytes 12292
  481.1 14.2 %copy-start.2 = (f32[2,512,768]{2,1,0:T(8,128)S(1)}, f32[2,512,768]{2,1,0:T(8,128)}, u32[]{:S(2)}) copy-start(f32[2,512,768]{2,1,0:T(8,128)} %copy-done.1) | copy-start | bytes 9437188
  763.4 12.3 %copy-start.71 = (f32[128]{0:T(128)S(1)}, f32[128]{0:T(128)}, u32[]{:S(2)}) copy-start(f32[128]{0:T(128)} %param.56) | copy-start | bytes 1540
  766.1 23.0 %copy-start.50 = (f32[4096]{0:T(1024)S(1)}, f32[4096]{0:T(1024)}, u32[]{:S(2)}) copy-start(f32[4096]{0:T(1024)} %param.54) | copy-start | bytes 49156
  766.1 23.0 %copy-start.52 = (f32[2304]{0:T(1024)S(1)}, f32[2304]{0:T(1024)}, u32[]{:S(2)}) copy-start(f32[2304]{0:T(1024)} %param.48) | copy-start | bytes 27652
  766.1 33.1 %copy-start.12 = (f32[48,4096]{1,0:T(8,128)S(1)}, f32[48,4096]{1,0:T(8,128)}, u32[]{:S(2)}) copy-start(f32[48,4096]{1,0:T(8,128)} %param.37) | copy-start | bytes 2359300
  768.5 33.8 %copy-start.30 = (f32[48,768]{1,0:T(8,128)S(1)}, f32[48,768]{1,0:T(8,128)}, u32[]{:S(2)}) copy-start(f32[48,768]{1,0:T(8,128)} %param.36) | copy-start | bytes 442372
  778.1 26.5 %copy-start.33 = (f32[16,768]{1,0:T(8,128)S(1)}, f32[16,768]{1,0:T(8,128)}, u32[]{:S(2)}) copy-start(f32[16,768]{1,0:T(8,128)} %param.33) | copy-start | bytes 147460
  789.1 18.1 %copy-start.35 = (f32[4096]{0:T(1024)}, f32[4096]{0:T(1024)S(1)}, u32[]{:S(2)}) copy-start(f32[4096]{0:T(1024)S(1)} %fusion.110) | copy-start | bytes 49156
  789.1 13.2 %copy-start.65 = (f32[48]{0:T(128)S(1)}, f32[48]{0:T(128)}, u32[]{:S(2)}) copy-start(f32[48]{0:T(128)} %multiply_add_fusion.11) | copy-start | bytes 580
  789.1 14.1 %copy-start.69 = (f32[48]{0:T(128)S(1)}, f32[48]{0:T(128)}, u32[]{:S(2)}) copy-start(f32[48]{0:T(128)} %multiply_add_fusion.12) | copy-start | bytes 580
  789.2 18.1 %copy-start.36 = (f32[2304]{0:T(1024)}, f32[2304]{0:T(1024)S(1)}, u32[]{:S(2)}) copy-start(f32[2304]{0:T(1024)S(1)} %fusion.113) | copy-start | bytes 27652
  791.3 15.9 %copy-start.53 = (f32[192]{0:T(256)}, f32[192]{0:T(256)S(1)}, u32[]{:S(2)}) copy-start(f32[192]{0:T(256)S(1)} %multiply_add_fusion.8) | copy-start | bytes 2308
  794.7 12.5 %copy-start.66 = (f32[16]{0:T(128)}, f32[16]{0:T(128)S(1)}, u32[]{:S(2)}) copy-start(f32[16]{0:T(128)S(1)} %multiply_add_fusion.13) | copy-start | bytes 196
  (46 other events, 292.3 us)
Sparse Core Ops, SparseCore 0:
  11.6 81.1 all-gather.3
  96.2 87.5 all-gather.5
  427.0 108.8 reduce-scatter.2
  542.8 162.0 reduce-scatter.4

commit v4 on v3

--- a/solution.py
+++ b/solution.py
@@ -1,3 +1,4 @@
+import functools
 import jax
 import jax.numpy as jnp
 from jax import lax
@@ -290,7 +291,131 @@
     return jnp.concatenate(grads, axis=-1)
 
 
+MESH_ID = pl.DeviceIdType.MESH
+
+
+def snake_position(chip):
+    z, y, x = chip // 4, (chip // 2) % 2, chip % 2
+    seg = 2 * y + (x + y) % 2
+    return 4 * seg + z + (seg % 2) * (3 - 2 * z)
+
+
+def snake_chip(position):
+    seg, zz = position // 4, position % 4
+    y = seg // 2
+    return 4 * (zz + (seg % 2) * (3 - 2 * zz)) + 2 * y + (seg % 2 + y) % 2
+
+
+def plain_position(chip):
+    return chip
+
+
+def ring_rs_kernel(snake, x_ref, out_ref, part_ref, send_ref, recv_ref, swap_sem, send_sem, recv_sem, credit):
+    count, steps = x_ref.shape[1], x_ref.shape[1] - 1
+    lanes = out_ref.shape[1] // 2
+    position_of = snake_position if snake else plain_position
+    chip_of = snake_chip if snake else plain_position
+    chip = lax.axis_index("fsdp")
+    core = lax.axis_index("dp")
+    here = position_of(chip)
+    ahead = (chip_of((here + 1) % count), core)
+    behind = (chip_of((here + count - 1) % count), core)
+    partner = (chip, 1 - core)
+    targets = (ahead, behind)
+    sources = (behind, ahead)
+
+    barrier = pltpu.get_barrier_semaphore()
+    for peer in (ahead, behind, partner):
+        pl.semaphore_signal(barrier, 1, device_id=peer, device_id_type=MESH_ID)
+    pl.semaphore_wait(barrier, 3)
+
+    swap = pltpu.make_async_remote_copy(
+        src_ref=x_ref.at[1 - core], dst_ref=part_ref,
+        send_sem=swap_sem.at[0], recv_sem=swap_sem.at[1],
+        device_id=partner, device_id_type=MESH_ID)
+    swap.start()
+    swap.wait_send()
+    swap.wait_recv()
+
+    def link(way, slot):
+        return pltpu.make_async_remote_copy(
+            src_ref=send_ref.at[way, slot], dst_ref=recv_ref.at[way, slot],
+            send_sem=send_sem.at[way, slot], recv_sem=recv_sem.at[way, slot],
+            device_id=targets[way], device_id_type=MESH_ID)
+
+    def own(way, step):
+        shift = step + 1
+        spot = (here - shift + count * 2) % count if way == 0 else (here + shift) % count
+        owner = chip_of(spot)
+        cols = pl.ds(way * lanes, lanes)
+        return (x_ref[core, owner, :, cols].astype(jnp.float32)
+                + part_ref[owner, :, cols].astype(jnp.float32))
+
+    for way in (0, 1):
+        send_ref[way, 0] = own(way, 0).astype(send_ref.dtype)
+        link(way, 0).start()
+
+    def step_body(step, carry):
+        slot_in = (step - 1) % 2
+        slot_out = step % 2
+        for way in (0, 1):
+            link(way, slot_in).wait_recv()
+            total = recv_ref[way, slot_in].astype(jnp.float32) + own(way, step)
+
+            @pl.when(step >= 2)
+            def _():
+                link(way, slot_out).wait_send()
+
+            send_ref[way, slot_out] = total.astype(send_ref.dtype)
+
+            @pl.when(step <= steps - 2)
+            def _():
+                pl.semaphore_signal(credit.at[way], 1, device_id=sources[way], device_id_type=MESH_ID)
+
+            @pl.when(step >= 2)
+            def _():
+                pl.semaphore_wait(credit.at[way], 1)
+
+            link(way, slot_out).start()
+        return carry
+
+    lax.fori_loop(1, steps, step_body, 0)
+
+    last = steps % 2
+    for way in (0, 1):
+        link(way, (steps - 1) % 2).wait_recv()
+        total = recv_ref[way, (steps - 1) % 2].astype(jnp.float32) + own(way, steps)
+        out_ref[:, pl.ds(way * lanes, lanes)] = total
+        link(way, (steps - 2) % 2).wait_send()
+        link(way, (steps - 1) % 2).wait_send()
+
+
+def ring_reduce_scatter(x, snake):
+    _, count, rows, width = x.shape
+    half = width // 2
+    return pl.pallas_call(
+        functools.partial(ring_rs_kernel, snake),
+        out_shape=jax.ShapeDtypeStruct((rows, width), jnp.float32),
+        in_specs=[pl.BlockSpec(memory_space=pltpu.VMEM)],
+        out_specs=pl.BlockSpec(memory_space=pltpu.VMEM),
+        scratch_shapes=[
+            pltpu.VMEM((count, rows, width), x.dtype),
+            pltpu.VMEM((2, 2, rows, half), x.dtype),
+            pltpu.VMEM((2, 2, rows, half), x.dtype),
+            pltpu.SemaphoreType.DMA((2,)),
+            pltpu.SemaphoreType.DMA((2, 2)),
+            pltpu.SemaphoreType.DMA((2, 2)),
+            pltpu.SemaphoreType.REGULAR((2,)),
+        ],
+        compiler_params=pltpu.CompilerParams(collective_id=0, has_side_effects=True,
+                                             vmem_limit_bytes=48 * 1024 * 1024),
+        cost_estimate=pl.CostEstimate(flops=2 * x.size, transcendentals=0,
+                                      bytes_accessed=2 * x.size * x.dtype.itemsize),
+    )(x)
+
+
 def body(
+    snake,
     byte_ids,
     lengths,
     cotangent,
@@ -468,9 +593,9 @@
         [grad_kernel.reshape(count_all, -1, D), grad_table.reshape(count_all, -1, D), piece_vec],
         axis=1).astype(jnp.bfloat16)
     late_rows = late.shape[1]
-    late_part = lax.psum_scatter(late.reshape(-1, D), groups, scatter_dimension=0, tiled=True)
+    late_grid = late.reshape(lax.axis_size("fsdp"), 2, late_rows, D).transpose(1, 0, 2, 3)
+    late_f = ring_reduce_scatter(late_grid, snake)
     early_f = early_part.astype(jnp.float32)
-    late_f = late_part.astype(jnp.float32)
     cut_a = width_project
     cut_b = cut_a + D
     cut_c = cut_b + width_expand
@@ -506,8 +631,7 @@
     sum_sq, sum_rows_old, sum_weights = stats[:7], stats[7:13], stats[13:19]
     sum_vectors, column_scaled_raw = stats[19:23], stats[23:]
     early_own = lax.all_gather(early_part, "dp", axis=0, tiled=True).astype(jnp.float32)
-    late_own = lax.all_gather(late_part.reshape(1, late_rows, D), "dp", axis=0, tiled=True)
-    late_own = late_own.astype(jnp.float32)
+    late_own = lax.all_gather(late_f.reshape(1, late_rows, D), "dp", axis=0, tiled=True)
     shards = (
         late_own[:, k_rows : k_rows + t_rows].reshape(-1, D),
         late_own[:, :k_rows].reshape(-1, D),
@@ -644,4 +768,21 @@
         P(None, "fsdp"),
         P(None, "fsdp"),
     )
-    return jax.shard_map(body, mesh=mesh, in_specs=in_specs, out_specs=out_specs, check_vma=False)
+    return jax.shard_map(
+        functools.partial(body, snake_ring(mesh)),
+        mesh=mesh, in_specs=in_specs, out_specs=out_specs, check_vma=False)
+
+
+def snake_ring(mesh):
+    if dict(mesh.shape) != {"fsdp": 16, "dp": 2}:
+        return False
+    try:
+        for chip in range(16):
+            for core in range(2):
+                device = mesh.devices[chip, core]
+                x, y, z = device.coords[:3]
+                if (4 * z + 2 * y + x, device.core_on_chip) != (chip, core):
+                    return False
+    except (AttributeError, TypeError, ValueError):
+        return False
+    return True

time: 824 us -> 683 us (0.83)
  waiting for transfers between devices: 305 us -> 96.4 us
  Pallas kernels: 55.9 us -> 135 us
  local copies, waits for them, and re-layouts: 78.3 us -> 66.9 us
  matrix products: 208 us -> 199 us
    reduce_scatter x1, waiting for transfers between devices: 164 us -> 0.01 us  [body(): lax.psum_scatter(early, groups, scatter_dimension=0, tiled=True)]
    pallas_call x0 -> x1, Pallas kernels: none -> 79 us  [ring_reduce_scatter(): pl.pallas_call(functools.partial(ring_rs_kernel, snake), out_shape=jax.Sh...]
    reduce_scatter x1 -> x0, waiting for transfers between devices: 32.3 us -> none  [body(): lax.psum_scatter(late.reshape(-1, D), groups, scatter_dimension=0, tiled=...]
  transfers between devices with their start and end apart: 4 -> 3, of which waited for: 4 -> 2; matrix products, arithmetic and copies ran while one was open for 17% -> 29% of each run, Pallas kernels for 0% -> 12%
where the time goes in v4:
time: 683 us; the launch traced here: 675 us
  matrix products  199 us (29%)
  Pallas kernels  135 us (20%)
  other arithmetic  103 us (15%)
  waiting for transfers between devices  96.4 us (14%)
  local copies, waits for them, and re-layouts  66.9 us (10%)
  blocking collectives  44.4 us (7%)
  between operations  30.7 us (4%)
    pallas_call x1, Pallas kernels, ring_reduce_scatter(): pl.pallas_call(functools.partial(ring_rs_kernel, snake), out_shape=jax.Sh...  79 us
    all_gather x1, waiting for transfers between devices, body(): first_all = lax.all_gather(first_group, groups, axis=0, tiled=True)  65.3 us
    psum x1, blocking collectives, body(): stats = lax.psum(stats, groups)  39.1 us
    pallas_call x1, Pallas kernels, attention_backward(): pl.pallas_call(attn_bwd_kernel, out_shape=(part, part, part), grid_spec=p...  34.2 us
    all_gather x1, waiting for transfers between devices, body(): second_all = lax.all_gather(second_group, groups, axis=0, tiled=True)  31 us
    dot_general x3, matrix products, body(): tokens, gbst_pull = jax.vjp(gbst_tokens, hidden, vector_vals[3])  25.3 us
    pallas_call x1, Pallas kernels, attention_forward(): pl.pallas_call(attn_fwd_kernel, out_shape=jax.ShapeDtypeStruct((count_ite...  21.6 us
    dot_general x1, matrix products, body(): jnp.einsum('xwu,xwo->uo', byte_windows, gradient_hidden_reduced, preferre...  18.2 us
  transfers between devices with their start and end apart: 3, of which 2 were waited for; matrix products, arithmetic and copies ran while one was open for 29% of the time, Pallas kernels for 12%

profile of v4, /device:TPU:0, one launch (start us, length us, event | category | flops | bytes accessed | tf_op | source)
XLA Modules:
  0.0 675.3 jit_solution(14287478153586175485)
XLA Ops:
  27.4 65.3 %all-gather.4.cloned.1.call-done = bf16[5632,768]{1,0:T(8,128)(2,1)} async-done(((bf16[176,768]{1,0:T(8,128)(2,1)}), bf16[5632,768]{1,0:T(8,128)(2,1)}) %all-gather.4.cloned.1.call-update) | async-done | bytes 8650768 | tf_op jit(solution)/shard_map/all_gather | solution.py:469
  92.8 4.8 slice.366
  101.7 4.6 pad_slice_fusion.5
  106.2 14.0 %fusion.30 = f32[2,1024,768]{2,1,0:T(8,128)S(1)} fusion(bf16[3072,768,1]{1,0,2:T(8,128)(2,1)} %bitcast.544, bf16[2,1024,768]{2,1,0:T(8,128)(2,1)} %copy-done.11, bf16[2,1024,768]{2,1,0:T(8,128)(2,1)} %get-tuple-element.97, bf16[2,1024,768]{2,1,0:T(8,128)(2,1)} %get-tuple-element.96, bf16[2,1024,768]{2,1,0:T(8,128)(2,1)} %get-tuple-element.95), kind=kOutput, calls=%fused_computation.75 | convolution fusion | flops 9714008064 | bytes 23592960 | tf_op jit(solution)/shard_map/hby,yj->hbj/dot_general | solution.py:502
  132.0 3.9 slice.378
  140.8 11.9 %multiply_reduce_fusion.5 = (f32[2,512]{1,0:T(2,128)S(1)}, f32[2,512,768]{2,1,0:T(8,128)S(1)}) fusion(f32[2,1024,768]{2,1,0:T(8,128)} %copy-done, f32[768]{0:T(1024)S(1)} %add.1771, f32[2,512]{1,0:T(2,128)S(1)} %add_multiply_fusion, f32[2,512]{1,0:T(2,128)S(1)} %add_multiply_fusion.1, f32[2,512]{1,0:T(2,128)S(1)} %add_multiply_fusion.2, ...), kind=kOutput, calls=%fused_computation.61 | convolution fusion | flops 4841274368 | bytes 12614656 | tf_op jit(solution)/shard_map/jvp(ntj,njd->ntd)/dot_general | solution.py:103
  152.8 31.0 %all-gather.6.cloned.1.call-done = bf16[768,7168]{1,0:T(8,128)(2,1)} async-done(((bf16[24,7168]{1,0:T(8,128)(2,1)}), bf16[768,7168]{1,0:T(8,128)(2,1)}) %all-gather.6.cloned.1.call-update) | async-done | bytes 11010064 | tf_op jit(solution)/shard_map/all_gather | solution.py:471
  183.8 7.6 %convolution_convert_fusion.q_ref.k_ref.v_ref = bf16[2,512,2304]{2,1,0:T(8,128)(2,1)} fusion(bf16[768,7168]{1,0:T(8,128)(2,1)} %all-gather.6.cloned.1.call-done, f32[2,512,768]{2,1,0:T(8,128)S(1)} %get-tuple-element.153, f32[768]{0:T(1024)S(1)} %mul.1569, f32[2,512]{1,0:T(2,128)S(1)} %fusion.178), kind=kOutput, calls=%fused_computation.26 | convolution fusion | flops 3628597248 | bytes 11410432 | tf_op jit(solution)/shard_map/std,de->ste/dot_general | solution.py:508
  191.4 21.6 %shard_map.565 = bf16[2,512,768]{2,1,0:T(8,128)(2,1)} custom-call(s32[2]{0:T(128)} %len_ref.3, bf16[2,512,2304]{2,1,0:T(8,128)(2,1)} %convolution_convert_fusion.q_ref.k_ref.v_ref, bf16[2,512,2304]{2,1,0:T(8,128)(2,1)} %convolution_convert_fusion.q_ref.k_ref.v_ref, bf16[2,512,2304]{2,1,0:T(8,128)(2,1)} %convolution_convert_fusion.q_ref.k_ref.v_ref), custom_call_target="tpu_custom_call" | custom-call | flops 3221225472 | bytes 6291456 | tf_op jit(solution)/shard_map/pallas_call | solution.py:254
  212.9 4.2 multiply_reduce_fusion.4
  217.2 14.2 %fusion.18 = f32[2,512,4096]{2,1,0:T(8,128)} fusion(bf16[768,7168]{1,0:T(8,128)(2,1)} %all-gather.6.cloned.1.call-done, f32[2,512,768]{2,1,0:T(8,128)S(1)} %get-tuple-element.155, f32[768]{0:T(1024)S(1)} %mul.1575, f32[2,512]{1,0:T(2,128)S(1)} %fusion.179), kind=kOutput, calls=%fused_computation.38 | convolution fusion | flops 6444810240 | bytes 26221568 | tf_op jit(solution)/shard_map/std,de->ste/dot_general | solution.py:519
  231.4 17.3 %bitcast_multiply_fusion.1 = (f32[2,512,2048]{2,1,0:T(8,128)}, f32[2,512,2048]{2,1,0:T(8,128)}, bf16[2,512,2048]{2,1,0:T(8,128)(2,1)}) fusion(f32[2,512,4096]{2,1,0:T(8,128)} %fusion.18, bf16[2048,768,1]{1,0,2:T(8,128)(2,1)S(1)} %bitcast.547, bf16[2,512,768]{2,1,0:T(8,128)(2,1)S(1)} %copy-done.21), kind=kOutput, calls=%fused_computation.18 | convolution fusion | flops 3271557120 | bytes 42467328 | tf_op jit(solution)/shard_map/std,fd->stf/dot_general | solution.py:532
  248.7 15.3 %bitcast_convert_fusion = bf16[768,4096]{1,0:T(8,128)(2,1)} fusion(f32[2,512,2048]{2,1,0:T(8,128)} %get-tuple-element.89, f32[2,512,2048]{2,1,0:T(8,128)} %get-tuple-element.88, f32[2,512,768]{2,1,0:T(8,128)S(1)} %get-tuple-element.155, f32[768]{0:T(1024)S(1)} %mul.1575, f32[2,512]{1,0:T(2,128)S(1)} %fusion.179), kind=kOutput, calls=%fused_computation.7 | convolution fusion | flops 6456344576 | bytes 26221568 | tf_op jit(solution)/shard_map/std,ste->de/dot_general | solution.py:537
  263.9 14.4 %multiply_reduce_fusion = (bf16[768]{0:T(1024)(128)(2,1)}, f32[2,512]{1,0:T(2,128)S(1)}, f32[2,512,768]{2,1,0:T(8,128)}) fusion(f32[2,512,768]{2,1,0:T(8,128)S(1)} %get-tuple-element.155, f32[2,512]{1,0:T(2,128)S(1)} %fusion.179, f32[768]{0:T(1024)S(1)} %mul.1575, bf16[768,7168]{1,0:T(8,128)(2,1)} %all-gather.6.cloned.1.call-done, ...), kind=kOutput, calls=%fused_computation.54 | convolution fusion | flops 6455556096 | bytes 29372928 | tf_op jit(solution)/shard_map/ste,de->std/dot_general | solution.py:540
  283.3 3.9 convolution_convert_fusion.1.do_ref
  287.3 34.2 %shard_map.566 = (bf16[2,512,768]{2,1,0:T(8,128)(2,1)}, bf16[2,512,768]{2,1,0:T(8,128)(2,1)}, bf16[2,512,768]{2,1,0:T(8,128)(2,1)}) custom-call(s32[2]{0:T(128)} %len_ref.3, bf16[2,512,2304]{2,1,0:T(8,128)(2,1)} %convolution_convert_fusion.q_ref.k_ref.v_ref, bf16[2,512,2304]{2,1,0:T(8,128)(2,1)} %convolution_convert_fusion.q_ref.k_ref.v_ref, ...), custom_call_target="tpu_custom_call" | custom-call | flops 8053063680 | bytes 11010048 | tf_op jit(solution)/shard_map/pallas_call | solution.py:276
  326.1 5.6 bitcast_convert_fusion.2
  333.5 7.3 %bitcast_convert_fusion.3 = bf16[2048,768]{1,0:T(8,128)(2,1)} fusion(bf16[2,512,2048]{2,1,0:T(8,128)(2,1)} %get-tuple-element.90, bf16[2,512,768]{2,1,0:T(8,128)(2,1)S(1)} %copy-done.22), kind=kOutput, calls=%fused_computation.23 | convolution fusion | flops 3222798336 | bytes 8912896 | tf_op jit(solution)/shard_map/stf,std->fd/dot_general | solution.py:529
  340.9 5.5 reshape.4376
  346.4 12.3 %pad_maximum_fusion = bf16[768,9216]{1,0:T(8,128)(2,1)} fusion(bf16[768,2048]{1,0:T(8,128)(2,1)S(1)} %reshape.4376, bf16[768,4096]{1,0:T(8,128)(2,1)} %bitcast_convert_fusion, bf16[768,768]{1,0:T(8,128)(2,1)} %copy.95, bf16[768,2304]{1,0:T(8,128)(2,1)} %bitcast_convert_fusion.2), kind=kLoop, calls=%fused_computation.1 | loop fusion | flops 56623104 | bytes 28311552 | tf_op jit(solution)/shard_map/concatenate | solution.py:585
  374.8 9.4 %multiply_reduce_fusion.1 = (bf16[768]{0:T(1024)(128)(2,1)S(1)}, f32[2,512]{1,0:T(2,128)S(1)}, f32[2,512,768]{2,1,0:T(8,128)S(1)}) fusion(f32[2,512,768]{2,1,0:T(8,128)} %copy-done.3, f32[2,512]{1,0:T(2,128)} %copy-done.70, f32[768]{0:T(1024)} %copy-done.68, bf16[2,512,2304]{2,1,0:T(8,128)(2,1)} %copy-done.26, ...), kind=kOutput, calls=%fused_computation.55 | convolution fusion | flops 3628595456 | bytes 14562816 | tf_op jit(solution)/shard_map/ste,de->std/dot_general | solution.py:556
  386.6 8.6 %select_reduce_fusion.2 = (f32[2,512]{1,0:T(2,128)S(1)}, f32[2,512]{1,0:T(2,128)S(1)}, f32[2,512]{1,0:T(2,128)S(1)}, f32[2,512]{1,0:T(2,128)S(1)}, f32[2,512]{1,0:T(2,128)S(1)}, /*index=5*/f32[2,512]{1,0:T(2,128)S(1)}) fusion(pred[512,1024]{1,0:T(8,128)(4,1)S(1)} %copy-done.28, pred[512,1024]{1,0:T(8,128)(4,1)S(1)} %copy-done.27, ...), kind=kOutput, calls=%fused_computation.43 | convolution fusion | flops 4845987840 | bytes 12610560 | tf_op jit(solution)/shard_map/transpose(jvp(ntd,njd->ntj))/dot_general | solution.py:505
  404.0 11.3 %add_convert_fusion.1 = bf16[2,1024,768]{2,1,0:T(8,128)(2,1)S(1)} fusion(f32[768]{0:T(1024)S(1)} %mul.1619, f32[2,1024]{1,0:T(2,128)S(1)} %fusion.109, f32[2,512,768]{2,1,0:T(8,128)} %copy-done.12, f32[2,512]{1,0:T(2,128)S(1)} %copy-done.93, f32[2,512]{1,0:T(2,128)S(1)} %copy-done.91, f32[2,512]{1,0:T(2,128)S(1)} %copy-done.97, ...), kind=kOutput, calls=%fused_computation.25 | convolution fusion | flops 4842848256 | bytes 9473024 | tf_op jit(solution)/shard_map/transpose(jvp(ntj,ntd->njd))/dot_general | solution.py:505
  415.3 4.4 pad_slice_fusion.2
  419.8 5.3 fusion.78
  425.6 9.6 %pad_maximum_fusion.2 = bf16[2,1024,3072]{2,1,0:T(8,128)(2,1)} fusion(bf16[2,1024,768]{2,1,0:T(8,128)(2,1)S(1)} %add_convert_fusion.1, bf16[2,1024,768]{2,1,0:T(8,128)(2,1)} %get-tuple-element.93, bf16[2,1024,768]{2,1,0:T(8,128)(2,1)} %get-tuple-element.92, bf16[2,1024,768]{2,1,0:T(8,128)(2,1)} %get-tuple-element.91), kind=kLoop, calls=%fused_computation.6 | loop fusion | flops 50331648 | bytes 25165824 | tf_op jit(solution)/shard_map/concatenate | solution.py:568
  435.2 16.4 %fusion.73 = bf16[256,768]{1,0:T(8,128)(2,1)} fusion(bf16[4,768,768,1]{2,1,0,3:T(8,128)(2,1)} %bitcast.545, bf16[2,128,4,8,768]{4,3,2,1,0:T(8,128)(2,1)} %bitcast.539, bf16[2,1024]{1,0:T(2,128)(2,1)S(1)} %copy-done.101, s32[2,1024]{1,0:T(2,128)S(1)} %copy-done.139), kind=kOutput, calls=%fused_computation.115 | convolution fusion | flops 10472849408 | bytes 17707008 | tf_op jit(solution)/shard_map/xpg,xpz->gz/dot_general | solution.py:579
  451.6 18.2 %bitcast_convert_fusion.1 = bf16[3072,768]{1,0:T(8,128)(2,1)} fusion(bf16[2,1024,768]{2,1,0:T(8,128)(2,1)S(1)} %add_convert_fusion.1, bf16[2,1024,768]{2,1,0:T(8,128)(2,1)} %copy-done.11, bf16[2,1024,768]{2,1,0:T(8,128)(2,1)} %get-tuple-element.97, bf16[2,1024,768]{2,1,0:T(8,128)(2,1)} %get-tuple-element.96, bf16[2,1024,768]{2,1,0:T(8,128)(2,1)} %get-tuple-element.95), kind=kOutput, calls=%fused_computation.10 | convolution fusion | flops 9716367360 | bytes 20447232 | tf_op jit(solution)/shard_map/xwu,xwo->uo/dot_general | solution.py:564
  473.2 79.0 %shard_map.567 = f32[112,768]{1,0:T(8,128)S(1)} custom-call(bf16[2,16,112,768]{3,2,1,0:T(8,128)(2,1)S(1)} %copy_bitcast_fusion.x_ref), custom_call_target="tpu_custom_call" | custom-call | flops 5505024 | bytes 11010048 | tf_op jit(solution)/shard_map/pallas_call | solution.py:396
  556.4 7.3 %convolution_add_fusion.1 = f32[2,512,768]{2,1,0:T(8,128)} fusion(f32[2,512,768]{2,1,0:T(8,128)S(1)} %copy-done.2, bf16[2,512,2048]{2,1,0:T(8,128)(2,1)} %get-tuple-element.90, bf16[2048,768,1]{1,0,2:T(8,128)(2,1)S(1)} %bitcast.548), kind=kOutput, calls=%fused_computation.111 | convolution fusion | flops 3222011904 | bytes 13631488 | tf_op jit(solution)/shard_map/stf,fd->std/dot_general | solution.py:522
  567.5 12.2 %concatenate.50 = f32[9495]{0:T(1024)S(1)} concatenate(f32[1]{0:T(128)} %bitcast.44, f32[1]{0:T(128)} %bitcast.45, f32[1]{0:T(128)} %bitcast.50, f32[1]{0:T(128)} %bitcast.51, f32[1]{0:T(128)} %bitcast.52, f32[1]{0:T(128)} %bitcast.53, f32[1]{0:T(128)} %bitcast.54, f32[1]{0:T(128)} %bitcast.55, f32[1]{0:T(128)} %bitcast.56, f32[1]{0:T(128)} %bitcast.57, f32[1]{0:T(128)} %bitcast.58, ...), dimensions={0} | concatenate | bytes 75960 | tf_op jit(solution)/shard_map/concatenate | solution.py:628
  579.7 39.1 %psum.7 = f32[9495]{0:T(1024)S(1)} all-reduce(f32[9495]{0:T(1024)S(1)} %concatenate.50), channel_id=1, replica_groups=mesh['fsdp'=16,'dp'=2] {'fsdp','dp'}, use_global_device_ids=true, to_apply=%region_48.49 | all-reduce | flops 9495 | bytes 75960 | tf_op jit(solution)/shard_map/psum | solution.py:630
  (510 shorter events, 125.0 us)
Async XLA Ops:
  7.2 85.5 %all-gather.4.cloned.1.call-start = ((), (), s32[]{:S(2)}) async-start(), calls=%async_computation.1 | async-start | bytes 8921088 | tf_op jit(solution)/shard_map/all_gather | solution.py:469
  11.5 172.3 %all-gather.6.cloned.1.call-start = ((), (), s32[]{:S(2)}) async-start(), calls=%async_computation.2 | async-start | bytes 11354112 | tf_op jit(solution)/shard_map/all_gather | solution.py:471
  15.2 548.5 %reduce-scatter.2.cloned.1.call-start = ((), (), s32[]{:S(2)}) async-start(), calls=%async_computation.3 | async-start | bytes 14598144 | tf_op jit(solution)/shard_map/reduce_scatter | solution.py:588
  15.2 122.3 %copy-start.104 = (pred[512]{0:T(512)(128)(4,1)}, pred[512]{0:T(512)(128)(4,1)S(1)}, u32[]{:S(2)}) copy-start(pred[512]{0:T(512)(128)(4,1)S(1)} %get-tuple-element.169) | copy-start | bytes 1540
  15.3 123.1 %copy-start.102 = (pred[512]{0:T(512)(128)(4,1)}, pred[512]{0:T(512)(128)(4,1)S(1)}, u32[]{:S(2)}) copy-start(pred[512]{0:T(512)(128)(4,1)S(1)} %get-tuple-element.168) | copy-start | bytes 1540
  15.3 122.3 %copy-start.127 = (pred[512]{0:T(512)(128)(4,1)}, pred[512]{0:T(512)(128)(4,1)S(1)}, u32[]{:S(2)}) copy-start(pred[512]{0:T(512)(128)(4,1)S(1)} %get-tuple-element.173) | copy-start | bytes 1540
  15.3 124.6 %copy-start.125 = (pred[512]{0:T(512)(128)(4,1)}, pred[512]{0:T(512)(128)(4,1)S(1)}, u32[]{:S(2)}) copy-start(pred[512]{0:T(512)(128)(4,1)S(1)} %get-tuple-element.172) | copy-start | bytes 1540
  15.3 122.2 %copy-start.110 = (pred[512]{0:T(512)(128)(4,1)}, pred[512]{0:T(512)(128)(4,1)S(1)}, u32[]{:S(2)}) copy-start(pred[512]{0:T(512)(128)(4,1)S(1)} %get-tuple-element.199) | copy-start | bytes 1540
  15.3 122.2 %copy-start.128 = (pred[512]{0:T(512)(128)(4,1)}, pred[512]{0:T(512)(128)(4,1)S(1)}, u32[]{:S(2)}) copy-start(pred[512]{0:T(512)(128)(4,1)S(1)} %get-tuple-element.198) | copy-start | bytes 1540
  15.9 121.6 %copy-start.112 = (pred[512]{0:T(512)(128)(4,1)}, pred[512]{0:T(512)(128)(4,1)S(1)}, u32[]{:S(2)}) copy-start(pred[512]{0:T(512)(128)(4,1)S(1)} %get-tuple-element.200) | copy-start | bytes 1540
  16.5 121.1 %copy-start.106 = (pred[512]{0:T(512)(128)(4,1)}, pred[512]{0:T(512)(128)(4,1)S(1)}, u32[]{:S(2)}) copy-start(pred[512]{0:T(512)(128)(4,1)S(1)} %get-tuple-element.202) | copy-start | bytes 1540
  17.7 120.7 %copy-start.118 = (pred[512]{0:T(512)(128)(4,1)}, pred[512]{0:T(512)(128)(4,1)S(1)}, u32[]{:S(2)}) copy-start(pred[512]{0:T(512)(128)(4,1)S(1)} %get-tuple-element.193) | copy-start | bytes 1540
  18.3 120.1 %copy-start.120 = (pred[512]{0:T(512)(128)(4,1)}, pred[512]{0:T(512)(128)(4,1)S(1)}, u32[]{:S(2)}) copy-start(pred[512]{0:T(512)(128)(4,1)S(1)} %get-tuple-element.194) | copy-start | bytes 1540
  18.8 119.5 %copy-start.108 = (pred[512]{0:T(512)(128)(4,1)}, pred[512]{0:T(512)(128)(4,1)S(1)}, u32[]{:S(2)}) copy-start(pred[512]{0:T(512)(128)(4,1)S(1)} %get-tuple-element.196) | copy-start | bytes 1540
  18.8 117.2 %copy-start.83 = (pred[512]{0:T(512)(128)(4,1)}, pred[512]{0:T(512)(128)(4,1)S(1)}, u32[]{:S(2)}) copy-start(pred[512]{0:T(512)(128)(4,1)S(1)} %get-tuple-element.204) | copy-start | bytes 1540
  18.8 118.0 %copy-start.81 = (pred[512]{0:T(512)(128)(4,1)}, pred[512]{0:T(512)(128)(4,1)S(1)}, u32[]{:S(2)}) copy-start(pred[512]{0:T(512)(128)(4,1)S(1)} %get-tuple-element.205) | copy-start | bytes 1540
  18.9 117.2 %copy-start.114 = (pred[512]{0:T(512)(128)(4,1)}, pred[512]{0:T(512)(128)(4,1)S(1)}, u32[]{:S(2)}) copy-start(pred[512]{0:T(512)(128)(4,1)S(1)} %get-tuple-element.167) | copy-start | bytes 1540
  18.9 117.9 %copy-start.131 = (pred[512]{0:T(512)(128)(4,1)}, pred[512]{0:T(512)(128)(4,1)S(1)}, u32[]{:S(2)}) copy-start(pred[512]{0:T(512)(128)(4,1)S(1)} %get-tuple-element.166) | copy-start | bytes 1540
  18.9 117.1 %copy-start.132 = (pred[512]{0:T(512)(128)(4,1)}, pred[512]{0:T(512)(128)(4,1)S(1)}, u32[]{:S(2)}) copy-start(pred[512]{0:T(512)(128)(4,1)S(1)} %get-tuple-element.189) | copy-start | bytes 1540
  18.9 117.9 %copy-start.129 = (pred[512]{0:T(512)(128)(4,1)}, pred[512]{0:T(512)(128)(4,1)S(1)}, u32[]{:S(2)}) copy-start(pred[512]{0:T(512)(128)(4,1)S(1)} %get-tuple-element.188) | copy-start | bytes 1540
  19.5 116.5 %copy-start.116 = (pred[512]{0:T(512)(128)(4,1)}, pred[512]{0:T(512)(128)(4,1)S(1)}, u32[]{:S(2)}) copy-start(pred[512]{0:T(512)(128)(4,1)S(1)} %get-tuple-element.190) | copy-start | bytes 1540
  20.1 116.7 %copy-start.130 = (pred[512]{0:T(512)(128)(4,1)}, pred[512]{0:T(512)(128)(4,1)S(1)}, u32[]{:S(2)}) copy-start(pred[512]{0:T(512)(128)(4,1)S(1)} %get-tuple-element.187) | copy-start | bytes 1540
  20.1 119.0 %copy-start.124 = (pred[512]{0:T(512)(128)(4,1)}, pred[512]{0:T(512)(128)(4,1)S(1)}, u32[]{:S(2)}) copy-start(pred[512]{0:T(512)(128)(4,1)S(1)} %get-tuple-element.165) | copy-start | bytes 1540
  20.1 119.8 %copy-start.122 = (pred[512]{0:T(512)(128)(4,1)}, pred[512]{0:T(512)(128)(4,1)S(1)}, u32[]{:S(2)}) copy-start(pred[512]{0:T(512)(128)(4,1)S(1)} %get-tuple-element.164) | copy-start | bytes 1540
  23.6 116.3 %copy-start.43 = (f32[512]{0:T(512)}, f32[512]{0:T(512)S(1)}, u32[]{:S(2)}) copy-start(f32[512]{0:T(512)S(1)} %get-tuple-element.159) | copy-start | bytes 6148
  23.6 116.3 %copy-start.47 = (f32[512]{0:T(512)}, f32[512]{0:T(512)S(1)}, u32[]{:S(2)}) copy-start(f32[512]{0:T(512)S(1)} %get-tuple-element.158) | copy-start | bytes 6148
  23.6 116.3 %copy-start.45 = (f32[512]{0:T(512)}, f32[512]{0:T(512)S(1)}, u32[]{:S(2)}) copy-start(f32[512]{0:T(512)S(1)} %get-tuple-element.160) | copy-start | bytes 6148
  23.6 116.3 %copy-start.51 = (f32[512]{0:T(512)}, f32[512]{0:T(512)S(1)}, u32[]{:S(2)}) copy-start(f32[512]{0:T(512)S(1)} %get-tuple-element.161) | copy-start | bytes 6148
  23.7 116.3 %copy-start.39 = (f32[512]{0:T(512)}, f32[512]{0:T(512)S(1)}, u32[]{:S(2)}) copy-start(f32[512]{0:T(512)S(1)} %get-tuple-element.162) | copy-start | bytes 6148
  23.7 116.3 %copy-start.53 = (f32[512]{0:T(512)}, f32[512]{0:T(512)S(1)}, u32[]{:S(2)}) copy-start(f32[512]{0:T(512)S(1)} %get-tuple-element.163) | copy-start | bytes 6148
  135.9 188.0 %copy-start.68 = (f32[768]{0:T(1024)}, f32[768]{0:T(1024)S(1)}, u32[]{:S(2)}) copy-start(f32[768]{0:T(1024)S(1)} %mul.1569) | copy-start | bytes 9220
  152.8 171.2 %copy-start.70 = (f32[2,512]{1,0:T(2,128)}, f32[2,512]{1,0:T(2,128)S(1)}, u32[]{:S(2)}) copy-start(f32[2,512]{1,0:T(2,128)S(1)} %fusion.178) | copy-start | bytes 12292
  (114 other events, 2096.0 us)
Sparse Core Ops, SparseCore 0:
  11.6 81.1 all-gather.3
  96.2 87.5 all-gather.5
  358.8 169.7 reduce-scatter.1

commit v5 on v4

--- a/solution.py
+++ b/solution.py
@@ -411,6 +411,81 @@
                                              vmem_limit_bytes=48 * 1024 * 1024),
         cost_estimate=pl.CostEstimate(flops=2 * x.size, transcendentals=0,
                                       bytes_accessed=2 * x.size * x.dtype.itemsize),
+    )(x)
+
+
+def sum_kernel(x_ref, out_ref, pair_ref, gather_ref, mine_ref, pair_sem, peer_send, peer_recv, back_sem):
+    count = gather_ref.shape[0]
+    half = gather_ref.shape[1]
+    chip = lax.axis_index("fsdp")
+    core = lax.axis_index("dp")
+    partner = (chip, 1 - core)
+
+    barrier = pltpu.get_barrier_semaphore()
+    pl.semaphore_signal(barrier, 1, device_id=partner, device_id_type=MESH_ID)
+    for other in range(1, count):
+        pl.semaphore_signal(barrier, 1, device_id=((chip + other) % count, core), device_id_type=MESH_ID)
+    pl.semaphore_wait(barrier, count)
+
+    swap = pltpu.make_async_remote_copy(
+        src_ref=x_ref, dst_ref=pair_ref, send_sem=pair_sem.at[0], recv_sem=pair_sem.at[1],
+        device_id=partner, device_id_type=MESH_ID)
+    swap.start()
+    swap.wait_send()
+    swap.wait_recv()
+    rows = pl.ds(core * half, half)
+    mine_ref[...] = x_ref[rows, :] + pair_ref[rows, :]
+
+    def link(other):
+        return pltpu.make_async_remote_copy(
+            src_ref=mine_ref, dst_ref=gather_ref.at[chip],
+            send_sem=peer_send.at[other], recv_sem=peer_recv.at[chip],
+            device_id=((chip + other) % count, core), device_id_type=MESH_ID)
+
+    for other in range(1, count):
+        link(other).start()
+    total = mine_ref[...]
+    for other in range(1, count):
+        source = (chip + other) % count
+        pltpu.make_async_remote_copy(
+            src_ref=mine_ref, dst_ref=gather_ref.at[source],
+            send_sem=peer_send.at[other], recv_sem=peer_recv.at[source],
+            device_id=((chip + count - other) % count, core), device_id_type=MESH_ID).wait_recv()
+        total = total + gather_ref[source]
+    for other in range(1, count):
+        link(other).wait_send()
+    out_ref[rows, :] = total
+    mine_ref[...] = total
+    back = pltpu.make_async_remote_copy(
+        src_ref=mine_ref, dst_ref=out_ref.at[rows],
+        send_sem=back_sem.at[0], recv_sem=back_sem.at[1],
+        device_id=partner, device_id_type=MESH_ID)
+    back.start()
+    back.wait_send()
+    back.wait_recv()
+
+
+def all_sum(x):
+    rows, width = x.shape
+    count = lax.axis_size("fsdp")
+    half = rows // 2
+    return pl.pallas_call(
+        sum_kernel,
+        out_shape=jax.ShapeDtypeStruct((rows, width), jnp.float32),
+        in_specs=[pl.BlockSpec(memory_space=pltpu.VMEM)],
+        out_specs=pl.BlockSpec(memory_space=pltpu.VMEM),
+        scratch_shapes=[
+            pltpu.VMEM((rows, width), jnp.float32),
+            pltpu.VMEM((count, half, width), jnp.float32),
+            pltpu.VMEM((half, width), jnp.float32),
+            pltpu.SemaphoreType.DMA((2,)),
+            pltpu.SemaphoreType.DMA((count,)),
+            pltpu.SemaphoreType.DMA((count,)),
+            pltpu.SemaphoreType.DMA((2,)),
+        ],
+        compiler_params=pltpu.CompilerParams(collective_id=1, has_side_effects=True),
+        cost_estimate=pl.CostEstimate(flops=count * x.size, transcendentals=0,
+                                      bytes_accessed=count * x.size * 4),
     )(x)
 
 
@@ -620,16 +695,34 @@
         expand_columns,
         contract_columns,
     )
-    grad_sq = [jnp.sum(piece * piece) for piece in pieces] + [jnp.sum(vec_part * vec_part)]
-    row_old_sums = [jnp.sum(own_half(entry)) for entry in rows_old]
-    weight_sq = [jnp.sum(jnp.square(own_half(masters[index_param]))) for index_param in range(6)]
-    vector_sq = jnp.sum(jnp.square(own_half(vectors, axis=1)), axis=1)
-    column_all = jnp.concatenate([jnp.sum(piece * piece, axis=0) for piece in pieces])
-    stats = jnp.concatenate(
-        [jnp.stack(grad_sq), jnp.stack(row_old_sums), jnp.stack(weight_sq), vector_sq, column_all])
-    stats = lax.psum(stats, groups)
-    sum_sq, sum_rows_old, sum_weights = stats[:7], stats[7:13], stats[13:19]
-    sum_vectors, column_scaled_raw = stats[19:23], stats[23:]
+    widths = [piece.shape[1] for piece in pieces]
+    column_parts = [jnp.sum(piece * piece, axis=0) for piece in pieces]
+    row_parts = [own_half(entry) for entry in rows_old]
+    weight_parts = [jnp.sum(jnp.square(own_half(masters[index_param])), axis=1) for index_param in range(6)]
+    vec_grad_part = jnp.square(vec_part).reshape(-1)
+    vec_weight_part = jnp.square(own_half(vectors, axis=1)).reshape(-1)
+    flat = jnp.concatenate(column_parts + [vec_grad_part] + row_parts + weight_parts + [vec_weight_part])
+    flat_size = flat.shape[0]
+    flat_padded = -(-flat_size // 2048) * 2048
+    stats = all_sum(jnp.pad(flat, (0, flat_padded - flat_size)).reshape(-1, 128)).reshape(-1)
+
+    def segments(start, lengths):
+        out = []
+        for length in lengths:
+            out.append(stats[start : start + length])
+            start += length
+        return out, start
+
+    column_pieces, at = segments(0, widths)
+    column_scaled_raw = stats[: sum(widths)]
+    (vec_grad_total,), at = segments(at, [vec_grad_part.shape[0]])
+    row_pieces, at = segments(at, [part.shape[0] for part in row_parts])
+    weight_pieces, at = segments(at, [part.shape[0] for part in weight_parts])
+    (vec_weight_total,), at = segments(at, [vec_weight_part.shape[0]])
+    sum_sq = jnp.stack([jnp.sum(part) for part in column_pieces] + [jnp.sum(vec_grad_total)])
+    sum_rows_old = jnp.stack([jnp.sum(part) for part in row_pieces])
+    sum_weights = jnp.stack([jnp.sum(part) for part in weight_pieces])
+    sum_vectors = jnp.sum(vec_weight_total.reshape(4, -1), axis=1)
     early_own = lax.all_gather(early_part, "dp", axis=0, tiled=True).astype(jnp.float32)
     late_own = lax.all_gather(late_f.reshape(1, late_rows, D), "dp", axis=0, tiled=True)
     shards = (

time: 683 us -> 652 us (0.955)
  blocking collectives: 44.4 us -> 5.02 us
  Pallas kernels: 135 us -> 145 us
    psum x1 -> x0, blocking collectives: 39.1 us -> none  [body(): stats = lax.psum(stats, groups)]
    pallas_call x0 -> x1, Pallas kernels: none -> 12.2 us  [all_sum(): pl.pallas_call(sum_kernel, out_shape=jax.ShapeDtypeStruct((rows, width),...]
    concatenate x1, local copies, waits for them, and re-layouts: 12.2 us -> 0.1 us  [body(): jnp.concatenate(column_parts + [vec_grad_part] + row_parts + weight_parts...]
    dynamic_slice x0 -> x6, local copies, waits for them, and re-layouts: none -> 7.61 us  [own_half(): return lax.dynamic_slice_in_dim(value, core * size, size, axis=axis)]
  transfers between devices with their start and end apart: 3 -> 3, of which waited for: 2 -> 2; matrix products, arithmetic and copies ran while one was open for 29% -> 30% of each run, Pallas kernels for 12% -> 12%
where the time goes in v5:
time: 652 us; the launch traced here: 643 us
  matrix products  199 us (31%)
  Pallas kernels  145 us (22%)
  other arithmetic  99 us (15%)
  waiting for transfers between devices  96.5 us (15%)
  local copies, waits for them, and re-layouts  62.8 us (10%)
  between operations  34.9 us (5%)
    pallas_call x1, Pallas kernels, ring_reduce_scatter(): pl.pallas_call(functools.partial(ring_rs_kernel, snake), out_shape=jax.Sh...  77.4 us
    all_gather x1, waiting for transfers between devices, body(): first_all = lax.all_gather(first_group, groups, axis=0, tiled=True)  65.6 us
    pallas_call x1, Pallas kernels, attention_backward(): pl.pallas_call(attn_bwd_kernel, out_shape=(part, part, part), grid_spec=p...  34.2 us
    all_gather x1, waiting for transfers between devices, body(): second_all = lax.all_gather(second_group, groups, axis=0, tiled=True)  30.9 us
    dot_general x3, matrix products, body(): tokens, gbst_pull = jax.vjp(gbst_tokens, hidden, vector_vals[3])  25.3 us
    pallas_call x1, Pallas kernels, attention_forward(): pl.pallas_call(attn_fwd_kernel, out_shape=jax.ShapeDtypeStruct((count_ite...  21.5 us
    dot_general x1, matrix products, body(): jnp.einsum('xwu,xwo->uo', byte_windows, gradient_hidden_reduced, preferre...  18 us
    dot_general x1, matrix products, body(): jnp.einsum('std,fd->stf', cotangent, back_contract, preferred_element_typ...  17.4 us
  transfers between devices with their start and end apart: 3, of which 2 were waited for; matrix products, arithmetic and copies ran while one was open for 30% of the time, Pallas kernels for 12%

profile of v5, /device:TPU:0, one launch (start us, length us, event | category | flops | bytes accessed | tf_op | source)
XLA Modules:
  0.0 642.7 jit_solution(6979223518435123845)
XLA Ops:
  27.2 65.6 %all-gather.4.cloned.1.call-done = bf16[5632,768]{1,0:T(8,128)(2,1)} async-done(((bf16[176,768]{1,0:T(8,128)(2,1)}), bf16[5632,768]{1,0:T(8,128)(2,1)}) %all-gather.4.cloned.1.call-update) | async-done | bytes 8650768 | tf_op jit(solution)/shard_map/all_gather | solution.py:544
  92.8 4.8 slice.359
  101.7 4.7 pad_slice_fusion.5
  106.4 14.0 %fusion.30 = f32[2,1024,768]{2,1,0:T(8,128)S(1)} fusion(bf16[3072,768,1]{1,0,2:T(8,128)(2,1)} %bitcast.536, bf16[2,1024,768]{2,1,0:T(8,128)(2,1)} %copy-done.11, bf16[2,1024,768]{2,1,0:T(8,128)(2,1)} %get-tuple-element.104, bf16[2,1024,768]{2,1,0:T(8,128)(2,1)} %get-tuple-element.103, bf16[2,1024,768]{2,1,0:T(8,128)(2,1)} %get-tuple-element.102), kind=kOutput, calls=%fused_computation.75 | convolution fusion | flops 9714008064 | bytes 23592960 | tf_op jit(solution)/shard_map/hby,yj->hbj/dot_general | solution.py:577
  132.1 3.9 slice.371
  140.9 11.9 %multiply_reduce_fusion.5 = (f32[2,512]{1,0:T(2,128)S(1)}, f32[2,512,768]{2,1,0:T(8,128)S(1)}) fusion(f32[2,1024,768]{2,1,0:T(8,128)} %copy-done, f32[768]{0:T(1024)S(1)} %add.1777, f32[2,512]{1,0:T(2,128)S(1)} %add_multiply_fusion, f32[2,512]{1,0:T(2,128)S(1)} %add_multiply_fusion.1, f32[2,512]{1,0:T(2,128)S(1)} %add_multiply_fusion.2, ...), kind=kOutput, calls=%fused_computation.61 | convolution fusion | flops 4841274368 | bytes 12614656 | tf_op jit(solution)/shard_map/jvp(ntj,njd->ntd)/dot_general | solution.py:103
  152.9 30.9 %all-gather.6.cloned.1.call-done = bf16[768,7168]{1,0:T(8,128)(2,1)} async-done(((bf16[24,7168]{1,0:T(8,128)(2,1)}), bf16[768,7168]{1,0:T(8,128)(2,1)}) %all-gather.6.cloned.1.call-update) | async-done | bytes 11010064 | tf_op jit(solution)/shard_map/all_gather | solution.py:546
  183.8 7.6 %convolution_convert_fusion.q_ref.k_ref.v_ref = bf16[2,512,2304]{2,1,0:T(8,128)(2,1)} fusion(bf16[768,7168]{1,0:T(8,128)(2,1)} %all-gather.6.cloned.1.call-done, f32[2,512,768]{2,1,0:T(8,128)S(1)} %get-tuple-element.141, f32[768]{0:T(1024)S(1)} %mul.1559, f32[2,512]{1,0:T(2,128)S(1)} %fusion.177), kind=kOutput, calls=%fused_computation.26 | convolution fusion | flops 3628597248 | bytes 11410432 | tf_op jit(solution)/shard_map/std,de->ste/dot_general | solution.py:583
  191.4 21.5 %shard_map.565 = bf16[2,512,768]{2,1,0:T(8,128)(2,1)} custom-call(s32[2]{0:T(128)} %len_ref.3, bf16[2,512,2304]{2,1,0:T(8,128)(2,1)} %convolution_convert_fusion.q_ref.k_ref.v_ref, bf16[2,512,2304]{2,1,0:T(8,128)(2,1)} %convolution_convert_fusion.q_ref.k_ref.v_ref, bf16[2,512,2304]{2,1,0:T(8,128)(2,1)} %convolution_convert_fusion.q_ref.k_ref.v_ref), custom_call_target="tpu_custom_call" | custom-call | flops 3221225472 | bytes 6291456 | tf_op jit(solution)/shard_map/pallas_call | solution.py:254
  212.9 4.2 multiply_reduce_fusion.4
  217.1 14.2 %fusion.18 = f32[2,512,4096]{2,1,0:T(8,128)} fusion(bf16[768,7168]{1,0:T(8,128)(2,1)} %all-gather.6.cloned.1.call-done, f32[2,512,768]{2,1,0:T(8,128)S(1)} %get-tuple-element.143, f32[768]{0:T(1024)S(1)} %mul.1565, f32[2,512]{1,0:T(2,128)S(1)} %fusion.178), kind=kOutput, calls=%fused_computation.38 | convolution fusion | flops 6444810240 | bytes 26221568 | tf_op jit(solution)/shard_map/std,de->ste/dot_general | solution.py:594
  231.3 17.4 %bitcast_multiply_fusion.1 = (f32[2,512,2048]{2,1,0:T(8,128)}, f32[2,512,2048]{2,1,0:T(8,128)}, bf16[2,512,2048]{2,1,0:T(8,128)(2,1)}) fusion(f32[2,512,4096]{2,1,0:T(8,128)} %fusion.18, bf16[2048,768,1]{1,0,2:T(8,128)(2,1)S(1)} %bitcast.539, bf16[2,512,768]{2,1,0:T(8,128)(2,1)S(1)} %copy-done.22), kind=kOutput, calls=%fused_computation.18 | convolution fusion | flops 3271557120 | bytes 42467328 | tf_op jit(solution)/shard_map/std,fd->stf/dot_general | solution.py:607
  248.7 15.3 %bitcast_convert_fusion = bf16[768,4096]{1,0:T(8,128)(2,1)} fusion(f32[2,512,2048]{2,1,0:T(8,128)} %get-tuple-element.96, f32[2,512,2048]{2,1,0:T(8,128)} %get-tuple-element.95, f32[2,512,768]{2,1,0:T(8,128)S(1)} %get-tuple-element.143, f32[768]{0:T(1024)S(1)} %mul.1565, f32[2,512]{1,0:T(2,128)S(1)} %fusion.178), kind=kOutput, calls=%fused_computation.7 | convolution fusion | flops 6456344576 | bytes 26221568 | tf_op jit(solution)/shard_map/std,ste->de/dot_general | solution.py:612
  263.9 14.4 %multiply_reduce_fusion = (bf16[768]{0:T(1024)(128)(2,1)}, f32[2,512]{1,0:T(2,128)S(1)}, f32[2,512,768]{2,1,0:T(8,128)}) fusion(f32[2,512,768]{2,1,0:T(8,128)S(1)} %get-tuple-element.143, f32[2,512]{1,0:T(2,128)S(1)} %fusion.178, f32[768]{0:T(1024)S(1)} %mul.1565, bf16[768,7168]{1,0:T(8,128)(2,1)} %all-gather.6.cloned.1.call-done, ...), kind=kOutput, calls=%fused_computation.54 | convolution fusion | flops 6455556096 | bytes 29372928 | tf_op jit(solution)/shard_map/ste,de->std/dot_general | solution.py:615
  283.4 3.9 convolution_convert_fusion.1.do_ref
  287.3 34.2 %shard_map.566 = (bf16[2,512,768]{2,1,0:T(8,128)(2,1)}, bf16[2,512,768]{2,1,0:T(8,128)(2,1)}, bf16[2,512,768]{2,1,0:T(8,128)(2,1)}) custom-call(s32[2]{0:T(128)} %len_ref.3, bf16[2,512,2304]{2,1,0:T(8,128)(2,1)} %convolution_convert_fusion.q_ref.k_ref.v_ref, bf16[2,512,2304]{2,1,0:T(8,128)(2,1)} %convolution_convert_fusion.q_ref.k_ref.v_ref, ...), custom_call_target="tpu_custom_call" | custom-call | flops 8053063680 | bytes 11010048 | tf_op jit(solution)/shard_map/pallas_call | solution.py:276
  326.1 5.6 bitcast_convert_fusion.2
  333.5 7.3 %bitcast_convert_fusion.3 = bf16[2048,768]{1,0:T(8,128)(2,1)} fusion(bf16[2,512,2048]{2,1,0:T(8,128)(2,1)} %get-tuple-element.97, bf16[2,512,768]{2,1,0:T(8,128)(2,1)S(1)} %copy-done.23), kind=kOutput, calls=%fused_computation.23 | convolution fusion | flops 3222798336 | bytes 8912896 | tf_op jit(solution)/shard_map/stf,std->fd/dot_general | solution.py:604
  340.9 5.5 reshape.4411
  346.4 12.3 %pad_maximum_fusion = bf16[768,9216]{1,0:T(8,128)(2,1)} fusion(bf16[768,2048]{1,0:T(8,128)(2,1)S(1)} %reshape.4411, bf16[768,4096]{1,0:T(8,128)(2,1)} %bitcast_convert_fusion, bf16[768,768]{1,0:T(8,128)(2,1)} %copy.95, bf16[768,2304]{1,0:T(8,128)(2,1)} %bitcast_convert_fusion.2), kind=kLoop, calls=%fused_computation.1 | loop fusion | flops 56623104 | bytes 28311552 | tf_op jit(solution)/shard_map/concatenate | solution.py:660
  376.8 9.4 %multiply_reduce_fusion.1 = (bf16[768]{0:T(1024)(128)(2,1)S(1)}, f32[2,512]{1,0:T(2,128)S(1)}, f32[2,512,768]{2,1,0:T(8,128)S(1)}) fusion(f32[2,512,768]{2,1,0:T(8,128)} %copy-done.3, f32[2,512]{1,0:T(2,128)} %copy-done.71, f32[768]{0:T(1024)} %copy-done.69, bf16[2,512,2304]{2,1,0:T(8,128)(2,1)} %copy-done.27, ...), kind=kOutput, calls=%fused_computation.55 | convolution fusion | flops 3628595456 | bytes 14562816 | tf_op jit(solution)/shard_map/ste,de->std/dot_general | solution.py:631
  388.5 8.6 %select_reduce_fusion.2 = (f32[2,512]{1,0:T(2,128)S(1)}, f32[2,512]{1,0:T(2,128)S(1)}, f32[2,512]{1,0:T(2,128)S(1)}, f32[2,512]{1,0:T(2,128)S(1)}, f32[2,512]{1,0:T(2,128)S(1)}, /*index=5*/f32[2,512]{1,0:T(2,128)S(1)}) fusion(pred[512,1024]{1,0:T(8,128)(4,1)S(1)} %copy-done.29, pred[512,1024]{1,0:T(8,128)(4,1)S(1)} %copy-done.28, ...), kind=kOutput, calls=%fused_computation.43 | convolution fusion | flops 4845987840 | bytes 12610560 | tf_op jit(solution)/shard_map/transpose(jvp(ntd,njd->ntj))/dot_general | solution.py:580
  405.9 11.3 %add_convert_fusion.1 = bf16[2,1024,768]{2,1,0:T(8,128)(2,1)S(1)} fusion(f32[768]{0:T(1024)S(1)} %mul.1609, f32[2,1024]{1,0:T(2,128)S(1)} %fusion.104, f32[2,512,768]{2,1,0:T(8,128)} %copy-done.12, f32[2,512]{1,0:T(2,128)S(1)} %copy-done.94, f32[2,512]{1,0:T(2,128)S(1)} %copy-done.92, f32[2,512]{1,0:T(2,128)S(1)} %copy-done.101, ...), kind=kOutput, calls=%fused_computation.25 | convolution fusion | flops 4842848256 | bytes 9473024 | tf_op jit(solution)/shard_map/transpose(jvp(ntj,ntd->njd))/dot_general | solution.py:580
  417.2 4.4 pad_slice_fusion.2
  421.6 5.3 fusion.78
  427.5 9.6 %pad_maximum_fusion.2 = bf16[2,1024,3072]{2,1,0:T(8,128)(2,1)} fusion(bf16[2,1024,768]{2,1,0:T(8,128)(2,1)S(1)} %add_convert_fusion.1, bf16[2,1024,768]{2,1,0:T(8,128)(2,1)} %get-tuple-element.100, bf16[2,1024,768]{2,1,0:T(8,128)(2,1)} %get-tuple-element.99, bf16[2,1024,768]{2,1,0:T(8,128)(2,1)} %get-tuple-element.98), kind=kLoop, calls=%fused_computation.6 | loop fusion | flops 50331648 | bytes 25165824 | tf_op jit(solution)/shard_map/concatenate | solution.py:643
  437.1 16.4 %fusion.73 = bf16[256,768]{1,0:T(8,128)(2,1)} fusion(bf16[4,768,768,1]{2,1,0,3:T(8,128)(2,1)} %bitcast.537, bf16[2,128,4,8,768]{4,3,2,1,0:T(8,128)(2,1)} %bitcast.531, bf16[2,1024]{1,0:T(2,128)(2,1)S(1)} %copy-done.105, s32[2,1024]{1,0:T(2,128)S(1)} %copy-done.155), kind=kOutput, calls=%fused_computation.115 | convolution fusion | flops 10472849408 | bytes 17707008 | tf_op jit(solution)/shard_map/xpg,xpz->gz/dot_general | solution.py:654
  453.6 18.0 %bitcast_convert_fusion.1 = bf16[3072,768]{1,0:T(8,128)(2,1)} fusion(bf16[2,1024,768]{2,1,0:T(8,128)(2,1)S(1)} %add_convert_fusion.1, bf16[2,1024,768]{2,1,0:T(8,128)(2,1)} %copy-done.11, bf16[2,1024,768]{2,1,0:T(8,128)(2,1)} %get-tuple-element.104, bf16[2,1024,768]{2,1,0:T(8,128)(2,1)} %get-tuple-element.103, bf16[2,1024,768]{2,1,0:T(8,128)(2,1)} %get-tuple-element.102), kind=kOutput, calls=%fused_computation.10 | convolution fusion | flops 9716367360 | bytes 20447232 | tf_op jit(solution)/shard_map/xwu,xwo->uo/dot_general | solution.py:639
  471.5 3.8 copy_bitcast_fusion.x_ref
  475.3 77.4 %shard_map.567 = f32[112,768]{1,0:T(8,128)S(1)} custom-call(bf16[2,16,112,768]{3,2,1,0:T(8,128)(2,1)S(1)} %copy_bitcast_fusion.x_ref), custom_call_target="tpu_custom_call" | custom-call | flops 5505024 | bytes 11010048 | tf_op jit(solution)/shard_map/pallas_call | solution.py:396
  552.9 7.3 %convolution_add_fusion.1 = f32[2,512,768]{2,1,0:T(8,128)} fusion(f32[2,512,768]{2,1,0:T(8,128)S(1)} %copy-done.2, bf16[2,512,2048]{2,1,0:T(8,128)(2,1)} %get-tuple-element.97, bf16[2048,768,1]{1,0,2:T(8,128)(2,1)S(1)} %bitcast.540), kind=kOutput, calls=%fused_computation.111 | convolution fusion | flops 3222011904 | bytes 13631488 | tf_op jit(solution)/shard_map/stf,fd->std/dot_general | solution.py:597
  564.7 12.2 %shard_map.568 = f32[80,128]{1,0:T(8,128)} custom-call(f32[80,128]{1,0:T(8,128)} %pad_bitcast_fusion.x_ref), custom_call_target="tpu_custom_call" | custom-call | flops 163840 | bytes 655360 | tf_op jit(solution)/shard_map/pallas_call | solution.py:472
  (552 shorter events, 125.1 us)
Async XLA Ops:
  7.2 85.5 %all-gather.4.cloned.1.call-start = ((), (), s32[]{:S(2)}) async-start(), calls=%async_computation.1 | async-start | bytes 8921088 | tf_op jit(solution)/shard_map/all_gather | solution.py:544
  11.5 172.3 %all-gather.6.cloned.1.call-start = ((), (), s32[]{:S(2)}) async-start(), calls=%async_computation.2 | async-start | bytes 11354112 | tf_op jit(solution)/shard_map/all_gather | solution.py:546
  15.2 545.0 %reduce-scatter.2.cloned.1.call-start = ((), (), s32[]{:S(2)}) async-start(), calls=%async_computation.3 | async-start | bytes 14598144 | tf_op jit(solution)/shard_map/reduce_scatter | solution.py:663
  15.2 122.4 %copy-start.108 = (pred[512]{0:T(512)(128)(4,1)}, pred[512]{0:T(512)(128)(4,1)S(1)}, u32[]{:S(2)}) copy-start(pred[512]{0:T(512)(128)(4,1)S(1)} %get-tuple-element.157) | copy-start | bytes 1540
  15.3 123.2 %copy-start.106 = (pred[512]{0:T(512)(128)(4,1)}, pred[512]{0:T(512)(128)(4,1)S(1)}, u32[]{:S(2)}) copy-start(pred[512]{0:T(512)(128)(4,1)S(1)} %get-tuple-element.156) | copy-start | bytes 1540
  15.3 122.4 %copy-start.131 = (pred[512]{0:T(512)(128)(4,1)}, pred[512]{0:T(512)(128)(4,1)S(1)}, u32[]{:S(2)}) copy-start(pred[512]{0:T(512)(128)(4,1)S(1)} %get-tuple-element.161) | copy-start | bytes 1540
  15.3 124.7 %copy-start.129 = (pred[512]{0:T(512)(128)(4,1)}, pred[512]{0:T(512)(128)(4,1)S(1)}, u32[]{:S(2)}) copy-start(pred[512]{0:T(512)(128)(4,1)S(1)} %get-tuple-element.160) | copy-start | bytes 1540
  15.3 122.3 %copy-start.114 = (pred[512]{0:T(512)(128)(4,1)}, pred[512]{0:T(512)(128)(4,1)S(1)}, u32[]{:S(2)}) copy-start(pred[512]{0:T(512)(128)(4,1)S(1)} %get-tuple-element.187) | copy-start | bytes 1540
  15.3 122.3 %copy-start.132 = (pred[512]{0:T(512)(128)(4,1)}, pred[512]{0:T(512)(128)(4,1)S(1)}, u32[]{:S(2)}) copy-start(pred[512]{0:T(512)(128)(4,1)S(1)} %get-tuple-element.186) | copy-start | bytes 1540
  15.9 121.8 %copy-start.116 = (pred[512]{0:T(512)(128)(4,1)}, pred[512]{0:T(512)(128)(4,1)S(1)}, u32[]{:S(2)}) copy-start(pred[512]{0:T(512)(128)(4,1)S(1)} %get-tuple-element.188) | copy-start | bytes 1540
  16.5 121.2 %copy-start.110 = (pred[512]{0:T(512)(128)(4,1)}, pred[512]{0:T(512)(128)(4,1)S(1)}, u32[]{:S(2)}) copy-start(pred[512]{0:T(512)(128)(4,1)S(1)} %get-tuple-element.190) | copy-start | bytes 1540
  17.6 120.8 %copy-start.122 = (pred[512]{0:T(512)(128)(4,1)}, pred[512]{0:T(512)(128)(4,1)S(1)}, u32[]{:S(2)}) copy-start(pred[512]{0:T(512)(128)(4,1)S(1)} %get-tuple-element.181) | copy-start | bytes 1540
  18.2 120.3 %copy-start.124 = (pred[512]{0:T(512)(128)(4,1)}, pred[512]{0:T(512)(128)(4,1)S(1)}, u32[]{:S(2)}) copy-start(pred[512]{0:T(512)(128)(4,1)S(1)} %get-tuple-element.182) | copy-start | bytes 1540
  18.7 119.8 %copy-start.112 = (pred[512]{0:T(512)(128)(4,1)}, pred[512]{0:T(512)(128)(4,1)S(1)}, u32[]{:S(2)}) copy-start(pred[512]{0:T(512)(128)(4,1)S(1)} %get-tuple-element.184) | copy-start | bytes 1540
  18.7 117.5 %copy-start.84 = (pred[512]{0:T(512)(128)(4,1)}, pred[512]{0:T(512)(128)(4,1)S(1)}, u32[]{:S(2)}) copy-start(pred[512]{0:T(512)(128)(4,1)S(1)} %get-tuple-element.192) | copy-start | bytes 1540
  18.7 118.2 %copy-start.82 = (pred[512]{0:T(512)(128)(4,1)}, pred[512]{0:T(512)(128)(4,1)S(1)}, u32[]{:S(2)}) copy-start(pred[512]{0:T(512)(128)(4,1)S(1)} %get-tuple-element.193) | copy-start | bytes 1540
  18.7 117.5 %copy-start.118 = (pred[512]{0:T(512)(128)(4,1)}, pred[512]{0:T(512)(128)(4,1)S(1)}, u32[]{:S(2)}) copy-start(pred[512]{0:T(512)(128)(4,1)S(1)} %get-tuple-element.155) | copy-start | bytes 1540
  18.8 118.2 %copy-start.135 = (pred[512]{0:T(512)(128)(4,1)}, pred[512]{0:T(512)(128)(4,1)S(1)}, u32[]{:S(2)}) copy-start(pred[512]{0:T(512)(128)(4,1)S(1)} %get-tuple-element.154) | copy-start | bytes 1540
  18.8 117.4 %copy-start.136 = (pred[512]{0:T(512)(128)(4,1)}, pred[512]{0:T(512)(128)(4,1)S(1)}, u32[]{:S(2)}) copy-start(pred[512]{0:T(512)(128)(4,1)S(1)} %get-tuple-element.177) | copy-start | bytes 1540
  18.8 118.2 %copy-start.133 = (pred[512]{0:T(512)(128)(4,1)}, pred[512]{0:T(512)(128)(4,1)S(1)}, u32[]{:S(2)}) copy-start(pred[512]{0:T(512)(128)(4,1)S(1)} %get-tuple-element.176) | copy-start | bytes 1540
  19.4 116.8 %copy-start.120 = (pred[512]{0:T(512)(128)(4,1)}, pred[512]{0:T(512)(128)(4,1)S(1)}, u32[]{:S(2)}) copy-start(pred[512]{0:T(512)(128)(4,1)S(1)} %get-tuple-element.178) | copy-start | bytes 1540
  19.9 117.1 %copy-start.134 = (pred[512]{0:T(512)(128)(4,1)}, pred[512]{0:T(512)(128)(4,1)S(1)}, u32[]{:S(2)}) copy-start(pred[512]{0:T(512)(128)(4,1)S(1)} %get-tuple-element.175) | copy-start | bytes 1540
  19.9 119.3 %copy-start.128 = (pred[512]{0:T(512)(128)(4,1)}, pred[512]{0:T(512)(128)(4,1)S(1)}, u32[]{:S(2)}) copy-start(pred[512]{0:T(512)(128)(4,1)S(1)} %get-tuple-element.153) | copy-start | bytes 1540
  19.9 120.1 %copy-start.126 = (pred[512]{0:T(512)(128)(4,1)}, pred[512]{0:T(512)(128)(4,1)S(1)}, u32[]{:S(2)}) copy-start(pred[512]{0:T(512)(128)(4,1)S(1)} %get-tuple-element.152) | copy-start | bytes 1540
  23.3 116.7 %copy-start.44 = (f32[512]{0:T(512)}, f32[512]{0:T(512)S(1)}, u32[]{:S(2)}) copy-start(f32[512]{0:T(512)S(1)} %get-tuple-element.147) | copy-start | bytes 6148
  23.4 116.7 %copy-start.48 = (f32[512]{0:T(512)}, f32[512]{0:T(512)S(1)}, u32[]{:S(2)}) copy-start(f32[512]{0:T(512)S(1)} %get-tuple-element.146) | copy-start | bytes 6148
  23.4 116.6 %copy-start.46 = (f32[512]{0:T(512)}, f32[512]{0:T(512)S(1)}, u32[]{:S(2)}) copy-start(f32[512]{0:T(512)S(1)} %get-tuple-element.148) | copy-start | bytes 6148
  23.4 116.6 %copy-start.52 = (f32[512]{0:T(512)}, f32[512]{0:T(512)S(1)}, u32[]{:S(2)}) copy-start(f32[512]{0:T(512)S(1)} %get-tuple-element.149) | copy-start | bytes 6148
  23.4 116.6 %copy-start.40 = (f32[512]{0:T(512)}, f32[512]{0:T(512)S(1)}, u32[]{:S(2)}) copy-start(f32[512]{0:T(512)S(1)} %get-tuple-element.150) | copy-start | bytes 6148
  23.4 116.6 %copy-start.54 = (f32[512]{0:T(512)}, f32[512]{0:T(512)S(1)}, u32[]{:S(2)}) copy-start(f32[512]{0:T(512)S(1)} %get-tuple-element.151) | copy-start | bytes 6148
  136.1 187.8 %copy-start.69 = (f32[768]{0:T(1024)}, f32[768]{0:T(1024)S(1)}, u32[]{:S(2)}) copy-start(f32[768]{0:T(1024)S(1)} %mul.1559) | copy-start | bytes 9220
  152.9 171.1 %copy-start.71 = (f32[2,512]{1,0:T(2,128)}, f32[2,512]{1,0:T(2,128)S(1)}, u32[]{:S(2)}) copy-start(f32[2,512]{1,0:T(2,128)S(1)} %fusion.177) | copy-start | bytes 12292
  (130 other events, 2309.2 us)
Sparse Core Ops, SparseCore 0:
  11.6 81.1 all-gather.3
  96.2 87.5 all-gather.5
  358.8 167.6 reduce-scatter.1

commit v6 on v5

--- a/solution.py
+++ b/solution.py
@@ -83,34 +83,38 @@
         rows.append(0.5 * total)
     return jnp.stack(rows, axis=1)
 
-def band_matrix(coef, count):
-    tok = lax.broadcasted_iota(jnp.int32, (1, count // 2, count), 1)
-    col = lax.broadcasted_iota(jnp.int32, (1, count // 2, count), 2)
-    gap = col - 2 * tok
-    band = jnp.zeros((coef.shape[0], count // 2, count), jnp.float32)
-    for index_o, o in enumerate(OFFSETS):
-        band = jnp.where(gap == o, coef[:, index_o, :, None], band)
-    return band
+def shift_down(values):
+    return jnp.pad(values[:, :-1], ((0, 0), (1, 0), (0, 0)))
+
+
+def shift_up(values):
+    return jnp.pad(values[:, 1:], ((0, 0), (0, 1), (0, 0)))
+
+
+def neighbours(hidden):
+    even, odd = hidden[:, 0::2], hidden[:, 1::2]
+    return (shift_down(even), shift_down(odd), even, odd, shift_up(even), shift_up(odd))
+
 
 @jax.custom_vjp
 def gbst_tokens(hidden, scorer):
     return gbst_fwd(hidden, scorer)[0]
 
+
 def gbst_fwd(hidden, scorer):
     count = hidden.shape[1]
     mixing = gbst_weights(hidden, scorer)
-    band = band_matrix(diagonals(mixing, count), count)
-    tokens = jnp.einsum("ntj,njd->ntd", band, hidden, precision=HIGH_3)
-    return tokens, (hidden, scorer, mixing, band)
+    coef = diagonals(mixing, count)
+    terms = neighbours(hidden)
+    tokens = sum(coef[:, index_o, :, None] * terms[index_o] for index_o in range(len(OFFSETS)))
+    return tokens, (hidden, scorer, mixing, coef)
+
 
 def gbst_bwd(saved, grad_tokens):
-    hidden, scorer, mixing, band = saved
+    hidden, scorer, mixing, coef = saved
     count = hidden.shape[1]
-    cross = jnp.einsum("ntd,njd->ntj", grad_tokens, hidden, precision=HIGH_3)
-    tok = lax.broadcasted_iota(jnp.int32, (1, count // 2, count), 1)
-    col = lax.broadcasted_iota(jnp.int32, (1, count // 2, count), 2)
-    gap = col - 2 * tok
-    diag = jnp.stack([jnp.sum(jnp.where(gap == o, cross, 0.0), axis=2) for o in OFFSETS], axis=1)
+    terms = neighbours(hidden)
+    diag = jnp.stack([jnp.sum(grad_tokens * term, axis=2) for term in terms], axis=1)
     tok1 = lax.broadcasted_iota(jnp.int32, (1, count // 2), 1)
     grad_mix = []
     for index_b, b in enumerate((1, 2, 3, 4)):
@@ -127,10 +131,15 @@
     grad_mix = jnp.stack(grad_mix, axis=1)
     grad_scores = mixing * (grad_mix - jnp.sum(mixing * grad_mix, axis=1, keepdims=True))
     spread = sum(pool_vec(grad_scores[:, index_b], b) for index_b, b in enumerate((1, 2, 3, 4)))
-    grad_hidden = jnp.einsum("ntj,ntd->njd", band, grad_tokens, precision=HIGH_3)
-    grad_hidden = grad_hidden + spread[:, :, None] * scorer
+    weighted = [coef[:, index_o, :, None] * grad_tokens for index_o in range(len(OFFSETS))]
+    grad_even = weighted[2] + shift_up(weighted[0]) + shift_down(weighted[4])
+    grad_odd = weighted[3] + shift_up(weighted[1]) + shift_down(weighted[5])
+    grad_even = grad_even + spread[:, 0::2, None] * scorer
+    grad_odd = grad_odd + spread[:, 1::2, None] * scorer
+    grad_hidden = jnp.stack([grad_even, grad_odd], axis=2).reshape(hidden.shape)
     grad_scorer = jnp.einsum("nj,njd->d", spread, hidden, precision=HIGHEST)
     return grad_hidden, grad_scorer
+
 
 gbst_tokens.defvjp(gbst_fwd, gbst_bwd)
 
@@ -706,23 +715,22 @@
     flat_padded = -(-flat_size // 2048) * 2048
     stats = all_sum(jnp.pad(flat, (0, flat_padded - flat_size)).reshape(-1, 128)).reshape(-1)
 
-    def segments(start, lengths):
-        out = []
-        for length in lengths:
-            out.append(stats[start : start + length])
-            start += length
-        return out, start
-
-    column_pieces, at = segments(0, widths)
     column_scaled_raw = stats[: sum(widths)]
-    (vec_grad_total,), at = segments(at, [vec_grad_part.shape[0]])
-    row_pieces, at = segments(at, [part.shape[0] for part in row_parts])
-    weight_pieces, at = segments(at, [part.shape[0] for part in weight_parts])
-    (vec_weight_total,), at = segments(at, [vec_weight_part.shape[0]])
-    sum_sq = jnp.stack([jnp.sum(part) for part in column_pieces] + [jnp.sum(vec_grad_total)])
-    sum_rows_old = jnp.stack([jnp.sum(part) for part in row_pieces])
-    sum_weights = jnp.stack([jnp.sum(part) for part in weight_pieces])
-    sum_vectors = jnp.sum(vec_weight_total.reshape(4, -1), axis=1)
+    bounds = []
+    start = 0
+    for length in widths + [vec_grad_part.shape[0]]:
+        bounds.append((start, start + length))
+        start += length
+    for part in row_parts + weight_parts:
+        bounds.append((start, start + part.shape[0]))
+        start += part.shape[0]
+    for row in range(4):
+        bounds.append((start + row * vec_width, start + (row + 1) * vec_width))
+    starts = jnp.array([lo for lo, _ in bounds], jnp.int32)[:, None]
+    ends = jnp.array([hi for _, hi in bounds], jnp.int32)[:, None]
+    spot = lax.broadcasted_iota(jnp.int32, (len(bounds), flat_padded), 1)
+    sums = jnp.sum(jnp.where((spot >= starts) & (spot < ends), stats[None, :], 0.0), axis=1)
+    sum_sq, sum_rows_old, sum_weights, sum_vectors = sums[:7], sums[7:13], sums[13:19], sums[19:23]
     early_own = lax.all_gather(early_part, "dp", axis=0, tiled=True).astype(jnp.float32)
     late_own = lax.all_gather(late_f.reshape(1, late_rows, D), "dp", axis=0, tiled=True)
     shards = (

time: 652 us -> 703 us (1.078)
  local copies, waits for them, and re-layouts: 62.8 us -> 162 us
  other arithmetic: 99 us -> 134 us
  waiting for transfers between devices: 96.5 us -> 63.1 us
  matrix products: 199 us -> 168 us
  Pallas kernels: 145 us -> 132 us
    slice x0 -> x5, local copies, waits for them, and re-layouts: none -> 45.8 us  [the longest x2 28.9 us: neighbours(): even, odd = (hidden[:, 0::2], hidden[:, 1::2])]
    concatenate x1, other arithmetic: 9.63 us -> 50.5 us  [body(): jnp.concatenate([grad_padded[:, KS - 1 - shift_at:KS - 1 - shift_at + cou...]
    concatenate x0 -> x1, local copies, waits for them, and re-layouts: none -> 31.3 us  [body(): jnp.concatenate([grad_padded[:, KS - 1 - shift_at:KS - 1 - shift_at + cou...]
    all_gather x1, waiting for transfers between devices: 30.9 us -> 0.02 us  [body(): second_all = lax.all_gather(second_group, groups, axis=0, tiled=True)]
    dot_general x3 -> x1, matrix products: 25.3 us -> 5.45 us  [body(): tokens, gbst_pull = jax.vjp(gbst_tokens, hidden, vector_vals[3])]
    dot_general x0 -> x1, local copies, waits for them, and re-layouts: none -> 17.2 us  [body(): jnp.einsum('xwu,xwo->uo', byte_windows, gradient_hidden_reduced, preferre...]
    pallas_call x1, Pallas kernels: 77.4 us -> 63.5 us  [ring_reduce_scatter(): pl.pallas_call(functools.partial(ring_rs_kernel, snake), out_shape=jax.Sh...]
    dot_general x1 -> x0, matrix products: 11.9 us -> none  [gbst_fwd(): tokens = jnp.einsum('ntj,njd->ntd', band, hidden, precision=HIGH_3)]
  transfers between devices with their start and end apart: 3 -> 3, of which waited for: 2 -> 1; matrix products, arithmetic and copies ran while one was open for 30% -> 43% of each run, Pallas kernels for 12% -> 9%
where the time goes in v6:
time: 703 us; the launch traced here: 695 us
  matrix products  168 us (24%)
  local copies, waits for them, and re-layouts  162 us (23%)
  other arithmetic  134 us (19%)
  Pallas kernels  132 us (19%)
  waiting for transfers between devices  63.1 us (9%)
  between operations  30.7 us (4%)
    pallas_call x1, Pallas kernels, ring_reduce_scatter(): pl.pallas_call(functools.partial(ring_rs_kernel, snake), out_shape=jax.Sh...  63.5 us
    all_gather x1, waiting for transfers between devices, body(): first_all = lax.all_gather(first_group, groups, axis=0, tiled=True)  63 us
    concatenate x1, other arithmetic, body(): jnp.concatenate([grad_padded[:, KS - 1 - shift_at:KS - 1 - shift_at + cou...  50.5 us
    pallas_call x1, Pallas kernels, attention_backward(): pl.pallas_call(attn_bwd_kernel, out_shape=(part, part, part), grid_spec=p...  34.2 us
    concatenate x1, local copies, waits for them, and re-layouts, body(): jnp.concatenate([grad_padded[:, KS - 1 - shift_at:KS - 1 - shift_at + cou...  31.3 us
    slice x2, local copies, waits for them, and re-layouts, neighbours(): even, odd = (hidden[:, 0::2], hidden[:, 1::2])  28.9 us
    pallas_call x1, Pallas kernels, attention_forward(): pl.pallas_call(attn_fwd_kernel, out_shape=jax.ShapeDtypeStruct((count_ite...  21.5 us
    dot_general x1, matrix products, body(): jnp.einsum('std,fd->stf', cotangent, back_contract, preferred_element_typ...  17.2 us
  transfers between devices with their start and end apart: 3, of which 1 were waited for; matrix products, arithmetic and copies ran while one was open for 43% of the time, Pallas kernels for 9%

profile of v6, /device:TPU:0, one launch (start us, length us, event | category | flops | bytes accessed | tf_op | source)
XLA Modules:
  0.0 694.6 jit_solution(6076814997189051624)
XLA Ops:
  30.0 63.0 %all-gather.4.cloned.1.call-done = bf16[5632,768]{1,0:T(8,128)(2,1)} async-done(((bf16[176,768]{1,0:T(8,128)(2,1)}), bf16[5632,768]{1,0:T(8,128)(2,1)}) %all-gather.4.cloned.1.call-update) | async-done | bytes 8650768 | tf_op jit(solution)/shard_map/all_gather | solution.py:553
  93.9 4.7 slice.427
  105.9 13.8 %broadcast_add_fusion = f32[2,1024,768]{2,1,0:T(8,128)S(1)} fusion(f32[768]{0:T(1024)S(1)} %add.1823, bf16[3072,768,1]{1,0,2:T(8,128)(2,1)} %bitcast.557, bf16[2,1024,768]{2,1,0:T(8,128)(2,1)} %copy-done.10, bf16[2,1024,768]{2,1,0:T(8,128)(2,1)} %get-tuple-element.101, bf16[2,1024,768]{2,1,0:T(8,128)(2,1)} %get-tuple-element.100, ...), kind=kOutput, calls=%fused_computation.53 | convolution fusion | flops 9715580928 | bytes 23596032 | tf_op jit(solution)/shard_map/hby,yj->hbj/dot_general | solution.py:586
  128.6 13.4 %slice.356 = f32[2,512,768]{2,1,0:T(8,128)S(1)} slice(f32[2,1024,768]{2,1,0:T(8,128)} %copy-done.2), slice={[0:2:1], [0:1024:2], [0:768:1]} | slice | bytes 6291456 | tf_op jit(solution)/shard_map/jvp()/slice | solution.py:95
  142.1 15.4 %slice.358 = f32[2,512,768]{2,1,0:T(8,128)} slice(f32[2,1024,768]{2,1,0:T(8,128)} %copy-done.2), slice={[0:2:1], [1:1024:2], [0:768:1]} | slice | bytes 6291456 | tf_op jit(solution)/shard_map/jvp()/slice | solution.py:95
  163.8 10.7 %fusion.15 = bf16[3072,1024,2]{0,1,2:T(8,128)(2,1)} fusion(bf16[2,1024,768]{2,1,0:T(8,128)(2,1)} %copy-done.10, bf16[2,1024,768]{2,1,0:T(8,128)(2,1)} %get-tuple-element.101, bf16[2,1024,768]{2,1,0:T(8,128)(2,1)} %get-tuple-element.100, bf16[2,1024,768]{2,1,0:T(8,128)(2,1)} %get-tuple-element.99), kind=kLoop, calls=%fused_computation.64 | loop fusion | flops 50331648 | bytes 25165824 | tf_op jit(solution)/shard_map/xwu,xwo->uo/dot_general | solution.py:648
  174.5 17.2 %copy.126 = bf16[3072,1024,2]{1,0,2:T(8,128)(2,1)} copy(bf16[3072,1024,2]{0,1,2:T(8,128)(2,1)} %fusion.15) | data formatting | bytes 25165824 | tf_op jit(solution)/shard_map/xwu,xwo->uo/dot_general | solution.py:648
  191.9 8.0 %fusion.228 = (f32[2,511,768]{2,1,0:T(8,128)}, f32[2,511,768]{2,1,0:T(8,128)}, f32[2,511,768]{2,1,0:T(8,128)}, f32[2,511,768]{2,1,0:T(8,128)}) fusion(f32[2,512,768]{2,1,0:T(8,128)S(1)} %slice.356, f32[2,512,768]{2,1,0:T(8,128)} %slice.358), kind=kLoop, calls=%fused_computation.549 | loop fusion | bytes 25116672 | tf_op jit(solution)/shard_map/jvp()/slice | solution.py:87
  199.8 6.8 multiply_reduce_fusion.11
  206.7 9.0 %convolution_convert_fusion.q_ref.k_ref.v_ref = bf16[2,512,2304]{2,1,0:T(8,128)(2,1)} fusion(bf16[768,7168]{1,0:T(8,128)(2,1)} %all-gather.6.cloned.1.call-done, f32[2,512,768]{2,1,0:T(8,128)} %get-tuple-element.80, f32[768]{0:T(1024)S(1)} %mul.1675, f32[2,512]{1,0:T(2,128)S(1)} %fusion.122), kind=kOutput, calls=%fused_computation.23 | convolution fusion | flops 3628597248 | bytes 11410432 | tf_op jit(solution)/shard_map/std,de->ste/dot_general | solution.py:592
  215.7 21.5 %shard_map.583 = bf16[2,512,768]{2,1,0:T(8,128)(2,1)} custom-call(s32[2]{0:T(128)} %len_ref.3, bf16[2,512,2304]{2,1,0:T(8,128)(2,1)} %convolution_convert_fusion.q_ref.k_ref.v_ref, bf16[2,512,2304]{2,1,0:T(8,128)(2,1)} %convolution_convert_fusion.q_ref.k_ref.v_ref, bf16[2,512,2304]{2,1,0:T(8,128)(2,1)} %convolution_convert_fusion.q_ref.k_ref.v_ref), custom_call_target="tpu_custom_call" | custom-call | flops 3221225472 | bytes 6291456 | tf_op jit(solution)/shard_map/pallas_call | solution.py:263
  241.5 14.2 %fusion.7 = f32[2,512,4096]{2,1,0:T(8,128)} fusion(bf16[768,7168]{1,0:T(8,128)(2,1)} %all-gather.6.cloned.1.call-done, f32[2,512,768]{2,1,0:T(8,128)S(1)} %get-tuple-element.149, f32[768]{0:T(1024)S(1)} %mul.1681, f32[2,512]{1,0:T(2,128)S(1)} %fusion.123), kind=kOutput, calls=%fused_computation.26 | convolution fusion | flops 6444810240 | bytes 26221568 | tf_op jit(solution)/shard_map/std,de->ste/dot_general | solution.py:603
  255.7 17.2 %bitcast_multiply_fusion.1 = (f32[2,512,2048]{2,1,0:T(8,128)}, f32[2,512,2048]{2,1,0:T(8,128)}, bf16[2,512,2048]{2,1,0:T(8,128)(2,1)}) fusion(f32[2,512,4096]{2,1,0:T(8,128)} %fusion.7, bf16[2048,768,1]{1,0,2:T(8,128)(2,1)S(1)} %bitcast.559, bf16[2,512,768]{2,1,0:T(8,128)(2,1)S(1)} %copy-done.26), kind=kOutput, calls=%fused_computation.15 | convolution fusion | flops 3271557120 | bytes 42467328 | tf_op jit(solution)/shard_map/std,fd->stf/dot_general | solution.py:616
  273.0 16.2 %bitcast_convert_fusion = bf16[768,4096]{1,0:T(8,128)(2,1)} fusion(f32[2,512,2048]{2,1,0:T(8,128)} %get-tuple-element.84, f32[2,512,2048]{2,1,0:T(8,128)} %get-tuple-element.83, f32[2,512,768]{2,1,0:T(8,128)} %copy-done.12, f32[768]{0:T(1024)S(1)} %mul.1681, f32[2,512]{1,0:T(2,128)S(1)} %fusion.123), kind=kOutput, calls=%fused_computation.4 | convolution fusion | flops 6456344576 | bytes 26221568 | tf_op jit(solution)/shard_map/std,ste->de/dot_general | solution.py:621
  289.2 14.3 %multiply_reduce_fusion = (bf16[768]{0:T(1024)(128)(2,1)S(1)}, f32[2,512]{1,0:T(2,128)S(1)}, f32[2,512,768]{2,1,0:T(8,128)}) fusion(f32[2,512,768]{2,1,0:T(8,128)} %copy-done.12, f32[2,512]{1,0:T(2,128)S(1)} %fusion.123, f32[768]{0:T(1024)S(1)} %mul.1681, bf16[768,7168]{1,0:T(8,128)(2,1)} %all-gather.6.cloned.1.call-done, ...), kind=kOutput, calls=%fused_computation.36 | convolution fusion | flops 6455556096 | bytes 29372928 | tf_op jit(solution)/shard_map/ste,de->std/dot_general | solution.py:624
  314.3 34.2 %shard_map.584 = (bf16[2,512,768]{2,1,0:T(8,128)(2,1)}, bf16[2,512,768]{2,1,0:T(8,128)(2,1)}, bf16[2,512,768]{2,1,0:T(8,128)(2,1)}) custom-call(s32[2]{0:T(128)} %len_ref.3, bf16[2,512,2304]{2,1,0:T(8,128)(2,1)} %convolution_convert_fusion.q_ref.k_ref.v_ref, bf16[2,512,2304]{2,1,0:T(8,128)(2,1)} %convolution_convert_fusion.q_ref.k_ref.v_ref, ...), custom_call_target="tpu_custom_call" | custom-call | flops 8053063680 | bytes 11010048 | tf_op jit(solution)/shard_map/pallas_call | solution.py:285
  353.2 5.6 bitcast_convert_fusion.1
  361.6 7.9 %bitcast_convert_fusion.2 = bf16[2048,768]{1,0:T(8,128)(2,1)} fusion(bf16[2,512,2048]{2,1,0:T(8,128)(2,1)} %get-tuple-element.85, bf16[2,512,768]{2,1,0:T(8,128)(2,1)} %param.34), kind=kOutput, calls=%fused_computation.21 | convolution fusion | flops 3222798336 | bytes 8912896 | tf_op jit(solution)/shard_map/stf,std->fd/dot_general | solution.py:613
  369.5 6.6 reshape.4362
  376.1 12.7 %pad_maximum_fusion = bf16[768,9216]{1,0:T(8,128)(2,1)} fusion(bf16[768,2048]{1,0:T(8,128)(2,1)} %reshape.4362, bf16[768,4096]{1,0:T(8,128)(2,1)} %bitcast_convert_fusion, bf16[768,768]{1,0:T(8,128)(2,1)} %copy.145, bf16[768,2304]{1,0:T(8,128)(2,1)} %bitcast_convert_fusion.1), kind=kLoop, calls=%fused_computation.1 | loop fusion | flops 56623104 | bytes 28311552 | tf_op jit(solution)/shard_map/concatenate | solution.py:669
  388.9 10.3 %multiply_reduce_fusion.1 = (bf16[768]{0:T(1024)(128)(2,1)S(1)}, f32[2,512]{1,0:T(2,128)S(1)}, f32[2,512,768]{2,1,0:T(8,128)}) fusion(f32[2,512,768]{2,1,0:T(8,128)} %get-tuple-element.80, f32[2,512]{1,0:T(2,128)S(1)} %fusion.122, f32[768]{0:T(1024)S(1)} %mul.1675, bf16[2,512,2304]{2,1,0:T(8,128)(2,1)} %copy-done.34, ...), kind=kOutput, calls=%fused_computation.37 | convolution fusion | flops 3628595456 | bytes 14561792 | tf_op jit(solution)/shard_map/ste,de->std/dot_general | solution.py:640
  401.2 7.0 %multiply_reduce_fusion.4 = (f32[2,512]{1,0:T(2,128)S(1)}, f32[2,512]{1,0:T(2,128)S(1)}, f32[2,512]{1,0:T(2,128)S(1)}, f32[2,512]{1,0:T(2,128)S(1)}, f32[2,512]{...) fusion(f32[2,512,768]{2,1,0:T(8,128)S(1)} %copy-done.1, f32[2,511,768]{2,1,0:T(8,128)S(1)} %copy-done.6, ...), kind=kLoop, calls=%fused_computation.42 | loop fusion | flops 14149632 | bytes 31468544 | tf_op jit(solution)/shard_map/transpose(jvp())/reduce_sum | solution.py:589
  414.4 5.4 convolution_reduce_fusion
  426.0 5.3 copy.132
  431.4 8.3 %pad_slice_fusion.5 = (bf16[2,1024,768]{2,0,1:T(2,128)(2,1)S(1)}, bf16[2,1024,768]{2,0,1:T(2,128)(2,1)S(1)}, bf16[2,1024,768]{2,0,1:T(2,128)(2,1)S(1)}) fusion(bf16[2,1024,768]{2,0,1:T(2,128)(2,1)S(1)} %bitcast.548), kind=kLoop, calls=%fused_computation.122 | loop fusion | bytes 12582912 | tf_op jit(solution)/shard_map/slice | solution.py:653
  439.7 50.5 %pad_maximum_fusion.2 = bf16[2,1024,3072]{2,0,1:T(2,128)(2,1)} fusion(bf16[2,1024,768]{2,0,1:T(2,128)(2,1)S(1)} %bitcast.549, bf16[2,1024,768]{2,0,1:T(2,128)(2,1)S(1)} %get-tuple-element.90, bf16[2,1024,768]{2,0,1:T(2,128)(2,1)S(1)} %get-tuple-element.89, bf16[2,1024,768]{2,0,1:T(2,128)(2,1)S(1)} %get-tuple-element.88), kind=kLoop, calls=%fused_computation.3 | loop fusion | flops 50331648 | bytes 25165824 | tf_op jit(solution)/shard_map/concatenate | solution.py:652
  490.2 31.3 %copy.135 = bf16[2,1024,3072]{1,2,0:T(8,128)(2,1)} copy(bf16[2,1024,3072]{2,0,1:T(2,128)(2,1)} %pad_maximum_fusion.2) | data formatting | bytes 25165824 | tf_op jit(solution)/shard_map/concatenate | solution.py:652
  521.6 14.7 %convolution_bitcast_fusion = bf16[16,2,96,768]{3,2,1,0:T(8,128)(2,1)} fusion(bf16[16,2,96,1024,2]{3,2,1,0,4:T(8,128)(2,1)} %bitcast.551, bf16[2,1024,768,1,1]{2,0,1,4,3:T(2,128)(2,1)S(1)} %bitcast.550), kind=kOutput, calls=%fused_computation.30 | convolution fusion | flops 9663676416 | bytes 20447232 | tf_op jit(solution)/shard_map/xwu,xwo->uo/dot_general | solution.py:648
  536.3 15.5 %fusion.22 = bf16[256,768]{1,0:T(8,128)(2,1)S(1)} fusion(bf16[2,1024,4,768]{1,3,2,0:T(8,128)(2,1)} %bitcast.552, bf16[4,768,768,1]{2,1,0,3:T(8,128)(2,1)} %bitcast.558, bf16[2,1024]{1,0:T(2,128)(2,1)S(1)} %copy-done.71, s32[2,1024]{1,0:T(2,128)S(1)} %copy-done.128), kind=kOutput, calls=%fused_computation.72 | convolution fusion | flops 10472849408 | bytes 17707008 | tf_op jit(solution)/shard_map/xpg,xpz->gz/dot_general | solution.py:663
  555.4 63.5 %shard_map.585 = f32[112,768]{1,0:T(8,128)S(1)} custom-call(bf16[2,16,112,768]{3,2,1,0:T(8,128)(2,1)S(1)} %maximum_bitcast_fusion.x_ref), custom_call_target="tpu_custom_call" | custom-call | flops 5505024 | bytes 11010048 | tf_op jit(solution)/shard_map/pallas_call | solution.py:405
  619.2 7.3 %convolution_add_fusion.1 = f32[2,512,768]{2,1,0:T(8,128)} fusion(f32[2,512,768]{2,1,0:T(8,128)S(1)} %copy-done.13, bf16[2,512,2048]{2,1,0:T(8,128)(2,1)} %get-tuple-element.85, bf16[2048,768,1]{1,0,2:T(8,128)(2,1)S(1)} %bitcast.560), kind=kOutput, calls=%fused_computation.68 | convolution fusion | flops 3222011904 | bytes 13631488 | tf_op jit(solution)/shard_map/stf,fd->std/dot_general | solution.py:606
  631.0 12.6 %shard_map.586 = f32[80,128]{1,0:T(8,128)} custom-call(f32[80,128]{1,0:T(8,128)} %pad_bitcast_fusion.x_ref), custom_call_target="tpu_custom_call" | custom-call | flops 163840 | bytes 655360 | tf_op jit(solution)/shard_map/pallas_call | solution.py:481
  (497 shorter events, 119.4 us)
Async XLA Ops:
  7.3 85.7 %all-gather.4.cloned.1.call-start = ((), (), s32[]{:S(2)}) async-start(), calls=%async_computation.1 | async-start | bytes 8921088 | tf_op jit(solution)/shard_map/all_gather | solution.py:553
  11.7 195.1 %all-gather.6.cloned.1.call-start = ((), (), s32[]{:S(2)}) async-start(), calls=%async_computation.2 | async-start | bytes 11354112 | tf_op jit(solution)/shard_map/all_gather | solution.py:555
  15.4 611.1 %reduce-scatter.2.cloned.1.call-start = ((), (), s32[]{:S(2)}) async-start(), calls=%async_computation.3 | async-start | bytes 14598144 | tf_op jit(solution)/shard_map/reduce_scatter | solution.py:672
  29.1 95.7 %copy-start.68 = (f32[256]{0:T(256)}, f32[256]{0:T(256)S(1)}, u32[]{:S(2)}) copy-start(f32[256]{0:T(256)S(1)} %minimum_convert_fusion.11) | copy-start | bytes 3076
  29.1 132.4 %copy-start.78 = (pred[512]{0:T(512)(128)(4,1)}, pred[512]{0:T(512)(128)(4,1)S(1)}, u32[]{:S(2)}) copy-start(pred[512]{0:T(512)(128)(4,1)S(1)} %get-tuple-element.163) | copy-start | bytes 1540
  29.1 132.4 %copy-start.94 = (pred[512]{0:T(512)(128)(4,1)}, pred[512]{0:T(512)(128)(4,1)S(1)}, u32[]{:S(2)}) copy-start(pred[512]{0:T(512)(128)(4,1)S(1)} %get-tuple-element.167) | copy-start | bytes 1540
  29.2 132.4 %copy-start.84 = (pred[512]{0:T(512)(128)(4,1)}, pred[512]{0:T(512)(128)(4,1)S(1)}, u32[]{:S(2)}) copy-start(pred[512]{0:T(512)(128)(4,1)S(1)} %get-tuple-element.193) | copy-start | bytes 1540
  29.2 132.4 %copy-start.96 = (pred[512]{0:T(512)(128)(4,1)}, pred[512]{0:T(512)(128)(4,1)S(1)}, u32[]{:S(2)}) copy-start(pred[512]{0:T(512)(128)(4,1)S(1)} %get-tuple-element.192) | copy-start | bytes 1540
  29.2 132.4 %copy-start.88 = (pred[512]{0:T(512)(128)(4,1)}, pred[512]{0:T(512)(128)(4,1)S(1)}, u32[]{:S(2)}) copy-start(pred[512]{0:T(512)(128)(4,1)S(1)} %get-tuple-element.194) | copy-start | bytes 1540
  29.2 132.4 %copy-start.102 = (pred[512]{0:T(512)(128)(4,1)}, pred[512]{0:T(512)(128)(4,1)S(1)}, u32[]{:S(2)}) copy-start(pred[512]{0:T(512)(128)(4,1)S(1)} %get-tuple-element.195) | copy-start | bytes 1540
  29.3 132.3 %copy-start.80 = (pred[512]{0:T(512)(128)(4,1)}, pred[512]{0:T(512)(128)(4,1)S(1)}, u32[]{:S(2)}) copy-start(pred[512]{0:T(512)(128)(4,1)S(1)} %get-tuple-element.196) | copy-start | bytes 1540
  29.3 132.3 %copy-start.104 = (pred[512]{0:T(512)(128)(4,1)}, pred[512]{0:T(512)(128)(4,1)S(1)}, u32[]{:S(2)}) copy-start(pred[512]{0:T(512)(128)(4,1)S(1)} %get-tuple-element.197) | copy-start | bytes 1540
  29.3 133.0 %copy-start.82 = (pred[512]{0:T(512)(128)(4,1)}, pred[512]{0:T(512)(128)(4,1)S(1)}, u32[]{:S(2)}) copy-start(pred[512]{0:T(512)(128)(4,1)S(1)} %get-tuple-element.161) | copy-start | bytes 1540
  29.3 133.0 %copy-start.98 = (pred[512]{0:T(512)(128)(4,1)}, pred[512]{0:T(512)(128)(4,1)S(1)}, u32[]{:S(2)}) copy-start(pred[512]{0:T(512)(128)(4,1)S(1)} %get-tuple-element.165) | copy-start | bytes 1540
  29.4 133.0 %copy-start.90 = (pred[512]{0:T(512)(128)(4,1)}, pred[512]{0:T(512)(128)(4,1)S(1)}, u32[]{:S(2)}) copy-start(pred[512]{0:T(512)(128)(4,1)S(1)} %get-tuple-element.187) | copy-start | bytes 1540
  29.4 133.0 %copy-start.100 = (pred[512]{0:T(512)(128)(4,1)}, pred[512]{0:T(512)(128)(4,1)S(1)}, u32[]{:S(2)}) copy-start(pred[512]{0:T(512)(128)(4,1)S(1)} %get-tuple-element.186) | copy-start | bytes 1540
  29.4 132.9 %copy-start.92 = (pred[512]{0:T(512)(128)(4,1)}, pred[512]{0:T(512)(128)(4,1)S(1)}, u32[]{:S(2)}) copy-start(pred[512]{0:T(512)(128)(4,1)S(1)} %get-tuple-element.188) | copy-start | bytes 1540
  29.4 132.9 %copy-start.106 = (pred[512]{0:T(512)(128)(4,1)}, pred[512]{0:T(512)(128)(4,1)S(1)}, u32[]{:S(2)}) copy-start(pred[512]{0:T(512)(128)(4,1)S(1)} %get-tuple-element.189) | copy-start | bytes 1540
  29.5 132.9 %copy-start.86 = (pred[512]{0:T(512)(128)(4,1)}, pred[512]{0:T(512)(128)(4,1)S(1)}, u32[]{:S(2)}) copy-start(pred[512]{0:T(512)(128)(4,1)S(1)} %get-tuple-element.190) | copy-start | bytes 1540
  29.5 132.9 %copy-start.108 = (pred[512]{0:T(512)(128)(4,1)}, pred[512]{0:T(512)(128)(4,1)S(1)}, u32[]{:S(2)}) copy-start(pred[512]{0:T(512)(128)(4,1)S(1)} %get-tuple-element.191) | copy-start | bytes 1540
  29.8 94.0 %copy-start.49 = (f32[512]{0:T(512)}, f32[512]{0:T(512)S(1)}, u32[]{:S(2)}) copy-start(f32[512]{0:T(512)S(1)} %minimum_convert_fusion.10) | copy-start | bytes 6148
  29.8 95.8 %copy-start.51 = (f32[342]{0:T(512)}, f32[342]{0:T(512)S(1)}, u32[]{:S(2)}) copy-start(f32[342]{0:T(512)S(1)} %minimum_convert_fusion.9) | copy-start | bytes 4108
  29.8 96.2 %copy-start.47 = (f32[1024]{0:T(1024)}, f32[1024]{0:T(1024)S(1)}, u32[]{:S(2)}) copy-start(f32[1024]{0:T(1024)S(1)} %minimum_convert_fusion) | copy-start | bytes 12292
  30.0 68.8 %copy-start.70 = (bf16[2,1024]{1,0:T(2,128)(2,1)}, bf16[2,1024]{1,0:T(2,128)(2,1)S(1)}, u32[]{:S(2)}) copy-start(bf16[2,1024]{1,0:T(2,128)(2,1)S(1)} %compare_convert_fusion) | copy-start | bytes 12292
  551.8 67.2 %copy-start.16 = (bf16[32,64,768]{2,1,0:T(8,128)(2,1)S(1)}, bf16[32,64,768]{2,1,0:T(8,128)(2,1)}, u32[]{:S(2)}) copy-start(bf16[32,64,768]{2,1,0:T(8,128)(2,1)} %slice.443) | copy-start | bytes 9437188
  555.4 63.6 %copy-start.13 = (f32[2,512,768]{2,1,0:T(8,128)S(1)}, f32[2,512,768]{2,1,0:T(8,128)}, u32[]{:S(2)}) copy-start(f32[2,512,768]{2,1,0:T(8,128)} %copy-done.12) | copy-start | bytes 9437188
  650.0 25.8 %copy-start.64 = (f32[768]{0:T(1024)S(1)}, f32[768]{0:T(1024)}, u32[]{:S(2)}) copy-start(f32[768]{0:T(1024)} %param.59) | copy-start | bytes 9220
  650.0 25.9 %copy-start.61 = (f32[4,48]{1,0:T(4,128)S(1)}, f32[4,48]{1,0:T(4,128)}, u32[]{:S(2)}) copy-start(f32[4,48]{1,0:T(4,128)} %param.41) | copy-start | bytes 2308
  650.1 25.9 %copy-start.112 = (f32[4,48]{1,0:T(4,128)S(1)}, f32[4,48]{1,0:T(4,128)}, u32[]{:S(2)}) copy-start(f32[4,48]{1,0:T(4,128)} %param.60) | copy-start | bytes 2308
  650.1 25.9 %copy-start.113 = (f32[4,48]{1,0:T(4,128)S(1)}, f32[4,48]{1,0:T(4,128)}, u32[]{:S(2)}) copy-start(f32[4,48]{1,0:T(4,128)} %param.61) | copy-start | bytes 2308
  650.1 27.3 %copy-start.18 = (f32[48,4096]{1,0:T(8,128)S(1)}, f32[48,4096]{1,0:T(8,128)}, u32[]{:S(2)}) copy-start(f32[48,4096]{1,0:T(8,128)} %param.39) | copy-start | bytes 2359300
  657.4 26.2 %copy-start.123 = (f32[128]{0:T(128)}, f32[128]{0:T(128)S(1)}, u32[]{:S(2)}) copy-start(f32[128]{0:T(128)S(1)} %multiply_add_fusion.10) | copy-start | bytes 1540
  (101 other events, 963.4 us)
Sparse Core Ops, SparseCore 0:
  11.8 81.1 all-gather.3
  96.5 87.5 all-gather.5
  389.0 161.5 reduce-scatter.1

commit v7 on v5

--- a/solution.py
+++ b/solution.py
@@ -537,23 +537,25 @@
     vec_piece = own_half(vectors, axis=1).astype(jnp.bfloat16)
     vec_block = jnp.pad(vec_piece, ((0, 8 - 4), (0, D - vec_width)))
     first_group = jnp.concatenate(
-        [own_half(table).astype(jnp.bfloat16), own_half(kernel).astype(jnp.bfloat16),
-         own_half(contract).astype(jnp.bfloat16), vec_block], axis=0)
+        [own_half(table).astype(jnp.bfloat16), own_half(kernel).astype(jnp.bfloat16), vec_block], axis=0)
+    contract_piece = own_half(contract).reshape(project.shape[0] // 2, -1)
     second_group = jnp.concatenate(
-        [own_half(project), own_half(combine), own_half(expand)], axis=1).astype(jnp.bfloat16)
+        [own_half(project), own_half(combine), own_half(expand), contract_piece], axis=1
+    ).astype(jnp.bfloat16)
     first_all = lax.all_gather(first_group, groups, axis=0, tiled=True)
     first_all = first_all.reshape(count_all, first_group.shape[0], D)
     second_all = lax.all_gather(second_group, groups, axis=0, tiled=True)
     at_kernel = rows_table
-    at_contract = at_kernel + rows_kernel
-    at_vec = at_contract + rows_contract
+    at_vec = at_kernel + rows_kernel
     complete_table = first_all[:, :at_kernel].reshape(V, D)
-    complete_kernel = first_all[:, at_kernel:at_contract].reshape(KS * D, D)
-    full_contract = first_all[:, at_contract:at_vec].reshape(-1, D)
+    complete_kernel = first_all[:, at_kernel:at_vec].reshape(KS * D, D)
     full_vectors = first_all[:, at_vec:at_vec + 4, :vec_width].transpose(1, 0, 2).reshape(4, D)
+    at_expand = 4 * D
+    at_contract = at_expand + expand.shape[1]
     full_project = second_all[:, : 3 * D]
-    full_combine = second_all[:, 3 * D : 4 * D]
-    full_expand = second_all[:, 4 * D :]
+    full_combine = second_all[:, 3 * D : at_expand]
+    full_expand = second_all[:, at_expand:at_contract]
+    full_contract = second_all[:, at_contract:].reshape(-1, D)
     vector_vals = full_vectors.astype(jnp.float32)
     count_items, count_bytes = byte_ids.shape
     count_tok = count_bytes // 2
@@ -706,23 +708,22 @@
     flat_padded = -(-flat_size // 2048) * 2048
     stats = all_sum(jnp.pad(flat, (0, flat_padded - flat_size)).reshape(-1, 128)).reshape(-1)
 
-    def segments(start, lengths):
-        out = []
-        for length in lengths:
-            out.append(stats[start : start + length])
-            start += length
-        return out, start
-
-    column_pieces, at = segments(0, widths)
     column_scaled_raw = stats[: sum(widths)]
-    (vec_grad_total,), at = segments(at, [vec_grad_part.shape[0]])
-    row_pieces, at = segments(at, [part.shape[0] for part in row_parts])
-    weight_pieces, at = segments(at, [part.shape[0] for part in weight_parts])
-    (vec_weight_total,), at = segments(at, [vec_weight_part.shape[0]])
-    sum_sq = jnp.stack([jnp.sum(part) for part in column_pieces] + [jnp.sum(vec_grad_total)])
-    sum_rows_old = jnp.stack([jnp.sum(part) for part in row_pieces])
-    sum_weights = jnp.stack([jnp.sum(part) for part in weight_pieces])
-    sum_vectors = jnp.sum(vec_weight_total.reshape(4, -1), axis=1)
+    bounds = []
+    start = 0
+    for length in widths + [vec_grad_part.shape[0]]:
+        bounds.append((start, start + length))
+        start += length
+    for part in row_parts + weight_parts:
+        bounds.append((start, start + part.shape[0]))
+        start += part.shape[0]
+    for row in range(4):
+        bounds.append((start + row * vec_width, start + (row + 1) * vec_width))
+    starts = jnp.array([lo for lo, _ in bounds], jnp.int32)[:, None]
+    ends = jnp.array([hi for _, hi in bounds], jnp.int32)[:, None]
+    spot = lax.broadcasted_iota(jnp.int32, (len(bounds), flat_padded), 1)
+    sums = jnp.sum(jnp.where((spot >= starts) & (spot < ends), stats[None, :], 0.0), axis=1)
+    sum_sq, sum_rows_old, sum_weights, sum_vectors = sums[:7], sums[7:13], sums[13:19], sums[19:23]
     early_own = lax.all_gather(early_part, "dp", axis=0, tiled=True).astype(jnp.float32)
     late_own = lax.all_gather(late_f.reshape(1, late_rows, D), "dp", axis=0, tiled=True)
     shards = (

time: 652 us -> 652 us (level)
    all_gather x1, waiting for transfers between devices: 30.9 us -> 49.4 us  [body(): second_all = lax.all_gather(second_group, groups, axis=0, tiled=True)]
    all_gather x1, waiting for transfers between devices: 65.6 us -> 52.9 us  [body(): first_all = lax.all_gather(first_group, groups, axis=0, tiled=True)]
    reduce_sum x8 -> x2, other arithmetic: 10.1 us -> 1.74 us  [the longest x1 1.13 us: body(): jnp.sum(jnp.where((spot >= starts) & (spot < ends), stats[None, :], 0.0),...]
where the time goes in v7:
time: 652 us; the launch traced here: 642 us
  matrix products  199 us (31%)
  Pallas kernels  145 us (22%)
  waiting for transfers between devices  102 us (16%)
  other arithmetic  93 us (14%)
  local copies, waits for them, and re-layouts  67 us (10%)
  between operations  30.9 us (5%)
    pallas_call x1, Pallas kernels, ring_reduce_scatter(): pl.pallas_call(functools.partial(ring_rs_kernel, snake), out_shape=jax.Sh...  77.6 us
    all_gather x1, waiting for transfers between devices, body(): first_all = lax.all_gather(first_group, groups, axis=0, tiled=True)  52.9 us
    all_gather x1, waiting for transfers between devices, body(): second_all = lax.all_gather(second_group, groups, axis=0, tiled=True)  49.4 us
    pallas_call x1, Pallas kernels, attention_backward(): pl.pallas_call(attn_bwd_kernel, out_shape=(part, part, part), grid_spec=p...  34.2 us
    dot_general x3, matrix products, body(): tokens, gbst_pull = jax.vjp(gbst_tokens, hidden, vector_vals[3])  25.2 us
    pallas_call x1, Pallas kernels, attention_forward(): pl.pallas_call(attn_fwd_kernel, out_shape=jax.ShapeDtypeStruct((count_ite...  21.6 us
    dot_general x1, matrix products, body(): jnp.einsum('xwu,xwo->uo', byte_windows, gradient_hidden_reduced, preferre...  18 us
    dot_general x1, matrix products, body(): jnp.einsum('std,fd->stf', cotangent, back_contract, preferred_element_typ...  17.5 us
  transfers between devices with their start and end apart: 3, of which 2 were waited for; matrix products, arithmetic and copies ran while one was open for 30% of the time, Pallas kernels for 12%

profile of v7, /device:TPU:0, one launch (start us, length us, event | category | flops | bytes accessed | tf_op | source)
XLA Modules:
  0.0 642.3 jit_solution(13099973153533119893)
XLA Ops:
  27.4 52.9 %all-gather.4.cloned.1.call-done = bf16[3584,768]{1,0:T(8,128)(2,1)} async-done(((bf16[112,768]{1,0:T(8,128)(2,1)}), bf16[3584,768]{1,0:T(8,128)(2,1)}) %all-gather.4.cloned.1.call-update) | async-done | bytes 5505040 | tf_op jit(solution)/shard_map/all_gather | solution.py:545
  80.3 4.8 slice.373
  89.3 4.6 pad_slice_fusion.5
  93.9 14.0 %fusion.30 = f32[2,1024,768]{2,1,0:T(8,128)S(1)} fusion(bf16[3072,768,1]{1,0,2:T(8,128)(2,1)} %bitcast.547, bf16[2,1024,768]{2,1,0:T(8,128)(2,1)} %copy-done.11, bf16[2,1024,768]{2,1,0:T(8,128)(2,1)} %get-tuple-element.87, bf16[2,1024,768]{2,1,0:T(8,128)(2,1)} %get-tuple-element.86, bf16[2,1024,768]{2,1,0:T(8,128)(2,1)} %get-tuple-element.85), kind=kOutput, calls=%fused_computation.75 | convolution fusion | flops 9714008064 | bytes 23592960 | tf_op jit(solution)/shard_map/hby,yj->hbj/dot_general | solution.py:579
  124.5 12.0 %multiply_reduce_fusion.5 = (f32[2,512]{1,0:T(2,128)S(1)}, f32[2,512,768]{2,1,0:T(8,128)S(1)}) fusion(f32[2,1024,768]{2,1,0:T(8,128)} %copy-done, f32[768]{0:T(1024)S(1)} %add.1776, f32[2,512]{1,0:T(2,128)S(1)} %add_multiply_fusion, f32[2,512]{1,0:T(2,128)S(1)} %add_multiply_fusion.1, f32[2,512]{1,0:T(2,128)S(1)} %add_multiply_fusion.2, ...), kind=kOutput, calls=%fused_computation.61 | convolution fusion | flops 4841274368 | bytes 12614656 | tf_op jit(solution)/shard_map/jvp(ntj,njd->ntd)/dot_general | solution.py:103
  136.6 49.4 %all-gather.6.cloned.1.call-done = bf16[768,9216]{1,0:T(8,128)(2,1)} async-done(((bf16[24,9216]{1,0:T(8,128)(2,1)}), bf16[768,9216]{1,0:T(8,128)(2,1)}) %all-gather.6.cloned.1.call-update) | async-done | bytes 14155792 | tf_op jit(solution)/shard_map/all_gather | solution.py:547
  186.0 7.5 %convolution_convert_fusion.q_ref.k_ref.v_ref = bf16[2,512,2304]{2,1,0:T(8,128)(2,1)} fusion(bf16[768,9216]{1,0:T(8,128)(2,1)} %all-gather.6.cloned.1.call-done, f32[2,512,768]{2,1,0:T(8,128)S(1)} %get-tuple-element.141, f32[768]{0:T(1024)S(1)} %mul.1576, f32[2,512]{1,0:T(2,128)S(1)} %fusion.178), kind=kOutput, calls=%fused_computation.26 | convolution fusion | flops 3628597248 | bytes 11410432 | tf_op jit(solution)/shard_map/std,de->ste/dot_general | solution.py:585
  193.5 21.6 %shard_map.583 = bf16[2,512,768]{2,1,0:T(8,128)(2,1)} custom-call(s32[2]{0:T(128)} %len_ref.3, bf16[2,512,2304]{2,1,0:T(8,128)(2,1)} %convolution_convert_fusion.q_ref.k_ref.v_ref, bf16[2,512,2304]{2,1,0:T(8,128)(2,1)} %convolution_convert_fusion.q_ref.k_ref.v_ref, bf16[2,512,2304]{2,1,0:T(8,128)(2,1)} %convolution_convert_fusion.q_ref.k_ref.v_ref), custom_call_target="tpu_custom_call" | custom-call | flops 3221225472 | bytes 6291456 | tf_op jit(solution)/shard_map/pallas_call | solution.py:254
  215.1 4.8 multiply_reduce_fusion.4
  221.8 4.4 reshape.4455
  226.2 13.2 %fusion.18 = f32[2,512,4096]{2,1,0:T(8,128)} fusion(bf16[768,9216]{1,0:T(8,128)(2,1)} %all-gather.6.cloned.1.call-done, f32[2,512,768]{2,1,0:T(8,128)} %get-tuple-element.143, f32[768]{0:T(1024)S(1)} %mul.1583, f32[2,512]{1,0:T(2,128)S(1)} %fusion.179), kind=kOutput, calls=%fused_computation.38 | convolution fusion | flops 6444810240 | bytes 26221568 | tf_op jit(solution)/shard_map/std,de->ste/dot_general | solution.py:596
  239.3 17.5 %bitcast_multiply_fusion.1 = (f32[2,512,2048]{2,1,0:T(8,128)}, f32[2,512,2048]{2,1,0:T(8,128)}, bf16[2,512,2048]{2,1,0:T(8,128)(2,1)}) fusion(f32[2,512,4096]{2,1,0:T(8,128)} %fusion.18, bf16[2048,768,1]{1,0,2:T(8,128)(2,1)S(1)} %copy-done.9, bf16[2,512,768]{2,1,0:T(8,128)(2,1)S(1)} %copy-done.22), kind=kOutput, calls=%fused_computation.18 | convolution fusion | flops 3271557120 | bytes 42467328 | tf_op jit(solution)/shard_map/std,fd->stf/dot_general | solution.py:609
  256.9 15.3 %bitcast_convert_fusion = bf16[768,4096]{1,0:T(8,128)(2,1)} fusion(f32[2,512,2048]{2,1,0:T(8,128)} %get-tuple-element.79, f32[2,512,2048]{2,1,0:T(8,128)} %get-tuple-element.78, f32[2,512,768]{2,1,0:T(8,128)S(1)} %copy-done.1, f32[768]{0:T(1024)S(1)} %mul.1583, f32[2,512]{1,0:T(2,128)S(1)} %fusion.179), kind=kOutput, calls=%fused_computation.7 | convolution fusion | flops 6456344576 | bytes 26221568 | tf_op jit(solution)/shard_map/std,ste->de/dot_general | solution.py:614
  272.1 14.4 %multiply_reduce_fusion = (bf16[768]{0:T(1024)(128)(2,1)}, f32[2,512]{1,0:T(2,128)S(1)}, f32[2,512,768]{2,1,0:T(8,128)}) fusion(f32[2,512,768]{2,1,0:T(8,128)S(1)} %copy-done.1, f32[2,512]{1,0:T(2,128)S(1)} %fusion.179, f32[768]{0:T(1024)S(1)} %mul.1583, bf16[768,9216]{1,0:T(8,128)(2,1)} %all-gather.6.cloned.1.call-done, ...), kind=kOutput, calls=%fused_computation.54 | convolution fusion | flops 6455556096 | bytes 29372928 | tf_op jit(solution)/shard_map/ste,de->std/dot_general | solution.py:617
  291.5 3.9 convolution_convert_fusion.1.do_ref
  295.4 34.2 %shard_map.584 = (bf16[2,512,768]{2,1,0:T(8,128)(2,1)}, bf16[2,512,768]{2,1,0:T(8,128)(2,1)}, bf16[2,512,768]{2,1,0:T(8,128)(2,1)}) custom-call(s32[2]{0:T(128)} %len_ref.3, bf16[2,512,2304]{2,1,0:T(8,128)(2,1)} %convolution_convert_fusion.q_ref.k_ref.v_ref, bf16[2,512,2304]{2,1,0:T(8,128)(2,1)} %convolution_convert_fusion.q_ref.k_ref.v_ref, ...), custom_call_target="tpu_custom_call" | custom-call | flops 8053063680 | bytes 11010048 | tf_op jit(solution)/shard_map/pallas_call | solution.py:276
  334.2 5.6 bitcast_convert_fusion.2
  341.6 7.4 %bitcast_convert_fusion.3 = bf16[2048,768]{1,0:T(8,128)(2,1)} fusion(bf16[2,512,2048]{2,1,0:T(8,128)(2,1)} %get-tuple-element.80, bf16[2,512,768]{2,1,0:T(8,128)(2,1)S(1)} %copy-done.23), kind=kOutput, calls=%fused_computation.23 | convolution fusion | flops 3222798336 | bytes 8912896 | tf_op jit(solution)/shard_map/stf,std->fd/dot_general | solution.py:606
  349.0 5.5 reshape.4439
  354.5 12.2 %pad_maximum_fusion = bf16[768,9216]{1,0:T(8,128)(2,1)} fusion(bf16[768,2048]{1,0:T(8,128)(2,1)S(1)} %reshape.4439, bf16[768,4096]{1,0:T(8,128)(2,1)} %bitcast_convert_fusion, bf16[768,768]{1,0:T(8,128)(2,1)} %copy.119, bf16[768,2304]{1,0:T(8,128)(2,1)} %bitcast_convert_fusion.2), kind=kLoop, calls=%fused_computation.1 | loop fusion | flops 56623104 | bytes 28311552 | tf_op jit(solution)/shard_map/concatenate | solution.py:662
  385.0 9.4 %multiply_reduce_fusion.1 = (bf16[768]{0:T(1024)(128)(2,1)S(1)}, f32[2,512]{1,0:T(2,128)S(1)}, f32[2,512,768]{2,1,0:T(8,128)S(1)}) fusion(f32[2,512,768]{2,1,0:T(8,128)} %copy-done.3, f32[2,512]{1,0:T(2,128)} %copy-done.72, f32[768]{0:T(1024)} %copy-done.70, bf16[2,512,2304]{2,1,0:T(8,128)(2,1)} %copy-done.27, ...), kind=kOutput, calls=%fused_computation.55 | convolution fusion | flops 3628595456 | bytes 14562816 | tf_op jit(solution)/shard_map/ste,de->std/dot_general | solution.py:633
  396.7 8.6 %select_reduce_fusion.2 = (f32[2,512]{1,0:T(2,128)S(1)}, f32[2,512]{1,0:T(2,128)S(1)}, f32[2,512]{1,0:T(2,128)S(1)}, f32[2,512]{1,0:T(2,128)S(1)}, f32[2,512]{1,0:T(2,128)S(1)}, /*index=5*/f32[2,512]{1,0:T(2,128)S(1)}) fusion(pred[512,1024]{1,0:T(8,128)(4,1)S(1)} %copy-done.29, pred[512,1024]{1,0:T(8,128)(4,1)S(1)} %copy-done.28, ...), kind=kOutput, calls=%fused_computation.43 | convolution fusion | flops 4845987840 | bytes 12610560 | tf_op jit(solution)/shard_map/transpose(jvp(ntd,njd->ntj))/dot_general | solution.py:582
  414.1 11.3 %add_convert_fusion.1 = bf16[2,1024,768]{2,1,0:T(8,128)(2,1)S(1)} fusion(f32[768]{0:T(1024)S(1)} %mul.1627, f32[2,1024]{1,0:T(2,128)S(1)} %fusion.105, f32[2,512,768]{2,1,0:T(8,128)} %copy-done.12, f32[2,512]{1,0:T(2,128)S(1)} %copy-done.95, f32[2,512]{1,0:T(2,128)S(1)} %copy-done.93, f32[2,512]{1,0:T(2,128)S(1)} %copy-done.99, ...), kind=kOutput, calls=%fused_computation.25 | convolution fusion | flops 4842848256 | bytes 9473024 | tf_op jit(solution)/shard_map/transpose(jvp(ntj,ntd->njd))/dot_general | solution.py:582
  425.4 4.4 pad_slice_fusion.2
  429.9 5.3 fusion.78
  435.7 9.6 %pad_maximum_fusion.2 = bf16[2,1024,3072]{2,1,0:T(8,128)(2,1)} fusion(bf16[2,1024,768]{2,1,0:T(8,128)(2,1)S(1)} %add_convert_fusion.1, bf16[2,1024,768]{2,1,0:T(8,128)(2,1)} %get-tuple-element.83, bf16[2,1024,768]{2,1,0:T(8,128)(2,1)} %get-tuple-element.82, bf16[2,1024,768]{2,1,0:T(8,128)(2,1)} %get-tuple-element.81), kind=kLoop, calls=%fused_computation.6 | loop fusion | flops 50331648 | bytes 25165824 | tf_op jit(solution)/shard_map/concatenate | solution.py:645
  445.3 16.4 %fusion.73 = bf16[256,768]{1,0:T(8,128)(2,1)} fusion(bf16[4,768,768,1]{2,1,0,3:T(8,128)(2,1)} %bitcast.548, bf16[2,128,4,8,768]{4,3,2,1,0:T(8,128)(2,1)} %bitcast.546, bf16[2,1024]{1,0:T(2,128)(2,1)S(1)} %copy-done.103, s32[2,1024]{1,0:T(2,128)S(1)} %copy-done.155), kind=kOutput, calls=%fused_computation.115 | convolution fusion | flops 10472849408 | bytes 17707008 | tf_op jit(solution)/shard_map/xpg,xpz->gz/dot_general | solution.py:656
  461.8 18.0 %bitcast_convert_fusion.1 = bf16[3072,768]{1,0:T(8,128)(2,1)} fusion(bf16[2,1024,768]{2,1,0:T(8,128)(2,1)S(1)} %add_convert_fusion.1, bf16[2,1024,768]{2,1,0:T(8,128)(2,1)} %copy-done.11, bf16[2,1024,768]{2,1,0:T(8,128)(2,1)} %get-tuple-element.87, bf16[2,1024,768]{2,1,0:T(8,128)(2,1)} %get-tuple-element.86, bf16[2,1024,768]{2,1,0:T(8,128)(2,1)} %get-tuple-element.85), kind=kOutput, calls=%fused_computation.10 | convolution fusion | flops 9716367360 | bytes 20447232 | tf_op jit(solution)/shard_map/xwu,xwo->uo/dot_general | solution.py:641
  479.8 4.0 copy_bitcast_fusion.x_ref
  483.8 77.6 %shard_map.585 = f32[112,768]{1,0:T(8,128)S(1)} custom-call(bf16[2,16,112,768]{3,2,1,0:T(8,128)(2,1)S(1)} %copy_bitcast_fusion.x_ref), custom_call_target="tpu_custom_call" | custom-call | flops 5505024 | bytes 11010048 | tf_op jit(solution)/shard_map/pallas_call | solution.py:396
  561.6 7.3 %convolution_add_fusion.1 = f32[2,512,768]{2,1,0:T(8,128)} fusion(f32[2,512,768]{2,1,0:T(8,128)S(1)} %copy-done.2, bf16[2,512,2048]{2,1,0:T(8,128)(2,1)} %get-tuple-element.80, bf16[2048,768,1]{1,0,2:T(8,128)(2,1)S(1)} %copy-done.10), kind=kOutput, calls=%fused_computation.111 | convolution fusion | flops 3222011904 | bytes 13631488 | tf_op jit(solution)/shard_map/stf,fd->std/dot_general | solution.py:599
  573.4 11.5 %shard_map.586 = f32[80,128]{1,0:T(8,128)} custom-call(f32[80,128]{1,0:T(8,128)} %pad_bitcast_fusion.x_ref), custom_call_target="tpu_custom_call" | custom-call | flops 163840 | bytes 655360 | tf_op jit(solution)/shard_map/pallas_call | solution.py:472
  (549 shorter events, 122.8 us)
Async XLA Ops:
  7.2 73.1 %all-gather.4.cloned.1.call-start = ((), (), s32[]{:S(2)}) async-start(), calls=%async_computation.1 | async-start | bytes 5677056 | tf_op jit(solution)/shard_map/all_gather | solution.py:545
  10.5 175.6 %all-gather.6.cloned.1.call-start = ((), (), s32[]{:S(2)}) async-start(), calls=%async_computation.2 | async-start | bytes 14598144 | tf_op jit(solution)/shard_map/all_gather | solution.py:547
  15.3 553.6 %reduce-scatter.2.cloned.1.call-start = ((), (), s32[]{:S(2)}) async-start(), calls=%async_computation.3 | async-start | bytes 14598144 | tf_op jit(solution)/shard_map/reduce_scatter | solution.py:665
  15.4 100.4 %copy-start.100 = (f32[256]{0:T(256)}, f32[256]{0:T(256)S(1)}, u32[]{:S(2)}) copy-start(f32[256]{0:T(256)S(1)} %minimum_convert_fusion.11) | copy-start | bytes 3076
  15.4 105.9 %copy-start.106 = (pred[512]{0:T(512)(128)(4,1)}, pred[512]{0:T(512)(128)(4,1)S(1)}, u32[]{:S(2)}) copy-start(pred[512]{0:T(512)(128)(4,1)S(1)} %get-tuple-element.157) | copy-start | bytes 1540
  15.4 106.6 %copy-start.104 = (pred[512]{0:T(512)(128)(4,1)}, pred[512]{0:T(512)(128)(4,1)S(1)}, u32[]{:S(2)}) copy-start(pred[512]{0:T(512)(128)(4,1)S(1)} %get-tuple-element.156) | copy-start | bytes 1540
  15.4 105.8 %copy-start.129 = (pred[512]{0:T(512)(128)(4,1)}, pred[512]{0:T(512)(128)(4,1)S(1)}, u32[]{:S(2)}) copy-start(pred[512]{0:T(512)(128)(4,1)S(1)} %get-tuple-element.161) | copy-start | bytes 1540
  15.4 108.1 %copy-start.127 = (pred[512]{0:T(512)(128)(4,1)}, pred[512]{0:T(512)(128)(4,1)S(1)}, u32[]{:S(2)}) copy-start(pred[512]{0:T(512)(128)(4,1)S(1)} %get-tuple-element.160) | copy-start | bytes 1540
  15.5 105.8 %copy-start.112 = (pred[512]{0:T(512)(128)(4,1)}, pred[512]{0:T(512)(128)(4,1)S(1)}, u32[]{:S(2)}) copy-start(pred[512]{0:T(512)(128)(4,1)S(1)} %get-tuple-element.187) | copy-start | bytes 1540
  15.5 105.8 %copy-start.130 = (pred[512]{0:T(512)(128)(4,1)}, pred[512]{0:T(512)(128)(4,1)S(1)}, u32[]{:S(2)}) copy-start(pred[512]{0:T(512)(128)(4,1)S(1)} %get-tuple-element.186) | copy-start | bytes 1540
  16.0 105.3 %copy-start.114 = (pred[512]{0:T(512)(128)(4,1)}, pred[512]{0:T(512)(128)(4,1)S(1)}, u32[]{:S(2)}) copy-start(pred[512]{0:T(512)(128)(4,1)S(1)} %get-tuple-element.188) | copy-start | bytes 1540
  16.6 104.7 %copy-start.108 = (pred[512]{0:T(512)(128)(4,1)}, pred[512]{0:T(512)(128)(4,1)S(1)}, u32[]{:S(2)}) copy-start(pred[512]{0:T(512)(128)(4,1)S(1)} %get-tuple-element.190) | copy-start | bytes 1540
  17.8 104.2 %copy-start.120 = (pred[512]{0:T(512)(128)(4,1)}, pred[512]{0:T(512)(128)(4,1)S(1)}, u32[]{:S(2)}) copy-start(pred[512]{0:T(512)(128)(4,1)S(1)} %get-tuple-element.181) | copy-start | bytes 1540
  18.4 103.7 %copy-start.122 = (pred[512]{0:T(512)(128)(4,1)}, pred[512]{0:T(512)(128)(4,1)S(1)}, u32[]{:S(2)}) copy-start(pred[512]{0:T(512)(128)(4,1)S(1)} %get-tuple-element.182) | copy-start | bytes 1540
  18.9 103.2 %copy-start.110 = (pred[512]{0:T(512)(128)(4,1)}, pred[512]{0:T(512)(128)(4,1)S(1)}, u32[]{:S(2)}) copy-start(pred[512]{0:T(512)(128)(4,1)S(1)} %get-tuple-element.184) | copy-start | bytes 1540
  18.9 100.9 %copy-start.85 = (pred[512]{0:T(512)(128)(4,1)}, pred[512]{0:T(512)(128)(4,1)S(1)}, u32[]{:S(2)}) copy-start(pred[512]{0:T(512)(128)(4,1)S(1)} %get-tuple-element.192) | copy-start | bytes 1540
  18.9 101.7 %copy-start.83 = (pred[512]{0:T(512)(128)(4,1)}, pred[512]{0:T(512)(128)(4,1)S(1)}, u32[]{:S(2)}) copy-start(pred[512]{0:T(512)(128)(4,1)S(1)} %get-tuple-element.193) | copy-start | bytes 1540
  18.9 100.9 %copy-start.116 = (pred[512]{0:T(512)(128)(4,1)}, pred[512]{0:T(512)(128)(4,1)S(1)}, u32[]{:S(2)}) copy-start(pred[512]{0:T(512)(128)(4,1)S(1)} %get-tuple-element.155) | copy-start | bytes 1540
  18.9 101.6 %copy-start.133 = (pred[512]{0:T(512)(128)(4,1)}, pred[512]{0:T(512)(128)(4,1)S(1)}, u32[]{:S(2)}) copy-start(pred[512]{0:T(512)(128)(4,1)S(1)} %get-tuple-element.154) | copy-start | bytes 1540
  19.0 100.9 %copy-start.134 = (pred[512]{0:T(512)(128)(4,1)}, pred[512]{0:T(512)(128)(4,1)S(1)}, u32[]{:S(2)}) copy-start(pred[512]{0:T(512)(128)(4,1)S(1)} %get-tuple-element.177) | copy-start | bytes 1540
  19.0 101.6 %copy-start.131 = (pred[512]{0:T(512)(128)(4,1)}, pred[512]{0:T(512)(128)(4,1)S(1)}, u32[]{:S(2)}) copy-start(pred[512]{0:T(512)(128)(4,1)S(1)} %get-tuple-element.176) | copy-start | bytes 1540
  19.6 100.3 %copy-start.118 = (pred[512]{0:T(512)(128)(4,1)}, pred[512]{0:T(512)(128)(4,1)S(1)}, u32[]{:S(2)}) copy-start(pred[512]{0:T(512)(128)(4,1)S(1)} %get-tuple-element.178) | copy-start | bytes 1540
  20.1 100.5 %copy-start.132 = (pred[512]{0:T(512)(128)(4,1)}, pred[512]{0:T(512)(128)(4,1)S(1)}, u32[]{:S(2)}) copy-start(pred[512]{0:T(512)(128)(4,1)S(1)} %get-tuple-element.175) | copy-start | bytes 1540
  20.1 102.7 %copy-start.126 = (pred[512]{0:T(512)(128)(4,1)}, pred[512]{0:T(512)(128)(4,1)S(1)}, u32[]{:S(2)}) copy-start(pred[512]{0:T(512)(128)(4,1)S(1)} %get-tuple-element.153) | copy-start | bytes 1540
  20.1 103.5 %copy-start.124 = (pred[512]{0:T(512)(128)(4,1)}, pred[512]{0:T(512)(128)(4,1)S(1)}, u32[]{:S(2)}) copy-start(pred[512]{0:T(512)(128)(4,1)S(1)} %get-tuple-element.152) | copy-start | bytes 1540
  23.5 100.1 %copy-start.45 = (f32[512]{0:T(512)}, f32[512]{0:T(512)S(1)}, u32[]{:S(2)}) copy-start(f32[512]{0:T(512)S(1)} %get-tuple-element.147) | copy-start | bytes 6148
  23.6 100.1 %copy-start.49 = (f32[512]{0:T(512)}, f32[512]{0:T(512)S(1)}, u32[]{:S(2)}) copy-start(f32[512]{0:T(512)S(1)} %get-tuple-element.146) | copy-start | bytes 6148
  23.6 100.0 %copy-start.47 = (f32[512]{0:T(512)}, f32[512]{0:T(512)S(1)}, u32[]{:S(2)}) copy-start(f32[512]{0:T(512)S(1)} %get-tuple-element.148) | copy-start | bytes 6148
  23.6 100.0 %copy-start.53 = (f32[512]{0:T(512)}, f32[512]{0:T(512)S(1)}, u32[]{:S(2)}) copy-start(f32[512]{0:T(512)S(1)} %get-tuple-element.149) | copy-start | bytes 6148
  23.6 100.0 %copy-start.41 = (f32[512]{0:T(512)}, f32[512]{0:T(512)S(1)}, u32[]{:S(2)}) copy-start(f32[512]{0:T(512)S(1)} %get-tuple-element.150) | copy-start | bytes 6148
  119.7 212.3 %copy-start.70 = (f32[768]{0:T(1024)}, f32[768]{0:T(1024)S(1)}, u32[]{:S(2)}) copy-start(f32[768]{0:T(1024)S(1)} %mul.1576) | copy-start | bytes 9220
  136.6 195.5 %copy-start.72 = (f32[2,512]{1,0:T(2,128)}, f32[2,512]{1,0:T(2,128)S(1)}, u32[]{:S(2)}) copy-start(f32[2,512]{1,0:T(2,128)S(1)} %fusion.178) | copy-start | bytes 12292
  (131 other events, 2180.2 us)
Sparse Core Ops, SparseCore 0:
  11.5 68.7 all-gather.3
  83.8 102.1 all-gather.5
  366.9 167.0 reduce-scatter.1

commit v8 on v7

--- a/solution.py
+++ b/solution.py
@@ -310,7 +310,7 @@
     return chip
 
 
-def ring_rs_kernel(snake, x_ref, out_ref, part_ref, send_ref, recv_ref, swap_sem, send_sem, recv_sem, credit):
+def ring_rs_kernel(snake, x_ref, out_ref, part_ref, send_ref, recv_ref, swap_sem, send_sem, recv_sem):
     count, steps = x_ref.shape[1], x_ref.shape[1] - 1
     lanes = out_ref.shape[1] // 2
     position_of = snake_position if snake else plain_position
@@ -322,7 +322,6 @@
     behind = (chip_of((here + count - 1) % count), core)
     partner = (chip, 1 - core)
     targets = (ahead, behind)
-    sources = (behind, ahead)
 
     barrier = pltpu.get_barrier_semaphore()
     for peer in (ahead, behind, partner):
@@ -356,38 +355,26 @@
         link(way, 0).start()
 
     def step_body(step, carry):
-        slot_in = (step - 1) % 2
-        slot_out = step % 2
         for way in (0, 1):
-            link(way, slot_in).wait_recv()
-            total = recv_ref[way, slot_in].astype(jnp.float32) + own(way, step)
-
-            @pl.when(step >= 2)
-            def _():
-                link(way, slot_out).wait_send()
-
-            send_ref[way, slot_out] = total.astype(send_ref.dtype)
-
-            @pl.when(step <= steps - 2)
-            def _():
-                pl.semaphore_signal(credit.at[way], 1, device_id=sources[way], device_id_type=MESH_ID)
-
-            @pl.when(step >= 2)
-            def _():
-                pl.semaphore_wait(credit.at[way], 1)
-
-            link(way, slot_out).start()
+            link(way, step - 1).wait_recv()
+            total = recv_ref[way, step - 1].astype(jnp.float32) + own(way, step)
+            send_ref[way, step] = total.astype(send_ref.dtype)
+            link(way, step).start()
         return carry
 
     lax.fori_loop(1, steps, step_body, 0)
 
-    last = steps % 2
     for way in (0, 1):
-        link(way, (steps - 1) % 2).wait_recv()
-        total = recv_ref[way, (steps - 1) % 2].astype(jnp.float32) + own(way, steps)
+        link(way, steps - 1).wait_recv()
+        total = recv_ref[way, steps - 1].astype(jnp.float32) + own(way, steps)
         out_ref[:, pl.ds(way * lanes, lanes)] = total
-        link(way, (steps - 2) % 2).wait_send()
-        link(way, (steps - 1) % 2).wait_send()
+
+    def drain(step, carry):
+        for way in (0, 1):
+            link(way, step).wait_send()
+        return carry
+
+    lax.fori_loop(0, steps, drain, 0)
 
 
 def ring_reduce_scatter(x, snake):
@@ -400,12 +387,11 @@
         out_specs=pl.BlockSpec(memory_space=pltpu.VMEM),
         scratch_shapes=[
             pltpu.VMEM((count, rows, width), x.dtype),
-            pltpu.VMEM((2, 2, rows, half), x.dtype),
-            pltpu.VMEM((2, 2, rows, half), x.dtype),
+            pltpu.VMEM((2, count - 1, rows, half), x.dtype),
+            pltpu.VMEM((2, count - 1, rows, half), x.dtype),
             pltpu.SemaphoreType.DMA((2,)),
-            pltpu.SemaphoreType.DMA((2, 2)),
-            pltpu.SemaphoreType.DMA((2, 2)),
-            pltpu.SemaphoreType.REGULAR((2,)),
+            pltpu.SemaphoreType.DMA((2, count - 1)),
+            pltpu.SemaphoreType.DMA((2, count - 1)),
         ],
         compiler_params=pltpu.CompilerParams(collective_id=0, has_side_effects=True,
                                              vmem_limit_bytes=48 * 1024 * 1024),
@@ -487,6 +473,38 @@
         cost_estimate=pl.CostEstimate(flops=count * x.size, transcendentals=0,
                                       bytes_accessed=count * x.size * 4),
     )(x)
+
+
+def adam_kernel(scalar_ref, master_ref, first_ref, grad_ref, rows_ref, cols_ref,
+                next_ref, moment_ref, rowstat_ref, copy_ref):
+    factor, mean_row, spread = scalar_ref[0], scalar_ref[1], scalar_ref[2]
+    clipped = grad_ref[...] * factor
+    momentum = beta_one * first_ref[...] + (1.0 - beta_one) * clipped
+    row_part = jnp.mean(clipped * clipped, axis=1, keepdims=True)
+    rowstat = beta_two * rows_ref[...] + (1.0 - beta_two) * (row_part + eps_square)
+    second = rowstat * cols_ref[...] / mean_row / second_fix
+    update = momentum / first_fix / (jnp.sqrt(second) + eps_divide)
+    nextval = master_ref[...] * (1.0 - learn_rate * weight_decay) - learn_rate * spread * update
+    next_ref[...] = nextval
+    moment_ref[...] = momentum
+    rowstat_ref[...] = rowstat
+    copy_ref[...] = nextval.astype(copy_ref.dtype)
+
+
+def adam_update(scalars, master, first, grad, rows_old, colstat):
+    count_rows, count_cols = master.shape
+    vmem = pl.BlockSpec(memory_space=pltpu.VMEM)
+    full = jax.ShapeDtypeStruct((count_rows, count_cols), jnp.float32)
+    nextval, momentum, rowstat, copy = pl.pallas_call(
+        adam_kernel,
+        out_shape=(full, full, jax.ShapeDtypeStruct((count_rows, 1), jnp.float32),
+                   jax.ShapeDtypeStruct((count_rows, count_cols), jnp.bfloat16)),
+        in_specs=[pl.BlockSpec(memory_space=pltpu.SMEM)] + [vmem] * 5,
+        out_specs=(vmem, vmem, vmem, vmem),
+        cost_estimate=pl.CostEstimate(flops=20 * master.size, transcendentals=master.size,
+                                      bytes_accessed=master.size * 22),
+    )(scalars, master, first, grad, rows_old.reshape(count_rows, 1), colstat.reshape(1, count_cols))
+    return nextval, momentum, rowstat.reshape(count_rows), copy
 
 
 def body(
@@ -746,14 +764,8 @@
     factor = jnp.minimum(1.0, clip_limit / global_norm)
     factor_sq = factor * factor
     column_scaled = column_scaled_raw * factor_sq
-    rowstats = []
     mean_rows = []
     for index_param in range(6):
-        clipped_sq = shards[index_param] * factor * (shards[index_param] * factor)
-        row_part = jnp.mean(clipped_sq, axis=1)
-        rowstats.append(
-            beta_two * rows_old[index_param] + (1.0 - beta_two) * (row_part + eps_square)
-        )
         total_new = beta_two * sum_rows_old[index_param] + (1.0 - beta_two) * (
             factor_sq * sum_sq[index_param] / col_widths[index_param]
             + rows_full[index_param] * eps_square
@@ -762,8 +774,6 @@
     results = [encoded, global_norm]
     for index_param in range(6):
         master = masters[index_param]
-        clipped = shards[index_param] * factor
-        momentum = beta_one * firsts[index_param] + (1.0 - beta_one) * clipped
         column_piece = lax.slice_in_dim(
             column_scaled,
             col_starts[index_param],
@@ -772,15 +782,14 @@
         colstat = beta_two * cols_old[index_param] + (1.0 - beta_two) * (
             column_piece / rows_full[index_param] + eps_square
         )
-        rowstat = rowstats[index_param]
-        second = rowstat[:, None] * colstat[None, :] / mean_rows[index_param] / second_fix
-        update = momentum / first_fix / (jnp.sqrt(second) + eps_divide)
         spread = jnp.maximum(
             jnp.sqrt(sum_weights[index_param] / (rows_full[index_param] * col_widths[index_param])),
             0.001,
         )
-        nextval = master * (1.0 - learn_rate * weight_decay) - learn_rate * spread * update
-        results += [nextval, momentum, rowstat, colstat, nextval.astype(jnp.bfloat16)]
+        scalars = jnp.stack([factor, mean_rows[index_param], spread]).astype(jnp.float32)
+        nextval, momentum, rowstat, copy = adam_update(
+            scalars, master, firsts[index_param], shards[index_param], rows_old[index_param], colstat)
+        results += [nextval, momentum, rowstat, colstat, copy]
     clipped = shards[6] * factor
     momentum = beta_one * vectors_first + (1.0 - beta_one) * clipped
     variance = beta_two * vectors_second + (1.0 - beta_two) * (clipped * clipped + eps_square)

time: 652 us -> 661 us (1.014)
  Pallas kernels: 145 us -> 160 us
  other arithmetic: 93 us -> 80.9 us
  local copies, waits for them, and re-layouts: 67 us -> 74.7 us
    pallas_call x0 -> x6, Pallas kernels: none -> 15.8 us  [adam_update(): pl.pallas_call(adam_kernel, out_shape=(full, full, jax.ShapeDtypeStruct((...]
    reshape x0 -> x13, local copies, waits for them, and re-layouts: none -> 12.6 us  [the longest x6 8.22 us: adam_update(): rows_old.reshape(count_rows, 1)]
    convert_element_type x7 -> x0, other arithmetic: 9.63 us -> none  [the longest x6 9.52 us: body(): nextval.astype(jnp.bfloat16)]
    pallas_call x0 -> x6, other arithmetic: none -> 8.44 us  [adam_update(): pl.pallas_call(adam_kernel, out_shape=(full, full, jax.ShapeDtypeStruct((...]
  transfers between devices with their start and end apart: 3 -> 3, of which waited for: 2 -> 2; matrix products, arithmetic and copies ran while one was open for 30% -> 31% of each run, Pallas kernels for 12% -> 12%
where the time goes in v8:
time: 661 us; the launch traced here: 651 us
  matrix products  198 us (30%)
  Pallas kernels  160 us (24%)
  waiting for transfers between devices  102 us (15%)
  other arithmetic  80.9 us (12%)
  local copies, waits for them, and re-layouts  74.7 us (11%)
  between operations  30.4 us (5%)
    pallas_call x1, Pallas kernels, ring_reduce_scatter(): pl.pallas_call(functools.partial(ring_rs_kernel, snake), out_shape=jax.Sh...  75.2 us
    all_gather x1, waiting for transfers between devices, body(): first_all = lax.all_gather(first_group, groups, axis=0, tiled=True)  52.8 us
    all_gather x1, waiting for transfers between devices, body(): second_all = lax.all_gather(second_group, groups, axis=0, tiled=True)  49.2 us
    pallas_call x1, Pallas kernels, attention_backward(): pl.pallas_call(attn_bwd_kernel, out_shape=(part, part, part), grid_spec=p...  34.2 us
    dot_general x3, matrix products, body(): tokens, gbst_pull = jax.vjp(gbst_tokens, hidden, vector_vals[3])  25.3 us
    pallas_call x1, Pallas kernels, attention_forward(): pl.pallas_call(attn_fwd_kernel, out_shape=jax.ShapeDtypeStruct((count_ite...  21.5 us
    dot_general x1, matrix products, body(): jnp.einsum('xwu,xwo->uo', byte_windows, gradient_hidden_reduced, preferre...  18.4 us
    dot_general x1, matrix products, body(): jnp.einsum('std,fd->stf', cotangent, back_contract, preferred_element_typ...  17.4 us
  transfers between devices with their start and end apart: 3, of which 2 were waited for; matrix products, arithmetic and copies ran while one was open for 31% of the time, Pallas kernels for 12%

profile of v8, /device:TPU:0, one launch (start us, length us, event | category | flops | bytes accessed | tf_op | source)
XLA Modules:
  0.0 651.3 jit_solution(3373282407245626153)
XLA Ops:
  27.5 52.8 %all-gather.4.cloned.1.call-done = bf16[3584,768]{1,0:T(8,128)(2,1)} async-done(((bf16[112,768]{1,0:T(8,128)(2,1)}), bf16[3584,768]{1,0:T(8,128)(2,1)}) %all-gather.4.cloned.1.call-update) | async-done | bytes 5505040 | tf_op jit(solution)/shard_map/all_gather | solution.py:563
  80.4 4.8 slice.373
  89.4 4.6 pad_slice_fusion.5
  94.0 14.1 %fusion.30 = f32[2,1024,768]{2,1,0:T(8,128)S(1)} fusion(bf16[3072,768,1]{1,0,2:T(8,128)(2,1)} %bitcast.552, bf16[2,1024,768]{2,1,0:T(8,128)(2,1)} %copy-done.11, bf16[2,1024,768]{2,1,0:T(8,128)(2,1)} %get-tuple-element.117, bf16[2,1024,768]{2,1,0:T(8,128)(2,1)} %get-tuple-element.116, bf16[2,1024,768]{2,1,0:T(8,128)(2,1)} %get-tuple-element.115), kind=kOutput, calls=%fused_computation.75 | convolution fusion | flops 9714008064 | bytes 23592960 | tf_op jit(solution)/shard_map/hby,yj->hbj/dot_general | solution.py:597
  124.7 12.1 %multiply_reduce_fusion.5 = (f32[2,512]{1,0:T(2,128)S(1)}, f32[2,512,768]{2,1,0:T(8,128)S(1)}) fusion(f32[2,1024,768]{2,1,0:T(8,128)} %copy-done, f32[768]{0:T(1024)S(1)} %add.1678, f32[2,512]{1,0:T(2,128)S(1)} %add_multiply_fusion, f32[2,512]{1,0:T(2,128)S(1)} %add_multiply_fusion.1, f32[2,512]{1,0:T(2,128)S(1)} %add_multiply_fusion.2, ...), kind=kOutput, calls=%fused_computation.61 | convolution fusion | flops 4841274368 | bytes 12614656 | tf_op jit(solution)/shard_map/jvp(ntj,njd->ntd)/dot_general | solution.py:103
  136.9 49.2 %all-gather.6.cloned.1.call-done = bf16[768,9216]{1,0:T(8,128)(2,1)} async-done(((bf16[24,9216]{1,0:T(8,128)(2,1)}), bf16[768,9216]{1,0:T(8,128)(2,1)}) %all-gather.6.cloned.1.call-update) | async-done | bytes 14155792 | tf_op jit(solution)/shard_map/all_gather | solution.py:565
  186.1 7.5 %convolution_convert_fusion.q_ref.k_ref.v_ref = bf16[2,512,2304]{2,1,0:T(8,128)(2,1)} fusion(bf16[768,9216]{1,0:T(8,128)(2,1)} %all-gather.6.cloned.1.call-done, f32[2,512,768]{2,1,0:T(8,128)S(1)} %get-tuple-element.167, f32[768]{0:T(1024)S(1)} %mul.1203, f32[2,512]{1,0:T(2,128)S(1)} %fusion.175), kind=kOutput, calls=%fused_computation.26 | convolution fusion | flops 3628597248 | bytes 11410432 | tf_op jit(solution)/shard_map/std,de->ste/dot_general | solution.py:603
  193.6 21.5 %shard_map.583 = bf16[2,512,768]{2,1,0:T(8,128)(2,1)} custom-call(s32[2]{0:T(128)} %len_ref.3, bf16[2,512,2304]{2,1,0:T(8,128)(2,1)} %convolution_convert_fusion.q_ref.k_ref.v_ref, bf16[2,512,2304]{2,1,0:T(8,128)(2,1)} %convolution_convert_fusion.q_ref.k_ref.v_ref, bf16[2,512,2304]{2,1,0:T(8,128)(2,1)} %convolution_convert_fusion.q_ref.k_ref.v_ref), custom_call_target="tpu_custom_call" | custom-call | flops 3221225472 | bytes 6291456 | tf_op jit(solution)/shard_map/pallas_call | solution.py:254
  215.1 4.8 multiply_reduce_fusion.4
  221.8 4.4 reshape.4503
  226.2 13.2 %fusion.18 = f32[2,512,4096]{2,1,0:T(8,128)} fusion(bf16[768,9216]{1,0:T(8,128)(2,1)} %all-gather.6.cloned.1.call-done, f32[2,512,768]{2,1,0:T(8,128)} %get-tuple-element.169, f32[768]{0:T(1024)S(1)} %mul.1210, f32[2,512]{1,0:T(2,128)S(1)} %fusion.176), kind=kOutput, calls=%fused_computation.38 | convolution fusion | flops 6444810240 | bytes 26221568 | tf_op jit(solution)/shard_map/std,de->ste/dot_general | solution.py:614
  239.4 17.4 %bitcast_multiply_fusion.1 = (f32[2,512,2048]{2,1,0:T(8,128)}, f32[2,512,2048]{2,1,0:T(8,128)}, bf16[2,512,2048]{2,1,0:T(8,128)(2,1)}) fusion(f32[2,512,4096]{2,1,0:T(8,128)} %fusion.18, bf16[2048,768,1]{1,0,2:T(8,128)(2,1)S(1)} %copy-done.9, bf16[2,512,768]{2,1,0:T(8,128)(2,1)S(1)} %copy-done.18), kind=kOutput, calls=%fused_computation.18 | convolution fusion | flops 3271557120 | bytes 42467328 | tf_op jit(solution)/shard_map/std,fd->stf/dot_general | solution.py:627
  256.8 15.3 %bitcast_convert_fusion = bf16[768,4096]{1,0:T(8,128)(2,1)} fusion(f32[2,512,2048]{2,1,0:T(8,128)} %get-tuple-element.109, f32[2,512,2048]{2,1,0:T(8,128)} %get-tuple-element.108, f32[2,512,768]{2,1,0:T(8,128)S(1)} %copy-done.1, f32[768]{0:T(1024)S(1)} %mul.1210, f32[2,512]{1,0:T(2,128)S(1)} %fusion.176), kind=kOutput, calls=%fused_computation.7 | convolution fusion | flops 6456344576 | bytes 26221568 | tf_op jit(solution)/shard_map/std,ste->de/dot_general | solution.py:632
  272.1 14.4 %multiply_reduce_fusion = (bf16[768]{0:T(1024)(128)(2,1)}, f32[2,512]{1,0:T(2,128)S(1)}, f32[2,512,768]{2,1,0:T(8,128)}) fusion(f32[2,512,768]{2,1,0:T(8,128)S(1)} %copy-done.1, f32[2,512]{1,0:T(2,128)S(1)} %fusion.176, f32[768]{0:T(1024)S(1)} %mul.1210, bf16[768,9216]{1,0:T(8,128)(2,1)} %all-gather.6.cloned.1.call-done, ...), kind=kOutput, calls=%fused_computation.54 | convolution fusion | flops 6455556096 | bytes 29372928 | tf_op jit(solution)/shard_map/ste,de->std/dot_general | solution.py:635
  292.4 3.9 convolution_convert_fusion.1.do_ref
  296.2 34.2 %shard_map.584 = (bf16[2,512,768]{2,1,0:T(8,128)(2,1)}, bf16[2,512,768]{2,1,0:T(8,128)(2,1)}, bf16[2,512,768]{2,1,0:T(8,128)(2,1)}) custom-call(s32[2]{0:T(128)} %len_ref.3, bf16[2,512,2304]{2,1,0:T(8,128)(2,1)} %convolution_convert_fusion.q_ref.k_ref.v_ref, bf16[2,512,2304]{2,1,0:T(8,128)(2,1)} %convolution_convert_fusion.q_ref.k_ref.v_ref, ...), custom_call_target="tpu_custom_call" | custom-call | flops 8053063680 | bytes 11010048 | tf_op jit(solution)/shard_map/pallas_call | solution.py:276
  333.7 5.6 bitcast_convert_fusion.2
  339.4 5.0 bitcast_convert_fusion.3
  344.4 5.5 reshape.4466
  349.9 12.6 %pad_maximum_fusion = bf16[768,9216]{1,0:T(8,128)(2,1)} fusion(bf16[768,2048]{1,0:T(8,128)(2,1)S(1)} %reshape.4466, bf16[768,4096]{1,0:T(8,128)(2,1)} %bitcast_convert_fusion, bf16[768,768]{1,0:T(8,128)(2,1)} %bitcast_convert_fusion.5, bf16[768,2304]{1,0:T(8,128)(2,1)} %bitcast_convert_fusion.2), kind=kLoop, calls=%fused_computation.1 | loop fusion | flops 56623104 | bytes 28311552 | tf_op jit(solution)/shard_map/concatenate | solution.py:680
  388.8 9.4 %multiply_reduce_fusion.1 = (bf16[768]{0:T(1024)(128)(2,1)S(1)}, f32[2,512]{1,0:T(2,128)S(1)}, f32[2,512,768]{2,1,0:T(8,128)S(1)}) fusion(f32[2,512,768]{2,1,0:T(8,128)} %copy-done.3, f32[2,512]{1,0:T(2,128)} %copy-done.58, f32[768]{0:T(1024)} %copy-done.56, bf16[2,512,2304]{2,1,0:T(8,128)(2,1)} %copy-done.20, ...), kind=kOutput, calls=%fused_computation.55 | convolution fusion | flops 3628595456 | bytes 14562816 | tf_op jit(solution)/shard_map/ste,de->std/dot_general | solution.py:651
  400.6 8.6 %select_reduce_fusion.2 = (f32[2,512]{1,0:T(2,128)S(1)}, f32[2,512]{1,0:T(2,128)S(1)}, f32[2,512]{1,0:T(2,128)S(1)}, f32[2,512]{1,0:T(2,128)S(1)}, f32[2,512]{1,0:T(2,128)S(1)}, /*index=5*/f32[2,512]{1,0:T(2,128)S(1)}) fusion(pred[512,1024]{1,0:T(8,128)(4,1)S(1)} %copy-done.22, pred[512,1024]{1,0:T(8,128)(4,1)S(1)} %copy-done.21, ...), kind=kOutput, calls=%fused_computation.43 | convolution fusion | flops 4845987840 | bytes 12610560 | tf_op jit(solution)/shard_map/transpose(jvp(ntd,njd->ntj))/dot_general | solution.py:600
  417.9 11.4 %add_convert_fusion.1 = bf16[2,1024,768]{2,1,0:T(8,128)(2,1)S(1)} fusion(f32[768]{0:T(1024)S(1)} %mul.1254, f32[2,1024]{1,0:T(2,128)S(1)} %fusion.102, f32[2,512,768]{2,1,0:T(8,128)} %copy-done.12, f32[2,512]{1,0:T(2,128)S(1)} %copy-done.80, f32[2,512]{1,0:T(2,128)S(1)} %copy-done.78, f32[2,512]{1,0:T(2,128)S(1)} %copy-done.88, ...), kind=kOutput, calls=%fused_computation.25 | convolution fusion | flops 4842848256 | bytes 9473024 | tf_op jit(solution)/shard_map/transpose(jvp(ntj,ntd->njd))/dot_general | solution.py:600
  429.3 4.4 pad_slice_fusion.2
  433.8 5.3 fusion.78
  439.7 9.6 %pad_maximum_fusion.2 = bf16[2,1024,3072]{2,1,0:T(8,128)(2,1)} fusion(bf16[2,1024,768]{2,1,0:T(8,128)(2,1)S(1)} %add_convert_fusion.1, bf16[2,1024,768]{2,1,0:T(8,128)(2,1)} %get-tuple-element.113, bf16[2,1024,768]{2,1,0:T(8,128)(2,1)} %get-tuple-element.112, bf16[2,1024,768]{2,1,0:T(8,128)(2,1)} %get-tuple-element.111), kind=kLoop, calls=%fused_computation.6 | loop fusion | flops 50331648 | bytes 25165824 | tf_op jit(solution)/shard_map/concatenate | solution.py:663
  449.3 16.5 %fusion.73 = bf16[256,768]{1,0:T(8,128)(2,1)} fusion(bf16[4,768,768,1]{2,1,0,3:T(8,128)(2,1)} %bitcast.553, bf16[2,128,4,8,768]{4,3,2,1,0:T(8,128)(2,1)} %bitcast.551, bf16[2,1024]{1,0:T(2,128)(2,1)S(1)} %copy-done.92, s32[2,1024]{1,0:T(2,128)S(1)} %copy-done.143), kind=kOutput, calls=%fused_computation.115 | convolution fusion | flops 10472849408 | bytes 17707008 | tf_op jit(solution)/shard_map/xpg,xpz->gz/dot_general | solution.py:674
  465.8 18.4 %bitcast_convert_fusion.1 = bf16[3072,768]{1,0:T(8,128)(2,1)} fusion(bf16[2,1024,768]{2,1,0:T(8,128)(2,1)S(1)} %add_convert_fusion.1, bf16[2,1024,768]{2,1,0:T(8,128)(2,1)} %copy-done.11, bf16[2,1024,768]{2,1,0:T(8,128)(2,1)} %get-tuple-element.117, bf16[2,1024,768]{2,1,0:T(8,128)(2,1)} %get-tuple-element.116, bf16[2,1024,768]{2,1,0:T(8,128)(2,1)} %get-tuple-element.115), kind=kOutput, calls=%fused_computation.10 | convolution fusion | flops 9716367360 | bytes 20447232 | tf_op jit(solution)/shard_map/xwu,xwo->uo/dot_general | solution.py:659
  487.6 75.2 %shard_map.585 = f32[112,768]{1,0:T(8,128)S(1)} custom-call(bf16[2,16,112,768]{3,2,1,0:T(8,128)(2,1)S(1)} %copy_bitcast_fusion.x_ref), custom_call_target="tpu_custom_call" | custom-call | flops 5505024 | bytes 11010048 | tf_op jit(solution)/shard_map/pallas_call | solution.py:383
  566.0 7.3 %convolution_add_fusion.1 = f32[2,512,768]{2,1,0:T(8,128)} fusion(f32[2,512,768]{2,1,0:T(8,128)S(1)} %copy-done.2, bf16[2,512,2048]{2,1,0:T(8,128)(2,1)} %get-tuple-element.110, bf16[2048,768,1]{1,0,2:T(8,128)(2,1)S(1)} %copy-done.10), kind=kOutput, calls=%fused_computation.111 | convolution fusion | flops 3222011904 | bytes 13631488 | tf_op jit(solution)/shard_map/stf,fd->std/dot_general | solution.py:617
  576.4 13.2 %shard_map.586 = f32[80,128]{1,0:T(8,128)} custom-call(f32[80,128]{1,0:T(8,128)} %pad_bitcast_fusion.x_ref), custom_call_target="tpu_custom_call" | custom-call | flops 163840 | bytes 655360 | tf_op jit(solution)/shard_map/pallas_call | solution.py:458
  609.8 3.8 shard_map.591
  (534 shorter events, 134.7 us)
Async XLA Ops:
  7.2 73.2 %all-gather.4.cloned.1.call-start = ((), (), s32[]{:S(2)}) async-start(), calls=%async_computation.1 | async-start | bytes 5677056 | tf_op jit(solution)/shard_map/all_gather | solution.py:563
  10.5 175.6 %all-gather.6.cloned.1.call-start = ((), (), s32[]{:S(2)}) async-start(), calls=%async_computation.2 | async-start | bytes 14598144 | tf_op jit(solution)/shard_map/all_gather | solution.py:565
  15.3 557.9 %reduce-scatter.2.cloned.1.call-start = ((), (), s32[]{:S(2)}) async-start(), calls=%async_computation.3 | async-start | bytes 14598144 | tf_op jit(solution)/shard_map/reduce_scatter | solution.py:683
  15.4 100.6 %copy-start.89 = (f32[256]{0:T(256)}, f32[256]{0:T(256)S(1)}, u32[]{:S(2)}) copy-start(f32[256]{0:T(256)S(1)} %minimum_convert_fusion.11) | copy-start | bytes 3076
  15.4 106.1 %copy-start.95 = (pred[512]{0:T(512)(128)(4,1)}, pred[512]{0:T(512)(128)(4,1)S(1)}, u32[]{:S(2)}) copy-start(pred[512]{0:T(512)(128)(4,1)S(1)} %get-tuple-element.183) | copy-start | bytes 1540
  15.4 106.8 %copy-start.93 = (pred[512]{0:T(512)(128)(4,1)}, pred[512]{0:T(512)(128)(4,1)S(1)}, u32[]{:S(2)}) copy-start(pred[512]{0:T(512)(128)(4,1)S(1)} %get-tuple-element.182) | copy-start | bytes 1540
  15.4 106.0 %copy-start.118 = (pred[512]{0:T(512)(128)(4,1)}, pred[512]{0:T(512)(128)(4,1)S(1)}, u32[]{:S(2)}) copy-start(pred[512]{0:T(512)(128)(4,1)S(1)} %get-tuple-element.187) | copy-start | bytes 1540
  15.4 108.4 %copy-start.116 = (pred[512]{0:T(512)(128)(4,1)}, pred[512]{0:T(512)(128)(4,1)S(1)}, u32[]{:S(2)}) copy-start(pred[512]{0:T(512)(128)(4,1)S(1)} %get-tuple-element.186) | copy-start | bytes 1540
  15.5 106.0 %copy-start.101 = (pred[512]{0:T(512)(128)(4,1)}, pred[512]{0:T(512)(128)(4,1)S(1)}, u32[]{:S(2)}) copy-start(pred[512]{0:T(512)(128)(4,1)S(1)} %get-tuple-element.213) | copy-start | bytes 1540
  15.5 106.0 %copy-start.119 = (pred[512]{0:T(512)(128)(4,1)}, pred[512]{0:T(512)(128)(4,1)S(1)}, u32[]{:S(2)}) copy-start(pred[512]{0:T(512)(128)(4,1)S(1)} %get-tuple-element.212) | copy-start | bytes 1540
  16.1 105.4 %copy-start.103 = (pred[512]{0:T(512)(128)(4,1)}, pred[512]{0:T(512)(128)(4,1)S(1)}, u32[]{:S(2)}) copy-start(pred[512]{0:T(512)(128)(4,1)S(1)} %get-tuple-element.214) | copy-start | bytes 1540
  16.7 104.8 %copy-start.97 = (pred[512]{0:T(512)(128)(4,1)}, pred[512]{0:T(512)(128)(4,1)S(1)}, u32[]{:S(2)}) copy-start(pred[512]{0:T(512)(128)(4,1)S(1)} %get-tuple-element.216) | copy-start | bytes 1540
  17.8 104.4 %copy-start.109 = (pred[512]{0:T(512)(128)(4,1)}, pred[512]{0:T(512)(128)(4,1)S(1)}, u32[]{:S(2)}) copy-start(pred[512]{0:T(512)(128)(4,1)S(1)} %get-tuple-element.207) | copy-start | bytes 1540
  18.4 103.8 %copy-start.111 = (pred[512]{0:T(512)(128)(4,1)}, pred[512]{0:T(512)(128)(4,1)S(1)}, u32[]{:S(2)}) copy-start(pred[512]{0:T(512)(128)(4,1)S(1)} %get-tuple-element.208) | copy-start | bytes 1540
  19.0 103.3 %copy-start.99 = (pred[512]{0:T(512)(128)(4,1)}, pred[512]{0:T(512)(128)(4,1)S(1)}, u32[]{:S(2)}) copy-start(pred[512]{0:T(512)(128)(4,1)S(1)} %get-tuple-element.210) | copy-start | bytes 1540
  19.0 101.0 %copy-start.71 = (pred[512]{0:T(512)(128)(4,1)}, pred[512]{0:T(512)(128)(4,1)S(1)}, u32[]{:S(2)}) copy-start(pred[512]{0:T(512)(128)(4,1)S(1)} %get-tuple-element.218) | copy-start | bytes 1540
  19.0 101.7 %copy-start.69 = (pred[512]{0:T(512)(128)(4,1)}, pred[512]{0:T(512)(128)(4,1)S(1)}, u32[]{:S(2)}) copy-start(pred[512]{0:T(512)(128)(4,1)S(1)} %get-tuple-element.219) | copy-start | bytes 1540
  19.0 101.0 %copy-start.105 = (pred[512]{0:T(512)(128)(4,1)}, pred[512]{0:T(512)(128)(4,1)S(1)}, u32[]{:S(2)}) copy-start(pred[512]{0:T(512)(128)(4,1)S(1)} %get-tuple-element.181) | copy-start | bytes 1540
  19.0 101.6 %copy-start.122 = (pred[512]{0:T(512)(128)(4,1)}, pred[512]{0:T(512)(128)(4,1)S(1)}, u32[]{:S(2)}) copy-start(pred[512]{0:T(512)(128)(4,1)S(1)} %get-tuple-element.180) | copy-start | bytes 1540
  19.1 100.9 %copy-start.123 = (pred[512]{0:T(512)(128)(4,1)}, pred[512]{0:T(512)(128)(4,1)S(1)}, u32[]{:S(2)}) copy-start(pred[512]{0:T(512)(128)(4,1)S(1)} %get-tuple-element.203) | copy-start | bytes 1540
  19.1 101.6 %copy-start.120 = (pred[512]{0:T(512)(128)(4,1)}, pred[512]{0:T(512)(128)(4,1)S(1)}, u32[]{:S(2)}) copy-start(pred[512]{0:T(512)(128)(4,1)S(1)} %get-tuple-element.202) | copy-start | bytes 1540
  19.6 100.4 %copy-start.107 = (pred[512]{0:T(512)(128)(4,1)}, pred[512]{0:T(512)(128)(4,1)S(1)}, u32[]{:S(2)}) copy-start(pred[512]{0:T(512)(128)(4,1)S(1)} %get-tuple-element.204) | copy-start | bytes 1540
  20.2 100.5 %copy-start.121 = (pred[512]{0:T(512)(128)(4,1)}, pred[512]{0:T(512)(128)(4,1)S(1)}, u32[]{:S(2)}) copy-start(pred[512]{0:T(512)(128)(4,1)S(1)} %get-tuple-element.201) | copy-start | bytes 1540
  20.2 102.8 %copy-start.115 = (pred[512]{0:T(512)(128)(4,1)}, pred[512]{0:T(512)(128)(4,1)S(1)}, u32[]{:S(2)}) copy-start(pred[512]{0:T(512)(128)(4,1)S(1)} %get-tuple-element.179) | copy-start | bytes 1540
  20.3 103.6 %copy-start.113 = (pred[512]{0:T(512)(128)(4,1)}, pred[512]{0:T(512)(128)(4,1)S(1)}, u32[]{:S(2)}) copy-start(pred[512]{0:T(512)(128)(4,1)S(1)} %get-tuple-element.178) | copy-start | bytes 1540
  23.7 100.1 %copy-start.33 = (f32[512]{0:T(512)}, f32[512]{0:T(512)S(1)}, u32[]{:S(2)}) copy-start(f32[512]{0:T(512)S(1)} %get-tuple-element.173) | copy-start | bytes 6148
  23.7 100.1 %copy-start.37 = (f32[512]{0:T(512)}, f32[512]{0:T(512)S(1)}, u32[]{:S(2)}) copy-start(f32[512]{0:T(512)S(1)} %get-tuple-element.172) | copy-start | bytes 6148
  23.8 100.1 %copy-start.35 = (f32[512]{0:T(512)}, f32[512]{0:T(512)S(1)}, u32[]{:S(2)}) copy-start(f32[512]{0:T(512)S(1)} %get-tuple-element.174) | copy-start | bytes 6148
  23.8 100.1 %copy-start.41 = (f32[512]{0:T(512)}, f32[512]{0:T(512)S(1)}, u32[]{:S(2)}) copy-start(f32[512]{0:T(512)S(1)} %get-tuple-element.175) | copy-start | bytes 6148
  23.8 100.0 %copy-start.29 = (f32[512]{0:T(512)}, f32[512]{0:T(512)S(1)}, u32[]{:S(2)}) copy-start(f32[512]{0:T(512)S(1)} %get-tuple-element.176) | copy-start | bytes 6148
  119.9 213.0 %copy-start.56 = (f32[768]{0:T(1024)}, f32[768]{0:T(1024)S(1)}, u32[]{:S(2)}) copy-start(f32[768]{0:T(1024)S(1)} %mul.1203) | copy-start | bytes 9220
  136.9 196.0 %copy-start.58 = (f32[2,512]{1,0:T(2,128)}, f32[2,512]{1,0:T(2,128)S(1)}, u32[]{:S(2)}) copy-start(f32[2,512]{1,0:T(2,128)S(1)} %fusion.175) | copy-start | bytes 12292
  (119 other events, 2271.0 us)
Sparse Core Ops, SparseCore 0:
  11.5 68.8 all-gather.3
  83.9 102.1 all-gather.5
  362.7 167.2 reduce-scatter.1

commit v9 on v7

--- a/solution.py
+++ b/solution.py
@@ -486,6 +486,101 @@
         compiler_params=pltpu.CompilerParams(collective_id=1, has_side_effects=True),
         cost_estimate=pl.CostEstimate(flops=count * x.size, transcendentals=0,
                                       bytes_accessed=count * x.size * 4),
+    )(x)
+
+
+def ring_ag_kernel(snake, x_ref, out_ref, send_sem, recv_sem, pair_sem):
+    count = out_ref.shape[0] // 2
+    steps = count - 1
+    lanes = out_ref.shape[2] // 2
+    position_of = snake_position if snake else plain_position
+    chip_of = snake_chip if snake else plain_position
+    chip = lax.axis_index("fsdp")
+    core = lax.axis_index("dp")
+    here = position_of(chip)
+    ahead = (chip_of((here + 1) % count), core)
+    behind = (chip_of((here + count - 1) % count), core)
+    partner = (chip, 1 - core)
+    targets = (ahead, behind)
+
+    barrier = pltpu.get_barrier_semaphore()
+    for peer in (ahead, behind, partner):
+        pl.semaphore_signal(barrier, 1, device_id=peer, device_id_type=MESH_ID)
+    pl.semaphore_wait(barrier, 3)
+
+    out_ref[2 * chip + core] = x_ref[...]
+
+    def slot(way, step):
+        spot = (here - step + count) % count if way == 0 else (here + step) % count
+        return 2 * chip_of(spot) + core
+
+    def link(way, step, index):
+        cols = pl.ds(way * lanes, lanes)
+        return pltpu.make_async_remote_copy(
+            src_ref=out_ref.at[index, :, cols], dst_ref=out_ref.at[index, :, cols],
+            send_sem=send_sem.at[way, step], recv_sem=recv_sem.at[way, step],
+            device_id=targets[way], device_id_type=MESH_ID)
+
+    for way in (0, 1):
+        link(way, 0, slot(way, 0)).start()
+
+    def step_body(step, carry):
+        for way in (0, 1):
+            index = slot(way, step)
+            link(way, step - 1, index).wait_recv()
+            link(way, step, index).start()
+        return carry
+
+    lax.fori_loop(1, steps, step_body, 0)
+
+    for way in (0, 1):
+        link(way, steps - 1, slot(way, steps)).wait_recv()
+
+    def drain(step, carry):
+        for way in (0, 1):
+            link(way, step, slot(way, step)).wait_send()
+        return carry
+
+    lax.fori_loop(0, steps, drain, 0)
+
+    def pair(other):
+        index = 2 * other + core
+        return pltpu.make_async_remote_copy(
+            src_ref=out_ref.at[index], dst_ref=out_ref.at[index],
+            send_sem=pair_sem.at[0, other], recv_sem=pair_sem.at[1, other],
+            device_id=partner, device_id_type=MESH_ID)
+
+    def pair_start(other, carry):
+        pair(other).start()
+        return carry
+
+    lax.fori_loop(0, count, pair_start, 0)
+
+    def pair_wait(other, carry):
+        pair(other).wait_send()
+        pair(other).wait_recv()
+        return carry
+
+    lax.fori_loop(0, count, pair_wait, 0)
+
+
+def ring_all_gather(x, snake):
+    rows, width = x.shape
+    count = lax.axis_size("fsdp")
+    return pl.pallas_call(
+        functools.partial(ring_ag_kernel, snake),
+        out_shape=jax.ShapeDtypeStruct((2 * count, rows, width), x.dtype),
+        in_specs=[pl.BlockSpec(memory_space=pltpu.VMEM)],
+        out_specs=pl.BlockSpec(memory_space=pltpu.VMEM),
+        scratch_shapes=[
+            pltpu.SemaphoreType.DMA((2, count - 1)),
+            pltpu.SemaphoreType.DMA((2, count - 1)),
+            pltpu.SemaphoreType.DMA((2, count)),
+        ],
+        compiler_params=pltpu.CompilerParams(collective_id=2, has_side_effects=True,
+                                             vmem_limit_bytes=48 * 1024 * 1024),
+        cost_estimate=pl.CostEstimate(flops=0, transcendentals=0,
+                                      bytes_accessed=4 * count * x.size * x.dtype.itemsize),
     )(x)
 
 
@@ -539,10 +634,12 @@
     first_group = jnp.concatenate(
         [own_half(table).astype(jnp.bfloat16), own_half(kernel).astype(jnp.bfloat16), vec_block], axis=0)
     contract_piece = own_half(contract).reshape(project.shape[0] // 2, -1)
-    second_group = jnp.concatenate(
-        [own_half(project), own_half(combine), own_half(expand), contract_piece], axis=1
-    ).astype(jnp.bfloat16)
+    front_piece = jnp.concatenate([own_half(project), own_half(combine)], axis=1).astype(jnp.bfloat16)
+    second_group = jnp.concatenate([own_half(expand), contract_piece], axis=1).astype(jnp.bfloat16)
     first_all = lax.all_gather(first_group, groups, axis=0, tiled=True)
+    front_all = ring_all_gather(front_piece, snake)
+    first_all, front_all = lax.optimization_barrier((first_all, front_all))
+    front_all = front_all.reshape(-1, front_piece.shape[1])
     first_all = first_all.reshape(count_all, first_group.shape[0], D)
     second_all = lax.all_gather(second_group, groups, axis=0, tiled=True)
     at_kernel = rows_table
@@ -550,12 +647,10 @@
     complete_table = first_all[:, :at_kernel].reshape(V, D)
     complete_kernel = first_all[:, at_kernel:at_vec].reshape(KS * D, D)
     full_vectors = first_all[:, at_vec:at_vec + 4, :vec_width].transpose(1, 0, 2).reshape(4, D)
-    at_expand = 4 * D
-    at_contract = at_expand + expand.shape[1]
-    full_project = second_all[:, : 3 * D]
-    full_combine = second_all[:, 3 * D : at_expand]
-    full_expand = second_all[:, at_expand:at_contract]
-    full_contract = second_all[:, at_contract:].reshape(-1, D)
+    full_project = front_all[:, : 3 * D]
+    full_combine = front_all[:, 3 * D :]
+    full_expand = second_all[:, : expand.shape[1]]
+    full_contract = second_all[:, expand.shape[1] :].reshape(-1, D)
     vector_vals = full_vectors.astype(jnp.float32)
     count_items, count_bytes = byte_ids.shape
     count_tok = count_bytes // 2

time: 652 us -> 630 us (0.966)
  waiting for transfers between devices: 102 us -> 0.07 us
  Pallas kernels: 145 us -> 224 us
    pallas_call x0 -> x1, Pallas kernels: none -> 77.5 us  [ring_all_gather(): pl.pallas_call(functools.partial(ring_ag_kernel, snake), out_shape=jax.Sh...]
    all_gather x1, waiting for transfers between devices: 52.9 us -> 0.01 us  [body(): first_all = lax.all_gather(first_group, groups, axis=0, tiled=True)]
    all_gather x1, waiting for transfers between devices: 49.4 us -> 0.02 us  [body(): second_all = lax.all_gather(second_group, groups, axis=0, tiled=True)]
    unnamed x326 -> x344, local copies, waits for them, and re-layouts: 9.86 us -> 13.4 us
  transfers between devices with their start and end apart: 3 -> 3, of which waited for: 2 -> 0; matrix products, arithmetic and copies ran while one was open for 30% -> 32% of each run, Pallas kernels for 12% -> 28%
where the time goes in v9:
time: 630 us; the launch traced here: 620 us
  Pallas kernels  224 us (36%)
  matrix products  198 us (31%)
  other arithmetic  92.3 us (15%)
  local copies, waits for them, and re-layouts  70.5 us (11%)
  between operations  31 us (5%)
    pallas_call x1, Pallas kernels, ring_all_gather(): pl.pallas_call(functools.partial(ring_ag_kernel, snake), out_shape=jax.Sh...  77.5 us
    pallas_call x1, Pallas kernels, ring_reduce_scatter(): pl.pallas_call(functools.partial(ring_rs_kernel, snake), out_shape=jax.Sh...  76.8 us
    pallas_call x1, Pallas kernels, attention_backward(): pl.pallas_call(attn_bwd_kernel, out_shape=(part, part, part), grid_spec=p...  34.2 us
    dot_general x3, matrix products, body(): tokens, gbst_pull = jax.vjp(gbst_tokens, hidden, vector_vals[3])  25.3 us
    pallas_call x1, Pallas kernels, attention_forward(): pl.pallas_call(attn_fwd_kernel, out_shape=jax.ShapeDtypeStruct((count_ite...  22 us
    dot_general x1, matrix products, body(): jnp.einsum('xwu,xwo->uo', byte_windows, gradient_hidden_reduced, preferre...  18 us
    dot_general x1, matrix products, body(): jnp.einsum('std,fd->stf', cotangent, back_contract, preferred_element_typ...  17.5 us
    dot_general x1, matrix products, body(): jnp.einsum('xpg,xpz->gz', one_hot_bytes, gradient_embedded_bytes, preferr...  16.5 us
  transfers between devices with their start and end apart: 3, of which 0 were waited for; matrix products, arithmetic and copies ran while one was open for 32% of the time, Pallas kernels for 28%

profile of v9, /device:TPU:0, one launch (start us, length us, event | category | flops | bytes accessed | tf_op | source)
XLA Modules:
  0.0 620.3 jit_solution(6817414907037992304)
XLA Ops:
  15.3 77.5 %shard_map.583 = bf16[32,24,3072]{2,1,0:T(8,128)(2,1)S(1)} custom-call(bf16[24,3072]{1,0:T(8,128)(2,1)S(1)} %pad_maximum_fusion.7.x_ref), custom_call_target="tpu_custom_call" | custom-call | bytes 9437184 | tf_op jit(solution)/shard_map/pallas_call | solution.py:570
  106.1 4.8 slice.373
  115.1 4.6 pad_slice_fusion.5
  119.7 14.1 %fusion.30 = f32[2,1024,768]{2,1,0:T(8,128)S(1)} fusion(bf16[3072,768,1]{1,0,2:T(8,128)(2,1)} %bitcast.554, bf16[2,1024,768]{2,1,0:T(8,128)(2,1)} %copy-done.13, bf16[2,1024,768]{2,1,0:T(8,128)(2,1)} %get-tuple-element.91, bf16[2,1024,768]{2,1,0:T(8,128)(2,1)} %get-tuple-element.90, bf16[2,1024,768]{2,1,0:T(8,128)(2,1)} %get-tuple-element.89), kind=kOutput, calls=%fused_computation.75 | convolution fusion | flops 9714008064 | bytes 23592960 | tf_op jit(solution)/shard_map/hby,yj->hbj/dot_general | solution.py:674
  150.2 11.4 %multiply_reduce_fusion.5 = (f32[2,512]{1,0:T(2,128)S(1)}, f32[2,512,768]{2,1,0:T(8,128)S(1)}) fusion(f32[2,1024,768]{2,1,0:T(8,128)} %copy-done.1, f32[768]{0:T(1024)S(1)} %add.1776, f32[2,512]{1,0:T(2,128)S(1)} %add_multiply_fusion, f32[2,512]{1,0:T(2,128)S(1)} %add_multiply_fusion.1, f32[2,512]{1,0:T(2,128)S(1)} %add_multiply_fusion.2, ...), kind=kOutput, calls=%fused_computation.61 | convolution fusion | flops 4841274368 | bytes 12614656 | tf_op jit(solution)/shard_map/jvp(ntj,njd->ntd)/dot_general | solution.py:103
  163.4 5.5 convolution_convert_fusion.q_ref.k_ref.v_ref
  168.9 22.0 %shard_map.584 = bf16[2,512,768]{2,1,0:T(8,128)(2,1)} custom-call(s32[2]{0:T(128)} %len_ref.3, bf16[2,512,2304]{2,1,0:T(8,128)(2,1)} %convolution_convert_fusion.q_ref.k_ref.v_ref, bf16[2,512,2304]{2,1,0:T(8,128)(2,1)} %convolution_convert_fusion.q_ref.k_ref.v_ref, bf16[2,512,2304]{2,1,0:T(8,128)(2,1)} %convolution_convert_fusion.q_ref.k_ref.v_ref), custom_call_target="tpu_custom_call" | custom-call | flops 3221225472 | bytes 6291456 | tf_op jit(solution)/shard_map/pallas_call | solution.py:254
  190.9 4.8 multiply_reduce_fusion.4
  197.6 4.4 reshape.4459
  202.0 13.2 %fusion.18 = f32[2,512,4096]{2,1,0:T(8,128)} fusion(bf16[768,6144]{1,0:T(8,128)(2,1)} %all-gather.6.cloned.1.call-done, f32[2,512,768]{2,1,0:T(8,128)} %get-tuple-element.147, f32[768]{0:T(1024)S(1)} %mul.1582, f32[2,512]{1,0:T(2,128)S(1)} %fusion.179), kind=kOutput, calls=%fused_computation.38 | convolution fusion | flops 6444810240 | bytes 26221568 | tf_op jit(solution)/shard_map/std,de->ste/dot_general | solution.py:691
  215.2 17.5 %bitcast_multiply_fusion.1 = (f32[2,512,2048]{2,1,0:T(8,128)}, f32[2,512,2048]{2,1,0:T(8,128)}, bf16[2,512,2048]{2,1,0:T(8,128)(2,1)}) fusion(f32[2,512,4096]{2,1,0:T(8,128)} %fusion.18, bf16[2048,768,1]{1,0,2:T(8,128)(2,1)S(1)} %copy-done.11, bf16[2,512,768]{2,1,0:T(8,128)(2,1)S(1)} %copy-done.24), kind=kOutput, calls=%fused_computation.18 | convolution fusion | flops 3271557120 | bytes 42467328 | tf_op jit(solution)/shard_map/std,fd->stf/dot_general | solution.py:704
  232.8 15.3 %bitcast_convert_fusion = bf16[768,4096]{1,0:T(8,128)(2,1)} fusion(f32[2,512,2048]{2,1,0:T(8,128)} %get-tuple-element.83, f32[2,512,2048]{2,1,0:T(8,128)} %get-tuple-element.82, f32[2,512,768]{2,1,0:T(8,128)S(1)} %copy-done.2, f32[768]{0:T(1024)S(1)} %mul.1582, f32[2,512]{1,0:T(2,128)S(1)} %fusion.179), kind=kOutput, calls=%fused_computation.7 | convolution fusion | flops 6456344576 | bytes 26221568 | tf_op jit(solution)/shard_map/std,ste->de/dot_general | solution.py:709
  248.1 14.5 %multiply_reduce_fusion = (bf16[768]{0:T(1024)(128)(2,1)}, f32[2,512]{1,0:T(2,128)S(1)}, f32[2,512,768]{2,1,0:T(8,128)}) fusion(f32[2,512,768]{2,1,0:T(8,128)S(1)} %copy-done.2, f32[2,512]{1,0:T(2,128)S(1)} %fusion.179, f32[768]{0:T(1024)S(1)} %mul.1582, bf16[768,6144]{1,0:T(8,128)(2,1)} %all-gather.6.cloned.1.call-done, ...), kind=kOutput, calls=%fused_computation.54 | convolution fusion | flops 6455556096 | bytes 29372928 | tf_op jit(solution)/shard_map/ste,de->std/dot_general | solution.py:712
  262.5 3.2 fusion.20
  265.7 4.9 convolution_convert_fusion.1.do_ref
  272.2 34.2 %shard_map.585 = (bf16[2,512,768]{2,1,0:T(8,128)(2,1)}, bf16[2,512,768]{2,1,0:T(8,128)(2,1)}, bf16[2,512,768]{2,1,0:T(8,128)(2,1)}) custom-call(s32[2]{0:T(128)} %len_ref.3, bf16[2,512,2304]{2,1,0:T(8,128)(2,1)} %convolution_convert_fusion.q_ref.k_ref.v_ref, bf16[2,512,2304]{2,1,0:T(8,128)(2,1)} %convolution_convert_fusion.q_ref.k_ref.v_ref, ...), custom_call_target="tpu_custom_call" | custom-call | flops 8053063680 | bytes 11010048 | tf_op jit(solution)/shard_map/pallas_call | solution.py:276
  311.0 5.6 bitcast_convert_fusion.2
  318.4 7.4 %bitcast_convert_fusion.3 = bf16[2048,768]{1,0:T(8,128)(2,1)} fusion(bf16[2,512,2048]{2,1,0:T(8,128)(2,1)} %get-tuple-element.84, bf16[2,512,768]{2,1,0:T(8,128)(2,1)S(1)} %copy-done.25), kind=kOutput, calls=%fused_computation.23 | convolution fusion | flops 3222798336 | bytes 8912896 | tf_op jit(solution)/shard_map/stf,std->fd/dot_general | solution.py:701
  325.8 5.5 reshape.4443
  331.3 12.3 %pad_maximum_fusion = bf16[768,9216]{1,0:T(8,128)(2,1)} fusion(bf16[768,2048]{1,0:T(8,128)(2,1)S(1)} %reshape.4443, bf16[768,4096]{1,0:T(8,128)(2,1)} %bitcast_convert_fusion, bf16[768,768]{1,0:T(8,128)(2,1)} %copy.119, bf16[768,2304]{1,0:T(8,128)(2,1)} %bitcast_convert_fusion.2), kind=kLoop, calls=%fused_computation.1 | loop fusion | flops 56623104 | bytes 28311552 | tf_op jit(solution)/shard_map/concatenate | solution.py:757
  361.7 9.4 %multiply_reduce_fusion.1 = (bf16[768]{0:T(1024)(128)(2,1)S(1)}, f32[2,512]{1,0:T(2,128)S(1)}, f32[2,512,768]{2,1,0:T(8,128)S(1)}) fusion(f32[2,512,768]{2,1,0:T(8,128)} %copy-done.4, f32[2,512]{1,0:T(2,128)} %copy-done.78, f32[768]{0:T(1024)} %copy-done.76, bf16[2,512,2304]{2,1,0:T(8,128)(2,1)} %copy-done.29, bf16[768,3072]{1,0:T(8,128)(2,1)} %bitcast.547), kind=kOutput, calls=%fused_computation.55 | convolution fusion | flops 3628595456 | bytes 14562816 | tf_op jit(solution)/shard_map/ste,de->std/dot_general | solution.py:728
  373.4 8.6 %select_reduce_fusion.2 = (f32[2,512]{1,0:T(2,128)S(1)}, f32[2,512]{1,0:T(2,128)S(1)}, f32[2,512]{1,0:T(2,128)S(1)}, f32[2,512]{1,0:T(2,128)S(1)}, f32[2,512]{1,0:T(2,128)S(1)}, /*index=5*/f32[2,512]{1,0:T(2,128)S(1)}) fusion(pred[512,1024]{1,0:T(8,128)(4,1)S(1)} %copy-done.33, pred[512,1024]{1,0:T(8,128)(4,1)S(1)} %copy-done.31, ...), kind=kOutput, calls=%fused_computation.43 | convolution fusion | flops 4845987840 | bytes 12610560 | tf_op jit(solution)/shard_map/transpose(jvp(ntd,njd->ntj))/dot_general | solution.py:677
  390.8 11.3 %add_convert_fusion.1 = bf16[2,1024,768]{2,1,0:T(8,128)(2,1)S(1)} fusion(f32[768]{0:T(1024)S(1)} %mul.1627, f32[2,1024]{1,0:T(2,128)S(1)} %fusion.105, f32[2,512,768]{2,1,0:T(8,128)} %copy-done.14, f32[2,512]{1,0:T(2,128)S(1)} %copy-done.101, f32[2,512]{1,0:T(2,128)S(1)} %copy-done.99, f32[2,512]{1,0:T(2,128)S(1)} %copy-done.105, ...), kind=kOutput, calls=%fused_computation.25 | convolution fusion | flops 4842848256 | bytes 9473024 | tf_op jit(solution)/shard_map/transpose(jvp(ntj,ntd->njd))/dot_general | solution.py:677
  402.1 4.5 pad_slice_fusion.2
  406.7 5.4 fusion.78
  412.5 9.6 %pad_maximum_fusion.2 = bf16[2,1024,3072]{2,1,0:T(8,128)(2,1)} fusion(bf16[2,1024,768]{2,1,0:T(8,128)(2,1)S(1)} %add_convert_fusion.1, bf16[2,1024,768]{2,1,0:T(8,128)(2,1)} %get-tuple-element.87, bf16[2,1024,768]{2,1,0:T(8,128)(2,1)} %get-tuple-element.86, bf16[2,1024,768]{2,1,0:T(8,128)(2,1)} %get-tuple-element.85), kind=kLoop, calls=%fused_computation.6 | loop fusion | flops 50331648 | bytes 25165824 | tf_op jit(solution)/shard_map/concatenate | solution.py:740
  422.1 16.5 %fusion.73 = bf16[256,768]{1,0:T(8,128)(2,1)} fusion(bf16[4,768,768,1]{2,1,0,3:T(8,128)(2,1)} %bitcast.555, bf16[2,128,4,8,768]{4,3,2,1,0:T(8,128)(2,1)} %bitcast.553, bf16[2,1024]{1,0:T(2,128)(2,1)S(1)} %copy-done.109, s32[2,1024]{1,0:T(2,128)S(1)} %copy-done.162), kind=kOutput, calls=%fused_computation.115 | convolution fusion | flops 10472849408 | bytes 17707008 | tf_op jit(solution)/shard_map/xpg,xpz->gz/dot_general | solution.py:751
  438.6 18.0 %bitcast_convert_fusion.1 = bf16[3072,768]{1,0:T(8,128)(2,1)} fusion(bf16[2,1024,768]{2,1,0:T(8,128)(2,1)S(1)} %add_convert_fusion.1, bf16[2,1024,768]{2,1,0:T(8,128)(2,1)} %copy-done.13, bf16[2,1024,768]{2,1,0:T(8,128)(2,1)} %get-tuple-element.91, bf16[2,1024,768]{2,1,0:T(8,128)(2,1)} %get-tuple-element.90, bf16[2,1024,768]{2,1,0:T(8,128)(2,1)} %get-tuple-element.89), kind=kOutput, calls=%fused_computation.10 | convolution fusion | flops 9716367360 | bytes 20447232 | tf_op jit(solution)/shard_map/xwu,xwo->uo/dot_general | solution.py:736
  456.6 4.4 copy_bitcast_fusion.x_ref
  461.0 76.8 %shard_map.586 = f32[112,768]{1,0:T(8,128)S(1)} custom-call(bf16[2,16,112,768]{3,2,1,0:T(8,128)(2,1)S(1)} %copy_bitcast_fusion.x_ref), custom_call_target="tpu_custom_call" | custom-call | flops 5505024 | bytes 11010048 | tf_op jit(solution)/shard_map/pallas_call | solution.py:396
  538.0 7.3 %convolution_add_fusion.1 = f32[2,512,768]{2,1,0:T(8,128)} fusion(f32[2,512,768]{2,1,0:T(8,128)S(1)} %copy-done.3, bf16[2,512,2048]{2,1,0:T(8,128)(2,1)} %get-tuple-element.84, bf16[2048,768,1]{1,0,2:T(8,128)(2,1)S(1)} %copy-done.12), kind=kOutput, calls=%fused_computation.111 | convolution fusion | flops 3222011904 | bytes 13631488 | tf_op jit(solution)/shard_map/stf,fd->std/dot_general | solution.py:694
  549.8 13.1 %shard_map.587 = f32[80,128]{1,0:T(8,128)} custom-call(f32[80,128]{1,0:T(8,128)} %pad_bitcast_fusion.x_ref), custom_call_target="tpu_custom_call" | custom-call | flops 163840 | bytes 655360 | tf_op jit(solution)/shard_map/pallas_call | solution.py:472
  (570 shorter events, 122.0 us)
Async XLA Ops:
  7.2 95.8 %copy-start.110 = (s32[2]{0:T(128)S(1)}, s32[2]{0:T(128)}, u32[]{:S(2)}) copy-start(s32[2]{0:T(128)} %len_ref.3) | copy-start | bytes 28
  7.2 98.9 %all-gather.4.cloned.1.call-start = ((), (), s32[]{:S(2)}) async-start(), calls=%async_computation.1 | async-start | bytes 5677056 | tf_op jit(solution)/shard_map/all_gather | solution.py:639
  10.5 185.3 %all-gather.6.cloned.1.call-start = ((), (), s32[]{:S(2)}) async-start(), calls=%async_computation.2 | async-start | bytes 9732096 | tf_op jit(solution)/shard_map/all_gather | solution.py:644
  13.4 531.9 %reduce-scatter.2.cloned.1.call-start = ((), (), s32[]{:S(2)}) async-start(), calls=%async_computation.3 | async-start | bytes 14598144 | tf_op jit(solution)/shard_map/reduce_scatter | solution.py:760
  94.9 46.6 %copy-start.106 = (f32[256]{0:T(256)}, f32[256]{0:T(256)S(1)}, u32[]{:S(2)}) copy-start(f32[256]{0:T(256)S(1)} %minimum_convert_fusion.11) | copy-start | bytes 3076
  94.9 52.0 %copy-start.113 = (pred[512]{0:T(512)(128)(4,1)}, pred[512]{0:T(512)(128)(4,1)S(1)}, u32[]{:S(2)}) copy-start(pred[512]{0:T(512)(128)(4,1)S(1)} %get-tuple-element.161) | copy-start | bytes 1540
  95.0 52.8 %copy-start.111 = (pred[512]{0:T(512)(128)(4,1)}, pred[512]{0:T(512)(128)(4,1)S(1)}, u32[]{:S(2)}) copy-start(pred[512]{0:T(512)(128)(4,1)S(1)} %get-tuple-element.160) | copy-start | bytes 1540
  95.0 52.0 %copy-start.136 = (pred[512]{0:T(512)(128)(4,1)}, pred[512]{0:T(512)(128)(4,1)S(1)}, u32[]{:S(2)}) copy-start(pred[512]{0:T(512)(128)(4,1)S(1)} %get-tuple-element.165) | copy-start | bytes 1540
  95.0 54.2 %copy-start.134 = (pred[512]{0:T(512)(128)(4,1)}, pred[512]{0:T(512)(128)(4,1)S(1)}, u32[]{:S(2)}) copy-start(pred[512]{0:T(512)(128)(4,1)S(1)} %get-tuple-element.164) | copy-start | bytes 1540
  95.0 52.0 %copy-start.119 = (pred[512]{0:T(512)(128)(4,1)}, pred[512]{0:T(512)(128)(4,1)S(1)}, u32[]{:S(2)}) copy-start(pred[512]{0:T(512)(128)(4,1)S(1)} %get-tuple-element.191) | copy-start | bytes 1540
  95.0 52.0 %copy-start.137 = (pred[512]{0:T(512)(128)(4,1)}, pred[512]{0:T(512)(128)(4,1)S(1)}, u32[]{:S(2)}) copy-start(pred[512]{0:T(512)(128)(4,1)S(1)} %get-tuple-element.190) | copy-start | bytes 1540
  95.5 51.5 %copy-start.121 = (pred[512]{0:T(512)(128)(4,1)}, pred[512]{0:T(512)(128)(4,1)S(1)}, u32[]{:S(2)}) copy-start(pred[512]{0:T(512)(128)(4,1)S(1)} %get-tuple-element.192) | copy-start | bytes 1540
  96.1 50.9 %copy-start.115 = (pred[512]{0:T(512)(128)(4,1)}, pred[512]{0:T(512)(128)(4,1)S(1)}, u32[]{:S(2)}) copy-start(pred[512]{0:T(512)(128)(4,1)S(1)} %get-tuple-element.194) | copy-start | bytes 1540
  97.2 50.6 %copy-start.127 = (pred[512]{0:T(512)(128)(4,1)}, pred[512]{0:T(512)(128)(4,1)S(1)}, u32[]{:S(2)}) copy-start(pred[512]{0:T(512)(128)(4,1)S(1)} %get-tuple-element.185) | copy-start | bytes 1540
  97.7 50.0 %copy-start.129 = (pred[512]{0:T(512)(128)(4,1)}, pred[512]{0:T(512)(128)(4,1)S(1)}, u32[]{:S(2)}) copy-start(pred[512]{0:T(512)(128)(4,1)S(1)} %get-tuple-element.186) | copy-start | bytes 1540
  98.3 49.5 %copy-start.117 = (pred[512]{0:T(512)(128)(4,1)}, pred[512]{0:T(512)(128)(4,1)S(1)}, u32[]{:S(2)}) copy-start(pred[512]{0:T(512)(128)(4,1)S(1)} %get-tuple-element.188) | copy-start | bytes 1540
  98.3 47.3 %copy-start.91 = (pred[512]{0:T(512)(128)(4,1)}, pred[512]{0:T(512)(128)(4,1)S(1)}, u32[]{:S(2)}) copy-start(pred[512]{0:T(512)(128)(4,1)S(1)} %get-tuple-element.196) | copy-start | bytes 1540
  98.3 48.0 %copy-start.89 = (pred[512]{0:T(512)(128)(4,1)}, pred[512]{0:T(512)(128)(4,1)S(1)}, u32[]{:S(2)}) copy-start(pred[512]{0:T(512)(128)(4,1)S(1)} %get-tuple-element.197) | copy-start | bytes 1540
  98.3 47.3 %copy-start.123 = (pred[512]{0:T(512)(128)(4,1)}, pred[512]{0:T(512)(128)(4,1)S(1)}, u32[]{:S(2)}) copy-start(pred[512]{0:T(512)(128)(4,1)S(1)} %get-tuple-element.159) | copy-start | bytes 1540
  98.3 48.0 %copy-start.140 = (pred[512]{0:T(512)(128)(4,1)}, pred[512]{0:T(512)(128)(4,1)S(1)}, u32[]{:S(2)}) copy-start(pred[512]{0:T(512)(128)(4,1)S(1)} %get-tuple-element.158) | copy-start | bytes 1540
  98.4 47.2 %copy-start.141 = (pred[512]{0:T(512)(128)(4,1)}, pred[512]{0:T(512)(128)(4,1)S(1)}, u32[]{:S(2)}) copy-start(pred[512]{0:T(512)(128)(4,1)S(1)} %get-tuple-element.181) | copy-start | bytes 1540
  98.4 47.9 %copy-start.138 = (pred[512]{0:T(512)(128)(4,1)}, pred[512]{0:T(512)(128)(4,1)S(1)}, u32[]{:S(2)}) copy-start(pred[512]{0:T(512)(128)(4,1)S(1)} %get-tuple-element.180) | copy-start | bytes 1540
  98.9 46.7 %copy-start.125 = (pred[512]{0:T(512)(128)(4,1)}, pred[512]{0:T(512)(128)(4,1)S(1)}, u32[]{:S(2)}) copy-start(pred[512]{0:T(512)(128)(4,1)S(1)} %get-tuple-element.182) | copy-start | bytes 1540
  99.5 46.8 %copy-start.139 = (pred[512]{0:T(512)(128)(4,1)}, pred[512]{0:T(512)(128)(4,1)S(1)}, u32[]{:S(2)}) copy-start(pred[512]{0:T(512)(128)(4,1)S(1)} %get-tuple-element.179) | copy-start | bytes 1540
  99.5 49.0 %copy-start.133 = (pred[512]{0:T(512)(128)(4,1)}, pred[512]{0:T(512)(128)(4,1)S(1)}, u32[]{:S(2)}) copy-start(pred[512]{0:T(512)(128)(4,1)S(1)} %get-tuple-element.157) | copy-start | bytes 1540
  99.5 49.8 %copy-start.131 = (pred[512]{0:T(512)(128)(4,1)}, pred[512]{0:T(512)(128)(4,1)S(1)}, u32[]{:S(2)}) copy-start(pred[512]{0:T(512)(128)(4,1)S(1)} %get-tuple-element.156) | copy-start | bytes 1540
  102.9 46.4 %copy-start.51 = (f32[512]{0:T(512)}, f32[512]{0:T(512)S(1)}, u32[]{:S(2)}) copy-start(f32[512]{0:T(512)S(1)} %get-tuple-element.151) | copy-start | bytes 6148
  102.9 46.4 %copy-start.55 = (f32[512]{0:T(512)}, f32[512]{0:T(512)S(1)}, u32[]{:S(2)}) copy-start(f32[512]{0:T(512)S(1)} %get-tuple-element.150) | copy-start | bytes 6148
  145.5 163.4 %copy-start.76 = (f32[768]{0:T(1024)}, f32[768]{0:T(1024)S(1)}, u32[]{:S(2)}) copy-start(f32[768]{0:T(1024)S(1)} %mul.1576) | copy-start | bytes 9220
  161.7 147.1 %copy-start.78 = (f32[2,512]{1,0:T(2,128)}, f32[2,512]{1,0:T(2,128)S(1)}, u32[]{:S(2)}) copy-start(f32[2,512]{1,0:T(2,128)S(1)} %fusion.178) | copy-start | bytes 12292
  456.6 81.3 %copy-start.12 = (bf16[2048,768,1]{1,0,2:T(8,128)(2,1)S(1)}, bf16[2048,768,1]{1,0,2:T(8,128)(2,1)}, u32[]{:S(2)}) copy-start(bf16[2048,768,1]{1,0,2:T(8,128)(2,1)} %reshape.4459) | copy-start | bytes 9437188
  461.0 76.9 %copy-start.3 = (f32[2,512,768]{2,1,0:T(8,128)S(1)}, f32[2,512,768]{2,1,0:T(8,128)}, u32[]{:S(2)}) copy-start(f32[2,512,768]{2,1,0:T(8,128)} %get-tuple-element.147) | copy-start | bytes 9437188
  (140 other events, 1765.7 us)
Sparse Core Ops, SparseCore 0:
  11.5 74.8 all-gather.3
  89.9 81.9 all-gather.5
  343.7 168.1 reduce-scatter.1

commit v10 on v9

--- a/solution.py
+++ b/solution.py
@@ -127,7 +127,7 @@
     grad_mix = jnp.stack(grad_mix, axis=1)
     grad_scores = mixing * (grad_mix - jnp.sum(mixing * grad_mix, axis=1, keepdims=True))
     spread = sum(pool_vec(grad_scores[:, index_b], b) for index_b, b in enumerate((1, 2, 3, 4)))
-    grad_hidden = jnp.einsum("ntj,ntd->njd", band, grad_tokens, precision=HIGH_3)
+    grad_hidden = jnp.einsum("ntj,ntd->njd", band, grad_tokens, preferred_element_type=jnp.float32)
     grad_hidden = grad_hidden + spread[:, :, None] * scorer
     grad_scorer = jnp.einsum("nj,njd->d", spread, hidden, precision=HIGHEST)
     return grad_hidden, grad_scorer
@@ -310,9 +310,11 @@
     return chip
 
 
-def ring_rs_kernel(snake, x_ref, out_ref, part_ref, send_ref, recv_ref, swap_sem, send_sem, recv_sem, credit):
+WAYS = ((0, 0, 256), (1, 384, 256), (0, 256, 128), (1, 640, 128))
+
+
+def ring_rs_kernel(snake, x_ref, out_ref, part_ref, send_ref, recv_ref, swap_sem, send_sem, recv_sem):
     count, steps = x_ref.shape[1], x_ref.shape[1] - 1
-    lanes = out_ref.shape[1] // 2
     position_of = snake_position if snake else plain_position
     chip_of = snake_chip if snake else plain_position
     chip = lax.axis_index("fsdp")
@@ -322,7 +324,6 @@
     behind = (chip_of((here + count - 1) % count), core)
     partner = (chip, 1 - core)
     targets = (ahead, behind)
-    sources = (behind, ahead)
 
     barrier = pltpu.get_barrier_semaphore()
     for peer in (ahead, behind, partner):
@@ -338,56 +339,51 @@
     swap.wait_recv()
 
     def link(way, slot):
+        direction, first, width = WAYS[way]
+        cols = pl.ds(first, width)
         return pltpu.make_async_remote_copy(
-            src_ref=send_ref.at[way, slot], dst_ref=recv_ref.at[way, slot],
+            src_ref=send_ref.at[slot, :, cols], dst_ref=recv_ref.at[slot, :, cols],
             send_sem=send_sem.at[way, slot], recv_sem=recv_sem.at[way, slot],
-            device_id=targets[way], device_id_type=MESH_ID)
+            device_id=targets[direction], device_id_type=MESH_ID)
 
     def own(way, step):
+        direction, first, width = WAYS[way]
         shift = step + 1
-        spot = (here - shift + count * 2) % count if way == 0 else (here + shift) % count
+        spot = (here - shift + count * 2) % count if direction == 0 else (here + shift) % count
         owner = chip_of(spot)
-        cols = pl.ds(way * lanes, lanes)
+        cols = pl.ds(first, width)
         return (x_ref[core, owner, :, cols].astype(jnp.float32)
                 + part_ref[owner, :, cols].astype(jnp.float32))
 
-    for way in (0, 1):
-        send_ref[way, 0] = own(way, 0).astype(send_ref.dtype)
+    for way in range(len(WAYS)):
+        first, width = WAYS[way][1], WAYS[way][2]
+        send_ref[0, :, pl.ds(first, width)] = own(way, 0).astype(send_ref.dtype)
         link(way, 0).start()
 
     def step_body(step, carry):
-        slot_in = (step - 1) % 2
-        slot_out = step % 2
-        for way in (0, 1):
-            link(way, slot_in).wait_recv()
-            total = recv_ref[way, slot_in].astype(jnp.float32) + own(way, step)
-
-            @pl.when(step >= 2)
-            def _():
-                link(way, slot_out).wait_send()
-
-            send_ref[way, slot_out] = total.astype(send_ref.dtype)
-
-            @pl.when(step <= steps - 2)
-            def _():
-                pl.semaphore_signal(credit.at[way], 1, device_id=sources[way], device_id_type=MESH_ID)
-
-            @pl.when(step >= 2)
-            def _():
-                pl.semaphore_wait(credit.at[way], 1)
-
-            link(way, slot_out).start()
+        for way in range(len(WAYS)):
+            first, width = WAYS[way][1], WAYS[way][2]
+            cols = pl.ds(first, width)
+            link(way, step - 1).wait_recv()
+            total = recv_ref[step - 1, :, cols].astype(jnp.float32) + own(way, step)
+            send_ref[step, :, cols] = total.astype(send_ref.dtype)
+            link(way, step).start()
         return carry
 
     lax.fori_loop(1, steps, step_body, 0)
 
-    last = steps % 2
-    for way in (0, 1):
-        link(way, (steps - 1) % 2).wait_recv()
-        total = recv_ref[way, (steps - 1) % 2].astype(jnp.float32) + own(way, steps)
-        out_ref[:, pl.ds(way * lanes, lanes)] = total
-        link(way, (steps - 2) % 2).wait_send()
-        link(way, (steps - 1) % 2).wait_send()
+    for way in range(len(WAYS)):
+        first, width = WAYS[way][1], WAYS[way][2]
+        cols = pl.ds(first, width)
+        link(way, steps - 1).wait_recv()
+        out_ref[:, cols] = recv_ref[steps - 1, :, cols].astype(jnp.float32) + own(way, steps)
+
+    def drain(step, carry):
+        for way in range(len(WAYS)):
+            link(way, step).wait_send()
+        return carry
+
+    lax.fori_loop(0, steps, drain, 0)
 
 
 def ring_reduce_scatter(x, snake):
@@ -400,19 +396,17 @@
         out_specs=pl.BlockSpec(memory_space=pltpu.VMEM),
         scratch_shapes=[
             pltpu.VMEM((count, rows, width), x.dtype),
-            pltpu.VMEM((2, 2, rows, half), x.dtype),
-            pltpu.VMEM((2, 2, rows, half), x.dtype),
+            pltpu.VMEM((count - 1, rows, width), x.dtype),
+            pltpu.VMEM((count - 1, rows, width), x.dtype),
             pltpu.SemaphoreType.DMA((2,)),
-            pltpu.SemaphoreType.DMA((2, 2)),
-            pltpu.SemaphoreType.DMA((2, 2)),
-            pltpu.SemaphoreType.REGULAR((2,)),
+            pltpu.SemaphoreType.DMA((len(WAYS), count - 1)),
+            pltpu.SemaphoreType.DMA((len(WAYS), count - 1)),
         ],
         compiler_params=pltpu.CompilerParams(collective_id=0, has_side_effects=True,
                                              vmem_limit_bytes=48 * 1024 * 1024),
         cost_estimate=pl.CostEstimate(flops=2 * x.size, transcendentals=0,
                                       bytes_accessed=2 * x.size * x.dtype.itemsize),
     )(x)
-
 
 def sum_kernel(x_ref, out_ref, pair_ref, gather_ref, mine_ref, pair_sem, peer_send, peer_recv, back_sem):
     count = gather_ref.shape[0]
@@ -492,7 +486,9 @@
 def ring_ag_kernel(snake, x_ref, out_ref, send_sem, recv_sem, pair_sem):
     count = out_ref.shape[0] // 2
     steps = count - 1
-    lanes = out_ref.shape[2] // 2
+    half = out_ref.shape[2] // 2
+    part = (half // 256) * 128
+    ways = ((0, 0, part), (1, half, part), (0, part, half - part), (1, half + part, half - part))
     position_of = snake_position if snake else plain_position
     chip_of = snake_chip if snake else plain_position
     chip = lax.axis_index("fsdp")
@@ -515,30 +511,31 @@
         return 2 * chip_of(spot) + core
 
     def link(way, step, index):
-        cols = pl.ds(way * lanes, lanes)
+        direction, first, width = ways[way]
+        cols = pl.ds(first, width)
         return pltpu.make_async_remote_copy(
             src_ref=out_ref.at[index, :, cols], dst_ref=out_ref.at[index, :, cols],
             send_sem=send_sem.at[way, step], recv_sem=recv_sem.at[way, step],
-            device_id=targets[way], device_id_type=MESH_ID)
-
-    for way in (0, 1):
-        link(way, 0, slot(way, 0)).start()
+            device_id=targets[direction], device_id_type=MESH_ID)
+
+    for way in range(4):
+        link(way, 0, slot(ways[way][0], 0)).start()
 
     def step_body(step, carry):
-        for way in (0, 1):
-            index = slot(way, step)
+        for way in range(4):
+            index = slot(ways[way][0], step)
             link(way, step - 1, index).wait_recv()
             link(way, step, index).start()
         return carry
 
     lax.fori_loop(1, steps, step_body, 0)
 
-    for way in (0, 1):
-        link(way, steps - 1, slot(way, steps)).wait_recv()
+    for way in range(4):
+        link(way, steps - 1, slot(ways[way][0], steps)).wait_recv()
 
     def drain(step, carry):
-        for way in (0, 1):
-            link(way, step, slot(way, step)).wait_send()
+        for way in range(4):
+            link(way, step, slot(ways[way][0], step)).wait_send()
         return carry
 
     lax.fori_loop(0, steps, drain, 0)
@@ -573,8 +570,8 @@
         in_specs=[pl.BlockSpec(memory_space=pltpu.VMEM)],
         out_specs=pl.BlockSpec(memory_space=pltpu.VMEM),
         scratch_shapes=[
-            pltpu.SemaphoreType.DMA((2, count - 1)),
-            pltpu.SemaphoreType.DMA((2, count - 1)),
+            pltpu.SemaphoreType.DMA((4, count - 1)),
+            pltpu.SemaphoreType.DMA((4, count - 1)),
             pltpu.SemaphoreType.DMA((2, count)),
         ],
         compiler_params=pltpu.CompilerParams(collective_id=2, has_side_effects=True,
@@ -582,7 +579,6 @@
         cost_estimate=pl.CostEstimate(flops=0, transcendentals=0,
                                       bytes_accessed=4 * count * x.size * x.dtype.itemsize),
     )(x)
-
 
 def body(
     snake,

time: 630 us -> 612 us (0.971)
  Pallas kernels: 224 us -> 209 us
    pallas_call x1, Pallas kernels: 77.5 us -> 65.8 us  [ring_all_gather(): pl.pallas_call(functools.partial(ring_ag_kernel, snake), out_shape=jax.Sh...]
  transfers between devices with their start and end apart: 3 -> 3, of which waited for: 0 -> 0; matrix products, arithmetic and copies ran while one was open for 32% -> 33% of each run, Pallas kernels for 28% -> 27%
where the time goes in v10:
time: 612 us; the launch traced here: 603 us
  Pallas kernels  209 us (34%)
  matrix products  195 us (32%)
  other arithmetic  91.7 us (15%)
  local copies, waits for them, and re-layouts  70.5 us (12%)
  between operations  31 us (5%)
    pallas_call x1, Pallas kernels, ring_reduce_scatter(): pl.pallas_call(functools.partial(ring_rs_kernel, snake), out_shape=jax.Sh...  74.6 us
    pallas_call x1, Pallas kernels, ring_all_gather(): pl.pallas_call(functools.partial(ring_ag_kernel, snake), out_shape=jax.Sh...  65.8 us
    pallas_call x1, Pallas kernels, attention_backward(): pl.pallas_call(attn_bwd_kernel, out_shape=(part, part, part), grid_spec=p...  34.2 us
    pallas_call x1, Pallas kernels, attention_forward(): pl.pallas_call(attn_fwd_kernel, out_shape=jax.ShapeDtypeStruct((count_ite...  22 us
    dot_general x3, matrix products, body(): tokens, gbst_pull = jax.vjp(gbst_tokens, hidden, vector_vals[3])  21.6 us
    dot_general x1, matrix products, body(): jnp.einsum('xwu,xwo->uo', byte_windows, gradient_hidden_reduced, preferre...  18.1 us
    dot_general x1, matrix products, body(): jnp.einsum('std,fd->stf', cotangent, back_contract, preferred_element_typ...  17.5 us
    dot_general x1, matrix products, body(): jnp.einsum('xpg,xpz->gz', one_hot_bytes, gradient_embedded_bytes, preferr...  16.4 us
  transfers between devices with their start and end apart: 3, of which 0 were waited for; matrix products, arithmetic and copies ran while one was open for 33% of the time, Pallas kernels for 27%

profile of v10, /device:TPU:0, one launch (start us, length us, event | category | flops | bytes accessed | tf_op | source)
XLA Modules:
  0.0 602.7 jit_solution(17240850984551683095)
XLA Ops:
  15.3 65.8 %shard_map.583 = bf16[32,24,3072]{2,1,0:T(8,128)(2,1)S(1)} custom-call(bf16[24,3072]{1,0:T(8,128)(2,1)S(1)} %pad_maximum_fusion.7.x_ref), custom_call_target="tpu_custom_call" | custom-call | bytes 9437184 | tf_op jit(solution)/shard_map/pallas_call | solution.py:567
  94.4 4.8 slice.373
  103.4 4.6 pad_slice_fusion.5
  108.0 14.0 %fusion.30 = f32[2,1024,768]{2,1,0:T(8,128)S(1)} fusion(bf16[3072,768,1]{1,0,2:T(8,128)(2,1)} %bitcast.554, bf16[2,1024,768]{2,1,0:T(8,128)(2,1)} %copy-done.13, bf16[2,1024,768]{2,1,0:T(8,128)(2,1)} %get-tuple-element.91, bf16[2,1024,768]{2,1,0:T(8,128)(2,1)} %get-tuple-element.90, bf16[2,1024,768]{2,1,0:T(8,128)(2,1)} %get-tuple-element.89), kind=kOutput, calls=%fused_computation.75 | convolution fusion | flops 9714008064 | bytes 23592960 | tf_op jit(solution)/shard_map/hby,yj->hbj/dot_general | solution.py:670
  138.5 12.3 %multiply_reduce_fusion.5 = (f32[2,512]{1,0:T(2,128)S(1)}, f32[2,512,768]{2,1,0:T(8,128)S(1)}) fusion(f32[2,1024,768]{2,1,0:T(8,128)} %copy-done.1, f32[768]{0:T(1024)S(1)} %add.1776, f32[2,512]{1,0:T(2,128)S(1)} %add_multiply_fusion, f32[2,512]{1,0:T(2,128)S(1)} %add_multiply_fusion.1, f32[2,512]{1,0:T(2,128)S(1)} %add_multiply_fusion.2, ...), kind=kOutput, calls=%fused_computation.61 | convolution fusion | flops 4841274368 | bytes 12614656 | tf_op jit(solution)/shard_map/jvp(ntj,njd->ntd)/dot_general | solution.py:103
  152.5 5.5 convolution_convert_fusion.q_ref.k_ref.v_ref
  158.0 22.0 %shard_map.584 = bf16[2,512,768]{2,1,0:T(8,128)(2,1)} custom-call(s32[2]{0:T(128)} %len_ref.3, bf16[2,512,2304]{2,1,0:T(8,128)(2,1)} %convolution_convert_fusion.q_ref.k_ref.v_ref, bf16[2,512,2304]{2,1,0:T(8,128)(2,1)} %convolution_convert_fusion.q_ref.k_ref.v_ref, bf16[2,512,2304]{2,1,0:T(8,128)(2,1)} %convolution_convert_fusion.q_ref.k_ref.v_ref), custom_call_target="tpu_custom_call" | custom-call | flops 3221225472 | bytes 6291456 | tf_op jit(solution)/shard_map/pallas_call | solution.py:254
  180.0 4.8 multiply_reduce_fusion.4
  186.8 4.4 reshape.4459
  191.2 13.2 %fusion.18 = f32[2,512,4096]{2,1,0:T(8,128)} fusion(bf16[768,6144]{1,0:T(8,128)(2,1)} %all-gather.6.cloned.1.call-done, f32[2,512,768]{2,1,0:T(8,128)} %get-tuple-element.147, f32[768]{0:T(1024)S(1)} %mul.1582, f32[2,512]{1,0:T(2,128)S(1)} %fusion.179), kind=kOutput, calls=%fused_computation.38 | convolution fusion | flops 6444810240 | bytes 26221568 | tf_op jit(solution)/shard_map/std,de->ste/dot_general | solution.py:687
  204.4 17.5 %bitcast_multiply_fusion.1 = (f32[2,512,2048]{2,1,0:T(8,128)}, f32[2,512,2048]{2,1,0:T(8,128)}, bf16[2,512,2048]{2,1,0:T(8,128)(2,1)}) fusion(f32[2,512,4096]{2,1,0:T(8,128)} %fusion.18, bf16[2048,768,1]{1,0,2:T(8,128)(2,1)S(1)} %copy-done.11, bf16[2,512,768]{2,1,0:T(8,128)(2,1)S(1)} %copy-done.24), kind=kOutput, calls=%fused_computation.18 | convolution fusion | flops 3271557120 | bytes 42467328 | tf_op jit(solution)/shard_map/std,fd->stf/dot_general | solution.py:700
  221.9 15.3 %bitcast_convert_fusion = bf16[768,4096]{1,0:T(8,128)(2,1)} fusion(f32[2,512,2048]{2,1,0:T(8,128)} %get-tuple-element.83, f32[2,512,2048]{2,1,0:T(8,128)} %get-tuple-element.82, f32[2,512,768]{2,1,0:T(8,128)S(1)} %copy-done.2, f32[768]{0:T(1024)S(1)} %mul.1582, f32[2,512]{1,0:T(2,128)S(1)} %fusion.179), kind=kOutput, calls=%fused_computation.7 | convolution fusion | flops 6456344576 | bytes 26221568 | tf_op jit(solution)/shard_map/std,ste->de/dot_general | solution.py:705
  237.2 14.5 %multiply_reduce_fusion = (bf16[768]{0:T(1024)(128)(2,1)}, f32[2,512]{1,0:T(2,128)S(1)}, f32[2,512,768]{2,1,0:T(8,128)}) fusion(f32[2,512,768]{2,1,0:T(8,128)S(1)} %copy-done.2, f32[2,512]{1,0:T(2,128)S(1)} %fusion.179, f32[768]{0:T(1024)S(1)} %mul.1582, bf16[768,6144]{1,0:T(8,128)(2,1)} %all-gather.6.cloned.1.call-done, ...), kind=kOutput, calls=%fused_computation.54 | convolution fusion | flops 6455556096 | bytes 29372928 | tf_op jit(solution)/shard_map/ste,de->std/dot_general | solution.py:708
  251.7 3.2 fusion.20
  254.9 4.9 convolution_convert_fusion.1.do_ref
  261.3 34.2 %shard_map.585 = (bf16[2,512,768]{2,1,0:T(8,128)(2,1)}, bf16[2,512,768]{2,1,0:T(8,128)(2,1)}, bf16[2,512,768]{2,1,0:T(8,128)(2,1)}) custom-call(s32[2]{0:T(128)} %len_ref.3, bf16[2,512,2304]{2,1,0:T(8,128)(2,1)} %convolution_convert_fusion.q_ref.k_ref.v_ref, bf16[2,512,2304]{2,1,0:T(8,128)(2,1)} %convolution_convert_fusion.q_ref.k_ref.v_ref, ...), custom_call_target="tpu_custom_call" | custom-call | flops 8053063680 | bytes 11010048 | tf_op jit(solution)/shard_map/pallas_call | solution.py:276
  300.1 5.6 bitcast_convert_fusion.2
  307.6 7.4 %bitcast_convert_fusion.3 = bf16[2048,768]{1,0:T(8,128)(2,1)} fusion(bf16[2,512,2048]{2,1,0:T(8,128)(2,1)} %get-tuple-element.84, bf16[2,512,768]{2,1,0:T(8,128)(2,1)S(1)} %copy-done.25), kind=kOutput, calls=%fused_computation.23 | convolution fusion | flops 3222798336 | bytes 8912896 | tf_op jit(solution)/shard_map/stf,std->fd/dot_general | solution.py:697
  315.0 5.5 reshape.4443
  320.5 12.3 %pad_maximum_fusion = bf16[768,9216]{1,0:T(8,128)(2,1)} fusion(bf16[768,2048]{1,0:T(8,128)(2,1)S(1)} %reshape.4443, bf16[768,4096]{1,0:T(8,128)(2,1)} %bitcast_convert_fusion, bf16[768,768]{1,0:T(8,128)(2,1)} %copy.119, bf16[768,2304]{1,0:T(8,128)(2,1)} %bitcast_convert_fusion.2), kind=kLoop, calls=%fused_computation.1 | loop fusion | flops 56623104 | bytes 28311552 | tf_op jit(solution)/shard_map/concatenate | solution.py:753
  350.8 9.4 %multiply_reduce_fusion.1 = (bf16[768]{0:T(1024)(128)(2,1)S(1)}, f32[2,512]{1,0:T(2,128)S(1)}, f32[2,512,768]{2,1,0:T(8,128)S(1)}) fusion(f32[2,512,768]{2,1,0:T(8,128)} %copy-done.4, f32[2,512]{1,0:T(2,128)} %copy-done.78, f32[768]{0:T(1024)} %copy-done.76, bf16[2,512,2304]{2,1,0:T(8,128)(2,1)} %copy-done.29, bf16[768,3072]{1,0:T(8,128)(2,1)} %bitcast.547), kind=kOutput, calls=%fused_computation.55 | convolution fusion | flops 3628595456 | bytes 14562816 | tf_op jit(solution)/shard_map/ste,de->std/dot_general | solution.py:724
  362.6 8.6 %select_reduce_fusion.2 = (f32[2,512]{1,0:T(2,128)S(1)}, f32[2,512]{1,0:T(2,128)S(1)}, f32[2,512]{1,0:T(2,128)S(1)}, f32[2,512]{1,0:T(2,128)S(1)}, f32[2,512]{1,0:T(2,128)S(1)}, /*index=5*/f32[2,512]{1,0:T(2,128)S(1)}) fusion(pred[512,1024]{1,0:T(8,128)(4,1)S(1)} %copy-done.33, pred[512,1024]{1,0:T(8,128)(4,1)S(1)} %copy-done.31, ...), kind=kOutput, calls=%fused_computation.43 | convolution fusion | flops 4845987840 | bytes 12610560 | tf_op jit(solution)/shard_map/transpose(jvp(ntd,njd->ntj))/dot_general | solution.py:673
  379.9 7.5 %add_convert_fusion.1 = bf16[2,1024,768]{2,1,0:T(8,128)(2,1)S(1)} fusion(f32[768]{0:T(1024)S(1)} %mul.1627, f32[2,1024]{1,0:T(2,128)S(1)} %fusion.105, f32[2,512,768]{2,1,0:T(8,128)} %copy-done.14, f32[2,512]{1,0:T(2,128)S(1)} %copy-done.101, f32[2,512]{1,0:T(2,128)S(1)} %copy-done.99, f32[2,512]{1,0:T(2,128)S(1)} %copy-done.105, ...), kind=kOutput, calls=%fused_computation.25 | convolution fusion | flops 1621622784 | bytes 9473024 | tf_op jit(solution)/shard_map/transpose(jvp(ntj,ntd->njd))/dot_general | solution.py:673
  387.4 4.6 pad_slice_fusion.2
  392.2 5.5 fusion.78
  398.2 9.6 %pad_maximum_fusion.2 = bf16[2,1024,3072]{2,1,0:T(8,128)(2,1)} fusion(bf16[2,1024,768]{2,1,0:T(8,128)(2,1)S(1)} %add_convert_fusion.1, bf16[2,1024,768]{2,1,0:T(8,128)(2,1)} %get-tuple-element.87, bf16[2,1024,768]{2,1,0:T(8,128)(2,1)} %get-tuple-element.86, bf16[2,1024,768]{2,1,0:T(8,128)(2,1)} %get-tuple-element.85), kind=kLoop, calls=%fused_computation.6 | loop fusion | flops 50331648 | bytes 25165824 | tf_op jit(solution)/shard_map/concatenate | solution.py:736
  407.8 16.4 %fusion.73 = bf16[256,768]{1,0:T(8,128)(2,1)} fusion(bf16[4,768,768,1]{2,1,0,3:T(8,128)(2,1)} %bitcast.555, bf16[2,128,4,8,768]{4,3,2,1,0:T(8,128)(2,1)} %bitcast.553, bf16[2,1024]{1,0:T(2,128)(2,1)S(1)} %copy-done.109, s32[2,1024]{1,0:T(2,128)S(1)} %copy-done.162), kind=kOutput, calls=%fused_computation.115 | convolution fusion | flops 10472849408 | bytes 17707008 | tf_op jit(solution)/shard_map/xpg,xpz->gz/dot_general | solution.py:747
  424.2 18.1 %bitcast_convert_fusion.1 = bf16[3072,768]{1,0:T(8,128)(2,1)} fusion(bf16[2,1024,768]{2,1,0:T(8,128)(2,1)S(1)} %add_convert_fusion.1, bf16[2,1024,768]{2,1,0:T(8,128)(2,1)} %copy-done.13, bf16[2,1024,768]{2,1,0:T(8,128)(2,1)} %get-tuple-element.91, bf16[2,1024,768]{2,1,0:T(8,128)(2,1)} %get-tuple-element.90, bf16[2,1024,768]{2,1,0:T(8,128)(2,1)} %get-tuple-element.89), kind=kOutput, calls=%fused_computation.10 | convolution fusion | flops 9716367360 | bytes 20447232 | tf_op jit(solution)/shard_map/xwu,xwo->uo/dot_general | solution.py:732
  442.3 3.6 copy_bitcast_fusion.x_ref
  446.0 74.6 %shard_map.586 = f32[112,768]{1,0:T(8,128)S(1)} custom-call(bf16[2,16,112,768]{3,2,1,0:T(8,128)(2,1)S(1)} %copy_bitcast_fusion.x_ref), custom_call_target="tpu_custom_call" | custom-call | flops 5505024 | bytes 11010048 | tf_op jit(solution)/shard_map/pallas_call | solution.py:392
  520.8 7.3 %convolution_add_fusion.1 = f32[2,512,768]{2,1,0:T(8,128)} fusion(f32[2,512,768]{2,1,0:T(8,128)S(1)} %copy-done.3, bf16[2,512,2048]{2,1,0:T(8,128)(2,1)} %get-tuple-element.84, bf16[2048,768,1]{1,0,2:T(8,128)(2,1)S(1)} %copy-done.12), kind=kOutput, calls=%fused_computation.111 | convolution fusion | flops 3222011904 | bytes 13631488 | tf_op jit(solution)/shard_map/stf,fd->std/dot_general | solution.py:690
  532.6 12.7 %shard_map.587 = f32[80,128]{1,0:T(8,128)} custom-call(f32[80,128]{1,0:T(8,128)} %pad_bitcast_fusion.x_ref), custom_call_target="tpu_custom_call" | custom-call | flops 163840 | bytes 655360 | tf_op jit(solution)/shard_map/pallas_call | solution.py:466
  (570 shorter events, 121.9 us)
Async XLA Ops:
  7.2 84.2 %copy-start.110 = (s32[2]{0:T(128)S(1)}, s32[2]{0:T(128)}, u32[]{:S(2)}) copy-start(s32[2]{0:T(128)} %len_ref.3) | copy-start | bytes 28
  7.2 87.2 %all-gather.4.cloned.1.call-start = ((), (), s32[]{:S(2)}) async-start(), calls=%async_computation.1 | async-start | bytes 5677056 | tf_op jit(solution)/shard_map/all_gather | solution.py:635
  10.5 174.4 %all-gather.6.cloned.1.call-start = ((), (), s32[]{:S(2)}) async-start(), calls=%async_computation.2 | async-start | bytes 9732096 | tf_op jit(solution)/shard_map/all_gather | solution.py:640
  13.4 514.7 %reduce-scatter.2.cloned.1.call-start = ((), (), s32[]{:S(2)}) async-start(), calls=%async_computation.3 | async-start | bytes 14598144 | tf_op jit(solution)/shard_map/reduce_scatter | solution.py:756
  83.3 46.5 %copy-start.106 = (f32[256]{0:T(256)}, f32[256]{0:T(256)S(1)}, u32[]{:S(2)}) copy-start(f32[256]{0:T(256)S(1)} %minimum_convert_fusion.11) | copy-start | bytes 3076
  83.3 52.0 %copy-start.113 = (pred[512]{0:T(512)(128)(4,1)}, pred[512]{0:T(512)(128)(4,1)S(1)}, u32[]{:S(2)}) copy-start(pred[512]{0:T(512)(128)(4,1)S(1)} %get-tuple-element.161) | copy-start | bytes 1540
  83.3 52.7 %copy-start.111 = (pred[512]{0:T(512)(128)(4,1)}, pred[512]{0:T(512)(128)(4,1)S(1)}, u32[]{:S(2)}) copy-start(pred[512]{0:T(512)(128)(4,1)S(1)} %get-tuple-element.160) | copy-start | bytes 1540
  83.3 52.0 %copy-start.136 = (pred[512]{0:T(512)(128)(4,1)}, pred[512]{0:T(512)(128)(4,1)S(1)}, u32[]{:S(2)}) copy-start(pred[512]{0:T(512)(128)(4,1)S(1)} %get-tuple-element.165) | copy-start | bytes 1540
  83.3 54.2 %copy-start.134 = (pred[512]{0:T(512)(128)(4,1)}, pred[512]{0:T(512)(128)(4,1)S(1)}, u32[]{:S(2)}) copy-start(pred[512]{0:T(512)(128)(4,1)S(1)} %get-tuple-element.164) | copy-start | bytes 1540
  83.4 51.9 %copy-start.119 = (pred[512]{0:T(512)(128)(4,1)}, pred[512]{0:T(512)(128)(4,1)S(1)}, u32[]{:S(2)}) copy-start(pred[512]{0:T(512)(128)(4,1)S(1)} %get-tuple-element.191) | copy-start | bytes 1540
  83.4 51.9 %copy-start.137 = (pred[512]{0:T(512)(128)(4,1)}, pred[512]{0:T(512)(128)(4,1)S(1)}, u32[]{:S(2)}) copy-start(pred[512]{0:T(512)(128)(4,1)S(1)} %get-tuple-element.190) | copy-start | bytes 1540
  83.9 51.4 %copy-start.121 = (pred[512]{0:T(512)(128)(4,1)}, pred[512]{0:T(512)(128)(4,1)S(1)}, u32[]{:S(2)}) copy-start(pred[512]{0:T(512)(128)(4,1)S(1)} %get-tuple-element.192) | copy-start | bytes 1540
  84.4 50.9 %copy-start.115 = (pred[512]{0:T(512)(128)(4,1)}, pred[512]{0:T(512)(128)(4,1)S(1)}, u32[]{:S(2)}) copy-start(pred[512]{0:T(512)(128)(4,1)S(1)} %get-tuple-element.194) | copy-start | bytes 1540
  85.5 50.5 %copy-start.127 = (pred[512]{0:T(512)(128)(4,1)}, pred[512]{0:T(512)(128)(4,1)S(1)}, u32[]{:S(2)}) copy-start(pred[512]{0:T(512)(128)(4,1)S(1)} %get-tuple-element.185) | copy-start | bytes 1540
  86.1 50.0 %copy-start.129 = (pred[512]{0:T(512)(128)(4,1)}, pred[512]{0:T(512)(128)(4,1)S(1)}, u32[]{:S(2)}) copy-start(pred[512]{0:T(512)(128)(4,1)S(1)} %get-tuple-element.186) | copy-start | bytes 1540
  86.6 49.4 %copy-start.117 = (pred[512]{0:T(512)(128)(4,1)}, pred[512]{0:T(512)(128)(4,1)S(1)}, u32[]{:S(2)}) copy-start(pred[512]{0:T(512)(128)(4,1)S(1)} %get-tuple-element.188) | copy-start | bytes 1540
  86.6 47.2 %copy-start.91 = (pred[512]{0:T(512)(128)(4,1)}, pred[512]{0:T(512)(128)(4,1)S(1)}, u32[]{:S(2)}) copy-start(pred[512]{0:T(512)(128)(4,1)S(1)} %get-tuple-element.196) | copy-start | bytes 1540
  86.6 47.9 %copy-start.89 = (pred[512]{0:T(512)(128)(4,1)}, pred[512]{0:T(512)(128)(4,1)S(1)}, u32[]{:S(2)}) copy-start(pred[512]{0:T(512)(128)(4,1)S(1)} %get-tuple-element.197) | copy-start | bytes 1540
  86.7 47.2 %copy-start.123 = (pred[512]{0:T(512)(128)(4,1)}, pred[512]{0:T(512)(128)(4,1)S(1)}, u32[]{:S(2)}) copy-start(pred[512]{0:T(512)(128)(4,1)S(1)} %get-tuple-element.159) | copy-start | bytes 1540
  86.7 47.9 %copy-start.140 = (pred[512]{0:T(512)(128)(4,1)}, pred[512]{0:T(512)(128)(4,1)S(1)}, u32[]{:S(2)}) copy-start(pred[512]{0:T(512)(128)(4,1)S(1)} %get-tuple-element.158) | copy-start | bytes 1540
  86.7 47.2 %copy-start.141 = (pred[512]{0:T(512)(128)(4,1)}, pred[512]{0:T(512)(128)(4,1)S(1)}, u32[]{:S(2)}) copy-start(pred[512]{0:T(512)(128)(4,1)S(1)} %get-tuple-element.181) | copy-start | bytes 1540
  86.7 47.9 %copy-start.138 = (pred[512]{0:T(512)(128)(4,1)}, pred[512]{0:T(512)(128)(4,1)S(1)}, u32[]{:S(2)}) copy-start(pred[512]{0:T(512)(128)(4,1)S(1)} %get-tuple-element.180) | copy-start | bytes 1540
  87.3 46.6 %copy-start.125 = (pred[512]{0:T(512)(128)(4,1)}, pred[512]{0:T(512)(128)(4,1)S(1)}, u32[]{:S(2)}) copy-start(pred[512]{0:T(512)(128)(4,1)S(1)} %get-tuple-element.182) | copy-start | bytes 1540
  87.8 46.8 %copy-start.139 = (pred[512]{0:T(512)(128)(4,1)}, pred[512]{0:T(512)(128)(4,1)S(1)}, u32[]{:S(2)}) copy-start(pred[512]{0:T(512)(128)(4,1)S(1)} %get-tuple-element.179) | copy-start | bytes 1540
  87.8 49.0 %copy-start.133 = (pred[512]{0:T(512)(128)(4,1)}, pred[512]{0:T(512)(128)(4,1)S(1)}, u32[]{:S(2)}) copy-start(pred[512]{0:T(512)(128)(4,1)S(1)} %get-tuple-element.157) | copy-start | bytes 1540
  87.8 49.7 %copy-start.131 = (pred[512]{0:T(512)(128)(4,1)}, pred[512]{0:T(512)(128)(4,1)S(1)}, u32[]{:S(2)}) copy-start(pred[512]{0:T(512)(128)(4,1)S(1)} %get-tuple-element.156) | copy-start | bytes 1540
  91.2 46.3 %copy-start.51 = (f32[512]{0:T(512)}, f32[512]{0:T(512)S(1)}, u32[]{:S(2)}) copy-start(f32[512]{0:T(512)S(1)} %get-tuple-element.151) | copy-start | bytes 6148
  91.2 46.3 %copy-start.55 = (f32[512]{0:T(512)}, f32[512]{0:T(512)S(1)}, u32[]{:S(2)}) copy-start(f32[512]{0:T(512)S(1)} %get-tuple-element.150) | copy-start | bytes 6148
  133.8 164.2 %copy-start.76 = (f32[768]{0:T(1024)}, f32[768]{0:T(1024)S(1)}, u32[]{:S(2)}) copy-start(f32[768]{0:T(1024)S(1)} %mul.1576) | copy-start | bytes 9220
  150.9 147.2 %copy-start.78 = (f32[2,512]{1,0:T(2,128)}, f32[2,512]{1,0:T(2,128)S(1)}, u32[]{:S(2)}) copy-start(f32[2,512]{1,0:T(2,128)S(1)} %fusion.178) | copy-start | bytes 12292
  442.3 78.3 %copy-start.12 = (bf16[2048,768,1]{1,0,2:T(8,128)(2,1)S(1)}, bf16[2048,768,1]{1,0,2:T(8,128)(2,1)}, u32[]{:S(2)}) copy-start(bf16[2048,768,1]{1,0,2:T(8,128)(2,1)} %reshape.4459) | copy-start | bytes 9437188
  446.0 74.7 %copy-start.3 = (f32[2,512,768]{2,1,0:T(8,128)S(1)}, f32[2,512,768]{2,1,0:T(8,128)}, u32[]{:S(2)}) copy-start(f32[2,512,768]{2,1,0:T(8,128)} %get-tuple-element.147) | copy-start | bytes 9437188
  (140 other events, 1770.6 us)
Sparse Core Ops, SparseCore 0:
  11.5 74.0 all-gather.3
  89.1 82.5 all-gather.5
  332.9 173.7 reduce-scatter.1

commit v11 on v10

--- a/solution.py
+++ b/solution.py
@@ -1,4 +1,6 @@
 import functools
+
+import numpy as np
 import jax
 import jax.numpy as jnp
 from jax import lax
@@ -67,9 +69,16 @@
     scores = jnp.stack([pool_vec(first, b) for b in (1, 2, 3, 4)], axis=1)
     return jax.nn.softmax(scores, axis=1)
 
+def static_same(block_size, position, column, count):
+    return (np.floor_divide(column, block_size) == position // block_size) & (column >= 0) & (column < count)
+
+
+def static_len(position, block_size, count):
+    return np.minimum(block_size, count - block_size * (position // block_size)).astype(np.float32)
+
+
 def diagonals(mixing, count):
-
-    tok = lax.broadcasted_iota(jnp.int32, (1, count // 2), 1)
+    tok = np.arange(count // 2)[None, :]
     rows = []
     for o in OFFSETS:
         col = 2 * tok + o
@@ -77,11 +86,11 @@
         for p in (0, 1):
             pos = 2 * tok + p
             for index_b, b in enumerate((1, 2, 3, 4)):
-                same = (jnp.floor_divide(col, b) == pos // b) & (col >= 0) & (col < count)
-                weight = mixing[:, index_b, p::2] / block_len(pos, b, count)
-                total = total + jnp.where(same, weight, 0.0)
+                weight = mixing[:, index_b, p::2] / static_len(pos, b, count)
+                total = total + jnp.where(static_same(b, pos, col, count), weight, 0.0)
         rows.append(0.5 * total)
     return jnp.stack(rows, axis=1)
+
 
 def band_matrix(coef, count):
     tok = lax.broadcasted_iota(jnp.int32, (1, count // 2, count), 1)
@@ -111,7 +120,7 @@
     col = lax.broadcasted_iota(jnp.int32, (1, count // 2, count), 2)
     gap = col - 2 * tok
     diag = jnp.stack([jnp.sum(jnp.where(gap == o, cross, 0.0), axis=2) for o in OFFSETS], axis=1)
-    tok1 = lax.broadcasted_iota(jnp.int32, (1, count // 2), 1)
+    tok1 = np.arange(count // 2)[None, :]
     grad_mix = []
     for index_b, b in enumerate((1, 2, 3, 4)):
         per_parity = []
@@ -120,9 +129,8 @@
             total = jnp.zeros((hidden.shape[0], count // 2), jnp.float32)
             for index_o, o in enumerate(OFFSETS):
                 col1 = 2 * tok1 + o
-                same = (jnp.floor_divide(col1, b) == pos // b) & (col1 >= 0) & (col1 < count)
-                total = total + jnp.where(same, diag[:, index_o], 0.0)
-            per_parity.append(0.5 * total / block_len(pos, b, count))
+                total = total + jnp.where(static_same(b, pos, col1, count), diag[:, index_o], 0.0)
+            per_parity.append(0.5 * total / static_len(pos, b, count))
         grad_mix.append(jnp.stack(per_parity, axis=-1).reshape(hidden.shape[0], count))
     grad_mix = jnp.stack(grad_mix, axis=1)
     grad_scores = mixing * (grad_mix - jnp.sum(mixing * grad_mix, axis=1, keepdims=True))

time: 612 us -> 598 us (0.977)
  other arithmetic: 91.7 us -> 76.6 us
    and x21 -> x0, other arithmetic: 7.69 us -> none  [diagonals(): same = (jnp.floor_divide(col, b) == pos // b) & (col >= 0) & (col < count)]
    unnamed x344 -> x282, local copies, waits for them, and re-layouts: 13.4 us -> 13.5 us
  transfers between devices with their start and end apart: 3 -> 3, of which waited for: 0 -> 0; matrix products, arithmetic and copies ran while one was open for 33% -> 31% of each run, Pallas kernels for 27% -> 28%
where the time goes in v11:
time: 598 us; the launch traced here: 591 us
  Pallas kernels  214 us (36%)
  matrix products  194 us (32%)
  other arithmetic  76.6 us (13%)
  local copies, waits for them, and re-layouts  70.5 us (12%)
  between operations  30.5 us (5%)
    pallas_call x1, Pallas kernels, ring_reduce_scatter(): pl.pallas_call(functools.partial(ring_rs_kernel, snake), out_shape=jax.Sh...  77.4 us
    pallas_call x1, Pallas kernels, ring_all_gather(): pl.pallas_call(functools.partial(ring_ag_kernel, snake), out_shape=jax.Sh...  66.8 us
    pallas_call x1, Pallas kernels, attention_backward(): pl.pallas_call(attn_bwd_kernel, out_shape=(part, part, part), grid_spec=p...  34.2 us
    dot_general x3, matrix products, body(): tokens, gbst_pull = jax.vjp(gbst_tokens, hidden, vector_vals[3])  22.1 us
    pallas_call x1, Pallas kernels, attention_forward(): pl.pallas_call(attn_fwd_kernel, out_shape=jax.ShapeDtypeStruct((count_ite...  21.9 us
    dot_general x1, matrix products, body(): jnp.einsum('xwu,xwo->uo', byte_windows, gradient_hidden_reduced, preferre...  17.9 us
    dot_general x1, matrix products, body(): jnp.einsum('std,fd->stf', cotangent, back_contract, preferred_element_typ...  17.5 us
    dot_general x1, matrix products, body(): jnp.einsum('xpg,xpz->gz', one_hot_bytes, gradient_embedded_bytes, preferr...  16.4 us
  transfers between devices with their start and end apart: 3, of which 0 were waited for; matrix products, arithmetic and copies ran while one was open for 31% of the time, Pallas kernels for 28%

profile of v11, /device:TPU:0, one launch (start us, length us, event | category | flops | bytes accessed | tf_op | source)
XLA Modules:
  0.0 590.6 jit_solution(7226897811655652850)
XLA Ops:
  15.3 66.8 %shard_map.1951 = bf16[32,24,3072]{2,1,0:T(8,128)(2,1)S(1)} custom-call(bf16[24,3072]{1,0:T(8,128)(2,1)S(1)} %pad_maximum_fusion.7.x_ref), custom_call_target="tpu_custom_call" | custom-call | bytes 9437184 | tf_op jit(solution)/shard_map/pallas_call | solution.py:575
  87.5 4.8 slice.373
  96.5 4.6 pad_slice_fusion.5
  101.1 14.0 %fusion.30 = f32[2,1024,768]{2,1,0:T(8,128)S(1)} fusion(bf16[3072,768,1]{1,0,2:T(8,128)(2,1)} %bitcast.394, bf16[2,1024,768]{2,1,0:T(8,128)(2,1)} %copy-done.13, bf16[2,1024,768]{2,1,0:T(8,128)(2,1)} %get-tuple-element.91, bf16[2,1024,768]{2,1,0:T(8,128)(2,1)} %get-tuple-element.90, bf16[2,1024,768]{2,1,0:T(8,128)(2,1)} %get-tuple-element.89), kind=kOutput, calls=%fused_computation.75 | convolution fusion | flops 9714008064 | bytes 23592960 | tf_op jit(solution)/shard_map/hby,yj->hbj/dot_general | solution.py:678
  127.3 11.4 %multiply_reduce_fusion.5 = (f32[2,512]{1,0:T(2,128)S(1)}, f32[2,512,768]{2,1,0:T(8,128)S(1)}) fusion(f32[2,1024,768]{2,1,0:T(8,128)} %copy-done.1, f32[768]{0:T(1024)S(1)} %add.1010, f32[2,512]{1,0:T(2,128)S(1)} %get-tuple-element.119, f32[2,512]{1,0:T(2,128)S(1)} %get-tuple-element.115, f32[2,512]{1,0:T(2,128)S(1)} %get-tuple-element.116, ...), kind=kOutput, calls=%fused_computation.61 | convolution fusion | flops 4841274368 | bytes 12614656 | tf_op jit(solution)/shard_map/jvp(ntj,njd->ntd)/dot_general | solution.py:112
  140.6 5.5 convolution_convert_fusion.q_ref.k_ref.v_ref
  146.1 21.9 %shard_map.1952 = bf16[2,512,768]{2,1,0:T(8,128)(2,1)} custom-call(s32[2]{0:T(128)} %len_ref.3, bf16[2,512,2304]{2,1,0:T(8,128)(2,1)} %convolution_convert_fusion.q_ref.k_ref.v_ref, bf16[2,512,2304]{2,1,0:T(8,128)(2,1)} %convolution_convert_fusion.q_ref.k_ref.v_ref, bf16[2,512,2304]{2,1,0:T(8,128)(2,1)} %convolution_convert_fusion.q_ref.k_ref.v_ref), custom_call_target="tpu_custom_call" | custom-call | flops 3221225472 | bytes 6291456 | tf_op jit(solution)/shard_map/pallas_call | solution.py:262
  168.0 4.8 multiply_reduce_fusion.4
  174.7 4.4 reshape.4267
  179.1 13.2 %fusion.18 = f32[2,512,4096]{2,1,0:T(8,128)} fusion(bf16[768,6144]{1,0:T(8,128)(2,1)} %all-gather.6.cloned.1.call-done, f32[2,512,768]{2,1,0:T(8,128)} %get-tuple-element.153, f32[768]{0:T(1024)S(1)} %mul.1037, f32[2,512]{1,0:T(2,128)S(1)} %fusion.162), kind=kOutput, calls=%fused_computation.38 | convolution fusion | flops 6444810240 | bytes 26221568 | tf_op jit(solution)/shard_map/std,de->ste/dot_general | solution.py:695
  192.3 17.5 %bitcast_multiply_fusion.1 = (f32[2,512,2048]{2,1,0:T(8,128)}, f32[2,512,2048]{2,1,0:T(8,128)}, bf16[2,512,2048]{2,1,0:T(8,128)(2,1)}) fusion(f32[2,512,4096]{2,1,0:T(8,128)} %fusion.18, bf16[2048,768,1]{1,0,2:T(8,128)(2,1)S(1)} %copy-done.11, bf16[2,512,768]{2,1,0:T(8,128)(2,1)S(1)} %copy-done.24), kind=kOutput, calls=%fused_computation.18 | convolution fusion | flops 3271557120 | bytes 42467328 | tf_op jit(solution)/shard_map/std,fd->stf/dot_general | solution.py:708
  209.8 15.3 %bitcast_convert_fusion = bf16[768,4096]{1,0:T(8,128)(2,1)} fusion(f32[2,512,2048]{2,1,0:T(8,128)} %get-tuple-element.83, f32[2,512,2048]{2,1,0:T(8,128)} %get-tuple-element.82, f32[2,512,768]{2,1,0:T(8,128)S(1)} %copy-done.2, f32[768]{0:T(1024)S(1)} %mul.1037, f32[2,512]{1,0:T(2,128)S(1)} %fusion.162), kind=kOutput, calls=%fused_computation.7 | convolution fusion | flops 6456344576 | bytes 26221568 | tf_op jit(solution)/shard_map/std,ste->de/dot_general | solution.py:713
  225.1 14.5 %multiply_reduce_fusion = (bf16[768]{0:T(1024)(128)(2,1)}, f32[2,512]{1,0:T(2,128)S(1)}, f32[2,512,768]{2,1,0:T(8,128)}) fusion(f32[2,512,768]{2,1,0:T(8,128)S(1)} %copy-done.2, f32[2,512]{1,0:T(2,128)S(1)} %fusion.162, f32[768]{0:T(1024)S(1)} %mul.1037, bf16[768,6144]{1,0:T(8,128)(2,1)} %all-gather.6.cloned.1.call-done, ...), kind=kOutput, calls=%fused_computation.54 | convolution fusion | flops 6455556096 | bytes 29372928 | tf_op jit(solution)/shard_map/ste,de->std/dot_general | solution.py:716
  239.7 3.2 fusion.20
  242.9 4.9 convolution_convert_fusion.1.do_ref
  249.3 34.2 %shard_map.1953 = (bf16[2,512,768]{2,1,0:T(8,128)(2,1)}, bf16[2,512,768]{2,1,0:T(8,128)(2,1)}, bf16[2,512,768]{2,1,0:T(8,128)(2,1)}) custom-call(s32[2]{0:T(128)} %len_ref.3, bf16[2,512,2304]{2,1,0:T(8,128)(2,1)} %convolution_convert_fusion.q_ref.k_ref.v_ref, bf16[2,512,2304]{2,1,0:T(8,128)(2,1)} %convolution_convert_fusion.q_ref.k_ref.v_ref, ...), custom_call_target="tpu_custom_call" | custom-call | flops 8053063680 | bytes 11010048 | tf_op jit(solution)/shard_map/pallas_call | solution.py:284
  288.1 5.6 bitcast_convert_fusion.2
  295.5 7.4 %bitcast_convert_fusion.3 = bf16[2048,768]{1,0:T(8,128)(2,1)} fusion(bf16[2,512,2048]{2,1,0:T(8,128)(2,1)} %get-tuple-element.84, bf16[2,512,768]{2,1,0:T(8,128)(2,1)S(1)} %copy-done.25), kind=kOutput, calls=%fused_computation.23 | convolution fusion | flops 3222798336 | bytes 8912896 | tf_op jit(solution)/shard_map/stf,std->fd/dot_general | solution.py:705
  302.9 5.5 reshape.4241
  308.4 12.3 %pad_maximum_fusion = bf16[768,9216]{1,0:T(8,128)(2,1)} fusion(bf16[768,2048]{1,0:T(8,128)(2,1)S(1)} %reshape.4241, bf16[768,4096]{1,0:T(8,128)(2,1)} %bitcast_convert_fusion, bf16[768,768]{1,0:T(8,128)(2,1)} %copy.271, bf16[768,2304]{1,0:T(8,128)(2,1)} %bitcast_convert_fusion.2), kind=kLoop, calls=%fused_computation.1 | loop fusion | flops 56623104 | bytes 28311552 | tf_op jit(solution)/shard_map/concatenate | solution.py:761
  338.5 9.4 %multiply_reduce_fusion.1 = (bf16[768]{0:T(1024)(128)(2,1)S(1)}, f32[2,512]{1,0:T(2,128)S(1)}, f32[2,512,768]{2,1,0:T(8,128)S(1)}) fusion(f32[2,512,768]{2,1,0:T(8,128)} %copy-done.4, f32[2,512]{1,0:T(2,128)} %copy-done.62, f32[768]{0:T(1024)} %copy-done.60, bf16[2,512,2304]{2,1,0:T(8,128)(2,1)} %copy-done.29, bf16[768,3072]{1,0:T(8,128)(2,1)} %bitcast.387), kind=kOutput, calls=%fused_computation.55 | convolution fusion | flops 3628595456 | bytes 14562816 | tf_op jit(solution)/shard_map/ste,de->std/dot_general | solution.py:732
  350.1 8.7 %select_reduce_fusion.5 = (f32[2,512]{1,0:T(2,128)S(1)}, f32[2,512]{1,0:T(2,128)S(1)}, f32[2,512]{1,0:T(2,128)S(1)}, f32[2,512]{1,0:T(2,128)S(1)}, f32[2,512]{1,0:T(2,128)S(1)}, /*index=5*/f32[2,512]{1,0:T(2,128)S(1)}) fusion(pred[512,1024]{1,0:T(8,128)(4,1)S(1)} %copy-done.39, pred[512,1024]{1,0:T(8,128)(4,1)S(1)} %copy-done.31, ...), kind=kOutput, calls=%fused_computation.46 | convolution fusion | flops 4845987840 | bytes 12610560 | tf_op jit(solution)/shard_map/transpose(jvp(ntd,njd->ntj))/dot_general | solution.py:681
  364.4 7.6 %add_convert_fusion.1 = bf16[2,1024,768]{2,1,0:T(8,128)(2,1)S(1)} fusion(f32[768]{0:T(1024)S(1)} %mul.1082, f32[2,1024]{1,0:T(2,128)S(1)} %fusion.105, f32[2,512,768]{2,1,0:T(8,128)} %copy-done.14, f32[2,512]{1,0:T(2,128)S(1)} %copy-done.87, f32[2,512]{1,0:T(2,128)S(1)} %copy-done.79, f32[2,512]{1,0:T(2,128)S(1)} %copy-done.81, ...), kind=kOutput, calls=%fused_computation.25 | convolution fusion | flops 1621622784 | bytes 9473024 | tf_op jit(solution)/shard_map/transpose(jvp(ntj,ntd->njd))/dot_general | solution.py:681
  372.0 4.5 pad_slice_fusion.2
  376.7 5.8 fusion.78
  383.0 9.6 %pad_maximum_fusion.2 = bf16[2,1024,3072]{2,1,0:T(8,128)(2,1)} fusion(bf16[2,1024,768]{2,1,0:T(8,128)(2,1)S(1)} %add_convert_fusion.1, bf16[2,1024,768]{2,1,0:T(8,128)(2,1)} %get-tuple-element.87, bf16[2,1024,768]{2,1,0:T(8,128)(2,1)} %get-tuple-element.86, bf16[2,1024,768]{2,1,0:T(8,128)(2,1)} %get-tuple-element.85), kind=kLoop, calls=%fused_computation.6 | loop fusion | flops 50331648 | bytes 25165824 | tf_op jit(solution)/shard_map/concatenate | solution.py:744
  392.6 16.4 %fusion.73 = bf16[256,768]{1,0:T(8,128)(2,1)} fusion(bf16[4,768,768,1]{2,1,0,3:T(8,128)(2,1)} %bitcast.395, bf16[2,128,4,8,768]{4,3,2,1,0:T(8,128)(2,1)} %bitcast.393, bf16[2,1024]{1,0:T(2,128)(2,1)S(1)} %copy-done.91, s32[2,1024]{1,0:T(2,128)S(1)} %copy-done.131), kind=kOutput, calls=%fused_computation.115 | convolution fusion | flops 10472849408 | bytes 17707008 | tf_op jit(solution)/shard_map/xpg,xpz->gz/dot_general | solution.py:755
  408.9 17.9 %bitcast_convert_fusion.1 = bf16[3072,768]{1,0:T(8,128)(2,1)} fusion(bf16[2,1024,768]{2,1,0:T(8,128)(2,1)S(1)} %add_convert_fusion.1, bf16[2,1024,768]{2,1,0:T(8,128)(2,1)} %copy-done.13, bf16[2,1024,768]{2,1,0:T(8,128)(2,1)} %get-tuple-element.91, bf16[2,1024,768]{2,1,0:T(8,128)(2,1)} %get-tuple-element.90, bf16[2,1024,768]{2,1,0:T(8,128)(2,1)} %get-tuple-element.89), kind=kOutput, calls=%fused_computation.10 | convolution fusion | flops 9716367360 | bytes 20447232 | tf_op jit(solution)/shard_map/xwu,xwo->uo/dot_general | solution.py:740
  426.8 3.8 copy_bitcast_fusion.x_ref
  430.6 77.4 %shard_map.1954 = f32[112,768]{1,0:T(8,128)S(1)} custom-call(bf16[2,16,112,768]{3,2,1,0:T(8,128)(2,1)S(1)} %copy_bitcast_fusion.x_ref), custom_call_target="tpu_custom_call" | custom-call | flops 5505024 | bytes 11010048 | tf_op jit(solution)/shard_map/pallas_call | solution.py:400
  508.2 7.3 %convolution_add_fusion.1 = f32[2,512,768]{2,1,0:T(8,128)} fusion(f32[2,512,768]{2,1,0:T(8,128)S(1)} %copy-done.3, bf16[2,512,2048]{2,1,0:T(8,128)(2,1)} %get-tuple-element.84, bf16[2048,768,1]{1,0,2:T(8,128)(2,1)S(1)} %copy-done.12), kind=kOutput, calls=%fused_computation.111 | convolution fusion | flops 3222011904 | bytes 13631488 | tf_op jit(solution)/shard_map/stf,fd->std/dot_general | solution.py:698
  520.1 13.5 %shard_map.1955 = f32[80,128]{1,0:T(8,128)} custom-call(f32[80,128]{1,0:T(8,128)} %pad_bitcast_fusion.x_ref), custom_call_target="tpu_custom_call" | custom-call | flops 163840 | bytes 655360 | tf_op jit(solution)/shard_map/pallas_call | solution.py:474
  (473 shorter events, 106.6 us)
Async XLA Ops:
  7.2 77.2 %copy-start.92 = (s32[2]{0:T(128)S(1)}, s32[2]{0:T(128)}, u32[]{:S(2)}) copy-start(s32[2]{0:T(128)} %len_ref.3) | copy-start | bytes 28
  7.2 80.3 %all-gather.4.cloned.1.call-start = ((), (), s32[]{:S(2)}) async-start(), calls=%async_computation.1 | async-start | bytes 5677056 | tf_op jit(solution)/shard_map/all_gather | solution.py:643
  10.5 162.3 %all-gather.6.cloned.1.call-start = ((), (), s32[]{:S(2)}) async-start(), calls=%async_computation.2 | async-start | bytes 9732096 | tf_op jit(solution)/shard_map/all_gather | solution.py:648
  13.4 502.1 %reduce-scatter.2.cloned.1.call-start = ((), (), s32[]{:S(2)}) async-start(), calls=%async_computation.3 | async-start | bytes 14598144 | tf_op jit(solution)/shard_map/reduce_scatter | solution.py:764
  84.4 38.6 %copy-start.88 = (f32[256]{0:T(256)}, f32[256]{0:T(256)S(1)}, u32[]{:S(2)}) copy-start(f32[256]{0:T(256)S(1)} %minimum_convert_fusion.3) | copy-start | bytes 3076
  84.4 37.6 %copy-start.56 = (f32[512]{0:T(512)}, f32[512]{0:T(512)S(1)}, u32[]{:S(2)}) copy-start(f32[512]{0:T(512)S(1)} %minimum_convert_fusion.2) | copy-start | bytes 6148
  84.4 39.5 %copy-start.58 = (f32[342]{0:T(512)}, f32[342]{0:T(512)S(1)}, u32[]{:S(2)}) copy-start(f32[342]{0:T(512)S(1)} %minimum_convert_fusion.1) | copy-start | bytes 4108
  84.4 39.9 %copy-start.52 = (f32[1024]{0:T(1024)}, f32[1024]{0:T(1024)S(1)}, u32[]{:S(2)}) copy-start(f32[1024]{0:T(1024)S(1)} %minimum_convert_fusion) | copy-start | bytes 12292
  93.9 33.4 %copy-start.54 = (f32[768]{0:T(1024)}, f32[768]{0:T(1024)S(1)}, u32[]{:S(2)}) copy-start(f32[768]{0:T(1024)S(1)} %add.1010) | copy-start | bytes 9220
  123.3 17.2 %slice-start = ((s8[4718592]{0:T(1024)(128)(4,1)}), s8[524288]{0:T(1024)(128)(4,1)S(1)}, s32[]{:S(2)}) async-start(s8[4718592]{0:T(1024)(128)(4,1)} %bitcast.388), calls=%async_computation.4 | async-start | bytes 1048576
  127.0 159.0 %copy-start.60 = (f32[768]{0:T(1024)}, f32[768]{0:T(1024)S(1)}, u32[]{:S(2)}) copy-start(f32[768]{0:T(1024)S(1)} %mul.1031) | copy-start | bytes 9220
  138.9 147.1 %copy-start.62 = (f32[2,512]{1,0:T(2,128)}, f32[2,512]{1,0:T(2,128)S(1)}, u32[]{:S(2)}) copy-start(f32[2,512]{1,0:T(2,128)S(1)} %fusion.161) | copy-start | bytes 12292
  146.1 21.9 %copy-start.5 = (f32[2,512,768]{2,1,0:T(8,128)S(1)}, f32[2,512,768]{2,1,0:T(8,128)}, u32[]{:S(2)}) copy-start(f32[2,512,768]{2,1,0:T(8,128)} %copy-done.4) | copy-start | bytes 9437188
  192.3 17.5 %copy-start.2 = (f32[2,512,768]{2,1,0:T(8,128)S(1)}, f32[2,512,768]{2,1,0:T(8,128)}, u32[]{:S(2)}) copy-start(f32[2,512,768]{2,1,0:T(8,128)} %get-tuple-element.153) | copy-start | bytes 9437188
  320.6 15.7 %copy-start.18 = (f32[192,768]{1,0:T(8,128)S(1)}, f32[192,768]{1,0:T(8,128)}, u32[]{:S(2)}) copy-start(f32[192,768]{1,0:T(8,128)} %param.188) | copy-start | bytes 1769476
  320.6 16.3 %copy-start.15 = (f32[48,4096]{1,0:T(8,128)S(1)}, f32[48,4096]{1,0:T(8,128)}, u32[]{:S(2)}) copy-start(f32[48,4096]{1,0:T(8,128)} %param.191) | copy-start | bytes 2359300
  320.6 28.1 %slice-start.2 = ((s8[6291456]{0:T(1024)(128)(4,1)}), s8[2097152]{0:T(1024)(128)(4,1)S(1)}, s32[]{:S(2)}) async-start(s8[6291456]{0:T(1024)(128)(4,1)} %bitcast.391), calls=%async_computation.6 | async-start | bytes 4194304
  426.8 81.2 %copy-start.12 = (bf16[2048,768,1]{1,0,2:T(8,128)(2,1)S(1)}, bf16[2048,768,1]{1,0,2:T(8,128)(2,1)}, u32[]{:S(2)}) copy-start(bf16[2048,768,1]{1,0,2:T(8,128)(2,1)} %reshape.4267) | copy-start | bytes 9437188
  430.6 77.5 %copy-start.3 = (f32[2,512,768]{2,1,0:T(8,128)S(1)}, f32[2,512,768]{2,1,0:T(8,128)}, u32[]{:S(2)}) copy-start(f32[2,512,768]{2,1,0:T(8,128)} %get-tuple-element.153) | copy-start | bytes 9437188
  515.5 18.0 %copy-start.119 = (s32[23]{0:T(128)S(1)}, s32[23]{0:T(128)}, u32[]{:S(2)}) copy-start(s32[23]{0:T(128)} %constant.316.clone) | copy-start | bytes 280
  515.5 18.1 %copy-start.120 = (s32[23]{0:T(128)S(1)}, s32[23]{0:T(128)}, u32[]{:S(2)}) copy-start(s32[23]{0:T(128)} %constant.317.clone) | copy-start | bytes 280
  515.5 21.8 %copy-start.20 = (bf16[24,9216]{1,0:T(8,128)(2,1)S(1)}, bf16[24,9216]{1,0:T(8,128)(2,1)}, u32[]{:S(2)}) copy-start(bf16[24,9216]{1,0:T(8,128)(2,1)} %reduce-scatter.2.cloned.1.call-done) | copy-start | bytes 1327108
  539.8 22.9 %copy-start.68 = (f32[4096]{0:T(1024)S(1)}, f32[4096]{0:T(1024)}, u32[]{:S(2)}) copy-start(f32[4096]{0:T(1024)} %param.208) | copy-start | bytes 49156
  539.8 23.0 %copy-start.72 = (f32[2304]{0:T(1024)S(1)}, f32[2304]{0:T(1024)}, u32[]{:S(2)}) copy-start(f32[2304]{0:T(1024)} %param.202) | copy-start | bytes 27652
  539.8 31.6 %copy-start.71 = (f32[4,48]{1,0:T(4,128)S(1)}, f32[4,48]{1,0:T(4,128)}, u32[]{:S(2)}) copy-start(f32[4,48]{1,0:T(4,128)} %param.193) | copy-start | bytes 2308
  539.8 33.1 %copy-start.16 = (f32[48,4096]{1,0:T(8,128)S(1)}, f32[48,4096]{1,0:T(8,128)}, u32[]{:S(2)}) copy-start(f32[48,4096]{1,0:T(8,128)} %param.191) | copy-start | bytes 2359300
  542.2 33.8 %copy-start.40 = (f32[48,768]{1,0:T(8,128)S(1)}, f32[48,768]{1,0:T(8,128)}, u32[]{:S(2)}) copy-start(f32[48,768]{1,0:T(8,128)} %param.190) | copy-start | bytes 442372
  551.8 26.4 %copy-start.45 = (f32[16,768]{1,0:T(8,128)S(1)}, f32[16,768]{1,0:T(8,128)}, u32[]{:S(2)}) copy-start(f32[16,768]{1,0:T(8,128)} %param.187) | copy-start | bytes 147460
  562.8 18.1 %copy-start.49 = (f32[4096]{0:T(1024)}, f32[4096]{0:T(1024)S(1)}, u32[]{:S(2)}) copy-start(f32[4096]{0:T(1024)S(1)} %fusion.98) | copy-start | bytes 49156
  562.8 14.1 %copy-start.129 = (f32[48]{0:T(128)S(1)}, f32[48]{0:T(128)}, u32[]{:S(2)}) copy-start(f32[48]{0:T(128)} %multiply_add_fusion.12) | copy-start | bytes 580
  562.8 18.1 %copy-start.50 = (f32[2304]{0:T(1024)}, f32[2304]{0:T(1024)S(1)}, u32[]{:S(2)}) copy-start(f32[2304]{0:T(1024)S(1)} %fusion.102) | copy-start | bytes 27652
  565.0 16.0 %copy-start.75 = (f32[192]{0:T(256)}, f32[192]{0:T(256)S(1)}, u32[]{:S(2)}) copy-start(f32[192]{0:T(256)S(1)} %multiply_add_fusion.8) | copy-start | bytes 2308
  (109 other events, 791.4 us)
Sparse Core Ops, SparseCore 0:
  11.5 73.9 all-gather.3
  89.0 82.5 all-gather.5
  320.8 172.9 reduce-scatter.1

commit v12 on v11

--- a/solution.py
+++ b/solution.py
@@ -109,7 +109,7 @@
     count = hidden.shape[1]
     mixing = gbst_weights(hidden, scorer)
     band = band_matrix(diagonals(mixing, count), count)
-    tokens = jnp.einsum("ntj,njd->ntd", band, hidden, precision=HIGH_3)
+    tokens = jnp.einsum("ntj,njd->ntd", band, hidden, preferred_element_type=jnp.float32)
     return tokens, (hidden, scorer, mixing, band)
 
 def gbst_bwd(saved, grad_tokens):

time: 598 us -> 590 us (0.987)
    unnamed x282 -> x298, local copies, waits for them, and re-layouts: 13.5 us -> 13.5 us
  transfers between devices with their start and end apart: 3 -> 3, of which waited for: 0 -> 1; matrix products, arithmetic and copies ran while one was open for 31% -> 30% of each run, Pallas kernels for 28% -> 28%
where the time goes in v12:
time: 590 us; the launch traced here: 582 us
  Pallas kernels  213 us (36%)
  matrix products  190 us (32%)
  other arithmetic  71.8 us (12%)
  local copies, waits for them, and re-layouts  69.4 us (12%)
  between operations  30.6 us (5%)
    pallas_call x1, Pallas kernels, ring_reduce_scatter(): pl.pallas_call(functools.partial(ring_rs_kernel, snake), out_shape=jax.Sh...  77 us
    pallas_call x1, Pallas kernels, ring_all_gather(): pl.pallas_call(functools.partial(ring_ag_kernel, snake), out_shape=jax.Sh...  66 us
    pallas_call x1, Pallas kernels, attention_backward(): pl.pallas_call(attn_bwd_kernel, out_shape=(part, part, part), grid_spec=p...  34.2 us
    dot_general x3, matrix products, body(): tokens, gbst_pull = jax.vjp(gbst_tokens, hidden, vector_vals[3])  21.8 us
    pallas_call x1, Pallas kernels, attention_forward(): pl.pallas_call(attn_fwd_kernel, out_shape=jax.ShapeDtypeStruct((count_ite...  21.8 us
    dot_general x1, matrix products, body(): jnp.einsum('xwu,xwo->uo', byte_windows, gradient_hidden_reduced, preferre...  17.8 us
    dot_general x1, matrix products, body(): jnp.einsum('std,fd->stf', cotangent, back_contract, preferred_element_typ...  17.5 us
    dot_general x1, matrix products, body(): jnp.einsum('xpg,xpz->gz', one_hot_bytes, gradient_embedded_bytes, preferr...  16.5 us
  transfers between devices with their start and end apart: 3, of which 1 were waited for; matrix products, arithmetic and copies ran while one was open for 30% of the time, Pallas kernels for 28%

profile of v12, /device:TPU:0, one launch (start us, length us, event | category | flops | bytes accessed | tf_op | source)
XLA Modules:
  0.0 582.3 jit_solution(11684157422876744275)
XLA Ops:
  15.3 66.0 %shard_map.1951 = bf16[32,24,3072]{2,1,0:T(8,128)(2,1)S(1)} custom-call(bf16[24,3072]{1,0:T(8,128)(2,1)S(1)} %pad_maximum_fusion.7.x_ref), custom_call_target="tpu_custom_call" | custom-call | bytes 9437184 | tf_op jit(solution)/shard_map/pallas_call | solution.py:575
  86.7 4.8 slice.373
  95.7 4.6 pad_slice_fusion.5
  100.3 14.0 %fusion.30 = f32[2,1024,768]{2,1,0:T(8,128)S(1)} fusion(bf16[3072,768,1]{1,0,2:T(8,128)(2,1)} %bitcast.394, bf16[2,1024,768]{2,1,0:T(8,128)(2,1)} %copy-done.13, bf16[2,1024,768]{2,1,0:T(8,128)(2,1)} %get-tuple-element.91, bf16[2,1024,768]{2,1,0:T(8,128)(2,1)} %get-tuple-element.90, bf16[2,1024,768]{2,1,0:T(8,128)(2,1)} %get-tuple-element.89), kind=kOutput, calls=%fused_computation.75 | convolution fusion | flops 9714008064 | bytes 23592960 | tf_op jit(solution)/shard_map/hby,yj->hbj/dot_general | solution.py:678
  126.6 7.4 %multiply_reduce_fusion.5 = (f32[2,512]{1,0:T(2,128)S(1)}, f32[2,512,768]{2,1,0:T(8,128)S(1)}) fusion(f32[2,1024,768]{2,1,0:T(8,128)} %copy-done.1, f32[768]{0:T(1024)S(1)} %add.1010, bf16[2,512]{1,0:T(2,128)(2,1)S(1)} %get-tuple-element.119, bf16[2,512]{1,0:T(2,128)(2,1)S(1)} %get-tuple-element.115, bf16[2,512]{1,0:T(2,128)(2,1)S(1)} %get-tuple-element.116, ...), kind=kOutput, calls=%fused_computation.61 | convolution fusion | flops 1620048896 | bytes 12602368 | tf_op jit(solution)/shard_map/jvp(ntj,njd->ntd)/dot_general | solution.py:112
  135.8 6.0 %convolution_convert_fusion.q_ref.k_ref.v_ref = bf16[2,512,2304]{2,1,0:T(8,128)(2,1)} fusion(bf16[768,3072]{1,0:T(8,128)(2,1)S(1)} %bitcast.390, f32[2,512,768]{2,1,0:T(8,128)S(1)} %get-tuple-element.151, f32[768]{0:T(1024)S(1)} %mul.1031, f32[2,512]{1,0:T(2,128)S(1)} %fusion.161), kind=kOutput, calls=%fused_computation.26 | convolution fusion | flops 3628597248 | bytes 11411456 | tf_op jit(solution)/shard_map/std,de->ste/dot_general | solution.py:684
  141.8 21.8 %shard_map.1952 = bf16[2,512,768]{2,1,0:T(8,128)(2,1)} custom-call(s32[2]{0:T(128)} %len_ref.3, bf16[2,512,2304]{2,1,0:T(8,128)(2,1)} %convolution_convert_fusion.q_ref.k_ref.v_ref, bf16[2,512,2304]{2,1,0:T(8,128)(2,1)} %convolution_convert_fusion.q_ref.k_ref.v_ref, bf16[2,512,2304]{2,1,0:T(8,128)(2,1)} %convolution_convert_fusion.q_ref.k_ref.v_ref), custom_call_target="tpu_custom_call" | custom-call | flops 3221225472 | bytes 6291456 | tf_op jit(solution)/shard_map/pallas_call | solution.py:262
  163.6 4.8 multiply_reduce_fusion.4
  173.0 4.4 reshape.4267
  177.3 13.2 %fusion.18 = f32[2,512,4096]{2,1,0:T(8,128)} fusion(bf16[768,6144]{1,0:T(8,128)(2,1)} %all-gather.6.cloned.1.call-done, f32[2,512,768]{2,1,0:T(8,128)} %get-tuple-element.153, f32[768]{0:T(1024)S(1)} %mul.1037, f32[2,512]{1,0:T(2,128)S(1)} %fusion.162), kind=kOutput, calls=%fused_computation.38 | convolution fusion | flops 6444810240 | bytes 26221568 | tf_op jit(solution)/shard_map/std,de->ste/dot_general | solution.py:695
  190.6 17.5 %bitcast_multiply_fusion.1 = (f32[2,512,2048]{2,1,0:T(8,128)}, f32[2,512,2048]{2,1,0:T(8,128)}, bf16[2,512,2048]{2,1,0:T(8,128)(2,1)}) fusion(f32[2,512,4096]{2,1,0:T(8,128)} %fusion.18, bf16[2048,768,1]{1,0,2:T(8,128)(2,1)S(1)} %copy-done.11, bf16[2,512,768]{2,1,0:T(8,128)(2,1)S(1)} %copy-done.24), kind=kOutput, calls=%fused_computation.18 | convolution fusion | flops 3271557120 | bytes 42467328 | tf_op jit(solution)/shard_map/std,fd->stf/dot_general | solution.py:708
  208.1 15.3 %bitcast_convert_fusion = bf16[768,4096]{1,0:T(8,128)(2,1)} fusion(f32[2,512,2048]{2,1,0:T(8,128)} %get-tuple-element.83, f32[2,512,2048]{2,1,0:T(8,128)} %get-tuple-element.82, f32[2,512,768]{2,1,0:T(8,128)S(1)} %copy-done.2, f32[768]{0:T(1024)S(1)} %mul.1037, f32[2,512]{1,0:T(2,128)S(1)} %fusion.162), kind=kOutput, calls=%fused_computation.7 | convolution fusion | flops 6456344576 | bytes 26221568 | tf_op jit(solution)/shard_map/std,ste->de/dot_general | solution.py:713
  223.3 14.4 %multiply_reduce_fusion = (bf16[768]{0:T(1024)(128)(2,1)}, f32[2,512]{1,0:T(2,128)S(1)}, f32[2,512,768]{2,1,0:T(8,128)}) fusion(f32[2,512,768]{2,1,0:T(8,128)S(1)} %copy-done.2, f32[2,512]{1,0:T(2,128)S(1)} %fusion.162, f32[768]{0:T(1024)S(1)} %mul.1037, bf16[768,6144]{1,0:T(8,128)(2,1)} %all-gather.6.cloned.1.call-done, ...), kind=kOutput, calls=%fused_computation.54 | convolution fusion | flops 6455556096 | bytes 29372928 | tf_op jit(solution)/shard_map/ste,de->std/dot_general | solution.py:716
  237.8 3.2 fusion.20
  241.0 4.9 convolution_convert_fusion.1.do_ref
  247.4 34.2 %shard_map.1953 = (bf16[2,512,768]{2,1,0:T(8,128)(2,1)}, bf16[2,512,768]{2,1,0:T(8,128)(2,1)}, bf16[2,512,768]{2,1,0:T(8,128)(2,1)}) custom-call(s32[2]{0:T(128)} %len_ref.3, bf16[2,512,2304]{2,1,0:T(8,128)(2,1)} %convolution_convert_fusion.q_ref.k_ref.v_ref, bf16[2,512,2304]{2,1,0:T(8,128)(2,1)} %convolution_convert_fusion.q_ref.k_ref.v_ref, ...), custom_call_target="tpu_custom_call" | custom-call | flops 8053063680 | bytes 11010048 | tf_op jit(solution)/shard_map/pallas_call | solution.py:284
  286.2 5.6 bitcast_convert_fusion.2
  293.7 7.4 %bitcast_convert_fusion.3 = bf16[2048,768]{1,0:T(8,128)(2,1)} fusion(bf16[2,512,2048]{2,1,0:T(8,128)(2,1)} %get-tuple-element.84, bf16[2,512,768]{2,1,0:T(8,128)(2,1)S(1)} %copy-done.25), kind=kOutput, calls=%fused_computation.23 | convolution fusion | flops 3222798336 | bytes 8912896 | tf_op jit(solution)/shard_map/stf,std->fd/dot_general | solution.py:705
  301.0 5.5 reshape.4241
  306.5 12.3 %pad_maximum_fusion = bf16[768,9216]{1,0:T(8,128)(2,1)} fusion(bf16[768,2048]{1,0:T(8,128)(2,1)S(1)} %reshape.4241, bf16[768,4096]{1,0:T(8,128)(2,1)} %bitcast_convert_fusion, bf16[768,768]{1,0:T(8,128)(2,1)} %copy.271, bf16[768,2304]{1,0:T(8,128)(2,1)} %bitcast_convert_fusion.2), kind=kLoop, calls=%fused_computation.1 | loop fusion | flops 56623104 | bytes 28311552 | tf_op jit(solution)/shard_map/concatenate | solution.py:761
  336.6 9.4 %multiply_reduce_fusion.1 = (bf16[768]{0:T(1024)(128)(2,1)S(1)}, f32[2,512]{1,0:T(2,128)S(1)}, f32[2,512,768]{2,1,0:T(8,128)S(1)}) fusion(f32[2,512,768]{2,1,0:T(8,128)} %copy-done.4, f32[2,512]{1,0:T(2,128)} %copy-done.62, f32[768]{0:T(1024)} %copy-done.60, bf16[2,512,2304]{2,1,0:T(8,128)(2,1)} %copy-done.29, bf16[768,3072]{1,0:T(8,128)(2,1)} %bitcast.387), kind=kOutput, calls=%fused_computation.55 | convolution fusion | flops 3628595456 | bytes 14562816 | tf_op jit(solution)/shard_map/ste,de->std/dot_general | solution.py:732
  348.3 8.7 %select_reduce_fusion.5 = (f32[2,512]{1,0:T(2,128)S(1)}, f32[2,512]{1,0:T(2,128)S(1)}, f32[2,512]{1,0:T(2,128)S(1)}, f32[2,512]{1,0:T(2,128)S(1)}, f32[2,512]{1,0:T(2,128)S(1)}, /*index=5*/f32[2,512]{1,0:T(2,128)S(1)}) fusion(pred[512,1024]{1,0:T(8,128)(4,1)S(1)} %copy-done.39, pred[512,1024]{1,0:T(8,128)(4,1)S(1)} %copy-done.31, ...), kind=kOutput, calls=%fused_computation.46 | convolution fusion | flops 4845987840 | bytes 12610560 | tf_op jit(solution)/shard_map/transpose(jvp(ntd,njd->ntj))/dot_general | solution.py:681
  362.6 7.6 %add_convert_fusion.1 = bf16[2,1024,768]{2,1,0:T(8,128)(2,1)S(1)} fusion(f32[768]{0:T(1024)S(1)} %mul.1082, f32[2,1024]{1,0:T(2,128)S(1)} %fusion.105, f32[2,512,768]{2,1,0:T(8,128)} %copy-done.14, bf16[2,512]{1,0:T(2,128)(2,1)S(1)} %copy-done.123, bf16[2,512]{1,0:T(2,128)(2,1)S(1)} %copy-done.115, bf16[2,512]{1,0:T(2,128)(2,1)S(1)} %copy-done.117, ...), kind=kOutput, calls=%fused_computation.25 | convolution fusion | flops 1621622784 | bytes 9460736 | tf_op jit(solution)/shard_map/transpose(jvp(ntj,ntd->njd))/dot_general | solution.py:681
  370.2 4.8 pad_slice_fusion.2
  375.1 5.5 fusion.78
  381.1 9.6 %pad_maximum_fusion.2 = bf16[2,1024,3072]{2,1,0:T(8,128)(2,1)} fusion(bf16[2,1024,768]{2,1,0:T(8,128)(2,1)S(1)} %add_convert_fusion.1, bf16[2,1024,768]{2,1,0:T(8,128)(2,1)} %get-tuple-element.87, bf16[2,1024,768]{2,1,0:T(8,128)(2,1)} %get-tuple-element.86, bf16[2,1024,768]{2,1,0:T(8,128)(2,1)} %get-tuple-element.85), kind=kLoop, calls=%fused_computation.6 | loop fusion | flops 50331648 | bytes 25165824 | tf_op jit(solution)/shard_map/concatenate | solution.py:744
  390.8 16.5 %fusion.73 = bf16[256,768]{1,0:T(8,128)(2,1)} fusion(bf16[4,768,768,1]{2,1,0,3:T(8,128)(2,1)} %bitcast.395, bf16[2,128,4,8,768]{4,3,2,1,0:T(8,128)(2,1)} %bitcast.393, bf16[2,1024]{1,0:T(2,128)(2,1)S(1)} %copy-done.83, s32[2,1024]{1,0:T(2,128)S(1)} %copy-done.139), kind=kOutput, calls=%fused_computation.115 | convolution fusion | flops 10472849408 | bytes 17707008 | tf_op jit(solution)/shard_map/xpg,xpz->gz/dot_general | solution.py:755
  407.2 17.8 %bitcast_convert_fusion.1 = bf16[3072,768]{1,0:T(8,128)(2,1)} fusion(bf16[2,1024,768]{2,1,0:T(8,128)(2,1)S(1)} %add_convert_fusion.1, bf16[2,1024,768]{2,1,0:T(8,128)(2,1)} %copy-done.13, bf16[2,1024,768]{2,1,0:T(8,128)(2,1)} %get-tuple-element.91, bf16[2,1024,768]{2,1,0:T(8,128)(2,1)} %get-tuple-element.90, bf16[2,1024,768]{2,1,0:T(8,128)(2,1)} %get-tuple-element.89), kind=kOutput, calls=%fused_computation.10 | convolution fusion | flops 9716367360 | bytes 20447232 | tf_op jit(solution)/shard_map/xwu,xwo->uo/dot_general | solution.py:740
  425.0 3.7 copy_bitcast_fusion.x_ref
  428.8 77.0 %shard_map.1954 = f32[112,768]{1,0:T(8,128)S(1)} custom-call(bf16[2,16,112,768]{3,2,1,0:T(8,128)(2,1)S(1)} %copy_bitcast_fusion.x_ref), custom_call_target="tpu_custom_call" | custom-call | flops 5505024 | bytes 11010048 | tf_op jit(solution)/shard_map/pallas_call | solution.py:400
  506.0 7.3 %convolution_add_fusion.1 = f32[2,512,768]{2,1,0:T(8,128)} fusion(f32[2,512,768]{2,1,0:T(8,128)S(1)} %copy-done.3, bf16[2,512,2048]{2,1,0:T(8,128)(2,1)} %get-tuple-element.84, bf16[2048,768,1]{1,0,2:T(8,128)(2,1)S(1)} %copy-done.12), kind=kOutput, calls=%fused_computation.111 | convolution fusion | flops 3222011904 | bytes 13631488 | tf_op jit(solution)/shard_map/stf,fd->std/dot_general | solution.py:698
  517.9 13.5 %shard_map.1955 = f32[80,128]{1,0:T(8,128)} custom-call(f32[80,128]{1,0:T(8,128)} %pad_bitcast_fusion.x_ref), custom_call_target="tpu_custom_call" | custom-call | flops 163840 | bytes 655360 | tf_op jit(solution)/shard_map/pallas_call | solution.py:474
  (489 shorter events, 103.0 us)
Async XLA Ops:
  7.2 79.5 %all-gather.4.cloned.1.call-start = ((), (), s32[]{:S(2)}) async-start(), calls=%async_computation.1 | async-start | bytes 5677056 | tf_op jit(solution)/shard_map/all_gather | solution.py:643
  10.5 160.6 %all-gather.6.cloned.1.call-start = ((), (), s32[]{:S(2)}) async-start(), calls=%async_computation.2 | async-start | bytes 9732096 | tf_op jit(solution)/shard_map/all_gather | solution.py:648
  12.6 71.0 %copy-start.84 = (s32[2]{0:T(128)S(1)}, s32[2]{0:T(128)}, u32[]{:S(2)}) copy-start(s32[2]{0:T(128)} %len_ref.3) | copy-start | bytes 28
  13.4 499.9 %reduce-scatter.2.cloned.1.call-start = ((), (), s32[]{:S(2)}) async-start(), calls=%async_computation.3 | async-start | bytes 14598144 | tf_op jit(solution)/shard_map/reduce_scatter | solution.py:764
  83.6 38.6 %copy-start.80 = (f32[256]{0:T(256)}, f32[256]{0:T(256)S(1)}, u32[]{:S(2)}) copy-start(f32[256]{0:T(256)S(1)} %minimum_convert_fusion.3) | copy-start | bytes 3076
  83.6 37.6 %copy-start.56 = (f32[512]{0:T(512)}, f32[512]{0:T(512)S(1)}, u32[]{:S(2)}) copy-start(f32[512]{0:T(512)S(1)} %minimum_convert_fusion.2) | copy-start | bytes 6148
  83.6 39.5 %copy-start.58 = (f32[342]{0:T(512)}, f32[342]{0:T(512)S(1)}, u32[]{:S(2)}) copy-start(f32[342]{0:T(512)S(1)} %minimum_convert_fusion.1) | copy-start | bytes 4108
  83.7 39.9 %copy-start.52 = (f32[1024]{0:T(1024)}, f32[1024]{0:T(1024)S(1)}, u32[]{:S(2)}) copy-start(f32[1024]{0:T(1024)S(1)} %minimum_convert_fusion) | copy-start | bytes 12292
  93.1 33.4 %copy-start.54 = (f32[768]{0:T(1024)}, f32[768]{0:T(1024)S(1)}, u32[]{:S(2)}) copy-start(f32[768]{0:T(1024)S(1)} %add.1010) | copy-start | bytes 9220
  126.2 157.9 %copy-start.60 = (f32[768]{0:T(1024)}, f32[768]{0:T(1024)S(1)}, u32[]{:S(2)}) copy-start(f32[768]{0:T(1024)S(1)} %mul.1031) | copy-start | bytes 9220
  134.1 150.0 %copy-start.62 = (f32[2,512]{1,0:T(2,128)}, f32[2,512]{1,0:T(2,128)S(1)}, u32[]{:S(2)}) copy-start(f32[2,512]{1,0:T(2,128)S(1)} %fusion.161) | copy-start | bytes 12292
  141.8 21.8 %copy-start.5 = (f32[2,512,768]{2,1,0:T(8,128)S(1)}, f32[2,512,768]{2,1,0:T(8,128)}, u32[]{:S(2)}) copy-start(f32[2,512,768]{2,1,0:T(8,128)} %copy-done.4) | copy-start | bytes 9437188
  190.6 17.5 %copy-start.2 = (f32[2,512,768]{2,1,0:T(8,128)S(1)}, f32[2,512,768]{2,1,0:T(8,128)}, u32[]{:S(2)}) copy-start(f32[2,512,768]{2,1,0:T(8,128)} %get-tuple-element.153) | copy-start | bytes 9437188
  318.8 28.2 %slice-start.2 = ((s8[6291456]{0:T(1024)(128)(4,1)}), s8[2097152]{0:T(1024)(128)(4,1)S(1)}, s32[]{:S(2)}) async-start(s8[6291456]{0:T(1024)(128)(4,1)} %bitcast.391), calls=%async_computation.6 | async-start | bytes 4194304
  425.0 80.9 %copy-start.12 = (bf16[2048,768,1]{1,0,2:T(8,128)(2,1)S(1)}, bf16[2048,768,1]{1,0,2:T(8,128)(2,1)}, u32[]{:S(2)}) copy-start(bf16[2048,768,1]{1,0,2:T(8,128)(2,1)} %reshape.4267) | copy-start | bytes 9437188
  428.7 77.1 %copy-start.3 = (f32[2,512,768]{2,1,0:T(8,128)S(1)}, f32[2,512,768]{2,1,0:T(8,128)}, u32[]{:S(2)}) copy-start(f32[2,512,768]{2,1,0:T(8,128)} %get-tuple-element.153) | copy-start | bytes 9437188
  513.3 18.1 %copy-start.126 = (s32[23]{0:T(128)S(1)}, s32[23]{0:T(128)}, u32[]{:S(2)}) copy-start(s32[23]{0:T(128)} %constant.316.clone) | copy-start | bytes 280
  513.3 18.1 %copy-start.127 = (s32[23]{0:T(128)S(1)}, s32[23]{0:T(128)}, u32[]{:S(2)}) copy-start(s32[23]{0:T(128)} %constant.317.clone) | copy-start | bytes 280
  513.3 21.8 %copy-start.20 = (bf16[24,9216]{1,0:T(8,128)(2,1)S(1)}, bf16[24,9216]{1,0:T(8,128)(2,1)}, u32[]{:S(2)}) copy-start(bf16[24,9216]{1,0:T(8,128)(2,1)} %reduce-scatter.2.cloned.1.call-done) | copy-start | bytes 1327108
  537.7 20.2 %copy-start.68 = (f32[4096]{0:T(1024)S(1)}, f32[4096]{0:T(1024)}, u32[]{:S(2)}) copy-start(f32[4096]{0:T(1024)} %param.208) | copy-start | bytes 49156
  537.7 20.2 %copy-start.72 = (f32[2304]{0:T(1024)S(1)}, f32[2304]{0:T(1024)}, u32[]{:S(2)}) copy-start(f32[2304]{0:T(1024)} %param.202) | copy-start | bytes 27652
  537.8 21.1 %copy-start.125 = (f32[192]{0:T(256)S(1)}, f32[192]{0:T(256)}, u32[]{:S(2)}) copy-start(f32[192]{0:T(256)} %param.198) | copy-start | bytes 2308
  537.8 25.8 %copy-start.76 = (f32[768]{0:T(1024)S(1)}, f32[768]{0:T(1024)}, u32[]{:S(2)}) copy-start(f32[768]{0:T(1024)} %param.211) | copy-start | bytes 9220
  537.8 25.8 %copy-start.77 = (f32[768]{0:T(1024)S(1)}, f32[768]{0:T(1024)}, u32[]{:S(2)}) copy-start(f32[768]{0:T(1024)} %param.205) | copy-start | bytes 9220
  537.8 25.8 %copy-start.78 = (f32[768]{0:T(1024)S(1)}, f32[768]{0:T(1024)}, u32[]{:S(2)}) copy-start(f32[768]{0:T(1024)} %param.199) | copy-start | bytes 9220
  537.8 25.8 %copy-start.79 = (f32[768]{0:T(1024)S(1)}, f32[768]{0:T(1024)}, u32[]{:S(2)}) copy-start(f32[768]{0:T(1024)} %param.196) | copy-start | bytes 9220
  537.8 25.9 %copy-start.71 = (f32[4,48]{1,0:T(4,128)S(1)}, f32[4,48]{1,0:T(4,128)}, u32[]{:S(2)}) copy-start(f32[4,48]{1,0:T(4,128)} %param.193) | copy-start | bytes 2308
  537.8 25.9 %copy-start.110 = (f32[4,48]{1,0:T(4,128)S(1)}, f32[4,48]{1,0:T(4,128)}, u32[]{:S(2)}) copy-start(f32[4,48]{1,0:T(4,128)} %param.212) | copy-start | bytes 2308
  537.8 25.9 %copy-start.111 = (f32[4,48]{1,0:T(4,128)S(1)}, f32[4,48]{1,0:T(4,128)}, u32[]{:S(2)}) copy-start(f32[4,48]{1,0:T(4,128)} %param.213) | copy-start | bytes 2308
  537.8 27.3 %copy-start.16 = (f32[48,4096]{1,0:T(8,128)S(1)}, f32[48,4096]{1,0:T(8,128)}, u32[]{:S(2)}) copy-start(f32[48,4096]{1,0:T(8,128)} %param.191) | copy-start | bytes 2359300
  544.0 24.3 %copy-start.40 = (f32[48,768]{1,0:T(8,128)S(1)}, f32[48,768]{1,0:T(8,128)}, u32[]{:S(2)}) copy-start(f32[48,768]{1,0:T(8,128)} %param.190) | copy-start | bytes 442372
  545.2 26.2 %copy-start.128 = (f32[128]{0:T(128)}, f32[128]{0:T(128)S(1)}, u32[]{:S(2)}) copy-start(f32[128]{0:T(128)S(1)} %multiply_add_fusion.9) | copy-start | bytes 1540
  (117 other events, 808.4 us)
Sparse Core Ops, SparseCore 0:
  11.5 73.7 all-gather.3
  88.7 82.2 all-gather.5
  319.0 172.4 reduce-scatter.1

commit v13 on v12

--- a/solution.py
+++ b/solution.py
@@ -338,13 +338,25 @@
         pl.semaphore_signal(barrier, 1, device_id=peer, device_id_type=MESH_ID)
     pl.semaphore_wait(barrier, 3)
 
-    swap = pltpu.make_async_remote_copy(
-        src_ref=x_ref.at[1 - core], dst_ref=part_ref,
-        send_sem=swap_sem.at[0], recv_sem=swap_sem.at[1],
-        device_id=partner, device_id_type=MESH_ID)
-    swap.start()
-    swap.wait_send()
-    swap.wait_recv()
+    def swap(index):
+        return pltpu.make_async_remote_copy(
+            src_ref=x_ref.at[1 - core, index], dst_ref=part_ref.at[index],
+            send_sem=swap_sem.at[0, index], recv_sem=swap_sem.at[1, index],
+            device_id=partner, device_id_type=MESH_ID)
+
+    middle = count // 2 - 1
+
+    def behind_chunk(step):
+        return chip_of((here - step - 1 + 2 * count) % count)
+
+    def ahead_chunk(step):
+        return chip_of((here + step + 1) % count)
+
+    for step in range(middle):
+        swap(behind_chunk(step)).start()
+        swap(ahead_chunk(step)).start()
+    swap(behind_chunk(middle)).start()
+    swap(chip).start()
 
     def link(way, slot):
         direction, first, width = WAYS[way]
@@ -363,12 +375,23 @@
         return (x_ref[core, owner, :, cols].astype(jnp.float32)
                 + part_ref[owner, :, cols].astype(jnp.float32))
 
+    swap(behind_chunk(0)).wait_recv()
+    swap(ahead_chunk(0)).wait_recv()
     for way in range(len(WAYS)):
         first, width = WAYS[way][1], WAYS[way][2]
         send_ref[0, :, pl.ds(first, width)] = own(way, 0).astype(send_ref.dtype)
         link(way, 0).start()
 
     def step_body(step, carry):
+        @pl.when(step < middle)
+        def _():
+            swap(behind_chunk(step)).wait_recv()
+            swap(ahead_chunk(step)).wait_recv()
+
+        @pl.when(step == middle)
+        def _():
+            swap(behind_chunk(step)).wait_recv()
+
         for way in range(len(WAYS)):
             first, width = WAYS[way][1], WAYS[way][2]
             cols = pl.ds(first, width)
@@ -380,6 +403,7 @@
 
     lax.fori_loop(1, steps, step_body, 0)
 
+    swap(chip).wait_recv()
     for way in range(len(WAYS)):
         first, width = WAYS[way][1], WAYS[way][2]
         cols = pl.ds(first, width)
@@ -392,6 +416,12 @@
         return carry
 
     lax.fori_loop(0, steps, drain, 0)
+
+    def swap_drain(index, carry):
+        swap(index).wait_send()
+        return carry
+
+    lax.fori_loop(0, count, swap_drain, 0)
 
 
 def ring_reduce_scatter(x, snake):
@@ -406,7 +436,7 @@
             pltpu.VMEM((count, rows, width), x.dtype),
             pltpu.VMEM((count - 1, rows, width), x.dtype),
             pltpu.VMEM((count - 1, rows, width), x.dtype),
-            pltpu.SemaphoreType.DMA((2,)),
+            pltpu.SemaphoreType.DMA((2, count)),
             pltpu.SemaphoreType.DMA((len(WAYS), count - 1)),
             pltpu.SemaphoreType.DMA((len(WAYS), count - 1)),
         ],

time: 590 us -> 586 us (level)
  transfers between devices with their start and end apart: 3 -> 3, of which waited for: 1 -> 1; matrix products, arithmetic and copies ran while one was open for 30% -> 31% of each run, Pallas kernels for 28% -> 28%
where the time goes in v13:
time: 586 us; the launch traced here: 578 us
  Pallas kernels  208 us (35%)
  matrix products  190 us (32%)
  other arithmetic  71.8 us (12%)
  local copies, waits for them, and re-layouts  69.4 us (12%)
  between operations  30.6 us (5%)
    pallas_call x1, Pallas kernels, ring_reduce_scatter(): pl.pallas_call(functools.partial(ring_rs_kernel, snake), out_shape=jax.Sh...  72.6 us
    pallas_call x1, Pallas kernels, ring_all_gather(): pl.pallas_call(functools.partial(ring_ag_kernel, snake), out_shape=jax.Sh...  66 us
    pallas_call x1, Pallas kernels, attention_backward(): pl.pallas_call(attn_bwd_kernel, out_shape=(part, part, part), grid_spec=p...  34.2 us
    dot_general x3, matrix products, body(): tokens, gbst_pull = jax.vjp(gbst_tokens, hidden, vector_vals[3])  21.8 us
    pallas_call x1, Pallas kernels, attention_forward(): pl.pallas_call(attn_fwd_kernel, out_shape=jax.ShapeDtypeStruct((count_ite...  21.8 us
    dot_general x1, matrix products, body(): jnp.einsum('xwu,xwo->uo', byte_windows, gradient_hidden_reduced, preferre...  17.8 us
    dot_general x1, matrix products, body(): jnp.einsum('std,fd->stf', cotangent, back_contract, preferred_element_typ...  17.5 us
    dot_general x1, matrix products, body(): jnp.einsum('xpg,xpz->gz', one_hot_bytes, gradient_embedded_bytes, preferr...  16.5 us
  transfers between devices with their start and end apart: 3, of which 1 were waited for; matrix products, arithmetic and copies ran while one was open for 31% of the time, Pallas kernels for 28%

profile of v13, /device:TPU:0, one launch (start us, length us, event | category | flops | bytes accessed | tf_op | source)
XLA Modules:
  0.0 577.7 jit_solution(11175844231762058741)
XLA Ops:
  15.3 66.0 %shard_map.1951 = bf16[32,24,3072]{2,1,0:T(8,128)(2,1)S(1)} custom-call(bf16[24,3072]{1,0:T(8,128)(2,1)S(1)} %pad_maximum_fusion.7.x_ref), custom_call_target="tpu_custom_call" | custom-call | bytes 9437184 | tf_op jit(solution)/shard_map/pallas_call | solution.py:605
  86.7 4.8 slice.373
  95.7 4.6 pad_slice_fusion.5
  100.3 14.0 %fusion.30 = f32[2,1024,768]{2,1,0:T(8,128)S(1)} fusion(bf16[3072,768,1]{1,0,2:T(8,128)(2,1)} %bitcast.394, bf16[2,1024,768]{2,1,0:T(8,128)(2,1)} %copy-done.13, bf16[2,1024,768]{2,1,0:T(8,128)(2,1)} %get-tuple-element.91, bf16[2,1024,768]{2,1,0:T(8,128)(2,1)} %get-tuple-element.90, bf16[2,1024,768]{2,1,0:T(8,128)(2,1)} %get-tuple-element.89), kind=kOutput, calls=%fused_computation.75 | convolution fusion | flops 9714008064 | bytes 23592960 | tf_op jit(solution)/shard_map/hby,yj->hbj/dot_general | solution.py:708
  126.6 7.4 %multiply_reduce_fusion.5 = (f32[2,512]{1,0:T(2,128)S(1)}, f32[2,512,768]{2,1,0:T(8,128)S(1)}) fusion(f32[2,1024,768]{2,1,0:T(8,128)} %copy-done.1, f32[768]{0:T(1024)S(1)} %add.1010, bf16[2,512]{1,0:T(2,128)(2,1)S(1)} %get-tuple-element.119, bf16[2,512]{1,0:T(2,128)(2,1)S(1)} %get-tuple-element.115, bf16[2,512]{1,0:T(2,128)(2,1)S(1)} %get-tuple-element.116, ...), kind=kOutput, calls=%fused_computation.61 | convolution fusion | flops 1620048896 | bytes 12602368 | tf_op jit(solution)/shard_map/jvp(ntj,njd->ntd)/dot_general | solution.py:112
  135.8 6.0 %convolution_convert_fusion.q_ref.k_ref.v_ref = bf16[2,512,2304]{2,1,0:T(8,128)(2,1)} fusion(bf16[768,3072]{1,0:T(8,128)(2,1)S(1)} %bitcast.390, f32[2,512,768]{2,1,0:T(8,128)S(1)} %get-tuple-element.151, f32[768]{0:T(1024)S(1)} %mul.1031, f32[2,512]{1,0:T(2,128)S(1)} %fusion.161), kind=kOutput, calls=%fused_computation.26 | convolution fusion | flops 3628597248 | bytes 11411456 | tf_op jit(solution)/shard_map/std,de->ste/dot_general | solution.py:714
  141.8 21.8 %shard_map.1952 = bf16[2,512,768]{2,1,0:T(8,128)(2,1)} custom-call(s32[2]{0:T(128)} %len_ref.3, bf16[2,512,2304]{2,1,0:T(8,128)(2,1)} %convolution_convert_fusion.q_ref.k_ref.v_ref, bf16[2,512,2304]{2,1,0:T(8,128)(2,1)} %convolution_convert_fusion.q_ref.k_ref.v_ref, bf16[2,512,2304]{2,1,0:T(8,128)(2,1)} %convolution_convert_fusion.q_ref.k_ref.v_ref), custom_call_target="tpu_custom_call" | custom-call | flops 3221225472 | bytes 6291456 | tf_op jit(solution)/shard_map/pallas_call | solution.py:262
  163.6 4.8 multiply_reduce_fusion.4
  173.0 4.4 reshape.4267
  177.3 13.2 %fusion.18 = f32[2,512,4096]{2,1,0:T(8,128)} fusion(bf16[768,6144]{1,0:T(8,128)(2,1)} %all-gather.6.cloned.1.call-done, f32[2,512,768]{2,1,0:T(8,128)} %get-tuple-element.153, f32[768]{0:T(1024)S(1)} %mul.1037, f32[2,512]{1,0:T(2,128)S(1)} %fusion.162), kind=kOutput, calls=%fused_computation.38 | convolution fusion | flops 6444810240 | bytes 26221568 | tf_op jit(solution)/shard_map/std,de->ste/dot_general | solution.py:725
  190.6 17.5 %bitcast_multiply_fusion.1 = (f32[2,512,2048]{2,1,0:T(8,128)}, f32[2,512,2048]{2,1,0:T(8,128)}, bf16[2,512,2048]{2,1,0:T(8,128)(2,1)}) fusion(f32[2,512,4096]{2,1,0:T(8,128)} %fusion.18, bf16[2048,768,1]{1,0,2:T(8,128)(2,1)S(1)} %copy-done.11, bf16[2,512,768]{2,1,0:T(8,128)(2,1)S(1)} %copy-done.24), kind=kOutput, calls=%fused_computation.18 | convolution fusion | flops 3271557120 | bytes 42467328 | tf_op jit(solution)/shard_map/std,fd->stf/dot_general | solution.py:738
  208.1 15.3 %bitcast_convert_fusion = bf16[768,4096]{1,0:T(8,128)(2,1)} fusion(f32[2,512,2048]{2,1,0:T(8,128)} %get-tuple-element.83, f32[2,512,2048]{2,1,0:T(8,128)} %get-tuple-element.82, f32[2,512,768]{2,1,0:T(8,128)S(1)} %copy-done.2, f32[768]{0:T(1024)S(1)} %mul.1037, f32[2,512]{1,0:T(2,128)S(1)} %fusion.162), kind=kOutput, calls=%fused_computation.7 | convolution fusion | flops 6456344576 | bytes 26221568 | tf_op jit(solution)/shard_map/std,ste->de/dot_general | solution.py:743
  223.3 14.4 %multiply_reduce_fusion = (bf16[768]{0:T(1024)(128)(2,1)}, f32[2,512]{1,0:T(2,128)S(1)}, f32[2,512,768]{2,1,0:T(8,128)}) fusion(f32[2,512,768]{2,1,0:T(8,128)S(1)} %copy-done.2, f32[2,512]{1,0:T(2,128)S(1)} %fusion.162, f32[768]{0:T(1024)S(1)} %mul.1037, bf16[768,6144]{1,0:T(8,128)(2,1)} %all-gather.6.cloned.1.call-done, ...), kind=kOutput, calls=%fused_computation.54 | convolution fusion | flops 6455556096 | bytes 29372928 | tf_op jit(solution)/shard_map/ste,de->std/dot_general | solution.py:746
  237.8 3.2 fusion.20
  241.0 4.9 convolution_convert_fusion.1.do_ref
  247.4 34.2 %shard_map.1953 = (bf16[2,512,768]{2,1,0:T(8,128)(2,1)}, bf16[2,512,768]{2,1,0:T(8,128)(2,1)}, bf16[2,512,768]{2,1,0:T(8,128)(2,1)}) custom-call(s32[2]{0:T(128)} %len_ref.3, bf16[2,512,2304]{2,1,0:T(8,128)(2,1)} %convolution_convert_fusion.q_ref.k_ref.v_ref, bf16[2,512,2304]{2,1,0:T(8,128)(2,1)} %convolution_convert_fusion.q_ref.k_ref.v_ref, ...), custom_call_target="tpu_custom_call" | custom-call | flops 8053063680 | bytes 11010048 | tf_op jit(solution)/shard_map/pallas_call | solution.py:284
  286.2 5.6 bitcast_convert_fusion.2
  293.7 7.4 %bitcast_convert_fusion.3 = bf16[2048,768]{1,0:T(8,128)(2,1)} fusion(bf16[2,512,2048]{2,1,0:T(8,128)(2,1)} %get-tuple-element.84, bf16[2,512,768]{2,1,0:T(8,128)(2,1)S(1)} %copy-done.25), kind=kOutput, calls=%fused_computation.23 | convolution fusion | flops 3222798336 | bytes 8912896 | tf_op jit(solution)/shard_map/stf,std->fd/dot_general | solution.py:735
  301.0 5.5 reshape.4241
  306.5 12.3 %pad_maximum_fusion = bf16[768,9216]{1,0:T(8,128)(2,1)} fusion(bf16[768,2048]{1,0:T(8,128)(2,1)S(1)} %reshape.4241, bf16[768,4096]{1,0:T(8,128)(2,1)} %bitcast_convert_fusion, bf16[768,768]{1,0:T(8,128)(2,1)} %copy.271, bf16[768,2304]{1,0:T(8,128)(2,1)} %bitcast_convert_fusion.2), kind=kLoop, calls=%fused_computation.1 | loop fusion | flops 56623104 | bytes 28311552 | tf_op jit(solution)/shard_map/concatenate | solution.py:791
  336.6 9.4 %multiply_reduce_fusion.1 = (bf16[768]{0:T(1024)(128)(2,1)S(1)}, f32[2,512]{1,0:T(2,128)S(1)}, f32[2,512,768]{2,1,0:T(8,128)S(1)}) fusion(f32[2,512,768]{2,1,0:T(8,128)} %copy-done.4, f32[2,512]{1,0:T(2,128)} %copy-done.62, f32[768]{0:T(1024)} %copy-done.60, bf16[2,512,2304]{2,1,0:T(8,128)(2,1)} %copy-done.29, bf16[768,3072]{1,0:T(8,128)(2,1)} %bitcast.387), kind=kOutput, calls=%fused_computation.55 | convolution fusion | flops 3628595456 | bytes 14562816 | tf_op jit(solution)/shard_map/ste,de->std/dot_general | solution.py:762
  348.3 8.7 %select_reduce_fusion.5 = (f32[2,512]{1,0:T(2,128)S(1)}, f32[2,512]{1,0:T(2,128)S(1)}, f32[2,512]{1,0:T(2,128)S(1)}, f32[2,512]{1,0:T(2,128)S(1)}, f32[2,512]{1,0:T(2,128)S(1)}, /*index=5*/f32[2,512]{1,0:T(2,128)S(1)}) fusion(pred[512,1024]{1,0:T(8,128)(4,1)S(1)} %copy-done.39, pred[512,1024]{1,0:T(8,128)(4,1)S(1)} %copy-done.31, ...), kind=kOutput, calls=%fused_computation.46 | convolution fusion | flops 4845987840 | bytes 12610560 | tf_op jit(solution)/shard_map/transpose(jvp(ntd,njd->ntj))/dot_general | solution.py:711
  362.6 7.6 %add_convert_fusion.1 = bf16[2,1024,768]{2,1,0:T(8,128)(2,1)S(1)} fusion(f32[768]{0:T(1024)S(1)} %mul.1082, f32[2,1024]{1,0:T(2,128)S(1)} %fusion.105, f32[2,512,768]{2,1,0:T(8,128)} %copy-done.14, bf16[2,512]{1,0:T(2,128)(2,1)S(1)} %copy-done.123, bf16[2,512]{1,0:T(2,128)(2,1)S(1)} %copy-done.115, bf16[2,512]{1,0:T(2,128)(2,1)S(1)} %copy-done.117, ...), kind=kOutput, calls=%fused_computation.25 | convolution fusion | flops 1621622784 | bytes 9460736 | tf_op jit(solution)/shard_map/transpose(jvp(ntj,ntd->njd))/dot_general | solution.py:711
  370.2 4.8 pad_slice_fusion.2
  375.1 5.5 fusion.78
  381.1 9.6 %pad_maximum_fusion.2 = bf16[2,1024,3072]{2,1,0:T(8,128)(2,1)} fusion(bf16[2,1024,768]{2,1,0:T(8,128)(2,1)S(1)} %add_convert_fusion.1, bf16[2,1024,768]{2,1,0:T(8,128)(2,1)} %get-tuple-element.87, bf16[2,1024,768]{2,1,0:T(8,128)(2,1)} %get-tuple-element.86, bf16[2,1024,768]{2,1,0:T(8,128)(2,1)} %get-tuple-element.85), kind=kLoop, calls=%fused_computation.6 | loop fusion | flops 50331648 | bytes 25165824 | tf_op jit(solution)/shard_map/concatenate | solution.py:774
  390.8 16.5 %fusion.73 = bf16[256,768]{1,0:T(8,128)(2,1)} fusion(bf16[4,768,768,1]{2,1,0,3:T(8,128)(2,1)} %bitcast.395, bf16[2,128,4,8,768]{4,3,2,1,0:T(8,128)(2,1)} %bitcast.393, bf16[2,1024]{1,0:T(2,128)(2,1)S(1)} %copy-done.83, s32[2,1024]{1,0:T(2,128)S(1)} %copy-done.139), kind=kOutput, calls=%fused_computation.115 | convolution fusion | flops 10472849408 | bytes 17707008 | tf_op jit(solution)/shard_map/xpg,xpz->gz/dot_general | solution.py:785
  407.2 17.8 %bitcast_convert_fusion.1 = bf16[3072,768]{1,0:T(8,128)(2,1)} fusion(bf16[2,1024,768]{2,1,0:T(8,128)(2,1)S(1)} %add_convert_fusion.1, bf16[2,1024,768]{2,1,0:T(8,128)(2,1)} %copy-done.13, bf16[2,1024,768]{2,1,0:T(8,128)(2,1)} %get-tuple-element.91, bf16[2,1024,768]{2,1,0:T(8,128)(2,1)} %get-tuple-element.90, bf16[2,1024,768]{2,1,0:T(8,128)(2,1)} %get-tuple-element.89), kind=kOutput, calls=%fused_computation.10 | convolution fusion | flops 9716367360 | bytes 20447232 | tf_op jit(solution)/shard_map/xwu,xwo->uo/dot_general | solution.py:770
  425.0 3.7 copy_bitcast_fusion.x_ref
  428.8 72.6 %shard_map.1954 = f32[112,768]{1,0:T(8,128)S(1)} custom-call(bf16[2,16,112,768]{3,2,1,0:T(8,128)(2,1)S(1)} %copy_bitcast_fusion.x_ref), custom_call_target="tpu_custom_call" | custom-call | flops 5505024 | bytes 11010048 | tf_op jit(solution)/shard_map/pallas_call | solution.py:430
  501.6 7.3 %convolution_add_fusion.1 = f32[2,512,768]{2,1,0:T(8,128)} fusion(f32[2,512,768]{2,1,0:T(8,128)S(1)} %copy-done.3, bf16[2,512,2048]{2,1,0:T(8,128)(2,1)} %get-tuple-element.84, bf16[2048,768,1]{1,0,2:T(8,128)(2,1)S(1)} %copy-done.12), kind=kOutput, calls=%fused_computation.111 | convolution fusion | flops 3222011904 | bytes 13631488 | tf_op jit(solution)/shard_map/stf,fd->std/dot_general | solution.py:728
  513.4 13.4 %shard_map.1955 = f32[80,128]{1,0:T(8,128)} custom-call(f32[80,128]{1,0:T(8,128)} %pad_bitcast_fusion.x_ref), custom_call_target="tpu_custom_call" | custom-call | flops 163840 | bytes 655360 | tf_op jit(solution)/shard_map/pallas_call | solution.py:504
  (489 shorter events, 103.0 us)
Async XLA Ops:
  7.2 79.5 %all-gather.4.cloned.1.call-start = ((), (), s32[]{:S(2)}) async-start(), calls=%async_computation.1 | async-start | bytes 5677056 | tf_op jit(solution)/shard_map/all_gather | solution.py:673
  10.5 160.6 %all-gather.6.cloned.1.call-start = ((), (), s32[]{:S(2)}) async-start(), calls=%async_computation.2 | async-start | bytes 9732096 | tf_op jit(solution)/shard_map/all_gather | solution.py:678
  12.6 71.0 %copy-start.84 = (s32[2]{0:T(128)S(1)}, s32[2]{0:T(128)}, u32[]{:S(2)}) copy-start(s32[2]{0:T(128)} %len_ref.3) | copy-start | bytes 28
  13.4 495.5 %reduce-scatter.2.cloned.1.call-start = ((), (), s32[]{:S(2)}) async-start(), calls=%async_computation.3 | async-start | bytes 14598144 | tf_op jit(solution)/shard_map/reduce_scatter | solution.py:794
  83.6 38.6 %copy-start.80 = (f32[256]{0:T(256)}, f32[256]{0:T(256)S(1)}, u32[]{:S(2)}) copy-start(f32[256]{0:T(256)S(1)} %minimum_convert_fusion.3) | copy-start | bytes 3076
  83.6 37.6 %copy-start.56 = (f32[512]{0:T(512)}, f32[512]{0:T(512)S(1)}, u32[]{:S(2)}) copy-start(f32[512]{0:T(512)S(1)} %minimum_convert_fusion.2) | copy-start | bytes 6148
  83.6 39.5 %copy-start.58 = (f32[342]{0:T(512)}, f32[342]{0:T(512)S(1)}, u32[]{:S(2)}) copy-start(f32[342]{0:T(512)S(1)} %minimum_convert_fusion.1) | copy-start | bytes 4108
  83.7 39.9 %copy-start.52 = (f32[1024]{0:T(1024)}, f32[1024]{0:T(1024)S(1)}, u32[]{:S(2)}) copy-start(f32[1024]{0:T(1024)S(1)} %minimum_convert_fusion) | copy-start | bytes 12292
  93.1 33.4 %copy-start.54 = (f32[768]{0:T(1024)}, f32[768]{0:T(1024)S(1)}, u32[]{:S(2)}) copy-start(f32[768]{0:T(1024)S(1)} %add.1010) | copy-start | bytes 9220
  126.2 157.9 %copy-start.60 = (f32[768]{0:T(1024)}, f32[768]{0:T(1024)S(1)}, u32[]{:S(2)}) copy-start(f32[768]{0:T(1024)S(1)} %mul.1031) | copy-start | bytes 9220
  134.1 150.0 %copy-start.62 = (f32[2,512]{1,0:T(2,128)}, f32[2,512]{1,0:T(2,128)S(1)}, u32[]{:S(2)}) copy-start(f32[2,512]{1,0:T(2,128)S(1)} %fusion.161) | copy-start | bytes 12292
  141.8 21.8 %copy-start.5 = (f32[2,512,768]{2,1,0:T(8,128)S(1)}, f32[2,512,768]{2,1,0:T(8,128)}, u32[]{:S(2)}) copy-start(f32[2,512,768]{2,1,0:T(8,128)} %copy-done.4) | copy-start | bytes 9437188
  190.6 17.5 %copy-start.2 = (f32[2,512,768]{2,1,0:T(8,128)S(1)}, f32[2,512,768]{2,1,0:T(8,128)}, u32[]{:S(2)}) copy-start(f32[2,512,768]{2,1,0:T(8,128)} %get-tuple-element.153) | copy-start | bytes 9437188
  318.8 28.2 %slice-start.2 = ((s8[6291456]{0:T(1024)(128)(4,1)}), s8[2097152]{0:T(1024)(128)(4,1)S(1)}, s32[]{:S(2)}) async-start(s8[6291456]{0:T(1024)(128)(4,1)} %bitcast.391), calls=%async_computation.6 | async-start | bytes 4194304
  425.0 76.4 %copy-start.12 = (bf16[2048,768,1]{1,0,2:T(8,128)(2,1)S(1)}, bf16[2048,768,1]{1,0,2:T(8,128)(2,1)}, u32[]{:S(2)}) copy-start(bf16[2048,768,1]{1,0,2:T(8,128)(2,1)} %reshape.4267) | copy-start | bytes 9437188
  428.7 72.7 %copy-start.3 = (f32[2,512,768]{2,1,0:T(8,128)S(1)}, f32[2,512,768]{2,1,0:T(8,128)}, u32[]{:S(2)}) copy-start(f32[2,512,768]{2,1,0:T(8,128)} %get-tuple-element.153) | copy-start | bytes 9437188
  508.9 17.9 %copy-start.126 = (s32[23]{0:T(128)S(1)}, s32[23]{0:T(128)}, u32[]{:S(2)}) copy-start(s32[23]{0:T(128)} %constant.316.clone) | copy-start | bytes 280
  508.9 17.9 %copy-start.127 = (s32[23]{0:T(128)S(1)}, s32[23]{0:T(128)}, u32[]{:S(2)}) copy-start(s32[23]{0:T(128)} %constant.317.clone) | copy-start | bytes 280
  508.9 21.6 %copy-start.20 = (bf16[24,9216]{1,0:T(8,128)(2,1)S(1)}, bf16[24,9216]{1,0:T(8,128)(2,1)}, u32[]{:S(2)}) copy-start(bf16[24,9216]{1,0:T(8,128)(2,1)} %reduce-scatter.2.cloned.1.call-done) | copy-start | bytes 1327108
  533.1 20.2 %copy-start.68 = (f32[4096]{0:T(1024)S(1)}, f32[4096]{0:T(1024)}, u32[]{:S(2)}) copy-start(f32[4096]{0:T(1024)} %param.208) | copy-start | bytes 49156
  533.1 20.2 %copy-start.72 = (f32[2304]{0:T(1024)S(1)}, f32[2304]{0:T(1024)}, u32[]{:S(2)}) copy-start(f32[2304]{0:T(1024)} %param.202) | copy-start | bytes 27652
  533.1 21.1 %copy-start.125 = (f32[192]{0:T(256)S(1)}, f32[192]{0:T(256)}, u32[]{:S(2)}) copy-start(f32[192]{0:T(256)} %param.198) | copy-start | bytes 2308
  533.1 25.8 %copy-start.76 = (f32[768]{0:T(1024)S(1)}, f32[768]{0:T(1024)}, u32[]{:S(2)}) copy-start(f32[768]{0:T(1024)} %param.211) | copy-start | bytes 9220
  533.2 25.8 %copy-start.77 = (f32[768]{0:T(1024)S(1)}, f32[768]{0:T(1024)}, u32[]{:S(2)}) copy-start(f32[768]{0:T(1024)} %param.205) | copy-start | bytes 9220
  533.2 25.8 %copy-start.78 = (f32[768]{0:T(1024)S(1)}, f32[768]{0:T(1024)}, u32[]{:S(2)}) copy-start(f32[768]{0:T(1024)} %param.199) | copy-start | bytes 9220
  533.2 25.8 %copy-start.79 = (f32[768]{0:T(1024)S(1)}, f32[768]{0:T(1024)}, u32[]{:S(2)}) copy-start(f32[768]{0:T(1024)} %param.196) | copy-start | bytes 9220
  533.2 25.9 %copy-start.71 = (f32[4,48]{1,0:T(4,128)S(1)}, f32[4,48]{1,0:T(4,128)}, u32[]{:S(2)}) copy-start(f32[4,48]{1,0:T(4,128)} %param.193) | copy-start | bytes 2308
  533.2 25.9 %copy-start.110 = (f32[4,48]{1,0:T(4,128)S(1)}, f32[4,48]{1,0:T(4,128)}, u32[]{:S(2)}) copy-start(f32[4,48]{1,0:T(4,128)} %param.212) | copy-start | bytes 2308
  533.2 25.9 %copy-start.111 = (f32[4,48]{1,0:T(4,128)S(1)}, f32[4,48]{1,0:T(4,128)}, u32[]{:S(2)}) copy-start(f32[4,48]{1,0:T(4,128)} %param.213) | copy-start | bytes 2308
  533.2 27.3 %copy-start.16 = (f32[48,4096]{1,0:T(8,128)S(1)}, f32[48,4096]{1,0:T(8,128)}, u32[]{:S(2)}) copy-start(f32[48,4096]{1,0:T(8,128)} %param.191) | copy-start | bytes 2359300
  539.4 24.3 %copy-start.40 = (f32[48,768]{1,0:T(8,128)S(1)}, f32[48,768]{1,0:T(8,128)}, u32[]{:S(2)}) copy-start(f32[48,768]{1,0:T(8,128)} %param.190) | copy-start | bytes 442372
  540.6 26.2 %copy-start.128 = (f32[128]{0:T(128)}, f32[128]{0:T(128)S(1)}, u32[]{:S(2)}) copy-start(f32[128]{0:T(128)S(1)} %multiply_add_fusion.9) | copy-start | bytes 1540
  (117 other events, 808.4 us)
Sparse Core Ops, SparseCore 0:
  11.5 73.7 all-gather.3
  88.7 82.2 all-gather.5
  319.0 173.5 reduce-scatter.1

commit v14 on v13

--- a/solution.py
+++ b/solution.py
@@ -521,7 +521,7 @@
     )(x)
 
 
-def ring_ag_kernel(snake, x_ref, out_ref, send_sem, recv_sem, pair_sem):
+def ring_ag_kernel(snake, x_ref, out_ref, send_sem, recv_sem, pair_sem, hand_sem):
     count = out_ref.shape[0] // 2
     steps = count - 1
     half = out_ref.shape[2] // 2
@@ -543,6 +543,11 @@
     pl.semaphore_wait(barrier, 3)
 
     out_ref[2 * chip + core] = x_ref[...]
+    mine = pltpu.make_async_remote_copy(
+        src_ref=x_ref, dst_ref=out_ref.at[2 * chip + core],
+        send_sem=pair_sem.at[0], recv_sem=pair_sem.at[1],
+        device_id=partner, device_id_type=MESH_ID)
+    mine.start()
 
     def slot(way, step):
         spot = (here - step + count) % count if way == 0 else (here + step) % count
@@ -559,17 +564,28 @@
     for way in range(4):
         link(way, 0, slot(ways[way][0], 0)).start()
 
+    def hand(way, step, index):
+        direction, first, width = ways[way]
+        cols = pl.ds(first, width)
+        return pltpu.make_async_remote_copy(
+            src_ref=out_ref.at[index, :, cols], dst_ref=out_ref.at[index, :, cols],
+            send_sem=hand_sem.at[0, way, step], recv_sem=hand_sem.at[1, way, step],
+            device_id=partner, device_id_type=MESH_ID)
+
     def step_body(step, carry):
         for way in range(4):
             index = slot(ways[way][0], step)
             link(way, step - 1, index).wait_recv()
             link(way, step, index).start()
+            hand(way, step - 1, index).start()
         return carry
 
     lax.fori_loop(1, steps, step_body, 0)
 
     for way in range(4):
-        link(way, steps - 1, slot(ways[way][0], steps)).wait_recv()
+        index = slot(ways[way][0], steps)
+        link(way, steps - 1, index).wait_recv()
+        hand(way, steps - 1, index).start()
 
     def drain(step, carry):
         for way in range(4):
@@ -578,25 +594,16 @@
 
     lax.fori_loop(0, steps, drain, 0)
 
-    def pair(other):
-        index = 2 * other + core
-        return pltpu.make_async_remote_copy(
-            src_ref=out_ref.at[index], dst_ref=out_ref.at[index],
-            send_sem=pair_sem.at[0, other], recv_sem=pair_sem.at[1, other],
-            device_id=partner, device_id_type=MESH_ID)
-
-    def pair_start(other, carry):
-        pair(other).start()
+    def hand_wait(step, carry):
+        for way in range(4):
+            index = slot(ways[way][0], step + 1)
+            hand(way, step, index).wait_send()
+            hand(way, step, index).wait_recv()
         return carry
 
-    lax.fori_loop(0, count, pair_start, 0)
-
-    def pair_wait(other, carry):
-        pair(other).wait_send()
-        pair(other).wait_recv()
-        return carry
-
-    lax.fori_loop(0, count, pair_wait, 0)
+    lax.fori_loop(0, steps, hand_wait, 0)
+    mine.wait_send()
+    mine.wait_recv()
 
 
 def ring_all_gather(x, snake):
@@ -610,7 +617,8 @@
         scratch_shapes=[
             pltpu.SemaphoreType.DMA((4, count - 1)),
             pltpu.SemaphoreType.DMA((4, count - 1)),
-            pltpu.SemaphoreType.DMA((2, count)),
+            pltpu.SemaphoreType.DMA((2,)),
+            pltpu.SemaphoreType.DMA((2, 4, count - 1)),
         ],
         compiler_params=pltpu.CompilerParams(collective_id=2, has_side_effects=True,
                                              vmem_limit_bytes=48 * 1024 * 1024),

time: 586 us -> 587 us (level)
  transfers between devices with their start and end apart: 3 -> 3, of which waited for: 1 -> 2; matrix products, arithmetic and copies ran while one was open for 31% -> 31% of each run, Pallas kernels for 28% -> 27%
where the time goes in v14:
time: 587 us; the launch traced here: 578 us
  Pallas kernels  206 us (35%)
  matrix products  190 us (32%)
  other arithmetic  71.8 us (12%)
  local copies, waits for them, and re-layouts  69.3 us (12%)
  between operations  30.6 us (5%)
    pallas_call x1, Pallas kernels, ring_reduce_scatter(): pl.pallas_call(functools.partial(ring_rs_kernel, snake), out_shape=jax.Sh...  73.5 us
    pallas_call x1, Pallas kernels, ring_all_gather(): pl.pallas_call(functools.partial(ring_ag_kernel, snake), out_shape=jax.Sh...  63.6 us
    pallas_call x1, Pallas kernels, attention_backward(): pl.pallas_call(attn_bwd_kernel, out_shape=(part, part, part), grid_spec=p...  34.2 us
    dot_general x3, matrix products, body(): tokens, gbst_pull = jax.vjp(gbst_tokens, hidden, vector_vals[3])  21.8 us
    pallas_call x1, Pallas kernels, attention_forward(): pl.pallas_call(attn_fwd_kernel, out_shape=jax.ShapeDtypeStruct((count_ite...  21.8 us
    dot_general x1, matrix products, body(): jnp.einsum('xwu,xwo->uo', byte_windows, gradient_hidden_reduced, preferre...  17.8 us
    dot_general x1, matrix products, body(): jnp.einsum('std,fd->stf', cotangent, back_contract, preferred_element_typ...  17.5 us
    dot_general x1, matrix products, body(): jnp.einsum('xpg,xpz->gz', one_hot_bytes, gradient_embedded_bytes, preferr...  16.5 us
  transfers between devices with their start and end apart: 3, of which 2 were waited for; matrix products, arithmetic and copies ran while one was open for 31% of the time, Pallas kernels for 27%

profile of v14, /device:TPU:0, one launch (start us, length us, event | category | flops | bytes accessed | tf_op | source)
XLA Modules:
  0.0 578.1 jit_solution(5957680505461201442)
XLA Ops:
  15.3 63.6 %shard_map.1951 = bf16[32,24,3072]{2,1,0:T(8,128)(2,1)S(1)} custom-call(bf16[24,3072]{1,0:T(8,128)(2,1)S(1)} %pad_maximum_fusion.7.x_ref), custom_call_target="tpu_custom_call" | custom-call | bytes 9437184 | tf_op jit(solution)/shard_map/pallas_call | solution.py:612
  85.5 4.8 slice.373
  94.5 4.6 pad_slice_fusion.5
  99.1 14.0 %fusion.30 = f32[2,1024,768]{2,1,0:T(8,128)S(1)} fusion(bf16[3072,768,1]{1,0,2:T(8,128)(2,1)} %bitcast.394, bf16[2,1024,768]{2,1,0:T(8,128)(2,1)} %copy-done.13, bf16[2,1024,768]{2,1,0:T(8,128)(2,1)} %get-tuple-element.91, bf16[2,1024,768]{2,1,0:T(8,128)(2,1)} %get-tuple-element.90, bf16[2,1024,768]{2,1,0:T(8,128)(2,1)} %get-tuple-element.89), kind=kOutput, calls=%fused_computation.75 | convolution fusion | flops 9714008064 | bytes 23592960 | tf_op jit(solution)/shard_map/hby,yj->hbj/dot_general | solution.py:716
  125.4 7.4 %multiply_reduce_fusion.5 = (f32[2,512]{1,0:T(2,128)S(1)}, f32[2,512,768]{2,1,0:T(8,128)S(1)}) fusion(f32[2,1024,768]{2,1,0:T(8,128)} %copy-done.1, f32[768]{0:T(1024)S(1)} %add.1010, bf16[2,512]{1,0:T(2,128)(2,1)S(1)} %get-tuple-element.119, bf16[2,512]{1,0:T(2,128)(2,1)S(1)} %get-tuple-element.115, bf16[2,512]{1,0:T(2,128)(2,1)S(1)} %get-tuple-element.116, ...), kind=kOutput, calls=%fused_computation.61 | convolution fusion | flops 1620048896 | bytes 12602368 | tf_op jit(solution)/shard_map/jvp(ntj,njd->ntd)/dot_general | solution.py:112
  134.6 6.0 %convolution_convert_fusion.q_ref.k_ref.v_ref = bf16[2,512,2304]{2,1,0:T(8,128)(2,1)} fusion(bf16[768,3072]{1,0:T(8,128)(2,1)S(1)} %bitcast.390, f32[2,512,768]{2,1,0:T(8,128)S(1)} %get-tuple-element.151, f32[768]{0:T(1024)S(1)} %mul.1031, f32[2,512]{1,0:T(2,128)S(1)} %fusion.161), kind=kOutput, calls=%fused_computation.26 | convolution fusion | flops 3628597248 | bytes 11411456 | tf_op jit(solution)/shard_map/std,de->ste/dot_general | solution.py:722
  140.6 21.8 %shard_map.1952 = bf16[2,512,768]{2,1,0:T(8,128)(2,1)} custom-call(s32[2]{0:T(128)} %len_ref.3, bf16[2,512,2304]{2,1,0:T(8,128)(2,1)} %convolution_convert_fusion.q_ref.k_ref.v_ref, bf16[2,512,2304]{2,1,0:T(8,128)(2,1)} %convolution_convert_fusion.q_ref.k_ref.v_ref, bf16[2,512,2304]{2,1,0:T(8,128)(2,1)} %convolution_convert_fusion.q_ref.k_ref.v_ref), custom_call_target="tpu_custom_call" | custom-call | flops 3221225472 | bytes 6291456 | tf_op jit(solution)/shard_map/pallas_call | solution.py:262
  162.3 4.8 multiply_reduce_fusion.4
  167.2 4.3 all-gather.6.cloned.1.call-done
  173.4 4.4 reshape.4267
  177.7 13.2 %fusion.18 = f32[2,512,4096]{2,1,0:T(8,128)} fusion(bf16[768,6144]{1,0:T(8,128)(2,1)} %all-gather.6.cloned.1.call-done, f32[2,512,768]{2,1,0:T(8,128)} %get-tuple-element.153, f32[768]{0:T(1024)S(1)} %mul.1037, f32[2,512]{1,0:T(2,128)S(1)} %fusion.162), kind=kOutput, calls=%fused_computation.38 | convolution fusion | flops 6444810240 | bytes 26221568 | tf_op jit(solution)/shard_map/std,de->ste/dot_general | solution.py:733
  191.0 17.5 %bitcast_multiply_fusion.1 = (f32[2,512,2048]{2,1,0:T(8,128)}, f32[2,512,2048]{2,1,0:T(8,128)}, bf16[2,512,2048]{2,1,0:T(8,128)(2,1)}) fusion(f32[2,512,4096]{2,1,0:T(8,128)} %fusion.18, bf16[2048,768,1]{1,0,2:T(8,128)(2,1)S(1)} %copy-done.11, bf16[2,512,768]{2,1,0:T(8,128)(2,1)S(1)} %copy-done.24), kind=kOutput, calls=%fused_computation.18 | convolution fusion | flops 3271557120 | bytes 42467328 | tf_op jit(solution)/shard_map/std,fd->stf/dot_general | solution.py:746
  208.5 15.3 %bitcast_convert_fusion = bf16[768,4096]{1,0:T(8,128)(2,1)} fusion(f32[2,512,2048]{2,1,0:T(8,128)} %get-tuple-element.83, f32[2,512,2048]{2,1,0:T(8,128)} %get-tuple-element.82, f32[2,512,768]{2,1,0:T(8,128)S(1)} %copy-done.2, f32[768]{0:T(1024)S(1)} %mul.1037, f32[2,512]{1,0:T(2,128)S(1)} %fusion.162), kind=kOutput, calls=%fused_computation.7 | convolution fusion | flops 6456344576 | bytes 26221568 | tf_op jit(solution)/shard_map/std,ste->de/dot_general | solution.py:751
  223.7 14.4 %multiply_reduce_fusion = (bf16[768]{0:T(1024)(128)(2,1)}, f32[2,512]{1,0:T(2,128)S(1)}, f32[2,512,768]{2,1,0:T(8,128)}) fusion(f32[2,512,768]{2,1,0:T(8,128)S(1)} %copy-done.2, f32[2,512]{1,0:T(2,128)S(1)} %fusion.162, f32[768]{0:T(1024)S(1)} %mul.1037, bf16[768,6144]{1,0:T(8,128)(2,1)} %all-gather.6.cloned.1.call-done, ...), kind=kOutput, calls=%fused_computation.54 | convolution fusion | flops 6455556096 | bytes 29372928 | tf_op jit(solution)/shard_map/ste,de->std/dot_general | solution.py:754
  241.4 4.9 convolution_convert_fusion.1.do_ref
  247.8 34.2 %shard_map.1953 = (bf16[2,512,768]{2,1,0:T(8,128)(2,1)}, bf16[2,512,768]{2,1,0:T(8,128)(2,1)}, bf16[2,512,768]{2,1,0:T(8,128)(2,1)}) custom-call(s32[2]{0:T(128)} %len_ref.3, bf16[2,512,2304]{2,1,0:T(8,128)(2,1)} %convolution_convert_fusion.q_ref.k_ref.v_ref, bf16[2,512,2304]{2,1,0:T(8,128)(2,1)} %convolution_convert_fusion.q_ref.k_ref.v_ref, ...), custom_call_target="tpu_custom_call" | custom-call | flops 8053063680 | bytes 11010048 | tf_op jit(solution)/shard_map/pallas_call | solution.py:284
  286.6 5.6 bitcast_convert_fusion.2
  294.1 7.4 %bitcast_convert_fusion.3 = bf16[2048,768]{1,0:T(8,128)(2,1)} fusion(bf16[2,512,2048]{2,1,0:T(8,128)(2,1)} %get-tuple-element.84, bf16[2,512,768]{2,1,0:T(8,128)(2,1)S(1)} %copy-done.25), kind=kOutput, calls=%fused_computation.23 | convolution fusion | flops 3222798336 | bytes 8912896 | tf_op jit(solution)/shard_map/stf,std->fd/dot_general | solution.py:743
  301.4 5.5 reshape.4241
  306.9 12.3 %pad_maximum_fusion = bf16[768,9216]{1,0:T(8,128)(2,1)} fusion(bf16[768,2048]{1,0:T(8,128)(2,1)S(1)} %reshape.4241, bf16[768,4096]{1,0:T(8,128)(2,1)} %bitcast_convert_fusion, bf16[768,768]{1,0:T(8,128)(2,1)} %copy.271, bf16[768,2304]{1,0:T(8,128)(2,1)} %bitcast_convert_fusion.2), kind=kLoop, calls=%fused_computation.1 | loop fusion | flops 56623104 | bytes 28311552 | tf_op jit(solution)/shard_map/concatenate | solution.py:799
  337.0 9.4 %multiply_reduce_fusion.1 = (bf16[768]{0:T(1024)(128)(2,1)S(1)}, f32[2,512]{1,0:T(2,128)S(1)}, f32[2,512,768]{2,1,0:T(8,128)S(1)}) fusion(f32[2,512,768]{2,1,0:T(8,128)} %copy-done.4, f32[2,512]{1,0:T(2,128)} %copy-done.62, f32[768]{0:T(1024)} %copy-done.60, bf16[2,512,2304]{2,1,0:T(8,128)(2,1)} %copy-done.29, bf16[768,3072]{1,0:T(8,128)(2,1)} %bitcast.387), kind=kOutput, calls=%fused_computation.55 | convolution fusion | flops 3628595456 | bytes 14562816 | tf_op jit(solution)/shard_map/ste,de->std/dot_general | solution.py:770
  348.6 8.7 %select_reduce_fusion.5 = (f32[2,512]{1,0:T(2,128)S(1)}, f32[2,512]{1,0:T(2,128)S(1)}, f32[2,512]{1,0:T(2,128)S(1)}, f32[2,512]{1,0:T(2,128)S(1)}, f32[2,512]{1,0:T(2,128)S(1)}, /*index=5*/f32[2,512]{1,0:T(2,128)S(1)}) fusion(pred[512,1024]{1,0:T(8,128)(4,1)S(1)} %copy-done.39, pred[512,1024]{1,0:T(8,128)(4,1)S(1)} %copy-done.31, ...), kind=kOutput, calls=%fused_computation.46 | convolution fusion | flops 4845987840 | bytes 12610560 | tf_op jit(solution)/shard_map/transpose(jvp(ntd,njd->ntj))/dot_general | solution.py:719
  362.9 7.6 %add_convert_fusion.1 = bf16[2,1024,768]{2,1,0:T(8,128)(2,1)S(1)} fusion(f32[768]{0:T(1024)S(1)} %mul.1082, f32[2,1024]{1,0:T(2,128)S(1)} %fusion.105, f32[2,512,768]{2,1,0:T(8,128)} %copy-done.14, bf16[2,512]{1,0:T(2,128)(2,1)S(1)} %copy-done.123, bf16[2,512]{1,0:T(2,128)(2,1)S(1)} %copy-done.115, bf16[2,512]{1,0:T(2,128)(2,1)S(1)} %copy-done.117, ...), kind=kOutput, calls=%fused_computation.25 | convolution fusion | flops 1621622784 | bytes 9460736 | tf_op jit(solution)/shard_map/transpose(jvp(ntj,ntd->njd))/dot_general | solution.py:719
  370.5 4.8 pad_slice_fusion.2
  375.4 5.5 fusion.78
  381.5 9.6 %pad_maximum_fusion.2 = bf16[2,1024,3072]{2,1,0:T(8,128)(2,1)} fusion(bf16[2,1024,768]{2,1,0:T(8,128)(2,1)S(1)} %add_convert_fusion.1, bf16[2,1024,768]{2,1,0:T(8,128)(2,1)} %get-tuple-element.87, bf16[2,1024,768]{2,1,0:T(8,128)(2,1)} %get-tuple-element.86, bf16[2,1024,768]{2,1,0:T(8,128)(2,1)} %get-tuple-element.85), kind=kLoop, calls=%fused_computation.6 | loop fusion | flops 50331648 | bytes 25165824 | tf_op jit(solution)/shard_map/concatenate | solution.py:782
  391.1 16.5 %fusion.73 = bf16[256,768]{1,0:T(8,128)(2,1)} fusion(bf16[4,768,768,1]{2,1,0,3:T(8,128)(2,1)} %bitcast.395, bf16[2,128,4,8,768]{4,3,2,1,0:T(8,128)(2,1)} %bitcast.393, bf16[2,1024]{1,0:T(2,128)(2,1)S(1)} %copy-done.83, s32[2,1024]{1,0:T(2,128)S(1)} %copy-done.139), kind=kOutput, calls=%fused_computation.115 | convolution fusion | flops 10472849408 | bytes 17707008 | tf_op jit(solution)/shard_map/xpg,xpz->gz/dot_general | solution.py:793
  407.6 17.8 %bitcast_convert_fusion.1 = bf16[3072,768]{1,0:T(8,128)(2,1)} fusion(bf16[2,1024,768]{2,1,0:T(8,128)(2,1)S(1)} %add_convert_fusion.1, bf16[2,1024,768]{2,1,0:T(8,128)(2,1)} %copy-done.13, bf16[2,1024,768]{2,1,0:T(8,128)(2,1)} %get-tuple-element.91, bf16[2,1024,768]{2,1,0:T(8,128)(2,1)} %get-tuple-element.90, bf16[2,1024,768]{2,1,0:T(8,128)(2,1)} %get-tuple-element.89), kind=kOutput, calls=%fused_computation.10 | convolution fusion | flops 9716367360 | bytes 20447232 | tf_op jit(solution)/shard_map/xwu,xwo->uo/dot_general | solution.py:778
  425.3 3.7 copy_bitcast_fusion.x_ref
  429.1 73.5 %shard_map.1954 = f32[112,768]{1,0:T(8,128)S(1)} custom-call(bf16[2,16,112,768]{3,2,1,0:T(8,128)(2,1)S(1)} %copy_bitcast_fusion.x_ref), custom_call_target="tpu_custom_call" | custom-call | flops 5505024 | bytes 11010048 | tf_op jit(solution)/shard_map/pallas_call | solution.py:430
  502.8 7.3 %convolution_add_fusion.1 = f32[2,512,768]{2,1,0:T(8,128)} fusion(f32[2,512,768]{2,1,0:T(8,128)S(1)} %copy-done.3, bf16[2,512,2048]{2,1,0:T(8,128)(2,1)} %get-tuple-element.84, bf16[2048,768,1]{1,0,2:T(8,128)(2,1)S(1)} %copy-done.12), kind=kOutput, calls=%fused_computation.111 | convolution fusion | flops 3222011904 | bytes 13631488 | tf_op jit(solution)/shard_map/stf,fd->std/dot_general | solution.py:736
  514.7 12.5 %shard_map.1955 = f32[80,128]{1,0:T(8,128)} custom-call(f32[80,128]{1,0:T(8,128)} %pad_bitcast_fusion.x_ref), custom_call_target="tpu_custom_call" | custom-call | flops 163840 | bytes 655360 | tf_op jit(solution)/shard_map/pallas_call | solution.py:504
  (489 shorter events, 104.7 us)
Async XLA Ops:
  7.2 78.3 %all-gather.4.cloned.1.call-start = ((), (), s32[]{:S(2)}) async-start(), calls=%async_computation.1 | async-start | bytes 5677056 | tf_op jit(solution)/shard_map/all_gather | solution.py:681
  10.5 161.0 %all-gather.6.cloned.1.call-start = ((), (), s32[]{:S(2)}) async-start(), calls=%async_computation.2 | async-start | bytes 9732096 | tf_op jit(solution)/shard_map/all_gather | solution.py:686
  12.6 68.6 %copy-start.84 = (s32[2]{0:T(128)S(1)}, s32[2]{0:T(128)}, u32[]{:S(2)}) copy-start(s32[2]{0:T(128)} %len_ref.3) | copy-start | bytes 28
  13.4 496.7 %reduce-scatter.2.cloned.1.call-start = ((), (), s32[]{:S(2)}) async-start(), calls=%async_computation.3 | async-start | bytes 14598144 | tf_op jit(solution)/shard_map/reduce_scatter | solution.py:802
  81.2 39.8 %copy-start.80 = (f32[256]{0:T(256)}, f32[256]{0:T(256)S(1)}, u32[]{:S(2)}) copy-start(f32[256]{0:T(256)S(1)} %minimum_convert_fusion.3) | copy-start | bytes 3076
  81.2 38.8 %copy-start.56 = (f32[512]{0:T(512)}, f32[512]{0:T(512)S(1)}, u32[]{:S(2)}) copy-start(f32[512]{0:T(512)S(1)} %minimum_convert_fusion.2) | copy-start | bytes 6148
  81.2 40.7 %copy-start.58 = (f32[342]{0:T(512)}, f32[342]{0:T(512)S(1)}, u32[]{:S(2)}) copy-start(f32[342]{0:T(512)S(1)} %minimum_convert_fusion.1) | copy-start | bytes 4108
  81.3 41.1 %copy-start.52 = (f32[1024]{0:T(1024)}, f32[1024]{0:T(1024)S(1)}, u32[]{:S(2)}) copy-start(f32[1024]{0:T(1024)S(1)} %minimum_convert_fusion) | copy-start | bytes 12292
  91.9 33.4 %copy-start.54 = (f32[768]{0:T(1024)}, f32[768]{0:T(1024)S(1)}, u32[]{:S(2)}) copy-start(f32[768]{0:T(1024)S(1)} %add.1010) | copy-start | bytes 9220
  125.0 159.5 %copy-start.60 = (f32[768]{0:T(1024)}, f32[768]{0:T(1024)S(1)}, u32[]{:S(2)}) copy-start(f32[768]{0:T(1024)S(1)} %mul.1031) | copy-start | bytes 9220
  132.9 151.6 %copy-start.62 = (f32[2,512]{1,0:T(2,128)}, f32[2,512]{1,0:T(2,128)S(1)}, u32[]{:S(2)}) copy-start(f32[2,512]{1,0:T(2,128)S(1)} %fusion.161) | copy-start | bytes 12292
  140.6 21.8 %copy-start.5 = (f32[2,512,768]{2,1,0:T(8,128)S(1)}, f32[2,512,768]{2,1,0:T(8,128)}, u32[]{:S(2)}) copy-start(f32[2,512,768]{2,1,0:T(8,128)} %copy-done.4) | copy-start | bytes 9437188
  191.0 17.5 %copy-start.2 = (f32[2,512,768]{2,1,0:T(8,128)S(1)}, f32[2,512,768]{2,1,0:T(8,128)}, u32[]{:S(2)}) copy-start(f32[2,512,768]{2,1,0:T(8,128)} %get-tuple-element.153) | copy-start | bytes 9437188
  319.2 28.1 %slice-start.2 = ((s8[6291456]{0:T(1024)(128)(4,1)}), s8[2097152]{0:T(1024)(128)(4,1)S(1)}, s32[]{:S(2)}) async-start(s8[6291456]{0:T(1024)(128)(4,1)} %bitcast.391), calls=%async_computation.6 | async-start | bytes 4194304
  425.3 77.3 %copy-start.12 = (bf16[2048,768,1]{1,0,2:T(8,128)(2,1)S(1)}, bf16[2048,768,1]{1,0,2:T(8,128)(2,1)}, u32[]{:S(2)}) copy-start(bf16[2048,768,1]{1,0,2:T(8,128)(2,1)} %reshape.4267) | copy-start | bytes 9437188
  429.1 73.6 %copy-start.3 = (f32[2,512,768]{2,1,0:T(8,128)S(1)}, f32[2,512,768]{2,1,0:T(8,128)}, u32[]{:S(2)}) copy-start(f32[2,512,768]{2,1,0:T(8,128)} %get-tuple-element.153) | copy-start | bytes 9437188
  510.1 17.1 %copy-start.126 = (s32[23]{0:T(128)S(1)}, s32[23]{0:T(128)}, u32[]{:S(2)}) copy-start(s32[23]{0:T(128)} %constant.316.clone) | copy-start | bytes 280
  510.1 17.1 %copy-start.127 = (s32[23]{0:T(128)S(1)}, s32[23]{0:T(128)}, u32[]{:S(2)}) copy-start(s32[23]{0:T(128)} %constant.317.clone) | copy-start | bytes 280
  510.2 20.8 %copy-start.20 = (bf16[24,9216]{1,0:T(8,128)(2,1)S(1)}, bf16[24,9216]{1,0:T(8,128)(2,1)}, u32[]{:S(2)}) copy-start(bf16[24,9216]{1,0:T(8,128)(2,1)} %reduce-scatter.2.cloned.1.call-done) | copy-start | bytes 1327108
  533.5 20.2 %copy-start.68 = (f32[4096]{0:T(1024)S(1)}, f32[4096]{0:T(1024)}, u32[]{:S(2)}) copy-start(f32[4096]{0:T(1024)} %param.208) | copy-start | bytes 49156
  533.6 20.2 %copy-start.72 = (f32[2304]{0:T(1024)S(1)}, f32[2304]{0:T(1024)}, u32[]{:S(2)}) copy-start(f32[2304]{0:T(1024)} %param.202) | copy-start | bytes 27652
  533.6 21.1 %copy-start.125 = (f32[192]{0:T(256)S(1)}, f32[192]{0:T(256)}, u32[]{:S(2)}) copy-start(f32[192]{0:T(256)} %param.198) | copy-start | bytes 2308
  533.6 25.8 %copy-start.76 = (f32[768]{0:T(1024)S(1)}, f32[768]{0:T(1024)}, u32[]{:S(2)}) copy-start(f32[768]{0:T(1024)} %param.211) | copy-start | bytes 9220
  533.6 25.8 %copy-start.77 = (f32[768]{0:T(1024)S(1)}, f32[768]{0:T(1024)}, u32[]{:S(2)}) copy-start(f32[768]{0:T(1024)} %param.205) | copy-start | bytes 9220
  533.6 25.8 %copy-start.78 = (f32[768]{0:T(1024)S(1)}, f32[768]{0:T(1024)}, u32[]{:S(2)}) copy-start(f32[768]{0:T(1024)} %param.199) | copy-start | bytes 9220
  533.6 25.8 %copy-start.79 = (f32[768]{0:T(1024)S(1)}, f32[768]{0:T(1024)}, u32[]{:S(2)}) copy-start(f32[768]{0:T(1024)} %param.196) | copy-start | bytes 9220
  533.6 25.9 %copy-start.71 = (f32[4,48]{1,0:T(4,128)S(1)}, f32[4,48]{1,0:T(4,128)}, u32[]{:S(2)}) copy-start(f32[4,48]{1,0:T(4,128)} %param.193) | copy-start | bytes 2308
  533.6 25.9 %copy-start.110 = (f32[4,48]{1,0:T(4,128)S(1)}, f32[4,48]{1,0:T(4,128)}, u32[]{:S(2)}) copy-start(f32[4,48]{1,0:T(4,128)} %param.212) | copy-start | bytes 2308
  533.7 25.9 %copy-start.111 = (f32[4,48]{1,0:T(4,128)S(1)}, f32[4,48]{1,0:T(4,128)}, u32[]{:S(2)}) copy-start(f32[4,48]{1,0:T(4,128)} %param.213) | copy-start | bytes 2308
  533.7 27.3 %copy-start.16 = (f32[48,4096]{1,0:T(8,128)S(1)}, f32[48,4096]{1,0:T(8,128)}, u32[]{:S(2)}) copy-start(f32[48,4096]{1,0:T(8,128)} %param.191) | copy-start | bytes 2359300
  539.8 24.3 %copy-start.40 = (f32[48,768]{1,0:T(8,128)S(1)}, f32[48,768]{1,0:T(8,128)}, u32[]{:S(2)}) copy-start(f32[48,768]{1,0:T(8,128)} %param.190) | copy-start | bytes 442372
  541.0 26.2 %copy-start.128 = (f32[128]{0:T(128)}, f32[128]{0:T(128)S(1)}, u32[]{:S(2)}) copy-start(f32[128]{0:T(128)S(1)} %multiply_add_fusion.9) | copy-start | bytes 1540
  (117 other events, 809.5 us)
Sparse Core Ops, SparseCore 0:
  11.5 73.9 all-gather.3
  89.0 82.4 all-gather.5
  319.4 174.0 reduce-scatter.1
